TPU v7x, 32 devices: a whole 2x2x4 slice. The times are simulated.
32 devices in a mesh: dp: 2 (over x), row: 4 (over y, core), col: 4 (over z).
Axes of the slice: x: 2, y: 2, z: 4, core: 2. Of those that a mesh axis runs over, the one named last changes fastest.
Arguments:
- tokens: bfloat16 [5120, 2048], P(('dp', 'col'), 'row'), may hold values from -6 to 6
- cotangent: bfloat16 [5120, 2048], P(('dp', 'col'), 'row'), may hold values from -6 to 6
- seg_ids: int32 [5120], P('dp'), may hold values from 0 to 12, as said below
- positions: int32 [5120], P('dp'), may hold values from 0 to 1279, as said below
- parents: int32 [2, 13], P('dp'), may hold values from 0 to 4, as said below
- tree_sets: int32 [2], P('dp'), may hold values from 0 to 7
- gain_q: float32 [2048], P('col'), may hold values from 0.25 to 1.75
- gain_k: float32 [2048], P('col'), may hold values from 0.25 to 1.75
- gain_attn: float32 [2048], P('row'), may hold values from 0.25 to 1.75
- gain_ffn: float32 [2048], P('row'), may hold values from 0.25 to 1.75
- query_key_value_weight: bfloat16 [2048, 3, 2048], P('row', None, 'col'), may hold values from -0.125 to 0.125
- output_weight: bfloat16 [2048, 2048], P('col', 'row'), may hold values from -0.125 to 0.125
- gate_up_weight: bfloat16 [2048, 2, 8192], P('row', None, 'col'), may hold values from -0.125 to 0.125
- down_weight: bfloat16 [8192, 2048], P('col', 'row'), may hold values from -0.0625 to 0.0625
- query_key_value_adapter_first: float32 [3, 8, 16, 2048], P(None, None, None, 'row'), may hold values from -0.125 to 0.125
- query_key_value_adapter_second: float32 [3, 8, 16, 2048], P(None, None, None, 'col'), may hold values from -0.5 to 0.5
- output_adapter_first: float32 [8, 16, 2048], P(None, None, 'col'), may hold values from -0.125 to 0.125
- output_adapter_second: float32 [8, 16, 2048], P(None, None, 'row'), may hold values from -0.5 to 0.5
- gate_up_adapter_first: float32 [2, 8, 16, 2048], P(None, None, None, 'row'), may hold values from -0.125 to 0.125
- gate_up_adapter_second: float32 [2, 8, 16, 8192], P(None, None, None, 'col'), may hold values from -0.5 to 0.5
- down_adapter_first: float32 [8, 16, 8192], P(None, None, 'col'), may hold values from -0.0625 to 0.0625
- down_adapter_second: float32 [8, 16, 2048], P(None, None, 'row'), may hold values from -0.5 to 0.5
Outputs:
- layer_out: bfloat16 [5120, 2048], P(('dp', 'col'), 'row')
- input_grad: float32 [5120, 2048], P(('dp', 'col'), 'row')
- grad_a_qkv: float32 [3, 8, 16, 2048], P(None, 'dp', 'col', 'row')
- grad_b_qkv: float32 [3, 8, 16, 2048], P(None, 'dp', 'row', 'col')
- grad_a_out: float32 [8, 16, 2048], P('dp', 'row', 'col')
- grad_b_out: float32 [8, 16, 2048], P('dp', 'col', 'row')
- grad_a_gu: float32 [2, 8, 16, 2048], P(None, 'dp', 'col', 'row')
- grad_b_gu: float32 [2, 8, 16, 8192], P(None, 'dp', 'row', 'col')
- grad_a_down: float32 [8, 16, 8192], P('dp', 'row', 'col')
- grad_b_down: float32 [8, 16, 2048], P('dp', 'col', 'row')
Inputs may be any that keep to these rules, and one draw needn't show every extreme that they name: `seg_ids`: in each tree the first 1024 tokens are segment 0, the trunk; the other 12 segments of 128 tokens each follow in any order: branches are 1 to 4, leaves the higher numbers. The trunk's tokens have positions 0 to 1023 in order, a branch's 1024 onward, a leaf's 1024 + 128 onward. `parents`: the trunk and the branches have parent 0; each leaf has a branch as parent, and each branch has 2 leaves.
All inputs are finite; a program needn't handle non-finite values.
Results may differ from a plain program's by a relative error of at most 0.025.
Values may be sent and summed in bfloat16 or wider, within the bound.
A program may use at most 320 MiB of HBM per device.

v0:
```python
import jax
import jax.numpy as jnp
from jax import lax
from jax.sharding import PartitionSpec as P

D = 2048
HEAD = 128
TREE_TOK = 2560
QBLOCK = 640


precise = lax.Precision.HIGHEST
epsilon = 1e-06
rope_base = 500000.0
masked_out = -1e30
contract_last = (((1,), (1,)), ((), ()))


def column_gather(values):
    return lax.all_gather(values, "col", axis=0, tiled=True)


def pair_gather(first_part, second_part):
    return (
        lax.all_gather(first_part, "row", axis=0, tiled=True),
        lax.all_gather(second_part, "row", axis=0, tiled=True),
    )


def heads_gather(values):
    return lax.all_gather(values, "row", axis=0, tiled=True)


def hidden_gather(values):
    return lax.all_gather(values, "row", axis=0, tiled=True)


def token_totals(values):
    return lax.psum(values, ("row", "col"))


def width_total(product, extra, row_count):
    return lax.psum_scatter(
        (product(jnp.int32(0), row_count * lax.axis_size("col")) + extra).astype(jnp.bfloat16),
        "col",
        scatter_dimension=0,
        tiled=True,
    ).astype(jnp.float32)


def spread(values, first_row, group_tokens):
    out_shape = values.shape[:-1] + (group_tokens,)
    return lax.dynamic_update_slice_in_dim(
        jnp.zeros(out_shape, jnp.float32), values, first_row, values.ndim - 1
    )


def own_part(values, first_row, row_total):
    return lax.dynamic_slice_in_dim(values, first_row, row_total, values.ndim - 1)


def norm_apply(values, square_sum):
    factor = lax.rsqrt(square_sum / D + epsilon)
    return (values * factor[:, None], factor)


def norm_back(upstream, flat, factor, cross_sum):
    return factor[:, None] * (upstream - flat * (cross_sum / D)[:, None])


def angles(positions):
    half_width = HEAD // 2
    frequency = rope_base ** (-(jnp.arange(half_width, dtype=jnp.float32) * 2.0) / HEAD)
    angle_table = positions.astype(jnp.float32)[:, None] * frequency[None, :]
    return (jnp.cos(angle_table)[:, None, :], jnp.sin(angle_table)[:, None, :])


def rotate(values, cosine, sine):
    half_width = values.shape[-1] // 2
    first_half = values[..., :half_width]
    second_half = values[..., half_width:]
    return jnp.concatenate(
        [first_half * cosine - second_half * sine, second_half * cosine + first_half * sine],
        axis=-1,
    )


def unrotate(gradient, cosine, sine):
    half_width = gradient.shape[-1] // 2
    first_half = gradient[..., :half_width]
    second_half = gradient[..., half_width:]
    return jnp.concatenate(
        [first_half * cosine + second_half * sine, second_half * cosine - first_half * sine],
        axis=-1,
    )


def select(weights_table, set_onehot):
    return jnp.einsum("ts,...skw->...tkw", set_onehot, weights_table, precision=precise)


def grouped(values, tree_count):
    return values.astype(jnp.float32).reshape(tree_count, -1, values.shape[-1])


def down_map(input_values, tables):
    return jnp.einsum("tnw,tkw->tnk", input_values, tables, precision=precise)


def up_map(reduced, tables):
    return jnp.einsum("tnk,tkw->tnw", reduced, tables, precision=precise).reshape(
        -1, tables.shape[-1]
    )


def to_sets(left_term, right_term, set_onehot):
    per_tree = jnp.einsum("tnk,tnw->tkw", left_term, right_term, precision=precise)
    return jnp.einsum("ts,tkw->skw", set_onehot, per_tree, precision=precise)


def stacked_sets(left_term, right_term, set_onehot):
    per_tree = jnp.einsum("jtnk,jtnw->jtkw", left_term, right_term, precision=precise)
    return jnp.einsum("ts,jtkw->jskw", set_onehot, per_tree, precision=precise)


def shared_sets(left_term, right_term, set_onehot):
    per_tree = jnp.einsum("jtnk,tnw->jtkw", left_term, right_term, precision=precise)
    return jnp.einsum("ts,jtkw->jskw", set_onehot, per_tree, precision=precise)


def owner_order(gradient, dp_count, other_count):
    lead_dims = gradient.shape[:-3]
    set_count, rank_count, width_all = gradient.shape[-3:]
    split_grad = gradient.reshape(
        lead_dims
        + (dp_count, set_count // dp_count, other_count, rank_count // other_count, width_all)
    )
    lead_len = len(lead_dims)
    axis_order = (
        (lead_len, lead_len + 2)
        + tuple(range(lead_len))
        + (lead_len + 1, lead_len + 3, lead_len + 4)
    )
    return jnp.transpose(split_grad, axis_order).reshape(
        (-1, set_count // dp_count, rank_count // other_count, width_all)
    )


def block_mask(seg_ids, positions, parents, first_row, tree_at):
    seg_query = lax.dynamic_slice_in_dim(seg_ids, first_row, QBLOCK, 0)
    pos_query = lax.dynamic_slice_in_dim(positions, first_row, QBLOCK, 0)
    parent_row = lax.dynamic_index_in_dim(parents, tree_at, 0, keepdims=False)
    labels = jnp.arange(parent_row.shape[0], dtype=jnp.int32)
    parent_query = jnp.sum(
        jnp.where(seg_query[:, None] == labels[None, :], parent_row[None, :], 0), axis=1
    )
    grand_query = jnp.sum(
        jnp.where(parent_query[:, None] == labels[None, :], parent_row[None, :], 0), axis=1
    )
    on_path = (
        (seg_ids[None, :] == seg_query[:, None])
        | (seg_ids[None, :] == parent_query[:, None])
        | (seg_ids[None, :] == grand_query[:, None])
    )
    return on_path & (positions[None, :] <= pos_query[:, None])


def per_device(
    tokens,
    cotangent,
    seg_ids,
    positions,
    parents,
    tree_sets,
    gain_q,
    gain_k,
    gain_attn,
    gain_ffn,
    query_key_value_weight,
    output_weight,
    gate_up_weight,
    down_weight,
    query_key_value_adapter_first,
    query_key_value_adapter_second,
    output_adapter_first,
    output_adapter_second,
    gate_up_adapter_first,
    gate_up_adapter_second,
    down_adapter_first,
    down_adapter_second,
):
    dp_count = lax.axis_size("dp")
    row_count = lax.axis_size("row")
    col_count = lax.axis_size("col")
    row_start = lax.axis_index("row") * (seg_ids.shape[0] // row_count)
    col_start = lax.axis_index("col") * (seg_ids.shape[0] // col_count)
    group_tokens = seg_ids.shape[0]
    tree_count = tree_sets.shape[0]
    set_count = output_adapter_first.shape[0]
    row_part = group_tokens // row_count
    col_part = group_tokens // col_count
    width_row = tokens.shape[1]
    width_col = gain_q.shape[0]
    hidden_col = down_weight.shape[0]
    heads_col = width_col // HEAD
    score_scale = HEAD ** (-0.5)
    blocks = row_part // QBLOCK
    set_onehot = (tree_sets[:, None] == jnp.arange(set_count, dtype=jnp.int32)[None, :]).astype(
        jnp.float32
    )
    a_qkv_sel = select(query_key_value_adapter_first, set_onehot)
    b_qkv_sel = select(query_key_value_adapter_second, set_onehot)
    a_out_sel = select(output_adapter_first, set_onehot)
    b_out_sel = select(output_adapter_second, set_onehot)
    a_gu_sel = select(gate_up_adapter_first, set_onehot)
    b_gu_sel = select(gate_up_adapter_second, set_onehot)
    a_down_sel = select(down_adapter_first, set_onehot)
    b_down_sel = select(down_adapter_second, set_onehot)
    tokens_all = column_gather(tokens)
    tokens_grp = grouped(tokens_all, tree_count)
    reduce_qkv = jnp.einsum("tnw,jtkw->jtnk", tokens_grp, a_qkv_sel, precision=precise)
    w_qkv_flat = query_key_value_weight.reshape(width_row, 3 * width_col)
    extra_qkv = jnp.einsum("jtnk,jtkf->tnjf", reduce_qkv, b_qkv_sel, precision=precise).reshape(
        group_tokens, 3 * width_col
    )
    projected = lax.psum_scatter(
        jnp.dot(tokens_all, w_qkv_flat, preferred_element_type=jnp.float32) + extra_qkv,
        "row",
        scatter_dimension=0,
        tiled=True,
    )
    query_raw = projected[:, :width_col]
    key_raw = projected[:, width_col : 2 * width_col]
    value_raw = projected[:, 2 * width_col :]
    square_qk = jnp.stack(
        [jnp.sum(query_raw * query_raw, axis=1), jnp.sum(key_raw * key_raw, axis=1)]
    )
    square_qk = own_part(
        token_totals(spread(square_qk, row_start, group_tokens)), row_start, row_part
    )
    query_flat, query_factor = norm_apply(query_raw, square_qk[0])
    key_flat, key_factor = norm_apply(key_raw, square_qk[1])
    cos_own, sin_own = angles(own_part(positions, row_start, row_part))
    query_low = rotate(
        (query_flat * gain_q).reshape(row_part, heads_col, HEAD), cos_own, sin_own
    ).astype(jnp.bfloat16)
    key_low = rotate(
        (key_flat * gain_k).reshape(row_part, heads_col, HEAD), cos_own, sin_own
    ).astype(jnp.bfloat16)
    value_low = value_raw.astype(jnp.bfloat16)
    key_all, value_all = pair_gather(key_low.reshape(row_part, width_col), value_low)
    key_heads = key_all.reshape(group_tokens, heads_col, HEAD)
    value_heads = value_all.reshape(group_tokens, heads_col, HEAD)

    def block_parts(block_at):
        first_row = row_start + block_at * QBLOCK
        tree_at = first_row // TREE_TOK
        visible = block_mask(seg_ids, positions, parents, first_row, tree_at)
        scores = (
            jnp.einsum("qhd,khd->hqk", query_low, key_heads, preferred_element_type=jnp.float32)
            * score_scale
        )
        scores = jnp.where(visible[None, :, :], scores, masked_out)
        return (query_low, key_heads, value_heads, scores, tree_at)

    def attend(block_at):
        query_blk, key_tree, value_tree, scores, tree_at = block_parts(block_at)
        highest = jnp.max(scores, axis=2, keepdims=True)
        raised = jnp.exp(scores - highest)
        total_sum = jnp.sum(raised, axis=2, keepdims=True)
        weights_p = raised / total_sum
        attended = jnp.einsum(
            "hqk,khd->qhd",
            weights_p.astype(jnp.bfloat16),
            value_tree,
            preferred_element_type=jnp.float32,
        )
        return (attended, (highest + jnp.log(total_sum))[:, :, 0])

    attended_all, log_totals = lax.map(attend, jnp.arange(blocks))
    attention_reduced = attended_all.reshape(row_part, width_col).astype(jnp.bfloat16)
    attn_all = heads_gather(attention_reduced)
    attn_grp = grouped(attn_all, tree_count)
    reduce_out = down_map(attn_grp, a_out_sel)
    extra_out = up_map(reduce_out, b_out_sel)

    def out_product(first_row, row_total):
        return jnp.dot(attn_all, output_weight, preferred_element_type=jnp.float32)

    attention_unscaled = width_total(out_product, extra_out, col_part)
    square_a = own_part(
        token_totals(
            spread(
                jnp.sum(attention_unscaled * attention_unscaled, axis=1), col_start, group_tokens
            )
        ),
        col_start,
        col_part,
    )
    attn_flat, attn_factor = norm_apply(attention_unscaled, square_a)
    hidden_in = tokens.astype(jnp.float32) + attn_flat * gain_attn
    hidden_reduced = hidden_in.astype(jnp.bfloat16)
    hidden_all = column_gather(hidden_reduced)
    hidden_grp = grouped(hidden_all, tree_count)
    reduce_gu = jnp.einsum("tnw,jtkw->jtnk", hidden_grp, a_gu_sel, precision=precise)
    w_gu_flat = gate_up_weight.reshape(width_row, 2 * hidden_col)
    extra_gu = jnp.einsum("jtnk,jtkf->tnjf", reduce_gu, b_gu_sel, precision=precise).reshape(
        group_tokens, 2 * hidden_col
    )
    expanded = lax.psum_scatter(
        (jnp.dot(hidden_all, w_gu_flat, preferred_element_type=jnp.float32) + extra_gu).astype(
            jnp.bfloat16
        ),
        "row",
        scatter_dimension=0,
        tiled=True,
    ).astype(jnp.float32)
    gate_unscaled = expanded[:, :hidden_col]
    up_unscaled = expanded[:, hidden_col:]
    product_reduced = (jax.nn.silu(gate_unscaled) * up_unscaled).astype(jnp.bfloat16)
    product_all = hidden_gather(product_reduced)
    product_grp = grouped(product_all, tree_count)
    reduce_down = down_map(product_grp, a_down_sel)
    extra_down = up_map(reduce_down, b_down_sel)

    def down_product(first_row, row_total):
        return jnp.dot(product_all, down_weight, preferred_element_type=jnp.float32)

    down_unscaled = width_total(down_product, extra_down, col_part)
    square_f = own_part(
        token_totals(
            spread(jnp.sum(down_unscaled * down_unscaled, axis=1), col_start, group_tokens)
        ),
        col_start,
        col_part,
    )
    down_flat, down_factor = norm_apply(down_unscaled, square_f)
    layer_out = (hidden_in + down_flat * gain_ffn).astype(jnp.bfloat16)
    grad_out = cotangent.astype(jnp.float32)
    scaled_f = grad_out * gain_ffn
    cross_f = own_part(
        token_totals(spread(jnp.sum(scaled_f * down_flat, axis=1), col_start, group_tokens)),
        col_start,
        col_part,
    )
    grad_down = norm_back(scaled_f, down_flat, down_factor, cross_f).astype(jnp.bfloat16)
    grad_down_all = column_gather(grad_down)
    grad_down_grp = grouped(grad_down_all, tree_count)
    back_down = down_map(grad_down_grp, b_down_sel)
    extra_hidden = up_map(back_down, a_down_sel)
    grad_product = lax.psum_scatter(
        (
            lax.dot_general(
                grad_down_all, down_weight, contract_last, preferred_element_type=jnp.float32
            )
            + extra_hidden
        ).astype(jnp.bfloat16),
        "row",
        scatter_dimension=0,
        tiled=True,
    ).astype(jnp.float32)
    sigmoid_gate = jax.nn.sigmoid(gate_unscaled)
    grad_gate = (
        grad_product * up_unscaled * sigmoid_gate * (1.0 + gate_unscaled * (1.0 - sigmoid_gate))
    ).astype(jnp.bfloat16)
    grad_up = (grad_product * (gate_unscaled * sigmoid_gate)).astype(jnp.bfloat16)
    gate_all, up_all = (
        lax.all_gather(grad_gate, "row", axis=0, tiled=True),
        lax.all_gather(grad_up, "row", axis=0, tiled=True),
    )
    grad_gu_grp = jnp.stack([grouped(gate_all, tree_count), grouped(up_all, tree_count)])
    back_gu = jnp.einsum("jtnf,jtkf->jtnk", grad_gu_grp, b_gu_sel, precision=precise)
    extra_hin = jnp.einsum("jtnk,jtkw->tnw", back_gu, a_gu_sel, precision=precise).reshape(
        group_tokens, width_row
    )

    def hin_product(first_row, row_total):
        return lax.dot_general(
            gate_all, gate_up_weight[:, 0, :], contract_last, preferred_element_type=jnp.float32
        ) + lax.dot_general(
            up_all, gate_up_weight[:, 1, :], contract_last, preferred_element_type=jnp.float32
        )

    grad_hidden = grad_out + width_total(hin_product, extra_hin, col_part)
    scaled_a = grad_hidden * gain_attn
    cross_a = own_part(
        token_totals(spread(jnp.sum(scaled_a * attn_flat, axis=1), col_start, group_tokens)),
        col_start,
        col_part,
    )
    grad_attn_raw = norm_back(scaled_a, attn_flat, attn_factor, cross_a).astype(jnp.bfloat16)
    grad_attn_all = column_gather(grad_attn_raw)
    grad_attn_grp = grouped(grad_attn_all, tree_count)
    back_out = down_map(grad_attn_grp, b_out_sel)
    extra_attn = up_map(back_out, a_out_sel)
    grad_attended = lax.psum_scatter(
        (
            lax.dot_general(
                grad_attn_all, output_weight, contract_last, preferred_element_type=jnp.float32
            )
            + extra_attn
        ).astype(jnp.bfloat16),
        "row",
        scatter_dimension=0,
        tiled=True,
    )
    grad_attended_low = grad_attended.reshape(row_part, heads_col, HEAD)

    def attend_back(totals, block_at):
        key_sum, value_sum = totals
        query_blk, key_tree, value_tree, scores, tree_at = block_parts(block_at)
        weights_p = jnp.exp(scores - log_totals[block_at][:, :, None])
        grad_weights = jnp.einsum(
            "qhd,khd->hqk", grad_attended_low, value_tree, preferred_element_type=jnp.float32
        )
        inner_sum = jnp.sum(weights_p * grad_weights, axis=2, keepdims=True)
        grad_scores = (weights_p * (grad_weights - inner_sum)).astype(jnp.bfloat16)
        grad_query = (
            jnp.einsum("hqk,khd->qhd", grad_scores, key_tree, preferred_element_type=jnp.float32)
            * score_scale
        )
        grad_key = (
            jnp.einsum("hqk,qhd->khd", grad_scores, query_blk, preferred_element_type=jnp.float32)
            * score_scale
        )
        grad_value = jnp.einsum(
            "hqk,qhd->khd",
            weights_p.astype(jnp.bfloat16),
            grad_attended_low,
            preferred_element_type=jnp.float32,
        )
        key_sum = key_sum + grad_key
        value_sum = value_sum + grad_value
        return ((key_sum, value_sum), grad_query)

    zero_heads = jnp.zeros((group_tokens, heads_col, HEAD), jnp.float32)
    (key_sum, value_sum), query_grads = lax.scan(
        attend_back, (zero_heads, zero_heads), jnp.arange(blocks)
    )
    key_own, value_own = (
        lax.psum_scatter(
            key_sum.reshape(group_tokens, width_col).astype(jnp.bfloat16),
            "row",
            scatter_dimension=0,
            tiled=True,
        ).astype(jnp.float32),
        lax.psum_scatter(
            value_sum.reshape(group_tokens, width_col).astype(jnp.bfloat16),
            "row",
            scatter_dimension=0,
            tiled=True,
        ).astype(jnp.float32),
    )
    grad_query_n = (
        unrotate(query_grads.reshape(row_part, heads_col, HEAD), cos_own, sin_own).reshape(
            row_part, width_col
        )
        * gain_q
    )
    grad_key_n = (
        unrotate(key_own.reshape(row_part, heads_col, HEAD), cos_own, sin_own).reshape(
            row_part, width_col
        )
        * gain_k
    )
    cross_qk = jnp.stack(
        [jnp.sum(grad_query_n * query_flat, axis=1), jnp.sum(grad_key_n * key_flat, axis=1)]
    )
    cross_qk = own_part(
        token_totals(spread(cross_qk, row_start, group_tokens)), row_start, row_part
    )
    grad_query_raw = norm_back(grad_query_n, query_flat, query_factor, cross_qk[0]).astype(
        jnp.bfloat16
    )
    grad_key_raw = norm_back(grad_key_n, key_flat, key_factor, cross_qk[1]).astype(jnp.bfloat16)
    grad_value_raw = value_own.astype(jnp.bfloat16)
    query_grad_all, key_grad_all = pair_gather(grad_query_raw, grad_key_raw)
    value_grad_all = heads_gather(grad_value_raw)
    grad_qkv_grp = jnp.stack(
        [
            grouped(query_grad_all, tree_count),
            grouped(key_grad_all, tree_count),
            grouped(value_grad_all, tree_count),
        ]
    )
    back_qkv = jnp.einsum("jtnf,jtkf->jtnk", grad_qkv_grp, b_qkv_sel, precision=precise)
    extra_input = jnp.einsum("jtnk,jtkw->tnw", back_qkv, a_qkv_sel, precision=precise).reshape(
        group_tokens, width_row
    )

    def input_product(first_row, row_total):
        total_rows = lax.dot_general(
            query_grad_all,
            query_key_value_weight[:, 0, :],
            contract_last,
            preferred_element_type=jnp.float32,
        )
        total_rows = total_rows + lax.dot_general(
            key_grad_all,
            query_key_value_weight[:, 1, :],
            contract_last,
            preferred_element_type=jnp.float32,
        )
        return total_rows + lax.dot_general(
            value_grad_all,
            query_key_value_weight[:, 2, :],
            contract_last,
            preferred_element_type=jnp.float32,
        )

    input_grad = grad_hidden + width_total(input_product, extra_input, col_part)
    tokens_back = grouped(column_gather(lax.optimization_barrier(tokens)), tree_count)
    hidden_back = grouped(column_gather(lax.optimization_barrier(hidden_reduced)), tree_count)
    attn_back = grouped(heads_gather(lax.optimization_barrier(attention_reduced)), tree_count)
    product_back = grouped(hidden_gather(lax.optimization_barrier(product_reduced)), tree_count)
    part_a_qkv = shared_sets(back_qkv, tokens_back, set_onehot)
    part_b_qkv = stacked_sets(reduce_qkv, grad_qkv_grp, set_onehot)
    part_a_out = to_sets(back_out, attn_back, set_onehot)
    part_b_out = to_sets(reduce_out, grad_attn_grp, set_onehot)
    part_a_gu = shared_sets(back_gu, hidden_back, set_onehot)
    part_b_gu = stacked_sets(reduce_gu, grad_gu_grp, set_onehot)
    part_a_down = to_sets(back_down, product_back, set_onehot)
    part_b_down = to_sets(reduce_down, grad_down_grp, set_onehot)
    sum_a_qkv, sum_a_gu, sum_b_out, sum_b_down = (
        lax.psum_scatter(
            owner_order(part_a_qkv, dp_count, col_count).astype(jnp.bfloat16),
            ("dp", "col"),
            scatter_dimension=0,
            tiled=True,
        ).astype(jnp.float32),
        lax.psum_scatter(
            owner_order(part_a_gu, dp_count, col_count).astype(jnp.bfloat16),
            ("dp", "col"),
            scatter_dimension=0,
            tiled=True,
        ).astype(jnp.float32),
        lax.psum_scatter(
            owner_order(part_b_out, dp_count, col_count).astype(jnp.bfloat16),
            ("dp", "col"),
            scatter_dimension=0,
            tiled=True,
        ).astype(jnp.float32),
        lax.psum_scatter(
            owner_order(part_b_down, dp_count, col_count).astype(jnp.bfloat16),
            ("dp", "col"),
            scatter_dimension=0,
            tiled=True,
        ).astype(jnp.float32),
    )
    sum_b_qkv, sum_b_gu, sum_a_out, sum_a_down = (
        lax.psum_scatter(
            owner_order(part_b_qkv, dp_count, row_count).astype(jnp.bfloat16),
            ("dp", "row"),
            scatter_dimension=0,
            tiled=True,
        ).astype(jnp.float32),
        lax.psum_scatter(
            owner_order(part_b_gu, dp_count, row_count).astype(jnp.bfloat16),
            ("dp", "row"),
            scatter_dimension=0,
            tiled=True,
        ).astype(jnp.float32),
        lax.psum_scatter(
            owner_order(part_a_out, dp_count, row_count).astype(jnp.bfloat16),
            ("dp", "row"),
            scatter_dimension=0,
            tiled=True,
        ).astype(jnp.float32),
        lax.psum_scatter(
            owner_order(part_a_down, dp_count, row_count).astype(jnp.bfloat16),
            ("dp", "row"),
            scatter_dimension=0,
            tiled=True,
        ).astype(jnp.float32),
    )
    return (
        layer_out,
        input_grad,
        sum_a_qkv,
        sum_b_qkv,
        sum_a_out[0],
        sum_b_out[0],
        sum_a_gu,
        sum_b_gu,
        sum_a_down[0],
        sum_b_down[0],
    )


def solution(mesh):
    in_specs = (
        P(("dp", "col"), "row"),
        P(("dp", "col"), "row"),
        P("dp"),
        P("dp"),
        P("dp", None),
        P("dp"),
        P("col"),
        P("col"),
        P("row"),
        P("row"),
        P("row", None, "col"),
        P("col", "row"),
        P("row", None, "col"),
        P("col", "row"),
        P(None, None, None, "row"),
        P(None, None, None, "col"),
        P(None, None, "col"),
        P(None, None, "row"),
        P(None, None, None, "row"),
        P(None, None, None, "col"),
        P(None, None, "col"),
        P(None, None, "row"),
    )
    out_specs = (
        P(("dp", "col"), "row"),
        P(("dp", "col"), "row"),
        P(None, "dp", "col", "row"),
        P(None, "dp", "row", "col"),
        P("dp", "row", "col"),
        P("dp", "col", "row"),
        P(None, "dp", "col", "row"),
        P(None, "dp", "row", "col"),
        P("dp", "row", "col"),
        P("dp", "col", "row"),
    )
    return jax.shard_map(
        per_device, mesh=mesh, in_specs=in_specs, out_specs=out_specs, check_vma=False
    )
```

profile of v0, /device:TPU:0, one launch (start us, length us, event | category | flops | bytes accessed | tf_op | source)
XLA Modules:
  0.0 2328.1 jit_solution(4552352331285815572)
XLA Ops:
  14.3 52.9 %all-gather.18.cloned.1.call-done = bf16[2560,512]{1,0:T(8,128)(2,1)} async-done(((bf16[640,512]{1,0:T(8,128)(2,1)}), bf16[2560,512]{1,0:T(8,128)(2,1)}) %all-gather.18.cloned.1.call-update) | async-done | bytes 2621456 | tf_op jit(solution)/shard_map/all_gather | solution.py:20
  121.4 116.0 %reduce-scatter.13.cloned.1.call-done = f32[640,1536]{1,0:T(8,128)} async-done(((f32[2560,1536]{1,0:T(8,128)}), f32[640,1536]{1,0:T(8,128)}) %reduce-scatter.13.cloned.1.call-update) | async-done | bytes 3932176 | tf_op jit(solution)/shard_map/reduce_scatter | solution.py:226
  239.4 60.6 %psum.42 = f32[2,2560]{1,0:T(2,128)S(1)} all-reduce(f32[2,2560]{1,0:T(2,128)S(1)} %maximum_dynamic-update-slice_fusion), channel_id=1, replica_groups=mesh['dp'=2,'row'=4,'col'=4] {'row','col'}, use_global_device_ids=true, to_apply=%region_5.6 | all-reduce | flops 5120 | bytes 40960 | tf_op jit(solution)/shard_map/psum | solution.py:39
  417.0 52.2 %reduce-scatter.15.cloned.1.call-done = bf16[640,512]{1,0:T(8,128)(2,1)} async-done(((bf16[2560,512]{1,0:T(8,128)(2,1)}), bf16[640,512]{1,0:T(8,128)(2,1)}) %reduce-scatter.15.cloned.1.call-update) | async-done | bytes 655376 | tf_op jit(solution)/shard_map/reduce_scatter | solution.py:43
  470.8 60.2 %psum.43 = f32[2560]{0:T(1024)S(1)} all-reduce(f32[2560]{0:T(1024)S(1)} %dynamic_update_slice.27), channel_id=1, replica_groups=mesh['dp'=2,'row'=4,'col'=4] {'row','col'}, use_global_device_ids=true, to_apply=%region_10.11 | all-reduce | flops 2560 | bytes 20480 | tf_op jit(solution)/shard_map/psum | solution.py:39
  544.2 42.0 %all-gather.26.cloned.1.call-done = bf16[2560,512]{1,0:T(8,128)(2,1)} async-done(((bf16[640,512]{1,0:T(8,128)(2,1)}), bf16[2560,512]{1,0:T(8,128)(2,1)}) %all-gather.26.cloned.1.call-update) | async-done | bytes 2621456 | tf_op jit(solution)/shard_map/all_gather | solution.py:20
  694.0 152.0 %reduce-scatter.17.cloned.1.call-done = bf16[640,4096]{1,0:T(8,128)(2,1)} async-done(((bf16[2560,4096]{1,0:T(8,128)(2,1)}), bf16[640,4096]{1,0:T(8,128)(2,1)}) %reduce-scatter.17.cloned.1.call-update) | async-done | bytes 5242896 | tf_op jit(solution)/shard_map/reduce_scatter | solution.py:310
  860.2 66.7 %all-gather.28.cloned.1.call-done = bf16[2560,2048]{1,0:T(8,128)(2,1)} async-done(((bf16[640,2048]{1,0:T(8,128)(2,1)}), bf16[2560,2048]{1,0:T(8,128)(2,1)}) %all-gather.28.cloned.1.call-update) | async-done | bytes 10485776 | tf_op jit(solution)/shard_map/all_gather | solution.py:35
  951.2 52.2 %reduce-scatter.19.cloned.1.call-done = bf16[640,512]{1,0:T(8,128)(2,1)} async-done(((bf16[2560,512]{1,0:T(8,128)(2,1)}), bf16[640,512]{1,0:T(8,128)(2,1)}) %reduce-scatter.19.cloned.1.call-update) | async-done | bytes 655376 | tf_op jit(solution)/shard_map/reduce_scatter | solution.py:43
  1005.0 60.7 %psum.44 = f32[2560]{0:T(1024)S(1)} all-reduce(f32[2560]{0:T(1024)S(1)} %dynamic_update_slice.28), channel_id=1, replica_groups=mesh['dp'=2,'row'=4,'col'=4] {'row','col'}, use_global_device_ids=true, to_apply=%region_14.15 | all-reduce | flops 2560 | bytes 20480 | tf_op jit(solution)/shard_map/psum | solution.py:39
  1067.6 57.9 %psum.45 = f32[2560]{0:T(1024)S(1)} all-reduce(f32[2560]{0:T(1024)S(1)} %dynamic_update_slice.29), channel_id=1, replica_groups=mesh['dp'=2,'row'=4,'col'=4] {'row','col'}, use_global_device_ids=true, to_apply=%region_16.17 | all-reduce | flops 2560 | bytes 20480 | tf_op jit(solution)/shard_map/psum | solution.py:39
  1128.0 52.2 %all-gather.30.cloned.1.call-done = bf16[2560,512]{1,0:T(8,128)(2,1)} async-done(((bf16[640,512]{1,0:T(8,128)(2,1)}), bf16[2560,512]{1,0:T(8,128)(2,1)}) %all-gather.30.cloned.1.call-update) | async-done | bytes 2621456 | tf_op jit(solution)/shard_map/all_gather | solution.py:20
  1216.1 84.2 %reduce-scatter.21.cloned.1.call-done = bf16[640,2048]{1,0:T(8,128)(2,1)} async-done(((bf16[2560,2048]{1,0:T(8,128)(2,1)}), bf16[640,2048]{1,0:T(8,128)(2,1)}) %reduce-scatter.21.cloned.1.call-update) | async-done | bytes 2621456 | tf_op jit(solution)/shard_map/reduce_scatter | solution.py:351
  1318.9 59.7 %all-gather.32.cloned.1.call-done = bf16[2560,2048]{1,0:T(8,128)(2,1)} async-done(((bf16[640,2048]{1,0:T(8,128)(2,1)}), bf16[2560,2048]{1,0:T(8,128)(2,1)}) %all-gather.32.cloned.1.call-update) | async-done | bytes 10485776 | tf_op jit(solution)/shard_map/all_gather | solution.py:368
  1378.6 71.7 %all-gather.34.cloned.1.call-done = bf16[2560,2048]{1,0:T(8,128)(2,1)} async-done(((bf16[640,2048]{1,0:T(8,128)(2,1)}), bf16[2560,2048]{1,0:T(8,128)(2,1)}) %all-gather.34.cloned.1.call-update) | async-done | bytes 10485776 | tf_op jit(solution)/shard_map/all_gather | solution.py:369
  1494.0 52.0 %reduce-scatter.23.cloned.1.call-done = bf16[640,512]{1,0:T(8,128)(2,1)} async-done(((bf16[2560,512]{1,0:T(8,128)(2,1)}), bf16[640,512]{1,0:T(8,128)(2,1)}) %reduce-scatter.23.cloned.1.call-update) | async-done | bytes 655376 | tf_op jit(solution)/shard_map/reduce_scatter | solution.py:43
  1547.8 60.2 %psum.46 = f32[2560]{0:T(1024)S(1)} all-reduce(f32[2560]{0:T(1024)S(1)} %dynamic_update_slice.30), channel_id=1, replica_groups=mesh['dp'=2,'row'=4,'col'=4] {'row','col'}, use_global_device_ids=true, to_apply=%region_20.21 | all-reduce | flops 2560 | bytes 20480 | tf_op jit(solution)/shard_map/psum | solution.py:39
  1611.2 52.1 %all-gather.36.cloned.1.call-done = bf16[2560,512]{1,0:T(8,128)(2,1)} async-done(((bf16[640,512]{1,0:T(8,128)(2,1)}), bf16[2560,512]{1,0:T(8,128)(2,1)}) %all-gather.36.cloned.1.call-update) | async-done | bytes 2621456 | tf_op jit(solution)/shard_map/all_gather | solution.py:20
  1802.2 61.2 %psum.47 = f32[2,2560]{1,0:T(2,128)S(1)} all-reduce(f32[2,2560]{1,0:T(2,128)S(1)} %maximum_dynamic-update-slice_fusion.1), channel_id=1, replica_groups=mesh['dp'=2,'row'=4,'col'=4] {'row','col'}, use_global_device_ids=true, to_apply=%region_26.27 | all-reduce | flops 5120 | bytes 40960 | tf_op jit(solution)/shard_map/psum | solution.py:39
  1910.3 45.3 %all-gather.48.cloned.1.call-done = bf16[2560,512]{1,0:T(8,128)(2,1)} async-done(((bf16[640,512]{1,0:T(8,128)(2,1)}), bf16[2560,512]{1,0:T(8,128)(2,1)}) %all-gather.48.cloned.1.call-update) | async-done | bytes 2621456 | tf_op jit(solution)/shard_map/all_gather | solution.py:20
  2075.0 44.1 %all-gather.44.cloned.1.call-done = bf16[2560,512]{1,0:T(8,128)(2,1)} async-done(((bf16[640,512]{1,0:T(8,128)(2,1)}), bf16[2560,512]{1,0:T(8,128)(2,1)}) %all-gather.44.cloned.1.call-update) | async-done | bytes 2621456 | tf_op jit(solution)/shard_map/all_gather | solution.py:20
  2156.9 42.2 %all-reduce.13.cloned.1.call-done = (bf16[24,4,4,512]{3,2,1,0:T(4,128)(2,1)}, bf16[8,4,4,512]{3,2,1,0:T(4,128)(2,1)}, bf16[16,4,4,512]{3,2,1,0:T(4,128)(2,1)}, bf16[8,4,4,512]{3,2,1,0:T(4,128)(2,1)}) async-done(((bf16[24,4,4,512]{3,2,1,0:T(4,128)(2,1)}, bf16[8,4,4,512]{3,2,1,0:T(4,128)(2,1)}, bf16[16,4,4,512]{3,2,1,0:T(4,128)(2,1)}, bf16[8,4,4,512]{3,2,1,0:T(4,128)(2,1)}), ...) | async-done | bytes 917520
  2205.9 59.2 %all-reduce.15.cloned.1.call-done = (bf16[24,4,4,512]{3,2,1,0:T(4,128)(2,1)}, bf16[8,4,4,512]{3,2,1,0:T(4,128)(2,1)}, bf16[16,4,4,2048]{3,2,1,0:T(4,128)(2,1)}, bf16[8,4,4,2048]{3,2,1,0:T(4,128)(2,1)}) async-done(((bf16[24,4,4,512]{3,2,1,0:T(4,128)(2,1)}, bf16[8,4,4,512]{3,2,1,0:T(4,128)(2,1)}, bf16[16,4,4,2048]{3,2,1,0:T(4,128)(2,1)}, bf16[8,4,4,2048]{3,2,1,0:T(4,128)(2,1)}), ...) | async-done | bytes 2097168
  2272.3 46.6 %reduce-scatter.29.cloned.1.call-done = bf16[640,512]{1,0:T(8,128)(2,1)} async-done(((bf16[2560,512]{1,0:T(8,128)(2,1)}), bf16[640,512]{1,0:T(8,128)(2,1)}) %reduce-scatter.29.cloned.1.call-update) | async-done | bytes 655376 | tf_op jit(solution)/shard_map/reduce_scatter | solution.py:43
  (385 shorter events, 804.9 us)
Async XLA Ops:
  7.9 229.4 %reduce-scatter.13.cloned.1.call-start = ((), (), s32[]{:S(2)}) async-start(), calls=%async_computation.11 | async-start | bytes 19660800 | tf_op jit(solution)/shard_map/reduce_scatter | solution.py:226
  118.6 220.8 %all-gather.22.cloned.1.call-start = ((), (), s32[]{:S(2)}) async-start(), calls=%async_computation.13 | async-start | bytes 3276800 | tf_op jit(solution)/shard_map/all_gather | solution.py:25
  417.0 169.3 %all-gather.26.cloned.1.call-start = ((), (), s32[]{:S(2)}) async-start(), calls=%async_computation.16 | async-start | bytes 3276800 | tf_op jit(solution)/shard_map/all_gather | solution.py:20
  534.0 312.0 %reduce-scatter.17.cloned.1.call-start = ((), (), s32[]{:S(2)}) async-start(), calls=%async_computation.17 | async-start | bytes 26214400 | tf_op jit(solution)/shard_map/reduce_scatter | solution.py:310
  694.0 232.9 %all-gather.28.cloned.1.call-start = ((), (), s32[]{:S(2)}) async-start(), calls=%async_computation.18 | async-start | bytes 13107200 | tf_op jit(solution)/shard_map/all_gather | solution.py:35
  856.5 146.9 %reduce-scatter.19.cloned.1.call-start = ((), (), s32[]{:S(2)}) async-start(), calls=%async_computation.19 | async-start | bytes 3276800 | tf_op jit(solution)/shard_map/reduce_scatter | solution.py:43
  951.2 229.0 %all-gather.30.cloned.1.call-start = ((), (), s32[]{:S(2)}) async-start(), calls=%async_computation.20 | async-start | bytes 3276800 | tf_op jit(solution)/shard_map/all_gather | solution.py:20
  1127.9 172.3 %reduce-scatter.21.cloned.1.call-start = ((), (), s32[]{:S(2)}) async-start(), calls=%async_computation.21 | async-start | bytes 13107200 | tf_op jit(solution)/shard_map/reduce_scatter | solution.py:351
  1216.0 162.6 %all-gather.32.cloned.1.call-start = ((), (), s32[]{:S(2)}) async-start(), calls=%async_computation.22 | async-start | bytes 13107200 | tf_op jit(solution)/shard_map/all_gather | solution.py:368
  1308.2 142.1 %all-gather.34.cloned.1.call-start = ((), (), s32[]{:S(2)}) async-start(), calls=%async_computation.23 | async-start | bytes 13107200 | tf_op jit(solution)/shard_map/all_gather | solution.py:369
  1308.8 237.2 %reduce-scatter.23.cloned.1.call-start = ((), (), s32[]{:S(2)}) async-start(), calls=%async_computation.24 | async-start | bytes 3276800 | tf_op jit(solution)/shard_map/reduce_scatter | solution.py:43
  1493.7 169.6 %all-gather.36.cloned.1.call-start = ((), (), s32[]{:S(2)}) async-start(), calls=%async_computation.25 | async-start | bytes 3276800 | tf_op jit(solution)/shard_map/all_gather | solution.py:20
  1674.9 114.9 %reduce-scatter.31.cloned.1.call-start = ((), (), s32[]{:S(2)}) async-start(), calls=%async_computation.36 | async-start | bytes 3276800
  1754.9 113.8 %reduce-scatter.27.cloned.1.call-start = ((), (), s32[]{:S(2)}) async-start(), calls=%async_computation.29 | async-start | bytes 3276800 | tf_op jit(solution)/shard_map/reduce_scatter | solution.py:447
  1772.7 126.6 %all-gather.50.cloned.1.call-start = ((), (), s32[]{:S(2)}) async-start(), calls=%async_computation.35 | async-start | bytes 13107200 | tf_op jit(solution)/shard_map/all_gather | solution.py:35
  1773.3 182.3 %all-gather.48.cloned.1.call-start = ((), (), s32[]{:S(2)}) async-start(), calls=%async_computation.34 | async-start | bytes 3276800 | tf_op jit(solution)/shard_map/all_gather | solution.py:20
  1774.0 207.5 %all-gather.46.cloned.1.call-start = ((), (), s32[]{:S(2)}) async-start(), calls=%async_computation.33 | async-start | bytes 3276800 | tf_op jit(solution)/shard_map/all_gather | solution.py:31
  1774.8 233.9 %all-gather.38.cloned.1.call-start = ((), (), s32[]{:S(2)}) async-start(), calls=%async_computation.27 | async-start | bytes 3276800 | tf_op jit(solution)/shard_map/all_gather | solution.py:25
  1868.1 167.6 %all-gather.40.cloned.1.call-start = ((), (), s32[]{:S(2)}) async-start(), calls=%async_computation.28 | async-start | bytes 3276800 | tf_op jit(solution)/shard_map/all_gather | solution.py:26
  1868.7 194.2 %all-gather.42.cloned.1.call-start = ((), (), s32[]{:S(2)}) async-start(), calls=%async_computation.30 | async-start | bytes 3276800 | tf_op jit(solution)/shard_map/all_gather | solution.py:31
  1869.4 249.7 %all-gather.44.cloned.1.call-start = ((), (), s32[]{:S(2)}) async-start(), calls=%async_computation.32 | async-start | bytes 3276800 | tf_op jit(solution)/shard_map/all_gather | solution.py:20
  1870.0 329.1 %all-reduce.13.cloned.1.call-start = ((), (), s32[]{:S(2)}) async-start(), calls=%async_computation.37 | async-start | bytes 1835008
  2123.6 141.5 %all-reduce.15.cloned.1.call-start = ((), (), s32[]{:S(2)}) async-start(), calls=%async_computation.38 | async-start | bytes 4194304
  2139.4 179.5 %reduce-scatter.29.cloned.1.call-start = ((), (), s32[]{:S(2)}) async-start(), calls=%async_computation.31 | async-start | bytes 3276800 | tf_op jit(solution)/shard_map/reduce_scatter | solution.py:43
  (90 other events, 4032.5 us)
Sparse Core Ops, SparseCore 0:
  9.6 57.4 all-gather.17
  118.7 118.6 reduce-scatter.12
  341.4 25.5 all-gather.19
  417.1 52.0 reduce-scatter.14
  534.1 52.0 all-gather.25
  694.1 151.8 reduce-scatter.16
  856.6 70.2 all-gather.27
  951.3 52.0 reduce-scatter.18
  1128.1 52.0 all-gather.29
  1216.1 84.0 reduce-scatter.20
  1308.3 70.2 all-gather.31
  1380.1 70.1 all-gather.33
  1493.8 52.1 reduce-scatter.22
  1611.2 52.0 all-gather.35
  1675.0 33.4 reduce-scatter.24
  1755.1 34.6 reduce-scatter.30
  1792.5 34.8 reduce-scatter.26
  1828.7 70.4 all-gather.49
  1900.9 54.7 all-gather.47
  1983.1 25.5 all-gather.37
  2064.3 54.7 all-gather.43
  2123.8 75.3 all-reduce.12
  2203.8 61.2 all-reduce.14
  2267.4 51.4 reduce-scatter.28
  (5 shorter events, 124.4 us)
where the time goes:
time: 2340 us; the launch traced here: 2330 us
  waiting for transfers between devices  1360 us (58%)
  matrix products  366 us (16%)
  blocking collectives  361 us (15%)
  local copies, waits for them, and re-layouts  123 us (5%)
  other arithmetic  97.7 us (4%)
    psum x6, blocking collectives, token_totals(): return lax.psum(values, ('row', 'col'))  361 us
    all_gather x6, waiting for transfers between devices, column_gather(): return lax.all_gather(values, 'col', axis=0, tiled=True)  289 us
    reduce_scatter x4, waiting for transfers between devices, width_total(): lax.psum_scatter((product(jnp.int32(0), row_count * lax.axis_size('col'))...  203 us
    reduce_scatter x1, waiting for transfers between devices, per_device(): lax.psum_scatter((jnp.dot(hidden_all, w_gu_flat, preferred_element_type=j...  152 us
    reduce_scatter x1, waiting for transfers between devices, per_device(): lax.psum_scatter(jnp.dot(tokens_all, w_qkv_flat, preferred_element_type=j...  116 us
    unnamed x32, waiting for transfers between devices  111 us
    all_gather x2, waiting for transfers between devices, hidden_gather(): return lax.all_gather(values, 'row', axis=0, tiled=True)  95.6 us
    reduce_scatter x1, waiting for transfers between devices, per_device(): lax.psum_scatter((lax.dot_general(grad_down_all, down_weight, contract_la...  84.2 us
  transfers between devices with their start and end apart: 29, of which 28 were waited for; matrix products, arithmetic and copies ran while one was open for 8% of the time, Pallas kernels for 0%

commit v1 on v0

v1 whole, which is shorter than its diff:
```python
import jax
import jax.numpy as jnp
from jax import lax
from jax.sharding import PartitionSpec as P

D = 2048
HEAD = 128
RANK = 16

epsilon = 1e-06
rope_base = 500000.0
masked_out = -1e30
low = jnp.bfloat16
wide = jnp.float32
last_last = (((1,), (1,)), ((), ()))
first_first = (((0,), (0,)), ((), ()))


def dot(left, right):
    return jnp.dot(left, right, preferred_element_type=wide)


def dot_t(left, right):
    return lax.dot_general(left, right, last_last, preferred_element_type=wide)


def t_dot(left, right):
    return lax.dot_general(left, right, first_first, preferred_element_type=wide)


def angles(positions):
    half_width = HEAD // 2
    frequency = rope_base ** (-(jnp.arange(half_width, dtype=wide) * 2.0) / HEAD)
    angle_table = positions.astype(wide)[:, None] * frequency[None, :]
    return (jnp.cos(angle_table)[:, None, :], jnp.sin(angle_table)[:, None, :])


def rotate(values, cosine, sine):
    half_width = values.shape[-1] // 2
    first_half = values[..., :half_width]
    second_half = values[..., half_width:]
    return jnp.concatenate(
        [first_half * cosine - second_half * sine, second_half * cosine + first_half * sine],
        axis=-1,
    )


def norm_factor(square_sum):
    return lax.rsqrt(square_sum / D + epsilon)


def norm_back(scaled, flat, factor, cross_sum):
    return factor[:, None] * (scaled - flat * (cross_sum / D)[:, None])


def tree_mask(seg_ids, positions, parents):
    parent_row = parents[0]
    labels = jnp.arange(parent_row.shape[0], dtype=jnp.int32)
    parent_tok = jnp.sum(jnp.where(seg_ids[:, None] == labels[None, :], parent_row[None, :], 0), axis=1)
    grand_tok = jnp.sum(jnp.where(parent_tok[:, None] == labels[None, :], parent_row[None, :], 0), axis=1)
    on_path = (
        (seg_ids[None, :] == seg_ids[:, None])
        | (seg_ids[None, :] == parent_tok[:, None])
        | (seg_ids[None, :] == grand_tok[:, None])
    )
    return on_path & (positions[None, :] <= positions[:, None])


def per_device(
    tokens,
    cotangent,
    seg_ids,
    positions,
    parents,
    tree_sets,
    gain_q,
    gain_k,
    gain_attn,
    gain_ffn,
    query_key_value_weight,
    output_weight,
    gate_up_weight,
    down_weight,
    query_key_value_adapter_first,
    query_key_value_adapter_second,
    output_adapter_first,
    output_adapter_second,
    gate_up_adapter_first,
    gate_up_adapter_second,
    down_adapter_first,
    down_adapter_second,
):
    dp_count = lax.axis_size("dp")
    row_count = lax.axis_size("row")
    col_count = lax.axis_size("col")
    row_at = lax.axis_index("row")
    tree_tokens = seg_ids.shape[0]
    assert tree_sets.shape[0] == 1
    set_count = output_adapter_first.shape[0]
    own = tokens.shape[0] // row_count
    group = own * col_count
    width_row = tokens.shape[1]
    width_col = gain_q.shape[0]
    hidden_col = down_weight.shape[0]
    heads_col = width_col // HEAD
    score_scale = HEAD ** (-0.5)
    tree_set = tree_sets[0]

    def pick(table, axis):
        return lax.dynamic_index_in_dim(table, tree_set, axis, keepdims=False)

    narrow = jnp.concatenate(
        [
            pick(query_key_value_adapter_first, 1),
            pick(gate_up_adapter_first, 1),
            pick(output_adapter_second, 0)[None],
            pick(down_adapter_second, 0)[None],
        ],
        axis=0,
    ).astype(low)
    narrow_all = lax.all_gather(narrow, "row", axis=2, tiled=True)
    a_qkv = narrow_all[:3].reshape(3 * RANK, D)
    a_gu = narrow_all[3:5].reshape(2 * RANK, D)
    b_out = narrow_all[5]
    b_down = narrow_all[6]
    b_qkv = pick(query_key_value_adapter_second, 1).astype(low)
    b_gu = pick(gate_up_adapter_second, 1).astype(low)
    a_out = pick(output_adapter_first, 0).astype(low)
    a_down = pick(down_adapter_first, 0).astype(low)
    gains = lax.all_gather(jnp.stack([gain_attn, gain_ffn]), "row", axis=1, tiled=True)

    w_qkv = lax.all_gather(query_key_value_weight, "row", axis=0, tiled=True).reshape(D, 3 * width_col)
    w_out = lax.all_gather(output_weight, "row", axis=1, tiled=True)
    w_gu = lax.all_gather(gate_up_weight, "row", axis=0, tiled=True).reshape(D, 2 * hidden_col)
    w_down = lax.all_gather(down_weight, "row", axis=1, tiled=True)

    def to_tokens(values):
        return lax.all_to_all(values, "row", split_axis=0, concat_axis=1, tiled=True)

    def to_width(values):
        return lax.all_to_all(values, "row", split_axis=1, concat_axis=0, tiled=True)

    def gather_col(values):
        return lax.all_gather(values, "col", axis=0, tiled=True)

    def scatter_col(values):
        return lax.psum_scatter(values.astype(low), "col", scatter_dimension=0, tiled=True).astype(wide)

    def to_heads(values, parts):
        by_head = values.reshape(group, parts, heads_col, HEAD).transpose(2, 0, 1, 3).reshape(heads_col, group, parts * HEAD)
        moved = lax.all_to_all(by_head, "row", split_axis=0, concat_axis=0, tiled=True)
        return (
            moved.reshape(row_count, col_count, own, parts * HEAD)
            .transpose(1, 0, 2, 3)
            .reshape(tree_tokens, parts * HEAD)
        )

    def from_heads(values, parts):
        by_row = (
            values.reshape(col_count, row_count, own, parts * HEAD)
            .transpose(1, 0, 2, 3)
            .reshape(row_count, group, parts * HEAD)
        )
        moved = lax.all_to_all(by_row, "row", split_axis=0, concat_axis=0, tiled=True)
        return moved.reshape(heads_col, group, parts, HEAD).transpose(1, 2, 0, 3).reshape(group, parts * width_col)

    x_own = to_tokens(tokens)
    x = gather_col(x_own)
    red_qkv = dot_t(x, a_qkv).astype(low)
    raw = dot(x, w_qkv)
    extra = jnp.concatenate([dot(red_qkv[:, RANK * j : RANK * (j + 1)], b_qkv[j]) for j in range(3)], axis=1)
    raw = raw + extra
    q_raw = raw[:, :width_col]
    k_raw = raw[:, width_col : 2 * width_col]
    v_raw = raw[:, 2 * width_col :]
    square_qk = lax.psum(jnp.stack([jnp.sum(q_raw * q_raw, axis=1), jnp.sum(k_raw * k_raw, axis=1)]), "col")
    q_factor = norm_factor(square_qk[0])
    k_factor = norm_factor(square_qk[1])
    q_flat = q_raw * q_factor[:, None]
    k_flat = k_raw * k_factor[:, None]
    pos_own = lax.dynamic_index_in_dim(
        positions.reshape(col_count, row_count, own), row_at, 1, keepdims=False
    ).reshape(group)
    cos_own, sin_own = angles(pos_own)

    def turn(values, sine):
        return rotate(values.reshape(group, heads_col, HEAD), cos_own, sine).reshape(group, width_col)

    q_low = turn(q_flat * gain_q, sin_own).astype(low)
    k_low = turn(k_flat * gain_k, sin_own).astype(low)
    qkv_head = to_heads(jnp.concatenate([q_low, k_low, v_raw.astype(low)], axis=1), 3)
    q_head = qkv_head[:, :HEAD]
    k_head = qkv_head[:, HEAD : 2 * HEAD]
    v_head = qkv_head[:, 2 * HEAD :]
    visible = tree_mask(seg_ids, positions, parents)
    scores = jnp.where(visible, dot_t(q_head, k_head) * score_scale, masked_out)
    highest = jnp.max(scores, axis=1, keepdims=True)
    raised = jnp.exp(scores - highest)
    probs = raised / jnp.sum(raised, axis=1, keepdims=True)
    probs_low = probs.astype(low)
    attn_head = dot(probs_low, v_head).astype(low)
    attn = from_heads(attn_head, 1)

    red_out = dot_t(attn, a_out).astype(low)
    a_raw = scatter_col(dot(attn, w_out) + dot(red_out, b_out))
    a_factor = norm_factor(jnp.sum(a_raw * a_raw, axis=1))
    a_flat = a_raw * a_factor[:, None]
    h_own = x_own.astype(wide) + a_flat * gains[0]
    h = gather_col(h_own.astype(low))

    red_gu = dot_t(h, a_gu).astype(low)
    gate = dot(h, w_gu[:, :hidden_col]) + dot(red_gu[:, :RANK], b_gu[0])
    up = dot(h, w_gu[:, hidden_col:]) + dot(red_gu[:, RANK:], b_gu[1])
    sigma = jax.nn.sigmoid(gate)
    hidden = (gate * sigma * up).astype(low)
    red_down = dot_t(hidden, a_down).astype(low)
    f_raw = scatter_col(dot(hidden, w_down) + dot(red_down, b_down))
    f_factor = norm_factor(jnp.sum(f_raw * f_raw, axis=1))
    f_flat = f_raw * f_factor[:, None]
    out_own = (h_own + f_flat * gains[1]).astype(low)
    layer_out = to_width(out_own)

    g_own = to_tokens(cotangent).astype(wide)
    scaled_f = g_own * gains[1]
    d_f_own = norm_back(scaled_f, f_flat, f_factor, jnp.sum(scaled_f * f_flat, axis=1)).astype(low)
    d_f = gather_col(d_f_own)
    back_down = dot_t(d_f, b_down).astype(low)
    d_hidden = dot_t(d_f, w_down) + dot(back_down, a_down)
    d_gate = (d_hidden * up * sigma * (1.0 + gate * (1.0 - sigma))).astype(low)
    d_up = (d_hidden * (gate * sigma)).astype(low)
    back_gate = dot_t(d_gate, b_gu[0]).astype(low)
    back_up = dot_t(d_up, b_gu[1]).astype(low)
    back_gu = jnp.concatenate([back_gate, back_up], axis=1)
    d_h = g_own + scatter_col(
        dot_t(d_gate, w_gu[:, :hidden_col]) + dot_t(d_up, w_gu[:, hidden_col:]) + dot(back_gu, a_gu)
    )
    scaled_a = d_h * gains[0]
    d_a_own = norm_back(scaled_a, a_flat, a_factor, jnp.sum(scaled_a * a_flat, axis=1)).astype(low)
    d_a = gather_col(d_a_own)
    back_out = dot_t(d_a, b_out).astype(low)
    d_attn = (dot_t(d_a, w_out) + dot(back_out, a_out)).astype(low)

    d_attn_head = to_heads(d_attn, 1)
    d_probs = dot_t(d_attn_head, v_head)
    inner = jnp.sum(probs * d_probs, axis=1, keepdims=True)
    d_scores = (probs * (d_probs - inner)).astype(low)
    dq_head = (dot(d_scores, k_head) * score_scale).astype(low)
    dk_head = (t_dot(d_scores, q_head) * score_scale).astype(low)
    dv_head = t_dot(probs_low, d_attn_head).astype(low)
    d_qkv = from_heads(jnp.concatenate([dq_head, dk_head, dv_head], axis=1), 3)
    dq_n = turn(d_qkv[:, :width_col].astype(wide), -sin_own) * gain_q
    dk_n = turn(d_qkv[:, width_col : 2 * width_col].astype(wide), -sin_own) * gain_k
    cross_qk = lax.psum(jnp.stack([jnp.sum(dq_n * q_flat, axis=1), jnp.sum(dk_n * k_flat, axis=1)]), "col")
    d_q = norm_back(dq_n, q_flat, q_factor, cross_qk[0]).astype(low)
    d_k = norm_back(dk_n, k_flat, k_factor, cross_qk[1]).astype(low)
    d_v = d_qkv[:, 2 * width_col :]
    d_raw = jnp.concatenate([d_q, d_k, d_v], axis=1)
    back_qkv = jnp.concatenate(
        [dot_t(d, b) for d, b in zip((d_q, d_k, d_v), (b_qkv[0], b_qkv[1], b_qkv[2]))], axis=1
    ).astype(low)
    in_own = d_h + scatter_col(dot_t(d_raw, w_qkv) + dot(back_qkv, a_qkv))
    input_grad = to_width(in_own.astype(low)).astype(wide)

    full_width = jnp.concatenate(
        [t_dot(back_qkv, x), t_dot(back_gu, h), t_dot(red_out, d_a), t_dot(red_down, d_f)], axis=0
    ).astype(low)
    full_width = lax.psum_scatter(full_width, "row", scatter_dimension=1, tiled=True)
    full_width = full_width.reshape(7, col_count, RANK // col_count, width_row).transpose(1, 0, 2, 3)
    full_width = lax.psum_scatter(full_width, "col", scatter_dimension=0, tiled=False)
    col_width = jnp.concatenate(
        [t_dot(red_qkv[:, RANK * j : RANK * (j + 1)], d) for j, d in enumerate((d_q, d_k, d_v))]
        + [t_dot(back_out, attn), t_dot(red_gu[:, :RANK], d_gate), t_dot(red_gu[:, RANK:], d_up), t_dot(back_down, hidden)],
        axis=1,
    ).astype(low)
    col_width = lax.psum_scatter(col_width, "row", scatter_dimension=0, tiled=True)
    onehot = (tree_set == jnp.arange(set_count, dtype=jnp.int32)).astype(wide)
    owner = jnp.concatenate([full_width.reshape(-1), col_width.reshape(-1)])
    owner_all = lax.all_gather(owner, "dp", axis=0, tiled=False).astype(wide)
    onehot_all = lax.all_gather(onehot, "dp", axis=0, tiled=False)
    sets_own = set_count // dp_count
    onehot_own = lax.dynamic_slice_in_dim(onehot_all, lax.axis_index("dp") * sets_own, sets_own, 1)
    per_set = jnp.sum(onehot_own[:, :, None] * owner_all[:, None, :], axis=0)
    split_at = full_width.size
    full_sets = per_set[:, :split_at].reshape(sets_own, 7, RANK // col_count, width_row)
    col_sets = per_set[:, split_at:].reshape(sets_own, RANK // row_count, -1)
    grad_a_qkv = full_sets[:, :3].transpose(1, 0, 2, 3)
    grad_a_gu = full_sets[:, 3:5].transpose(1, 0, 2, 3)
    grad_b_out = full_sets[:, 5]
    grad_b_down = full_sets[:, 6]
    grad_b_qkv = jnp.stack([col_sets[..., width_col * j : width_col * (j + 1)] for j in range(3)])
    grad_a_out = col_sets[..., 3 * width_col : 4 * width_col]
    gu_at = 4 * width_col
    grad_b_gu = jnp.stack([col_sets[..., gu_at + hidden_col * j : gu_at + hidden_col * (j + 1)] for j in range(2)])
    grad_a_down = col_sets[..., gu_at + 2 * hidden_col :]
    return (
        layer_out,
        input_grad,
        grad_a_qkv,
        grad_b_qkv,
        grad_a_out,
        grad_b_out,
        grad_a_gu,
        grad_b_gu,
        grad_a_down,
        grad_b_down,
    )


def solution(mesh):
    in_specs = (
        P(("dp", "col"), "row"),
        P(("dp", "col"), "row"),
        P("dp"),
        P("dp"),
        P("dp", None),
        P("dp"),
        P("col"),
        P("col"),
        P("row"),
        P("row"),
        P("row", None, "col"),
        P("col", "row"),
        P("row", None, "col"),
        P("col", "row"),
        P(None, None, None, "row"),
        P(None, None, None, "col"),
        P(None, None, "col"),
        P(None, None, "row"),
        P(None, None, None, "row"),
        P(None, None, None, "col"),
        P(None, None, "col"),
        P(None, None, "row"),
    )
    out_specs = (
        P(("dp", "col"), "row"),
        P(("dp", "col"), "row"),
        P(None, "dp", "col", "row"),
        P(None, "dp", "row", "col"),
        P("dp", "row", "col"),
        P("dp", "col", "row"),
        P(None, "dp", "col", "row"),
        P(None, "dp", "row", "col"),
        P("dp", "row", "col"),
        P("dp", "col", "row"),
    )
    return jax.shard_map(
        per_device, mesh=mesh, in_specs=in_specs, out_specs=out_specs, check_vma=False
    )
```

time: 2340 us -> 1170 us (0.50)
  waiting for transfers between devices: 1360 us -> 654 us
  blocking collectives: 361 us -> 95.3 us
  matrix products: 366 us -> 212 us
  other arithmetic: 97.7 us -> 66.5 us
  local copies, waits for them, and re-layouts: 123 us -> 96.2 us
    reduce_scatter x9 -> x5, waiting for transfers between devices: 588 us -> 178 us  [the longest x4 174 us: scatter_col(): lax.psum_scatter(values.astype(low), 'col', scatter_dimension=0, tiled=True)]
    psum x6 -> x2, blocking collectives: 361 us -> 21.6 us  [the longest x1 12 us: per_device(): lax.psum(jnp.stack([jnp.sum(q_raw * q_raw, axis=1), jnp.sum(k_raw * k_raw...]
    all_gather x17 -> x8, waiting for transfers between devices: 659 us -> 365 us  [the longest x4 200 us: gather_col(): return lax.all_gather(values, 'col', axis=0, tiled=True)]
    dot_general x48 -> x49, matrix products: 363 us -> 212 us  [the longest x18 93.1 us: dot(): return jnp.dot(left, right, preferred_element_type=wide)]
    unnamed x32 -> x17, waiting for transfers between devices: 111 us -> 50.7 us
    all_to_all x0 -> x4, waiting for transfers between devices: none -> 59.2 us  [the longest x1 34.3 us: to_heads(): lax.all_to_all(by_head, 'row', split_axis=0, concat_axis=0, tiled=True)]
    all_to_all x0 -> x4, blocking collectives: none -> 52.7 us  [the longest x2 27.3 us: to_tokens(): lax.all_to_all(values, 'row', split_axis=0, concat_axis=1, tiled=True)]
    reshape x5 -> x13, local copies, waits for them, and re-layouts: 63 us -> 22.6 us  [the longest x3 9.49 us: to_heads(): values.reshape(group, parts, heads_col, HEAD).transpose(2, 0, 1, 3)]
  transfers between devices with their start and end apart: 29 -> 19, of which waited for: 28 -> 18; matrix products, arithmetic and copies ran while one was open for 8% -> 11% of each run, Pallas kernels for 0% -> 0%
where the time goes in v1:
time: 1170 us; the launch traced here: 1160 us
  waiting for transfers between devices  654 us (56%)
  matrix products  212 us (18%)
  local copies, waits for them, and re-layouts  96.2 us (8%)
  blocking collectives  95.3 us (8%)
  other arithmetic  66.5 us (6%)
  starting transfers between devices  16.9 us (1%)
  between operations  16.6 us (1%)
    all_gather x4, waiting for transfers between devices, gather_col(): return lax.all_gather(values, 'col', axis=0, tiled=True)  200 us
    reduce_scatter x4, waiting for transfers between devices, scatter_col(): lax.psum_scatter(values.astype(low), 'col', scatter_dimension=0, tiled=True)  174 us
    all_gather x1, waiting for transfers between devices, per_device(): lax.all_gather(gate_up_weight, 'row', axis=0, tiled=True)  104 us
    dot_general x18, matrix products, dot(): return jnp.dot(left, right, preferred_element_type=wide)  93.1 us
    dot_general x18, matrix products, dot_t(): return lax.dot_general(left, right, last_last, preferred_element_type=wide)  84.8 us
    unnamed x17, waiting for transfers between devices  50.7 us
    unnamed x173, local copies, waits for them, and re-layouts  41 us
    all_gather x1, waiting for transfers between devices, per_device(): lax.all_gather(query_key_value_weight, 'row', axis=0, tiled=True)  40.9 us
  transfers between devices with their start and end apart: 19, of which 18 were waited for; matrix products, arithmetic and copies ran while one was open for 11% of the time, Pallas kernels for 0%

profile of v1, /device:TPU:0, one launch (start us, length us, event | category | flops | bytes accessed | tf_op | source)
XLA Modules:
  0.0 1157.5 jit_solution(14469267757178420043)
XLA Ops:
  7.2 14.6 %all_to_all.84 = bf16[4,160,512]{2,1,0:T(8,128)(2,1)S(1)} all-to-all(bf16[4,160,512]{2,1,0:T(8,128)(2,1)} %bitcast.270), channel_id=1, replica_groups=mesh['dp'=2,'row'=4,'col'=4] {'row'}, dimensions={0} | all-to-all | bytes 1310720 | tf_op jit(solution)/shard_map/all_to_all | solution.py:138
  39.2 39.6 %all-gather.11.cloned.1.call-done = bf16[640,2048]{1,0:T(8,128)(2,1)} async-done(((bf16[160,2048]{1,0:T(8,128)(2,1)}), bf16[640,2048]{1,0:T(8,128)(2,1)}) %all-gather.11.cloned.1.call-update) | async-done | bytes 2621456 | tf_op jit(solution)/shard_map/all_gather | solution.py:144
  84.6 40.9 %all-gather.13.cloned.1.call-done = bf16[2048,3,512]{0,2,1:T(8,128)(2,1)} async-done(((bf16[512,3,512]{0,2,1:T(8,128)(2,1)}), bf16[2048,3,512]{0,2,1:T(8,128)(2,1)}) %all-gather.13.cloned.1.call-update) | async-done | bytes 6291472 | tf_op jit(solution)/shard_map/all_gather | solution.py:132
  137.0 12.0 %psum.14 = f32[2,640]{1,0:T(2,128)S(1)} all-reduce(f32[2,640]{1,0:T(2,128)S(1)} %pad_maximum_fusion.17), channel_id=1, replica_groups=mesh['dp'=2,'row'=4,'col'=4] {'col'}, use_global_device_ids=true, to_apply=%region_4.5 | all-reduce | flops 1280 | bytes 10240 | tf_op jit(solution)/shard_map/psum | solution.py:176
  179.4 34.3 %all-to-all-done.1 = bf16[4,640,384]{1,2,0:T(8,128)(2,1)} async-done(((bf16[4,640,384]{1,2,0:T(8,128)(2,1)}), bf16[4,640,384]{1,2,0:T(8,128)(2,1)}, u32[]{:S(2)}, u32[]{:S(2)}) %all-to-all-start.1) | async-done | bytes 1966112 | tf_op jit(solution)/shard_map/all_to_all | solution.py:151
  251.5 12.7 %all_to_all.85 = bf16[4,640,128]{2,1,0:T(8,128)(2,1)S(1)} all-to-all(bf16[4,640,128]{2,1,0:T(8,128)(2,1)S(1)} %bitcast.254), channel_id=1, replica_groups=mesh['dp'=2,'row'=4,'col'=4] {'row'}, dimensions={0} | all-to-all | bytes 1310720 | tf_op jit(solution)/shard_map/all_to_all | solution.py:164
  277.8 43.6 %reduce-scatter.7.cloned.1.call-done = bf16[160,2048]{1,0:T(8,128)(2,1)} async-done(((bf16[640,2048]{1,0:T(8,128)(2,1)}), bf16[160,2048]{1,0:T(8,128)(2,1)}) %reduce-scatter.7.cloned.1.call-update) | async-done | bytes 655376 | tf_op jit(solution)/shard_map/reduce_scatter | solution.py:147
  327.8 51.8 %all-gather.17.cloned.1.call-done = bf16[640,2048]{1,0:T(8,128)(2,1)} async-done(((bf16[160,2048]{1,0:T(8,128)(2,1)}), bf16[640,2048]{1,0:T(8,128)(2,1)}) %all-gather.17.cloned.1.call-update) | async-done | bytes 2621456 | tf_op jit(solution)/shard_map/all_gather | solution.py:144
  382.2 103.5 %all-gather.19.cloned.1.call-done = bf16[2048,2,2048]{2,1,0:T(2,128)(2,1)} async-done(((bf16[512,2,2048]{2,1,0:T(2,128)(2,1)}), bf16[2048,2,2048]{2,1,0:T(2,128)(2,1)}) %all-gather.19.cloned.1.call-update) | async-done | bytes 16777232 | tf_op jit(solution)/shard_map/all_gather | solution.py:134
  485.8 13.0 %copy.133 = bf16[256,8,2,2048]{3,1,2,0:T(8,128)(2,1)S(1)} copy(bf16[256,8,2,2048]{3,2,1,0:T(2,128)(2,1)} %bitcast.231) | data formatting | bytes 33554432
  525.1 20.5 %all-gather.21.cloned.1.call-done = bf16[2048,2048]{1,0:T(8,128)(2,1)} async-done(((bf16[2048,512]{1,0:T(8,128)(2,1)}), bf16[2048,2048]{1,0:T(8,128)(2,1)}) %all-gather.21.cloned.1.call-update) | async-done | bytes 8388624 | tf_op jit(solution)/shard_map/all_gather | solution.py:135
  558.7 12.6 %all_to_all.86 = bf16[4,160,512]{2,1,0:T(8,128)(2,1)S(1)} all-to-all(bf16[4,160,512]{2,1,0:T(8,128)(2,1)S(1)} %bitcast.271), channel_id=1, replica_groups=mesh['dp'=2,'row'=4,'col'=4] {'row'}, dimensions={0} | all-to-all | bytes 1310720 | tf_op jit(solution)/shard_map/all_to_all | solution.py:138
  571.7 38.2 %reduce-scatter.9.cloned.1.call-done = bf16[160,2048]{1,0:T(8,128)(2,1)} async-done(((bf16[640,2048]{1,0:T(8,128)(2,1)}), bf16[160,2048]{1,0:T(8,128)(2,1)}) %reduce-scatter.9.cloned.1.call-update) | async-done | bytes 655376 | tf_op jit(solution)/shard_map/reduce_scatter | solution.py:147
  614.2 54.4 %all-gather.23.cloned.1.call-done = bf16[640,2048]{1,0:T(8,128)(2,1)} async-done(((bf16[160,2048]{1,0:T(8,128)(2,1)}), bf16[640,2048]{1,0:T(8,128)(2,1)}) %all-gather.23.cloned.1.call-update) | async-done | bytes 2621456 | tf_op jit(solution)/shard_map/all_gather | solution.py:144
  716.6 51.0 %reduce-scatter.11.cloned.1.call-done = bf16[160,2048]{1,0:T(8,128)(2,1)} async-done(((bf16[640,2048]{1,0:T(8,128)(2,1)}), bf16[160,2048]{1,0:T(8,128)(2,1)}) %reduce-scatter.11.cloned.1.call-update) | async-done | bytes 655376 | tf_op jit(solution)/shard_map/reduce_scatter | solution.py:147
  772.2 54.6 %all-gather.25.cloned.1.call-done = bf16[640,2048]{1,0:T(8,128)(2,1)} async-done(((bf16[160,2048]{1,0:T(8,128)(2,1)}), bf16[640,2048]{1,0:T(8,128)(2,1)}) %all-gather.25.cloned.1.call-update) | async-done | bytes 2621456 | tf_op jit(solution)/shard_map/all_gather | solution.py:144
  834.3 12.8 %all_to_all.87 = bf16[4,640,128]{2,1,0:T(8,128)(2,1)S(1)} all-to-all(bf16[4,640,128]{2,1,0:T(8,128)(2,1)S(1)} %bitcast.256), channel_id=1, replica_groups=mesh['dp'=2,'row'=4,'col'=4] {'row'}, dimensions={0} | all-to-all | bytes 1310720 | tf_op jit(solution)/shard_map/all_to_all | solution.py:151
  847.2 11.3 fusion.20
  858.5 20.5 %multiply_reduce_fusion = (f32[2560]{0:T(1024)S(1)}, f32[2560,2560]{0,1:T(8,128)}) fusion(f32[2560]{0:T(1024)S(1)} %copy-done.64, f32[2560,2560]{0,1:T(8,128)} %copy-done.2, f32[2560]{0:T(1024)S(1)} %copy-done.62, bf16[2560,128]{1,0:T(8,128)(2,1)S(1)} %bitcast.273, bf16[2560,384]{1,0:T(8,128)(2,1)S(1)} %bitcast.249), kind=kOutput, calls=%fused_computation.1 | convolution fusion | flops 1703933440 | bytes 53774336 | tf_op jit(solution)/shard_map/dot_general | solution.py:24
  878.9 22.4 %multiply_convert_fusion = bf16[2560,2560]{0,1:T(8,128)(2,1)} fusion(f32[2560,2560]{0,1:T(8,128)} %get-tuple-element.100, f32[2560]{0:T(1024)S(1)} %get-tuple-element.99, f32[2560]{0:T(1024)S(1)} %copy-done.64, f32[2560,2560]{0,1:T(8,128)} %copy-done.2, f32[2560]{0:T(1024)S(1)} %copy-done.62), kind=kLoop, calls=%fused_computation | loop fusion | flops 32768000 | bytes 65566720 | tf_op jit(solution)/shard_map/convert_element_type | solution.py:246
  933.0 17.8 %all-to-all-done.6 = bf16[4,640,384]{2,1,0:T(8,128)(2,1)S(1)} async-done(((bf16[4,640,384]{2,1,0:T(8,128)(2,1)}), bf16[4,640,384]{2,1,0:T(8,128)(2,1)S(1)}, u32[]{:S(2)}, u32[]{:S(2)}) %all-to-all-start.6) | async-done | bytes 1966112 | tf_op jit(solution)/shard_map/all_to_all | solution.py:164
  1028.8 12.6 %all-reduce.7.cloned.1.call-done = bf16[16,8192]{1,0:T(8,128)(2,1)} async-done(((bf16[16,8192]{1,0:T(8,128)(2,1)}), bf16[16,8192]{1,0:T(8,128)(2,1)}) %all-reduce.7.cloned.1.call-update) | async-done | bytes 262160
  1042.3 36.0 %all-reduce.5.cloned.1.call-done = bf16[4,7,4,512]{3,2,0,1:T(4,128)(2,1)} async-done(((bf16[4,7,4,512]{3,2,0,1:T(4,128)(2,1)}), bf16[4,7,4,512]{3,2,0,1:T(4,128)(2,1)}) %all-reduce.5.cloned.1.call-update) | async-done | bytes 114704
  1091.2 41.5 %reduce-scatter.13.cloned.1.call-done = bf16[160,2048]{1,0:T(8,128)(2,1)} async-done(((bf16[640,2048]{1,0:T(8,128)(2,1)}), bf16[160,2048]{1,0:T(8,128)(2,1)}) %reduce-scatter.13.cloned.1.call-update) | async-done | bytes 655376 | tf_op jit(solution)/shard_map/reduce_scatter | solution.py:147
  (356 shorter events, 368.7 us)
Async XLA Ops:
  7.2 320.6 %copy-start = (f32[2,8,16,2048]{3,2,1,0:T(8,128)S(1)}, f32[2,8,16,2048]{3,2,1,0:T(8,128)}, u32[]{:S(2)}) copy-start(f32[2,8,16,2048]{3,2,1,0:T(8,128)} %param.41) | copy-start | bytes 6291460
  7.2 71.5 %all-gather.11.cloned.1.call-start = ((), (), s32[]{:S(2)}) async-start(), calls=%async_computation.13 | async-start | bytes 3276800 | tf_op jit(solution)/shard_map/all_gather | solution.py:144
  22.8 102.7 %all-gather.13.cloned.1.call-start = ((), (), s32[]{:S(2)}) async-start(), calls=%async_computation.14 | async-start | bytes 7864320 | tf_op jit(solution)/shard_map/all_gather | solution.py:132
  173.6 40.1 %all-to-all-start.1 = ((bf16[4,640,384]{1,2,0:T(8,128)(2,1)}), bf16[4,640,384]{1,2,0:T(8,128)(2,1)}, u32[]{:S(2)}, u32[]{:S(2)}) async-start(bf16[4,640,384]{1,2,0:T(8,128)(2,1)} %bitcast.242), calls=%async_computation.1 | async-start | bytes 3932160 | tf_op jit(solution)/shard_map/all_to_all | solution.py:151
  178.1 87.4 %all-gather.15.cloned.1.call-start = ((), (), s32[]{:S(2)}) async-start(), calls=%async_computation.15 | async-start | bytes 2621440 | tf_op jit(solution)/shard_map/all_gather | solution.py:133
  178.9 142.6 %reduce-scatter.7.cloned.1.call-start = ((), (), s32[]{:S(2)}) async-start(), calls=%async_computation.16 | async-start | bytes 3276800 | tf_op jit(solution)/shard_map/reduce_scatter | solution.py:147
  271.9 50.9 %copy-start.20 = (bf16[4,20,8,512]{3,2,0,1:T(8,128)(2,1)S(1)}, bf16[4,20,8,512]{3,2,0,1:T(8,128)(2,1)}, u32[]{:S(2)}) copy-start(bf16[4,20,8,512]{3,2,0,1:T(8,128)(2,1)} %copy.129) | copy-start | bytes 1966084
  271.9 107.7 %all-gather.17.cloned.1.call-start = ((), (), s32[]{:S(2)}) async-start(), calls=%async_computation.17 | async-start | bytes 3276800 | tf_op jit(solution)/shard_map/all_gather | solution.py:144
  325.0 160.8 %all-gather.19.cloned.1.call-start = ((), (), s32[]{:S(2)}) async-start(), calls=%async_computation.18 | async-start | bytes 20971520 | tf_op jit(solution)/shard_map/all_gather | solution.py:134
  325.6 220.1 %all-gather.21.cloned.1.call-start = ((), (), s32[]{:S(2)}) async-start(), calls=%async_computation.19 | async-start | bytes 10485760 | tf_op jit(solution)/shard_map/all_gather | solution.py:135
  326.3 283.6 %reduce-scatter.9.cloned.1.call-start = ((), (), s32[]{:S(2)}) async-start(), calls=%async_computation.20 | async-start | bytes 3276800 | tf_op jit(solution)/shard_map/reduce_scatter | solution.py:147
  382.2 134.7 %copy-start.48 = (bf16[640,32]{0,1:T(8,128)(2,1)}, bf16[640,32]{0,1:T(8,128)(2,1)S(1)}, u32[]{:S(2)}) copy-start(bf16[640,32]{0,1:T(8,128)(2,1)S(1)} %convolution_convert_fusion.8) | copy-start | bytes 122884
  557.7 111.0 %all-gather.23.cloned.1.call-start = ((), (), s32[]{:S(2)}) async-start(), calls=%async_computation.21 | async-start | bytes 3276800 | tf_op jit(solution)/shard_map/all_gather | solution.py:144
  571.7 197.5 %copy-start.3 = (f32[4,20,8,512]{3,2,0,1:T(8,128)}, f32[4,20,8,512]{3,2,0,1:T(8,128)S(1)}, u32[]{:S(2)}) copy-start(f32[4,20,8,512]{3,2,0,1:T(8,128)S(1)} %copy.130) | copy-start | bytes 3932164
  614.0 153.6 %reduce-scatter.11.cloned.1.call-start = ((), (), s32[]{:S(2)}) async-start(), calls=%async_computation.22 | async-start | bytes 3276800 | tf_op jit(solution)/shard_map/reduce_scatter | solution.py:147
  716.5 51.1 %copy-start.21 = (bf16[160,2048]{1,0:T(8,128)(2,1)S(1)}, bf16[160,2048]{1,0:T(8,128)(2,1)}, u32[]{:S(2)}) copy-start(bf16[160,2048]{1,0:T(8,128)(2,1)} %reduce-scatter.7.cloned.1.call-done) | copy-start | bytes 1966084
  716.5 110.3 %all-gather.25.cloned.1.call-start = ((), (), s32[]{:S(2)}) async-start(), calls=%async_computation.23 | async-start | bytes 3276800 | tf_op jit(solution)/shard_map/all_gather | solution.py:144
  922.8 28.0 %all-to-all-start.6 = ((bf16[4,640,384]{2,1,0:T(8,128)(2,1)}), bf16[4,640,384]{2,1,0:T(8,128)(2,1)S(1)}, u32[]{:S(2)}, u32[]{:S(2)}) async-start(bf16[4,640,384]{2,1,0:T(8,128)(2,1)} %bitcast.243), calls=%async_computation.9 | async-start | bytes 3932160 | tf_op jit(solution)/shard_map/all_to_all | solution.py:164
  926.5 79.7 %reduce-scatter.15.cloned.1.call-start = ((), (), s32[]{:S(2)}) async-start(), calls=%async_computation.25 | async-start | bytes 573440 | tf_op jit(solution)/shard_map/reduce_scatter | solution.py:267
  987.2 54.2 %all-reduce.7.cloned.1.call-start = ((), (), s32[]{:S(2)}) async-start(), calls=%async_computation.27 | async-start | bytes 524288
  993.4 85.0 %all-reduce.5.cloned.1.call-start = ((), (), s32[]{:S(2)}) async-start(), calls=%async_computation.26 | async-start | bytes 229376
  1007.8 124.9 %reduce-scatter.13.cloned.1.call-start = ((), (), s32[]{:S(2)}) async-start(), calls=%async_computation.24 | async-start | bytes 3276800 | tf_op jit(solution)/shard_map/reduce_scatter | solution.py:147
  1014.8 14.1 %all-to-all-start.3 = ((bf16[160,4,512]{2,0,1:T(8,128)(2,1)}), bf16[160,4,512]{2,0,1:T(8,128)(2,1)S(1)}, u32[]{:S(2)}, u32[]{:S(2)}) async-start(bf16[160,4,512]{2,0,1:T(8,128)(2,1)} %bitcast.215), calls=%async_computation.5 | async-start | bytes 1310720 | tf_op jit(solution)/shard_map/all_to_all | solution.py:141
  1134.9 13.8 %all-to-all-start.7 = ((bf16[160,4,512]{2,0,1:T(8,128)(2,1)}), bf16[160,4,512]{2,0,1:T(8,128)(2,1)S(1)}, u32[]{:S(2)}, u32[]{:S(2)}) async-start(bf16[160,4,512]{2,0,1:T(8,128)(2,1)} %bitcast.214), calls=%async_computation.11 | async-start | bytes 1310720 | tf_op jit(solution)/shard_map/all_to_all | solution.py:141
  (75 other events, 678.0 us)
Sparse Core Ops, SparseCore 0:
  22.9 55.7 all-gather.10
  80.3 45.1 all-gather.12
  180.5 32.5 all-gather.14
  272.0 49.3 reduce-scatter.6
  325.1 54.4 all-gather.16
  381.0 104.6 all-gather.18
  487.3 58.2 all-gather.20
  557.8 52.0 reduce-scatter.8
  614.1 54.4 all-gather.22
  716.6 50.8 reduce-scatter.10
  772.3 54.4 all-gather.24
  987.3 18.8 reduce-scatter.14
  1009.1 32.2 all-reduce.6
  1044.2 34.0 all-reduce.4
  1080.5 52.0 reduce-scatter.12

commit v2 on v1

--- a/solution.py
+++ b/solution.py
@@ -1,11 +1,20 @@
+import functools
+
 import jax
 import jax.numpy as jnp
 from jax import lax
+from jax.experimental import pallas as pl
+from jax.experimental.pallas import tpu as pltpu
 from jax.sharding import PartitionSpec as P
 
 D = 2048
 HEAD = 128
 RANK = 16
+SEG = 128
+TRUNK = 1024
+QT = 256
+MESH = pl.DeviceIdType.MESH
+VM = pl.BlockSpec(memory_space=pltpu.VMEM)
 
 epsilon = 1e-06
 rope_base = 500000.0
@@ -46,24 +55,300 @@
 
 
 def norm_factor(square_sum):
-    return lax.rsqrt(square_sum / D + epsilon)
+    return lax.rsqrt(square_sum * (1.0 / D) + epsilon)
 
 
 def norm_back(scaled, flat, factor, cross_sum):
     return factor[:, None] * (scaled - flat * (cross_sum / D)[:, None])
 
 
-def tree_mask(seg_ids, positions, parents):
-    parent_row = parents[0]
-    labels = jnp.arange(parent_row.shape[0], dtype=jnp.int32)
-    parent_tok = jnp.sum(jnp.where(seg_ids[:, None] == labels[None, :], parent_row[None, :], 0), axis=1)
-    grand_tok = jnp.sum(jnp.where(parent_tok[:, None] == labels[None, :], parent_row[None, :], 0), axis=1)
-    on_path = (
-        (seg_ids[None, :] == seg_ids[:, None])
-        | (seg_ids[None, :] == parent_tok[:, None])
-        | (seg_ids[None, :] == grand_tok[:, None])
-    )
-    return on_path & (positions[None, :] <= positions[:, None])
+def tail_scores(q, k_ref, own_at, parent_at, has_parent, pos_q, pos_k):
+    scale = HEAD ** -0.5
+    s_trunk = dot_t(q, k_ref[:TRUNK, :]) * scale
+    s_par = dot_t(q, k_ref[pl.ds(parent_at, SEG), :]) * scale
+    s_par = jnp.where(has_parent > 0, s_par, masked_out)
+    s_own = dot_t(q, k_ref[pl.ds(own_at, SEG), :]) * scale
+    s_own = jnp.where(pos_k <= pos_q, s_own, masked_out)
+    return s_trunk, s_par, s_own
+
+def trunk_scores(q, k_ref, pos_q, pos_k):
+    s = dot_t(q, k_ref[:TRUNK, :]) * HEAD ** -0.5
+    return jnp.where(pos_k <= pos_q, s, masked_out)
+
+def fwd_kernel(parent_ref, flag_ref, q_ref, k_ref, v_ref, posq_ref, posk_ref, o_ref, lse_ref):
+    tails = (q_ref.shape[0] - TRUNK) // SEG
+    @pl.loop(0, TRUNK // QT)
+    def _(i):
+        at = pl.multiple_of(i * QT, QT)
+        s = trunk_scores(q_ref[pl.ds(at, QT), :], k_ref, posq_ref[pl.ds(at, QT), :], posk_ref[:, :TRUNK])
+        top = jnp.max(s, axis=1, keepdims=True)
+        e = jnp.exp(s - top)
+        total = jnp.sum(e, axis=1, keepdims=True)
+        p = (e * (1.0 / total)).astype(low)
+        o_ref[pl.ds(at, QT), :] = dot(p, v_ref[:TRUNK, :]).astype(low)
+        lse_ref[pl.ds(at, QT), :] = top + jnp.log(total)
+    @pl.loop(0, tails)
+    def _(j):
+        at = pl.multiple_of(TRUNK + j * SEG, SEG)
+        par = pl.multiple_of(parent_ref[j] * SEG, SEG)
+        s1, s2, s3 = tail_scores(q_ref[pl.ds(at, SEG), :], k_ref, at, par, flag_ref[j],
+                                 posq_ref[pl.ds(at, SEG), :], posk_ref[:, pl.ds(at, SEG)])
+        top = jnp.maximum(jnp.maximum(jnp.max(s1, axis=1, keepdims=True), jnp.max(s2, axis=1, keepdims=True)),
+                          jnp.max(s3, axis=1, keepdims=True))
+        e1 = jnp.exp(s1 - top); e2 = jnp.exp(s2 - top); e3 = jnp.exp(s3 - top)
+        total = jnp.sum(e1, axis=1, keepdims=True) + jnp.sum(e2, axis=1, keepdims=True) + jnp.sum(e3, axis=1, keepdims=True)
+        inv = 1.0 / total
+        o = dot((e1 * inv).astype(low), v_ref[:TRUNK, :])
+        o += dot((e2 * inv).astype(low), v_ref[pl.ds(par, SEG), :])
+        o += dot((e3 * inv).astype(low), v_ref[pl.ds(at, SEG), :])
+        o_ref[pl.ds(at, SEG), :] = o.astype(low)
+        lse_ref[pl.ds(at, SEG), :] = top + jnp.log(total)
+
+def bwd_kernel(parent_ref, flag_ref, q_ref, k_ref, v_ref, do_ref, posq_ref, posk_ref, lse_ref, d_ref, dk_acc, dv_acc):
+    scale = HEAD ** -0.5
+    tails = (q_ref.shape[0] - TRUNK) // SEG
+    dk_acc[...] = jnp.zeros_like(dk_acc)
+    dv_acc[...] = jnp.zeros_like(dv_acc)
+    @pl.loop(0, TRUNK // QT)
+    def _(i):
+        at = pl.multiple_of(i * QT, QT)
+        q = q_ref[pl.ds(at, QT), :]
+        do = do_ref[pl.ds(at, QT), :]
+        s = trunk_scores(q, k_ref, posq_ref[pl.ds(at, QT), :], posk_ref[:, :TRUNK])
+        p = jnp.exp(s - lse_ref[pl.ds(at, QT), :])
+        dp = dot_t(do, v_ref[:TRUNK, :])
+        inner = jnp.sum(p * dp, axis=1, keepdims=True)
+        ds = (p * (dp - inner)).astype(low)
+        d_ref[pl.ds(at, QT), :HEAD] = (dot(ds, k_ref[:TRUNK, :]) * scale).astype(low)
+        dk_acc[:TRUNK, :] += t_dot(ds, q)
+        dv_acc[:TRUNK, :] += t_dot(p.astype(low), do)
+    @pl.loop(0, tails)
+    def _(j):
+        at = pl.multiple_of(TRUNK + j * SEG, SEG)
+        par = pl.multiple_of(parent_ref[j] * SEG, SEG)
+        q = q_ref[pl.ds(at, SEG), :]
+        do = do_ref[pl.ds(at, SEG), :]
+        lse = lse_ref[pl.ds(at, SEG), :]
+        s1, s2, s3 = tail_scores(q, k_ref, at, par, flag_ref[j],
+                                 posq_ref[pl.ds(at, SEG), :], posk_ref[:, pl.ds(at, SEG)])
+        p1 = jnp.exp(s1 - lse); p2 = jnp.exp(s2 - lse); p3 = jnp.exp(s3 - lse)
+        d1 = dot_t(do, v_ref[:TRUNK, :])
+        d2 = dot_t(do, v_ref[pl.ds(par, SEG), :])
+        d3 = dot_t(do, v_ref[pl.ds(at, SEG), :])
+        inner = jnp.sum(p1 * d1, axis=1, keepdims=True) + jnp.sum(p2 * d2, axis=1, keepdims=True) + jnp.sum(p3 * d3, axis=1, keepdims=True)
+        g1 = (p1 * (d1 - inner)).astype(low)
+        g2 = (p2 * (d2 - inner)).astype(low)
+        g3 = (p3 * (d3 - inner)).astype(low)
+        dq = dot(g1, k_ref[:TRUNK, :]) + dot(g2, k_ref[pl.ds(par, SEG), :]) + dot(g3, k_ref[pl.ds(at, SEG), :])
+        d_ref[pl.ds(at, SEG), :HEAD] = (dq * scale).astype(low)
+        dk_acc[:TRUNK, :] += t_dot(g1, q)
+        dv_acc[:TRUNK, :] += t_dot(p1.astype(low), do)
+        dk_acc[pl.ds(par, SEG), :] += t_dot(g2, q)
+        dv_acc[pl.ds(par, SEG), :] += t_dot(p2.astype(low), do)
+        dk_acc[pl.ds(at, SEG), :] += t_dot(g3, q)
+        dv_acc[pl.ds(at, SEG), :] += t_dot(p3.astype(low), do)
+    d_ref[:, HEAD:2 * HEAD] = (dk_acc[...] * scale).astype(low)
+    d_ref[:, 2 * HEAD:] = dv_acc[...].astype(low)
+
+def whole(shape, at=0):
+    return pl.BlockSpec(shape, lambda i, *_: (0, at))
+
+def attend(qkv, parent_at, flag, posq, posk):
+    n = qkv.shape[0]
+    return pl.pallas_call(
+        fwd_kernel,
+        grid_spec=pltpu.PrefetchScalarGridSpec(
+            num_scalar_prefetch=2, grid=(1,),
+            in_specs=[whole((n, HEAD), 0), whole((n, HEAD), 1), whole((n, HEAD), 2), whole((n, 1)), whole((1, n))],
+            out_specs=[whole((n, HEAD)), whole((n, 1))]),
+        out_shape=[jax.ShapeDtypeStruct((n, HEAD), low), jax.ShapeDtypeStruct((n, 1), wide)],
+        name="attend",
+    )(parent_at, flag, qkv, qkv, qkv, posq, posk)
+
+def attend_back(qkv, d_o, parent_at, flag, posq, posk, lse):
+    n = qkv.shape[0]
+    return pl.pallas_call(
+        bwd_kernel,
+        grid_spec=pltpu.PrefetchScalarGridSpec(
+            num_scalar_prefetch=2, grid=(1,),
+            in_specs=[whole((n, HEAD), 0), whole((n, HEAD), 1), whole((n, HEAD), 2), whole((n, HEAD)), whole((n, 1)), whole((1, n)), whole((n, 1))],
+            out_specs=whole((n, 3 * HEAD)),
+            scratch_shapes=[pltpu.VMEM((n, HEAD), wide), pltpu.VMEM((n, HEAD), wide)]),
+        out_shape=jax.ShapeDtypeStruct((n, 3 * HEAD), low),
+        name="attend_back",
+    )(parent_at, flag, qkv, qkv, qkv, d_o, posq, posk, lse)
+
+def tree_tables(seg_ids, parents):
+    tail_seg = seg_ids[TRUNK::SEG]
+    labels = jnp.arange(parents.shape[1], dtype=jnp.int32)
+    tail_parent = jnp.sum(jnp.where(tail_seg[:, None] == labels[None, :], parents[0][None, :], 0), axis=1)
+    hit = (tail_seg[None, :] == tail_parent[:, None])
+    at = jnp.arange(tail_seg.shape[0], dtype=jnp.int32) + TRUNK // SEG
+    parent_at = jnp.sum(jnp.where(hit, at[None, :], 0), axis=1)
+    flag = (tail_parent > 0).astype(jnp.int32)
+    return parent_at, flag
+
+
+def row_sum(v): return jnp.sum(v, axis=1, keepdims=True)
+
+def owner_step(mode, total, rows_all, rows_own, ins, outs):
+    if mode == "attn":
+        x_ref, gain_ref = ins
+        (raw_ref,) = outs
+        raw_ref[rows_own, :] = total
+        flat = total * norm_factor(row_sum(total * total))
+        return (x_ref[rows_all, :].astype(wide) + flat * gain_ref[0:1, :]).astype(low)
+    if mode == "ffn":
+        x_ref, gain_ref, raw_ref, cot_ref = ins
+        (out_ref,) = outs
+        raw = raw_ref[rows_own, :]
+        h = x_ref[rows_all, :].astype(wide) + raw * norm_factor(row_sum(raw * raw)) * gain_ref[0:1, :]
+        factor = norm_factor(row_sum(total * total))
+        flat = total * factor
+        gain = gain_ref[1:2, :]
+        out_ref[rows_own, :] = (h + flat * gain).astype(low)
+        scaled = cot_ref[rows_own, :].astype(wide) * gain
+        return (factor * (scaled - flat * (row_sum(scaled * flat) * (1.0 / D)))).astype(low)
+    gain_ref, raw_ref, cot_ref = ins
+    (grad_ref,) = outs
+    grad = cot_ref[rows_own, :].astype(wide) + total
+    grad_ref[rows_own, :] = grad
+    raw = raw_ref[rows_own, :]
+    factor = norm_factor(row_sum(raw * raw))
+    flat = raw * factor
+    scaled = grad * gain_ref[0:1, :]
+    return (factor * (scaled - flat * (row_sum(scaled * flat) * (1.0 / D)))).astype(low)
+
+def relay_kernel(mode, n, m, hop, n_in, part_ref, *refs):
+    ins = refs[:n_in]
+    all_ref = refs[n_in]
+    outs = refs[n_in + 1:n_in + 2]
+    recv_right, recv_left, send_right, send_left, sems_send, sems_recv = refs[n_in + 2:]
+    c = lax.axis_index("col")
+    half = part_ref.shape[0] // 2
+    chunks = half // m
+    left = {"col": jnp.maximum(c - 1, 0)}
+    right = {"col": jnp.minimum(c + 1, n - 1)}
+    first = c == 0
+    last = c == n - 1
+    inner = jnp.logical_and(c > 0, c < n - 1)
+
+    def rows(j, base=0):
+        return pl.ds(pl.multiple_of(base + j * m, m), m)
+
+    def send(kind, j, src, dst, to):
+        return pltpu.make_async_remote_copy(src_ref=src, dst_ref=dst, send_sem=sems_send.at[kind, j],
+                                            recv_sem=sems_recv.at[kind, j], device_id=to, device_id_type=MESH)
+
+    def reduce_right(j):
+        return send(0, j, part_ref.at[rows(j, half)], recv_right.at[rows(j)], right)
+    def reduce_right_mid(j):
+        return send(0, j, send_right.at[rows(j)], recv_right.at[rows(j)], right)
+    def reduce_left(j):
+        return send(1, j, part_ref.at[rows(j)], recv_left.at[rows(j)], left)
+    def reduce_left_mid(j):
+        return send(1, j, send_left.at[rows(j)], recv_left.at[rows(j)], left)
+    def spread_left(j):
+        return send(2, j, all_ref.at[rows(j, half)], all_ref.at[rows(j, half)], left)
+    def spread_right(j):
+        return send(3, j, all_ref.at[rows(j)], all_ref.at[rows(j)], right)
+
+    barrier = pltpu.get_barrier_semaphore()
+    @pl.when(c > 0)
+    def _():
+        pl.semaphore_signal(barrier, inc=1, device_id=left, device_id_type=MESH)
+    @pl.when(c < n - 1)
+    def _():
+        pl.semaphore_signal(barrier, inc=1, device_id=right, device_id_type=MESH)
+    @pl.when(inner)
+    def _():
+        pl.semaphore_wait(barrier, 2)
+    @pl.when(jnp.logical_not(inner))
+    def _():
+        pl.semaphore_wait(barrier, 1)
+
+    @pl.loop(0, chunks + hop * 2 * (n - 1))
+    def _(i):
+        def on(offset, who, run):
+            j = i - offset
+            @pl.when(jnp.logical_and(who, jnp.logical_and(j >= 0, j < chunks)))
+            def _():
+                run(j)
+
+        def first_right(j):
+            reduce_right(j).start()
+        def mid_right(j):
+            reduce_right_mid(j).wait_recv()
+            send_right[rows(j), :] = (part_ref[rows(j, half), :].astype(wide) + recv_right[rows(j), :].astype(wide)).astype(low)
+            reduce_right_mid(j).start()
+        def end_right(j):
+            reduce_right_mid(j).wait_recv()
+            total = part_ref[rows(j, half), :].astype(wide) + recv_right[rows(j), :].astype(wide)
+            all_ref[rows(j, half), :] = owner_step(mode, total, rows(j, half), rows(j), ins, outs)
+            spread_left(j).start()
+        def first_left(j):
+            reduce_left(j).start()
+        def mid_left(j):
+            reduce_left_mid(j).wait_recv()
+            send_left[rows(j), :] = (part_ref[rows(j), :].astype(wide) + recv_left[rows(j), :].astype(wide)).astype(low)
+            reduce_left_mid(j).start()
+        def end_left(j):
+            reduce_left_mid(j).wait_recv()
+            total = part_ref[rows(j), :].astype(wide) + recv_left[rows(j), :].astype(wide)
+            all_ref[rows(j), :] = owner_step(mode, total, rows(j), rows(j), ins, outs)
+            spread_right(j).start()
+        def pass_left(j):
+            spread_left(j).wait_recv()
+            spread_left(j).start()
+        def pass_right(j):
+            spread_right(j).wait_recv()
+            spread_right(j).start()
+
+        on(0, first, first_right)
+        on(0, last, first_left)
+        on(hop * c, inner, mid_right)
+        on(hop * (n - 1 - c), inner, mid_left)
+        on(hop * (n - 1), last, end_right)
+        on(hop * (n - 1), first, end_left)
+        on(hop * (2 * (n - 1) - c), inner, pass_left)
+        on(hop * (n - 1 + c), inner, pass_right)
+
+    @pl.loop(0, chunks)
+    def _(j):
+        @pl.when(first)
+        def _():
+            reduce_right(j).wait_send()
+            spread_right(j).wait_send()
+            spread_left(j).wait_recv()
+        @pl.when(last)
+        def _():
+            reduce_left(j).wait_send()
+            spread_left(j).wait_send()
+            spread_right(j).wait_recv()
+        @pl.when(inner)
+        def _():
+            reduce_right_mid(j).wait_send()
+            reduce_left_mid(j).wait_send()
+            spread_left(j).wait_send()
+            spread_right(j).wait_send()
+
+kinds = {"attn": 0, "ffn": 1, "back": 2}
+
+def relay(mode, part, ins, n, m=16, hop=2):
+    group, width = part.shape
+    half = group // 2
+    chunks = half // m
+    saved = jax.ShapeDtypeStruct((half, width), low if mode == "ffn" else wide)
+    return pl.pallas_call(
+        functools.partial(relay_kernel, mode, n, m, hop, len(ins)),
+        out_shape=[jax.ShapeDtypeStruct((group, width), low), saved],
+        in_specs=[VM] * (1 + len(ins)),
+        out_specs=[VM] * 2,
+        scratch_shapes=[pltpu.VMEM((half, width), low)] * 4
+        + [pltpu.SemaphoreType.DMA((4, chunks))] * 2,
+        compiler_params=pltpu.CompilerParams(collective_id=kinds[mode], has_side_effects=True, vmem_limit_bytes=60 << 20),
+        name="relay_" + mode,
+    )(part, *ins)
 
 
 def per_device(
@@ -95,7 +380,7 @@
     col_count = lax.axis_size("col")
     row_at = lax.axis_index("row")
     tree_tokens = seg_ids.shape[0]
-    assert tree_sets.shape[0] == 1
+    assert tree_sets.shape[0] == 1 and col_count == 4
     set_count = output_adapter_first.shape[0]
     own = tokens.shape[0] // row_count
     group = own * col_count
@@ -103,7 +388,6 @@
     width_col = gain_q.shape[0]
     hidden_col = down_weight.shape[0]
     heads_col = width_col // HEAD
-    score_scale = HEAD ** (-0.5)
     tree_set = tree_sets[0]
 
     def pick(table, axis):
@@ -164,7 +448,12 @@
         moved = lax.all_to_all(by_row, "row", split_axis=0, concat_axis=0, tiled=True)
         return moved.reshape(heads_col, group, parts, HEAD).transpose(1, 2, 0, 3).reshape(group, parts * width_col)
 
+    first = lax.axis_index("col") == 0
+    final = lax.axis_index("col") == col_count - 1
     x_own = to_tokens(tokens)
+    g_own = to_tokens(cotangent)
+    g_moved = lax.ppermute(g_own, "col", [(1, 0), (col_count - 2, col_count - 1)])
+    g_half = jnp.concatenate([jnp.where(first, g_own, g_moved), jnp.where(first, g_moved, g_own)], axis=0)
     x = gather_col(x_own)
     red_qkv = dot_t(x, a_qkv).astype(low)
     raw = dot(x, w_qkv)
@@ -189,24 +478,14 @@
     q_low = turn(q_flat * gain_q, sin_own).astype(low)
     k_low = turn(k_flat * gain_k, sin_own).astype(low)
     qkv_head = to_heads(jnp.concatenate([q_low, k_low, v_raw.astype(low)], axis=1), 3)
-    q_head = qkv_head[:, :HEAD]
-    k_head = qkv_head[:, HEAD : 2 * HEAD]
-    v_head = qkv_head[:, 2 * HEAD :]
-    visible = tree_mask(seg_ids, positions, parents)
-    scores = jnp.where(visible, dot_t(q_head, k_head) * score_scale, masked_out)
-    highest = jnp.max(scores, axis=1, keepdims=True)
-    raised = jnp.exp(scores - highest)
-    probs = raised / jnp.sum(raised, axis=1, keepdims=True)
-    probs_low = probs.astype(low)
-    attn_head = dot(probs_low, v_head).astype(low)
+    parent_at, branch_flag = tree_tables(seg_ids, parents)
+    pos_down, pos_across = positions[:, None], positions[None, :]
+    attn_head, lse = attend(qkv_head, parent_at, branch_flag, pos_down, pos_across)
     attn = from_heads(attn_head, 1)
 
     red_out = dot_t(attn, a_out).astype(low)
-    a_raw = scatter_col(dot(attn, w_out) + dot(red_out, b_out))
-    a_factor = norm_factor(jnp.sum(a_raw * a_raw, axis=1))
-    a_flat = a_raw * a_factor[:, None]
-    h_own = x_own.astype(wide) + a_flat * gains[0]
-    h = gather_col(h_own.astype(low))
+    part_a = (dot(attn, w_out) + dot(red_out, b_out)).astype(low)
+    h, a_raw = relay("attn", part_a, (x, gains), col_count)
 
     red_gu = dot_t(h, a_gu).astype(low)
     gate = dot(h, w_gu[:, :hidden_col]) + dot(red_gu[:, :RANK], b_gu[0])
@@ -214,16 +493,14 @@
     sigma = jax.nn.sigmoid(gate)
     hidden = (gate * sigma * up).astype(low)
     red_down = dot_t(hidden, a_down).astype(low)
-    f_raw = scatter_col(dot(hidden, w_down) + dot(red_down, b_down))
-    f_factor = norm_factor(jnp.sum(f_raw * f_raw, axis=1))
-    f_flat = f_raw * f_factor[:, None]
-    out_own = (h_own + f_flat * gains[1]).astype(low)
+    part_f = (dot(hidden, w_down) + dot(red_down, b_down)).astype(low)
+    d_f, out_half = relay("ffn", part_f, (x, gains, a_raw, g_half), col_count)
+    out_moved = lax.ppermute(
+        jnp.where(first, out_half[own:], out_half[:own]), "col", [(0, 1), (col_count - 1, col_count - 2)]
+    )
+    out_own = jnp.where(first, out_half[:own], jnp.where(final, out_half[own:], out_moved))
     layer_out = to_width(out_own)
 
-    g_own = to_tokens(cotangent).astype(wide)
-    scaled_f = g_own * gains[1]
-    d_f_own = norm_back(scaled_f, f_flat, f_factor, jnp.sum(scaled_f * f_flat, axis=1)).astype(low)
-    d_f = gather_col(d_f_own)
     back_down = dot_t(d_f, b_down).astype(low)
     d_hidden = dot_t(d_f, w_down) + dot(back_down, a_down)
     d_gate = (d_hidden * up * sigma * (1.0 + gate * (1.0 - sigma))).astype(low)
@@ -231,23 +508,18 @@
     back_gate = dot_t(d_gate, b_gu[0]).astype(low)
     back_up = dot_t(d_up, b_gu[1]).astype(low)
     back_gu = jnp.concatenate([back_gate, back_up], axis=1)
-    d_h = g_own + scatter_col(
+    part_h = (
         dot_t(d_gate, w_gu[:, :hidden_col]) + dot_t(d_up, w_gu[:, hidden_col:]) + dot(back_gu, a_gu)
-    )
-    scaled_a = d_h * gains[0]
-    d_a_own = norm_back(scaled_a, a_flat, a_factor, jnp.sum(scaled_a * a_flat, axis=1)).astype(low)
-    d_a = gather_col(d_a_own)
+    ).astype(low)
+    d_a, d_h_half = relay("back", part_h, (gains, a_raw, g_half), col_count)
     back_out = dot_t(d_a, b_out).astype(low)
     d_attn = (dot_t(d_a, w_out) + dot(back_out, a_out)).astype(low)
 
     d_attn_head = to_heads(d_attn, 1)
-    d_probs = dot_t(d_attn_head, v_head)
-    inner = jnp.sum(probs * d_probs, axis=1, keepdims=True)
-    d_scores = (probs * (d_probs - inner)).astype(low)
-    dq_head = (dot(d_scores, k_head) * score_scale).astype(low)
-    dk_head = (t_dot(d_scores, q_head) * score_scale).astype(low)
-    dv_head = t_dot(probs_low, d_attn_head).astype(low)
-    d_qkv = from_heads(jnp.concatenate([dq_head, dk_head, dv_head], axis=1), 3)
+    d_qkv_head = attend_back(
+        qkv_head, d_attn_head, parent_at, branch_flag, pos_down, pos_across, lse
+    )
+    d_qkv = from_heads(d_qkv_head, 3)
     dq_n = turn(d_qkv[:, :width_col].astype(wide), -sin_own) * gain_q
     dk_n = turn(d_qkv[:, width_col : 2 * width_col].astype(wide), -sin_own) * gain_k
     cross_qk = lax.psum(jnp.stack([jnp.sum(dq_n * q_flat, axis=1), jnp.sum(dk_n * k_flat, axis=1)]), "col")
@@ -258,7 +530,8 @@
     back_qkv = jnp.concatenate(
         [dot_t(d, b) for d, b in zip((d_q, d_k, d_v), (b_qkv[0], b_qkv[1], b_qkv[2]))], axis=1
     ).astype(low)
-    in_own = d_h + scatter_col(dot_t(d_raw, w_qkv) + dot(back_qkv, a_qkv))
+    d_h_all = jnp.concatenate([jnp.where(first, d_h_half, 0.0), jnp.where(final, d_h_half, 0.0)], axis=0)
+    in_own = scatter_col(dot_t(d_raw, w_qkv) + dot(back_qkv, a_qkv) + d_h_all)
     input_grad = to_width(in_own.astype(low)).astype(wide)
 
     full_width = jnp.concatenate(

time: 1170 us -> 886 us (0.76)
  waiting for transfers between devices: 654 us -> 211 us
  Pallas kernels: 0 us -> 260 us
  matrix products: 212 us -> 137 us
  other arithmetic: 66.5 us -> 32.3 us
  starting transfers between devices: 16.9 us -> 31.7 us
    pallas_call x0 -> x5, Pallas kernels: none -> 260 us  [the longest x3 225 us: relay(): pl.pallas_call(functools.partial(relay_kernel, mode, n, m, hop, len(ins))...]
    all_gather x4 -> x1, waiting for transfers between devices: 200 us -> 30.1 us  [gather_col(): return lax.all_gather(values, 'col', axis=0, tiled=True)]
    reduce_scatter x4 -> x1, waiting for transfers between devices: 174 us -> 43.6 us  [scatter_col(): lax.psum_scatter(values.astype(low), 'col', scatter_dimension=0, tiled=True)]
    all_gather x1, waiting for transfers between devices: 104 us -> 0.03 us  [per_device(): lax.all_gather(gate_up_weight, 'row', axis=0, tiled=True)]
    all_gather x1, blocking collectives: 5.18 us -> 42.8 us  [per_device(): lax.all_gather(jnp.stack([gain_attn, gain_ffn]), 'row', axis=1, tiled=True)]
    dot_general x18 -> x16, matrix products: 84.8 us -> 53.1 us  [dot_t(): return lax.dot_general(left, right, last_last, preferred_element_type=wide)]
    convert_element_type x4 -> x1, other arithmetic: 28.8 us -> 0.56 us  [tree_tables(): flag = (tail_parent > 0).astype(jnp.int32)]
    all_to_all x2 -> x0, blocking collectives: 25.5 us -> none  [the longest x1 12.8 us: to_heads(): lax.all_to_all(by_head, 'row', split_axis=0, concat_axis=0, tiled=True)]
  transfers between devices with their start and end apart: 19 -> 18, of which waited for: 18 -> 11; matrix products, arithmetic and copies ran while one was open for 11% -> 17% of each run, Pallas kernels for 0% -> 11%
where the time goes in v2:
time: 886 us; the launch traced here: 877 us
  Pallas kernels  260 us (29%)
  waiting for transfers between devices  211 us (24%)
  matrix products  137 us (15%)
  blocking collectives  99.5 us (11%)
  local copies, waits for them, and re-layouts  89.1 us (10%)
  other arithmetic  32.3 us (4%)
  starting transfers between devices  31.7 us (4%)
  between operations  16.8 us (2%)
    pallas_call x3, Pallas kernels, relay(): pl.pallas_call(functools.partial(relay_kernel, mode, n, m, hop, len(ins))...  225 us
    dot_general x16, matrix products, dot(): return jnp.dot(left, right, preferred_element_type=wide)  69.4 us
    dot_general x16, matrix products, dot_t(): return lax.dot_general(left, right, last_last, preferred_element_type=wide)  53.1 us
    reduce_scatter x1, waiting for transfers between devices, scatter_col(): lax.psum_scatter(values.astype(low), 'col', scatter_dimension=0, tiled=True)  43.6 us
    all_gather x1, blocking collectives, per_device(): lax.all_gather(jnp.stack([gain_attn, gain_ffn]), 'row', axis=1, tiled=True)  42.8 us
    all_gather x1, waiting for transfers between devices, per_device(): lax.all_gather(query_key_value_weight, 'row', axis=0, tiled=True)  40.9 us
    unnamed x11, waiting for transfers between devices  31.4 us
    all_to_all x2, waiting for transfers between devices, from_heads(): lax.all_to_all(by_row, 'row', split_axis=0, concat_axis=0, tiled=True)  30.7 us
  transfers between devices with their start and end apart: 18, of which 11 were waited for; matrix products, arithmetic and copies ran while one was open for 17% of the time, Pallas kernels for 11%

profile of v2, /device:TPU:0, one launch (start us, length us, event | category | flops | bytes accessed | tf_op | source)
XLA Modules:
  0.0 877.4 jit_solution(16394950827561682727)
XLA Ops:
  7.2 14.6 %all_to_all.90 = bf16[4,160,512]{2,1,0:T(8,128)(2,1)S(1)} all-to-all(bf16[4,160,512]{2,1,0:T(8,128)(2,1)} %bitcast.257), channel_id=1, replica_groups=mesh['dp'=2,'row'=4,'col'=4] {'row'}, dimensions={0} | all-to-all | bytes 1310720 | tf_op jit(solution)/shard_map/all_to_all | solution.py:422
  34.9 9.7 %all_gather.33 = bf16[7,16,2048]{2,1,0:T(8,128)(2,1)S(1)} all-gather(bf16[7,16,512]{2,1,0:T(8,128)(2,1)S(1)} %pad_maximum_fusion.8), channel_id=1, replica_groups=mesh['dp'=2,'row'=4,'col'=4] {'row'}, dimensions={2}, use_global_device_ids=true | all-gather | bytes 573440 | tf_op jit(solution)/shard_map/all_gather | solution.py:405
  48.7 30.1 %all-gather.8.cloned.1.call-done.refs_0_ = bf16[640,2048]{1,0:T(8,128)(2,1)} async-done(((bf16[160,2048]{1,0:T(8,128)(2,1)}), bf16[640,2048]{1,0:T(8,128)(2,1)}) %all-gather.8.cloned.1.call-update) | async-done | bytes 2621456 | tf_op jit(solution)/shard_map/all_gather | solution.py:428
  84.6 40.9 %all-gather.10.cloned.1.call-done = bf16[2048,3,512]{0,2,1:T(8,128)(2,1)} async-done(((bf16[512,3,512]{0,2,1:T(8,128)(2,1)}), bf16[2048,3,512]{0,2,1:T(8,128)(2,1)}) %all-gather.10.cloned.1.call-update) | async-done | bytes 6291472 | tf_op jit(solution)/shard_map/all_gather | solution.py:416
  136.4 12.1 %psum.14 = f32[2,640]{1,0:T(2,128)S(1)} all-reduce(f32[2,640]{1,0:T(2,128)S(1)} %pad_maximum_fusion.17), channel_id=1, replica_groups=mesh['dp'=2,'row'=4,'col'=4] {'col'}, use_global_device_ids=true, to_apply=%region_4.5 | all-reduce | flops 1280 | bytes 10240 | tf_op jit(solution)/shard_map/psum | solution.py:465
  182.0 42.8 %all_gather.35.refs_1_.refs_0_ = f32[2,2048]{1,0:T(2,128)} all-gather(f32[2,512]{1,0:T(2,128)S(1)} %pad_maximum_fusion.19), channel_id=1, replica_groups=mesh['dp'=2,'row'=4,'col'=4] {'row'}, dimensions={1}, use_global_device_ids=true | all-gather | bytes 20480 | tf_op jit(solution)/shard_map/all_gather | solution.py:414
  233.7 15.4 %attend.1 = (bf16[2560,128]{1,0:T(8,128)(2,1)}, f32[2560,1]{1,0:T(8,128)}) custom-call(s32[12]{0:T(128)} %select_reduce_fusion.parent_ref, s32[12]{0:T(128)} %compare_convert_fusion.1.flag_ref, bf16[2560,384]{1,0:T(8,128)(2,1)} %bitcast.213, bf16[2560,384]{1,0:T(8,128)(2,1)} %bitcast.214, bf16[2560,384]{1,0:T(8,128)(2,1)} %bitcast.215, ...), custom_call_target="tpu_custom_call" | custom-call | tf_op jit(solution)/shard_map/attend/pallas_call | solution.py:158
  255.9 16.2 %all-to-all-done.2 = bf16[4,640,128]{2,1,0:T(8,128)(2,1)S(1)} async-done(((bf16[4,640,128]{2,1,0:T(8,128)(2,1)}), bf16[4,640,128]{2,1,0:T(8,128)(2,1)S(1)}, u32[]{:S(2)}, u32[]{:S(2)}) %all-to-all-start.2) | async-done | bytes 655392 | tf_op jit(solution)/shard_map/all_to_all | solution.py:448
  279.8 77.3 %relay_attn.1 = (bf16[640,2048]{1,0:T(8,128)(2,1)}, f32[320,2048]{1,0:T(8,128)}) custom-call(bf16[640,2048]{1,0:T(8,128)(2,1)} %add_convert_fusion.2.part_ref, bf16[640,2048]{1,0:T(8,128)(2,1)} %all-gather.8.cloned.1.call-done.refs_0_, f32[2,2048]{1,0:T(2,128)} %all_gather.35.refs_1_.refs_0_), custom_call_target="tpu_custom_call" | custom-call | tf_op jit(solution)/shard_map/relay_attn/pallas_call | solution.py:342
  359.8 12.4 %copy.116 = bf16[256,8,2,2048]{3,1,2,0:T(8,128)(2,1)S(1)} copy(bf16[256,8,2,2048]{3,2,1,0:T(2,128)(2,1)} %bitcast.219) | data formatting | bytes 33554432
  390.9 8.8 %fusion.72 = f32[640,2048]{1,0:T(8,128)S(1)} fusion(bf16[640,2048]{1,0:T(8,128)(2,1)} %copy-done.9, bf16[2048,2048]{1,0:T(8,128)(2,1)} %all-gather.16.cloned.1.call-done), kind=kOutput, calls=%fused_computation.192 | convolution fusion | flops 5368709120 | bytes 16252928 | tf_op jit(solution)/shard_map/dot_general | solution.py:29
  402.9 76.6 %relay_ffn.1 = (bf16[640,2048]{1,0:T(8,128)(2,1)}, bf16[320,2048]{1,0:T(8,128)(2,1)}) custom-call(bf16[640,2048]{1,0:T(8,128)(2,1)} %add_convert_fusion.1.part_ref, bf16[640,2048]{1,0:T(8,128)(2,1)} %all-gather.8.cloned.1.call-done.refs_0_, f32[2,2048]{1,0:T(2,128)} %all_gather.35.refs_1_.refs_0_, f32[320,2048]{1,0:T(8,128)} %get-tuple-element.20.refs_2_.refs_1_, ...), custom_call_target="tpu_custom_call" | custom-call | tf_op jit(solution)/shard_map/relay_ffn/pallas_call | solution.py:342
  482.2 9.6 %fusion.73 = f32[640,2048]{1,0:T(8,128)} fusion(bf16[640,2048]{1,0:T(8,128)(2,1)S(1)} %copy-done.15, bf16[2048,2048]{1,0:T(8,128)(2,1)} %all-gather.16.cloned.1.call-done), kind=kOutput, calls=%fused_computation.193 | convolution fusion | flops 5368709120 | bytes 16252928 | tf_op jit(solution)/shard_map/dot_general | solution.py:33
  491.9 9.8 %multiply_convert_fusion = (bf16[640,2048]{1,0:T(8,128)(2,1)S(1)}, bf16[640,2048]{1,0:T(8,128)(2,1)}) fusion(f32[640,2048]{1,0:T(8,128)} %copy-done.19, f32[640,2048]{1,0:T(8,128)} %get-tuple-element.102, f32[640,2048]{1,0:T(8,128)} %fusion.73, bf16[640,16]{0,1:T(8,128)(2,1)S(1)} %convolution_convert_fusion.16, f32[8,16,2048]{2,1,0:T(8,128)} %param.42, ...), kind=kOutput, calls=%fused_computation.11 | convolution fusion | flops 60293120 | bytes 21057540 | tf_op jit(solution)/shard_map/dot_general | solution.py:29
  509.8 9.3 %fusion.4 = f32[640,2048]{1,0:T(8,128)} fusion(bf16[640,2048]{1,0:T(8,128)(2,1)} %get-tuple-element.65, bf16[2048,4096]{1,0:T(8,128)(2,1)S(1)} %bitcast.225), kind=kOutput, calls=%fused_computation.4 | convolution fusion | flops 5368709120 | bytes 16252928 | tf_op jit(solution)/shard_map/dot_general | solution.py:33
  526.4 70.9 %relay_back.1 = (bf16[640,2048]{1,0:T(8,128)(2,1)}, f32[320,2048]{1,0:T(8,128)}) custom-call(bf16[640,2048]{1,0:T(8,128)(2,1)} %add_convert_fusion.part_ref, f32[2,2048]{1,0:T(2,128)} %all_gather.35.refs_1_.refs_0_, f32[320,2048]{1,0:T(8,128)} %get-tuple-element.20.refs_2_.refs_1_, bf16[320,2048]{1,0:T(8,128)(2,1)} %pad_maximum_fusion.1.refs_3_.refs_2_), custom_call_target="tpu_custom_call" | custom-call | tf_op jit(solution)/shard_map/relay_back/pallas_call | solution.py:342
  607.6 10.2 %all-to-all-done.5 = bf16[4,640,128]{2,1,0:T(8,128)(2,1)S(1)} async-done(((bf16[4,640,128]{2,1,0:T(8,128)(2,1)}), bf16[4,640,128]{2,1,0:T(8,128)(2,1)S(1)}, u32[]{:S(2)}, u32[]{:S(2)}) %all-to-all-start.5) | async-done | bytes 655392 | tf_op jit(solution)/shard_map/all_to_all | solution.py:435
  618.7 19.9 %attend_back.1 = bf16[2560,384]{1,0:T(8,128)(2,1)} custom-call(s32[12]{0:T(128)} %select_reduce_fusion.parent_ref, s32[12]{0:T(128)} %compare_convert_fusion.1.flag_ref, bf16[2560,384]{1,0:T(8,128)(2,1)} %bitcast.216, bf16[2560,384]{1,0:T(8,128)(2,1)} %bitcast.217, bf16[2560,384]{1,0:T(8,128)(2,1)} %bitcast.218, bf16[2560,128]{1,0:T(8,128)(2,1)} %bitcast.238, ...), custom_call_target="tpu_custom_call" | custom-call | tf_op jit(solution)/shard_map/attend_back/pallas_call | solution.py:170
  655.1 14.5 %all-to-all-done.6 = bf16[4,640,384]{2,1,0:T(8,128)(2,1)S(1)} async-done(((bf16[4,640,384]{2,1,0:T(8,128)(2,1)}), bf16[4,640,384]{2,1,0:T(8,128)(2,1)S(1)}, u32[]{:S(2)}, u32[]{:S(2)}) %all-to-all-start.6) | async-done | bytes 1966112 | tf_op jit(solution)/shard_map/all_to_all | solution.py:448
  690.4 10.8 %psum.15 = f32[2,640]{1,0:T(2,128)S(1)} all-reduce(f32[2,640]{1,0:T(2,128)S(1)} %pad_maximum_fusion.18), channel_id=1, replica_groups=mesh['dp'=2,'row'=4,'col'=4] {'col'}, use_global_device_ids=true, to_apply=%region_7.8 | all-reduce | flops 1280 | bytes 10240 | tf_op jit(solution)/shard_map/psum | solution.py:525
  713.6 8.8 fusion.13
  738.9 14.0 %collective-permute-done.1 = bf16[160,2048]{1,0:T(8,128)(2,1)S(1)} collective-permute-done((bf16[160,2048]{1,0:T(8,128)(2,1)S(1)}, bf16[160,2048]{1,0:T(8,128)(2,1)S(1)}, u32[]{:S(2)}, u32[]{:S(2)}) %collective-permute-start.1) | collective-permute-done | bytes 655392 | tf_op jit(solution)/shard_map/ppermute | solution.py:498
  768.5 29.6 %all-reduce.5.cloned.1.call-done = bf16[4,7,4,512]{3,2,0,1:T(4,128)(2,1)} async-done(((bf16[4,7,4,512]{3,2,0,1:T(4,128)(2,1)}), bf16[4,7,4,512]{3,2,0,1:T(4,128)(2,1)}) %all-reduce.5.cloned.1.call-update) | async-done | bytes 114704
  808.9 43.6 %reduce-scatter.4.cloned.1.call-done = bf16[160,2048]{1,0:T(8,128)(2,1)} async-done(((bf16[640,2048]{1,0:T(8,128)(2,1)}), bf16[160,2048]{1,0:T(8,128)(2,1)}) %reduce-scatter.4.cloned.1.call-update) | async-done | bytes 655376 | tf_op jit(solution)/shard_map/reduce_scatter | solution.py:431
  (308 shorter events, 252.9 us)
Async XLA Ops:
  7.2 221.5 %copy-start = (f32[2,8,16,2048]{3,2,1,0:T(8,128)S(1)}, f32[2,8,16,2048]{3,2,1,0:T(8,128)}, u32[]{:S(2)}) copy-start(f32[2,8,16,2048]{3,2,1,0:T(8,128)} %param.41) | copy-start | bytes 6291460
  7.2 71.5 %all-gather.8.cloned.1.call-start = ((), (), s32[]{:S(2)}) async-start(), calls=%async_computation.10 | async-start | bytes 3276800 | tf_op jit(solution)/shard_map/all_gather | solution.py:428
  22.8 102.7 %all-gather.10.cloned.1.call-start = ((), (), s32[]{:S(2)}) async-start(), calls=%async_computation.11 | async-start | bytes 7864320 | tf_op jit(solution)/shard_map/all_gather | solution.py:416
  25.5 247.9 %all-gather.12.cloned.1.call-start = ((), (), s32[]{:S(2)}) async-start(), calls=%async_computation.12 | async-start | bytes 2621440 | tf_op jit(solution)/shard_map/all_gather | solution.py:417
  26.2 333.6 %all-gather.14.cloned.1.call-start = ((), (), s32[]{:S(2)}) async-start(), calls=%async_computation.13 | async-start | bytes 20971520 | tf_op jit(solution)/shard_map/all_gather | solution.py:418
  26.8 146.2 %all-to-all-start.3 = ((bf16[4,160,512]{2,1,0:T(8,128)(2,1)}), bf16[4,160,512]{2,1,0:T(8,128)(2,1)}, u32[]{:S(2)}, u32[]{:S(2)}) async-start(bf16[4,160,512]{2,1,0:T(8,128)(2,1)} %bitcast.32), calls=%async_computation.3 | async-start | bytes 1310720 | tf_op jit(solution)/shard_map/all_to_all | solution.py:422
  31.0 359.8 %all-gather.16.cloned.1.call-start = ((), (), s32[]{:S(2)}) async-start(), calls=%async_computation.14 | async-start | bytes 10485760 | tf_op jit(solution)/shard_map/all_gather | solution.py:419
  45.3 37.4 %copy-start.26 = (bf16[3,16,2048]{2,1,0:T(8,128)(2,1)}, bf16[3,16,2048]{2,1,0:T(8,128)(2,1)S(1)}, u32[]{:S(2)}) copy-start(bf16[3,16,2048]{2,1,0:T(8,128)(2,1)S(1)} %slice.220) | copy-start | bytes 589828
  46.3 37.9 %copy-start.34 = (bf16[3,1,16,512]{3,2,1,0:T(8,128)(2,1)}, bf16[3,1,16,512]{3,2,1,0:T(8,128)(2,1)S(1)}, u32[]{:S(2)}) copy-start(bf16[3,1,16,512]{3,2,1,0:T(8,128)(2,1)S(1)} %dynamic-slice_convert_fusion.2) | copy-start | bytes 147460
  173.0 51.7 %copy-start.59 = (s32[1,13]{1,0:T(1,128)S(1)}, s32[1,13]{1,0:T(1,128)}, u32[]{:S(2)}) copy-start(s32[1,13]{1,0:T(1,128)} %param.26) | copy-start | bytes 160
  173.0 56.3 %all-to-all-start.1 = ((bf16[4,640,384]{1,2,0:T(8,128)(2,1)}), bf16[4,640,384]{1,2,0:T(8,128)(2,1)}, u32[]{:S(2)}, u32[]{:S(2)}) async-start(bf16[4,640,384]{1,2,0:T(8,128)(2,1)} %bitcast.233), calls=%async_computation.1 | async-start | bytes 3932160 | tf_op jit(solution)/shard_map/all_to_all | solution.py:435
  226.1 28.5 %collective-permute-start = (bf16[160,2048]{1,0:T(8,128)(2,1)S(1)}, bf16[160,2048]{1,0:T(8,128)(2,1)S(1)}, u32[]{:S(2)}, u32[]{:S(2)}) collective-permute-start(bf16[160,2048]{1,0:T(8,128)(2,1)S(1)} %bitcast.245), channel_id=1, source_target_pairs={{1,0},{2,3},{5,4},{6,7},{9,8},{10,11},{13,12},{14,15},{17,16},{18,... | collective-permute-start | bytes 1966088 | tf_op jit(solution)/shard_map/ppermute | solution.py:455
  251.1 21.0 %all-to-all-start.2 = ((bf16[4,640,128]{2,1,0:T(8,128)(2,1)}), bf16[4,640,128]{2,1,0:T(8,128)(2,1)S(1)}, u32[]{:S(2)}, u32[]{:S(2)}) async-start(bf16[4,640,128]{2,1,0:T(8,128)(2,1)} %bitcast.19), calls=%async_computation.2 | async-start | bytes 1310720 | tf_op jit(solution)/shard_map/all_to_all | solution.py:448
  526.4 73.6 %copy-start.25 = (bf16[512,2048]{1,0:T(8,128)(2,1)S(1)}, bf16[512,2048]{1,0:T(8,128)(2,1)}, u32[]{:S(2)}) copy-start(bf16[512,2048]{1,0:T(8,128)(2,1)} %all-gather.12.cloned.1.call-done) | copy-start | bytes 6291460
  604.1 13.7 %all-to-all-start.5 = ((bf16[4,640,128]{2,1,0:T(8,128)(2,1)}), bf16[4,640,128]{2,1,0:T(8,128)(2,1)S(1)}, u32[]{:S(2)}, u32[]{:S(2)}) async-start(bf16[4,640,128]{2,1,0:T(8,128)(2,1)} %bitcast.38), calls=%async_computation.5 | async-start | bytes 1310720 | tf_op jit(solution)/shard_map/all_to_all | solution.py:435
  641.6 28.0 %all-to-all-start.6 = ((bf16[4,640,384]{2,1,0:T(8,128)(2,1)}), bf16[4,640,384]{2,1,0:T(8,128)(2,1)S(1)}, u32[]{:S(2)}, u32[]{:S(2)}) async-start(bf16[4,640,384]{2,1,0:T(8,128)(2,1)} %bitcast.234), calls=%async_computation.6 | async-start | bytes 3932160 | tf_op jit(solution)/shard_map/all_to_all | solution.py:448
  645.4 80.6 %reduce-scatter.6.cloned.1.call-start = ((), (), s32[]{:S(2)}) async-start(), calls=%async_computation.16 | async-start | bytes 573440 | tf_op jit(solution)/shard_map/reduce_scatter | solution.py:540
  707.3 60.3 %all-reduce.7.cloned.1.call-start = ((), (), s32[]{:S(2)}) async-start(), calls=%async_computation.18 | async-start | bytes 524288
  713.5 84.6 %all-reduce.5.cloned.1.call-start = ((), (), s32[]{:S(2)}) async-start(), calls=%async_computation.17 | async-start | bytes 229376
  727.6 125.0 %reduce-scatter.4.cloned.1.call-start = ((), (), s32[]{:S(2)}) async-start(), calls=%async_computation.15 | async-start | bytes 3276800 | tf_op jit(solution)/shard_map/reduce_scatter | solution.py:431
  735.4 26.7 %copy-start.60 = (u32[32]{0:T(128)S(1)}, u32[32]{0:T(128)}, u32[]{:S(2)}) copy-start(u32[32]{0:T(128)} %constant.76) | copy-start | bytes 388
  735.5 17.4 %collective-permute-start.1 = (bf16[160,2048]{1,0:T(8,128)(2,1)S(1)}, bf16[160,2048]{1,0:T(8,128)(2,1)S(1)}, u32[]{:S(2)}, u32[]{:S(2)}) collective-permute-start(bf16[160,2048]{1,0:T(8,128)(2,1)S(1)} %broadcast_select_fusion.2), channel_id=1, source_target_pairs={{0,1},{3,2},{4,5},{7,6},{8,9},{11,10},{12,13},{15,14},{16,17},{19,... | collective-permute-start | bytes 1966088 | tf_op jit(solution)/shard_map/ppermute | solution.py:498
  753.9 13.7 %all-to-all-start.4 = ((bf16[160,4,512]{2,0,1:T(8,128)(2,1)}), bf16[160,4,512]{2,0,1:T(8,128)(2,1)S(1)}, u32[]{:S(2)}, u32[]{:S(2)}) async-start(bf16[160,4,512]{2,0,1:T(8,128)(2,1)} %bitcast.208), calls=%async_computation.4 | async-start | bytes 1310720 | tf_op jit(solution)/shard_map/all_to_all | solution.py:425
  854.6 13.8 %all-to-all-start.7 = ((bf16[160,4,512]{2,0,1:T(8,128)(2,1)}), bf16[160,4,512]{2,0,1:T(8,128)(2,1)S(1)}, u32[]{:S(2)}, u32[]{:S(2)}) async-start(bf16[160,4,512]{2,0,1:T(8,128)(2,1)} %bitcast.207), calls=%async_computation.8 | async-start | bytes 1310720 | tf_op jit(solution)/shard_map/all_to_all | solution.py:425
  (60 other events, 380.6 us)
Sparse Core Ops, SparseCore 0:
  22.9 55.7 all-gather.7
  80.3 45.1 all-gather.9
  127.0 22.5 all-gather.11
  151.1 134.0 all-gather.13
  286.6 58.2 all-gather.15
  707.4 18.5 reduce-scatter.5
  728.9 31.9 all-reduce.6
  763.9 34.1 all-reduce.4
  800.4 52.0 reduce-scatter.3

commit v3 on v2

--- a/solution.py
+++ b/solution.py
@@ -15,6 +15,7 @@
 QT = 256
 MESH = pl.DeviceIdType.MESH
 VM = pl.BlockSpec(memory_space=pltpu.VMEM)
+precise = lax.Precision.HIGHEST
 
 epsilon = 1e-06
 rope_base = 500000.0
@@ -41,25 +42,11 @@
     half_width = HEAD // 2
     frequency = rope_base ** (-(jnp.arange(half_width, dtype=wide) * 2.0) / HEAD)
     angle_table = positions.astype(wide)[:, None] * frequency[None, :]
-    return (jnp.cos(angle_table)[:, None, :], jnp.sin(angle_table)[:, None, :])
-
-
-def rotate(values, cosine, sine):
-    half_width = values.shape[-1] // 2
-    first_half = values[..., :half_width]
-    second_half = values[..., half_width:]
-    return jnp.concatenate(
-        [first_half * cosine - second_half * sine, second_half * cosine + first_half * sine],
-        axis=-1,
-    )
+    return (jnp.cos(angle_table), jnp.sin(angle_table))
 
 
 def norm_factor(square_sum):
     return lax.rsqrt(square_sum * (1.0 / D) + epsilon)
-
-
-def norm_back(scaled, flat, factor, cross_sum):
-    return factor[:, None] * (scaled - flat * (cross_sum / D)[:, None])
 
 
 def tail_scores(q, k_ref, own_at, parent_at, has_parent, pos_q, pos_k):
@@ -351,6 +338,683 @@
     )(part, *ins)
 
 
+def params(collective):
+    return pltpu.CompilerParams(collective_id=collective, has_side_effects=True, vmem_limit_bytes=60 << 20)
+
+
+def span(at, size):
+    return pl.ds(pl.multiple_of(at, size), size)
+
+
+def remote(src, dst, send_sem, recv_sem, to):
+    return pltpu.make_async_remote_copy(
+        src_ref=src, dst_ref=dst, send_sem=send_sem, recv_sem=recv_sem, device_id=to, device_id_type=MESH
+    )
+
+
+def greet(n, nr):
+    r, c = lax.axis_index("row"), lax.axis_index("col")
+    me = r * n + c
+    barrier = pltpu.get_barrier_semaphore()
+
+    @pl.loop(1, n * nr)
+    def _(d):
+        peer = lax.rem(me + d, n * nr)
+        pl.semaphore_signal(barrier, inc=1, device_id={"row": peer // n, "col": lax.rem(peer, n)}, device_id_type=MESH)
+
+    pl.semaphore_wait(barrier, n * nr - 1)
+
+
+def enter_kernel(n, nr, m, tok_ref, x_ref, send_a, recv_a, send_z, recv_z, local_sem):
+    r, c = lax.axis_index("row"), lax.axis_index("col")
+    own = tok_ref.shape[0] // nr
+    width = tok_ref.shape[1]
+    chunks = own // m
+    left = {"col": jnp.maximum(c - 1, 0)}
+    right = {"col": jnp.minimum(c + 1, n - 1)}
+
+    def piece(d, j):
+        peer = lax.rem(r + d, nr)
+        return remote(
+            tok_ref.at[span(peer * own + j * m, m)],
+            x_ref.at[span(c * own + j * m, m), span(r * width, width)],
+            send_a.at[d - 1, j], recv_a.at[d - 1, j], {"row": peer},
+        )
+
+    def block(kind, s, at, j, to):
+        rows = span(at * own + j * m, m)
+        return remote(x_ref.at[rows], x_ref.at[rows], send_z.at[kind, s, j], recv_z.at[kind, s, j], to)
+
+    keep = pltpu.make_async_copy(
+        tok_ref.at[span(r * own, own)], x_ref.at[span(c * own, own), span(r * width, width)], local_sem
+    )
+    keep.start()
+    barrier = pltpu.get_barrier_semaphore()
+    for d in range(1, nr):
+        pl.semaphore_signal(barrier, inc=1, device_id={"row": lax.rem(r + d, nr)}, device_id_type=MESH)
+
+    @pl.when(c > 0)
+    def _():
+        pl.semaphore_signal(barrier, inc=1, device_id=left, device_id_type=MESH)
+
+    @pl.when(c < n - 1)
+    def _():
+        pl.semaphore_signal(barrier, inc=1, device_id=right, device_id_type=MESH)
+
+    inner = jnp.logical_and(c > 0, c < n - 1)
+
+    @pl.when(inner)
+    def _():
+        pl.semaphore_wait(barrier, nr + 1)
+
+    @pl.when(jnp.logical_not(inner))
+    def _():
+        pl.semaphore_wait(barrier, nr)
+
+    @pl.loop(0, chunks)
+    def _(j):
+        for d in range(1, nr):
+            piece(d, j).start()
+
+    keep.wait()
+
+    for s in range(n):
+        @pl.loop(0, chunks)
+        def _(j):
+            if s == 0:
+                for d in range(1, nr):
+                    piece(d, j).wait_recv()
+
+            @pl.when(c - s >= 0)
+            def _():
+                if s > 0:
+                    block(0, s - 1, jnp.maximum(c - s, 0), j, right).wait_recv()
+                if s < n - 1:
+                    @pl.when(c < n - 1)
+                    def _():
+                        block(0, s, jnp.maximum(c - s, 0), j, right).start()
+
+            @pl.when(c + s <= n - 1)
+            def _():
+                if s > 0:
+                    block(1, s - 1, jnp.minimum(c + s, n - 1), j, left).wait_recv()
+                if s < n - 1:
+                    @pl.when(c > 0)
+                    def _():
+                        block(1, s, jnp.minimum(c + s, n - 1), j, left).start()
+
+    @pl.loop(0, chunks)
+    def _(j):
+        for d in range(1, nr):
+            piece(d, j).wait_send()
+        for s in range(n - 1):
+            @pl.when(jnp.logical_and(c - s >= 0, c < n - 1))
+            def _():
+                block(0, s, jnp.maximum(c - s, 0), j, right).wait_send()
+
+            @pl.when(jnp.logical_and(c + s <= n - 1, c > 0))
+            def _():
+                block(1, s, jnp.minimum(c + s, n - 1), j, left).wait_send()
+
+
+def enter(tokens, n, nr, m=32):
+    own = tokens.shape[0] // nr
+    chunks = own // m
+    dma = pltpu.SemaphoreType.DMA
+    return pl.pallas_call(
+        functools.partial(enter_kernel, n, nr, m),
+        out_shape=jax.ShapeDtypeStruct((own * n, tokens.shape[1] * nr), tokens.dtype),
+        in_specs=[VM],
+        out_specs=VM,
+        scratch_shapes=[dma((nr - 1, chunks)), dma((nr - 1, chunks)), dma((2, n - 1, chunks)), dma((2, n - 1, chunks)), dma],
+        compiler_params=params(3),
+        name="enter",
+    )(tokens)
+
+
+def row_sums(first, second):
+    ones = jnp.ones((8, first.shape[1]), wide)
+    at = lax.broadcasted_iota(jnp.int32, (8, first.shape[0]), 0)
+    sum_first = lax.dot_general(ones, first, last_last, preferred_element_type=wide, precision=precise)
+    sum_second = lax.dot_general(ones, second, last_last, preferred_element_type=wide, precision=precise)
+    return jnp.where(at < 4, sum_first, sum_second)
+
+
+def down_columns(values, at):
+    pick = (lax.broadcasted_iota(jnp.int32, (8, HEAD), 0) == at).astype(wide)
+    return lax.dot_general(values, pick, first_first, preferred_element_type=wide, precision=precise)
+
+
+def swap_stats(stats, n, send_sem, recv_sem):
+    c = lax.axis_index("col")
+
+    def copy(d):
+        peer = lax.rem(c + d, n)
+        return remote(stats.at[c], stats.at[c], send_sem.at[d - 1], recv_sem.at[d - 1], {"col": peer})
+
+    for d in range(1, n):
+        copy(d).start()
+    for d in range(1, n):
+        copy(d).wait()
+
+
+def heads_kernel(n, nr, m, raw_ref, gq_ref, gk_ref, cos_ref, sin_ref, cot_ref, out_ref, factor_ref, half_ref,
+                 stats, buf, fq, fk, send_s, recv_s, send_h, recv_h, send_g, recv_g, local_sem, local_g):
+    r, c = lax.axis_index("row"), lax.axis_index("col")
+    rows_all = raw_ref.shape[0]
+    own = rows_all // n
+    width = gq_ref.shape[1]
+    heads = width // HEAD
+    tree_part = own * nr
+    q_all = raw_ref[:, :width]
+    k_all = raw_ref[:, width:2 * width]
+    stats[c] = row_sums(q_all * q_all, k_all * k_all)
+    greet(n, nr)
+    middle = n // 2
+    owner = jnp.where(c < middle, 0, n - 1)
+    at_owner = jnp.where(c < middle, c, c - middle)
+    cot_width = cot_ref.shape[1]
+
+    def cot_piece(d):
+        peer = lax.rem(r + d, nr)
+        return remote(
+            cot_ref.at[span(peer * own, own)],
+            half_ref.at[span(at_owner * own, own), span(r * cot_width, cot_width)],
+            send_g.at[d], recv_g.at[at_owner, d], {"row": peer, "col": owner},
+        )
+
+    def cot_local():
+        return pltpu.make_async_copy(
+            cot_ref.at[span(r * own, own)],
+            half_ref.at[span(at_owner * own, own), span(r * cot_width, cot_width)], local_g
+        )
+
+    swap_stats(stats, n, send_s, recv_s)
+    for d in range(1, nr):
+        cot_piece(d).start()
+
+    @pl.when(owner == c)
+    def _():
+        cot_local().start()
+
+    @pl.when(owner != c)
+    def _():
+        cot_piece(0).start()
+
+    total = stats[0]
+    for s in range(1, n):
+        total = total + stats[s]
+    factor = lax.rsqrt(total * (1.0 / D) + epsilon)
+    factor_ref[...] = factor
+    fq[...] = down_columns(factor, 0)
+    fk[...] = down_columns(factor, 4)
+
+    def piece(d, i, at):
+        peer = lax.rem(r + d, nr)
+        block = i // (own // m)
+        inside = lax.rem(i, own // m)
+        return remote(
+            buf.at[peer, span(i * m, m)],
+            out_ref.at[span(block * tree_part + r * own + inside * m, m)],
+            send_h.at[d - 1, i], recv_h.at[d - 1, i], {"row": peer},
+        )
+
+    def local(i):
+        block = i // (own // m)
+        inside = lax.rem(i, own // m)
+        return pltpu.make_async_copy(
+            buf.at[r, span(i * m, m)], out_ref.at[span(block * tree_part + r * own + inside * m, m)], local_sem.at[i]
+        )
+
+    steps = rows_all // m
+
+    @pl.loop(0, steps)
+    def _(i):
+        rows = span(i * m, m)
+        cosine = cos_ref[rows, :]
+        sine = sin_ref[rows, :]
+        for h in range(heads):
+            lanes = slice(h * HEAD, (h + 1) * HEAD)
+            u = raw_ref[rows, lanes] * fq[rows, :] * gq_ref[:, lanes]
+            buf[h, rows, :HEAD] = (u * cosine + pltpu.roll(u, HEAD // 2, 1) * sine).astype(low)
+            k_lanes = slice(width + h * HEAD, width + (h + 1) * HEAD)
+            u = raw_ref[rows, k_lanes] * fk[rows, :] * gk_ref[:, lanes]
+            buf[h, rows, HEAD:2 * HEAD] = (u * cosine + pltpu.roll(u, HEAD // 2, 1) * sine).astype(low)
+            v_lanes = slice(2 * width + h * HEAD, 2 * width + (h + 1) * HEAD)
+            buf[h, rows, 2 * HEAD:] = raw_ref[rows, v_lanes].astype(low)
+        for d in range(1, nr):
+            piece(d, i, 0).start()
+        local(i).start()
+
+    @pl.loop(0, steps)
+    def _(i):
+        for d in range(1, nr):
+            piece(d, i, 0).wait()
+        local(i).wait()
+
+    for d in range(1, nr):
+        cot_piece(d).wait_send()
+
+    @pl.when(owner != c)
+    def _():
+        cot_piece(0).wait_send()
+
+    @pl.when(owner == c)
+    def _():
+        cot_local().wait()
+        for b in range(middle):
+            for d in range(nr):
+                def take():
+                    remote(
+                        cot_ref.at[span(r * own, own)],
+                        half_ref.at[span(b * own, own), span(0, cot_width)],
+                        send_g.at[d], recv_g.at[b, d], {"row": r, "col": c},
+                    ).wait_recv()
+                if d == 0:
+                    pl.when(b != at_owner)(take)
+                else:
+                    take()
+
+
+def to_heads_call(raw, gain_q, gain_k, cos2, sin2, cot, n, nr, m=80):
+    rows_all, wide3 = raw.shape
+    width = wide3 // 3
+    own = rows_all // n
+    dma = pltpu.SemaphoreType.DMA
+    steps = rows_all // m
+    return pl.pallas_call(
+        functools.partial(heads_kernel, n, nr, m),
+        out_shape=[
+            jax.ShapeDtypeStruct((own * n * nr, 3 * HEAD), low),
+            jax.ShapeDtypeStruct((8, rows_all), wide),
+            jax.ShapeDtypeStruct((own * n // 2, cot.shape[1] * nr), low),
+        ],
+        in_specs=[VM] * 6,
+        out_specs=[VM] * 3,
+        scratch_shapes=[
+            pltpu.VMEM((n, 8, rows_all), wide),
+            pltpu.VMEM((width // HEAD, rows_all, 3 * HEAD), low),
+            pltpu.VMEM((rows_all, HEAD), wide),
+            pltpu.VMEM((rows_all, HEAD), wide),
+            dma((n - 1,)), dma((n - 1,)), dma((nr - 1, steps)), dma((nr - 1, steps)),
+            dma((nr,)), dma((n // 2, nr)), dma((steps,)), dma,
+        ],
+        compiler_params=params(4),
+        name="to_heads",
+    )(raw, gain_q, gain_k, cos2, sin2, cot)
+
+
+def unheads_kernel(n, nr, d_ref, raw_ref, factor_ref, gq_ref, gk_ref, cos_ref, sin_ref, res_ref, out_ref, res_out,
+                   stats, buf, nq, nk, pq, pk, fq, fk, send_s, recv_s, send_h, recv_h, send_o, recv_o, local_sem, local_o):
+    r, c = lax.axis_index("row"), lax.axis_index("col")
+    rows_all = raw_ref.shape[0]
+    own = rows_all // n
+    width = gq_ref.shape[1]
+    heads = width // HEAD
+    tree_part = own * nr
+    middle = n // 2
+    out_width = res_out.shape[1]
+
+    def piece(d, b):
+        peer = lax.rem(r + d, nr)
+        return remote(
+            d_ref.at[span(b * tree_part + peer * own, own)],
+            buf.at[r, span(b * own, own)],
+            send_h.at[d - 1, b], recv_h.at[d - 1, b], {"row": peer},
+        )
+
+    def local(b):
+        return pltpu.make_async_copy(
+            d_ref.at[span(b * tree_part + r * own, own)], buf.at[r, span(b * own, own)], local_sem.at[b]
+        )
+
+    is_owner = jnp.logical_or(c == 0, c == n - 1)
+    base = jnp.where(c == 0, 0, middle)
+
+    def result_piece(b, d):
+        peer = lax.rem(r + d, nr)
+        return remote(
+            res_ref.at[span(b * own, own), span(peer * out_width, out_width)],
+            res_out.at[span(r * own, own)],
+            send_o.at[b, d], recv_o.at[d], {"row": peer, "col": base + b},
+        )
+
+    def result_local(b):
+        return pltpu.make_async_copy(
+            res_ref.at[span(b * own, own), span(r * out_width, out_width)], res_out.at[span(r * own, own)], local_o
+        )
+
+    for b in range(n):
+        local(b).start()
+    greet(n, nr)
+    for b in range(n):
+        for d in range(1, nr):
+            piece(d, b).start()
+
+    @pl.when(is_owner)
+    def _():
+        for b in range(middle):
+            for d in range(nr):
+                if d == 0:
+                    @pl.when(base + b == c)
+                    def _():
+                        result_local(b).start()
+
+                    @pl.when(base + b != c)
+                    def _():
+                        result_piece(b, d).start()
+                else:
+                    result_piece(b, d).start()
+
+    fq[...] = down_columns(factor_ref[...], 0)
+    fk[...] = down_columns(factor_ref[...], 4)
+    for b in range(n):
+        for d in range(1, nr):
+            piece(d, b).wait_recv()
+        local(b).wait()
+        rows = slice(b * own, (b + 1) * own)
+        cosine = cos_ref[rows, :]
+        sine = sin_ref[rows, :]
+        for h in range(heads):
+            lanes = slice(h * HEAD, (h + 1) * HEAD)
+            u = buf[h, rows, :HEAD].astype(wide)
+            u = (u * cosine - pltpu.roll(u, HEAD // 2, 1) * sine) * gq_ref[:, lanes]
+            nq[rows, lanes] = u
+            pq[rows, lanes] = u * raw_ref[rows, lanes] * fq[rows, :]
+            u = buf[h, rows, HEAD:2 * HEAD].astype(wide)
+            u = (u * cosine - pltpu.roll(u, HEAD // 2, 1) * sine) * gk_ref[:, lanes]
+            nk[rows, lanes] = u
+            pk[rows, lanes] = u * raw_ref[rows, slice(width + h * HEAD, width + (h + 1) * HEAD)] * fk[rows, :]
+            out_ref[rows, slice(2 * width + h * HEAD, 2 * width + (h + 1) * HEAD)] = buf[h, rows, 2 * HEAD:]
+    stats[c] = row_sums(pq[...], pk[...])
+    swap_stats(stats, n, send_s, recv_s)
+    total = stats[0]
+    for s in range(1, n):
+        total = total + stats[s]
+    mean = total * (1.0 / D) * factor_ref[...]
+    pq[:, :HEAD] = down_columns(mean, 0)
+    pk[:, :HEAD] = down_columns(mean, 4)
+    for b in range(n):
+        rows = slice(b * own, (b + 1) * own)
+        for h in range(heads):
+            lanes = slice(h * HEAD, (h + 1) * HEAD)
+            k_lanes = slice(width + h * HEAD, width + (h + 1) * HEAD)
+            out_ref[rows, lanes] = (fq[rows, :] * (nq[rows, lanes] - raw_ref[rows, lanes] * pq[rows, :HEAD])).astype(low)
+            out_ref[rows, k_lanes] = (fk[rows, :] * (nk[rows, lanes] - raw_ref[rows, k_lanes] * pk[rows, :HEAD])).astype(low)
+    for b in range(n):
+        for d in range(1, nr):
+            piece(d, b).wait_send()
+
+    @pl.when(is_owner)
+    def _():
+        for b in range(middle):
+            for d in range(nr):
+                if d == 0:
+                    @pl.when(base + b == c)
+                    def _():
+                        result_local(b).wait()
+
+                    @pl.when(base + b != c)
+                    def _():
+                        result_piece(b, d).wait_send()
+                else:
+                    result_piece(b, d).wait_send()
+
+    for d in range(nr):
+        def take():
+            remote(
+                res_ref.at[span(0, own), span(0, out_width)], res_out.at[span(r * own, own)],
+                send_o.at[0, d], recv_o.at[d], {"row": r, "col": c},
+            ).wait_recv()
+        if d == 0:
+            pl.when(jnp.logical_not(is_owner))(take)
+        else:
+            take()
+
+
+def from_heads_call(d_head, raw, factor, gain_q, gain_k, cos2, sin2, result, n, nr):
+    rows_all, wide3 = raw.shape
+    width = wide3 // 3
+    dma = pltpu.SemaphoreType.DMA
+    square = pltpu.VMEM((rows_all, width), wide)
+    return pl.pallas_call(
+        functools.partial(unheads_kernel, n, nr),
+        out_shape=[
+            jax.ShapeDtypeStruct((rows_all, wide3), low),
+            jax.ShapeDtypeStruct((rows_all // n * nr, result.shape[1] // nr), low),
+        ],
+        in_specs=[VM] * 8,
+        out_specs=[VM] * 2,
+        scratch_shapes=[
+            pltpu.VMEM((n, 8, rows_all), wide),
+            pltpu.VMEM((nr, rows_all, 3 * HEAD), low),
+            square, square, square, square,
+            pltpu.VMEM((rows_all, HEAD), wide),
+            pltpu.VMEM((rows_all, HEAD), wide),
+            dma((n - 1,)), dma((n - 1,)), dma((nr - 1, n)), dma((nr - 1, n)),
+            dma((n // 2, nr)), dma((nr,)), dma((n,)), dma,
+        ],
+        compiler_params=params(5),
+        name="from_heads",
+    )(d_head, raw, factor, gain_q, gain_k, cos2, sin2, result)
+
+
+def finish_kernel(n, nr, ndp, m, part_ref, full_ref, col_ref, hot_ref, grad_ref, sets_ref,
+                  recv_right, recv_left, send_right, send_left, own_buf, in_buf, full_recv, full_sum, full_last,
+                  col_recv, owned, hot_all,
+                  send_z, recv_z, send_w, recv_w, local_w, send_f, recv_f, send_c, recv_c, send_l, recv_l,
+                  send_d, recv_d, send_k, recv_k):
+    g, r, c = lax.axis_index("dp"), lax.axis_index("row"), lax.axis_index("col")
+    own = part_ref.shape[0] // n
+    width = in_buf.shape[1]
+    chunks = own // m
+    left = {"col": jnp.maximum(c - 1, 0)}
+    right = {"col": jnp.minimum(c + 1, n - 1)}
+    full_rows = full_last.shape[1]
+    col_rows = col_recv.shape[1]
+
+    def full_piece(d):
+        peer = lax.rem(r + d, nr)
+        return remote(full_ref.at[:, span(peer * width, width)], full_recv.at[r], send_f.at[d - 1], recv_f.at[d - 1], {"row": peer})
+
+    def col_piece(d):
+        peer = lax.rem(r + d, nr)
+        return remote(col_ref.at[span(peer * col_rows, col_rows)], col_recv.at[r], send_c.at[d - 1], recv_c.at[d - 1], {"row": peer})
+
+    def last_piece(d):
+        peer = lax.rem(c + d, n)
+        return remote(full_sum.at[span(peer * full_rows, full_rows)], full_last.at[c], send_l.at[d - 1], recv_l.at[d - 1], {"col": peer})
+
+    def tree_piece(d):
+        peer = lax.rem(g + d, ndp)
+        return remote(owned.at[g], owned.at[g], send_d.at[d - 1], recv_d.at[d - 1], {"dp": peer})
+
+    def hot_piece(d):
+        peer = lax.rem(g + d, ndp)
+        return remote(hot_all.at[g], hot_all.at[g], send_k.at[d - 1], recv_k.at[d - 1], {"dp": peer})
+
+    def reduce(kind, b, j, src):
+        rows = span(b * own + j * m, m)
+        dst, to = ((recv_right, right), (recv_left, left))[kind]
+        return remote(src.at[rows], dst.at[rows], send_z.at[kind, b, j], recv_z.at[kind, b, j], to)
+
+    def width_piece(d, j):
+        peer = lax.rem(r + d, nr)
+        return remote(
+            own_buf.at[span(j * m, m), span(peer * width, width)], in_buf.at[span(r * own + j * m, m)],
+            send_w.at[d - 1, j], recv_w.at[d - 1, j], {"row": peer},
+        )
+
+    def width_local(j):
+        return pltpu.make_async_copy(
+            own_buf.at[span(j * m, m), span(r * width, width)], in_buf.at[span(r * own + j * m, m)], local_w.at[j]
+        )
+
+    me = r * n + c
+    barrier = pltpu.get_barrier_semaphore()
+    for d in range(1, ndp):
+        pl.semaphore_signal(barrier, inc=1, device_id={"dp": lax.rem(g + d, ndp)}, device_id_type=MESH)
+
+    @pl.loop(1, n * nr)
+    def _(d):
+        peer = lax.rem(me + d, n * nr)
+        pl.semaphore_signal(barrier, inc=1, device_id={"row": peer // n, "col": lax.rem(peer, n)}, device_id_type=MESH)
+
+    pl.semaphore_wait(barrier, n * nr - 1 + ndp - 1)
+    hot_all[g] = hot_ref[...]
+    for d in range(1, nr):
+        full_piece(d).start()
+        col_piece(d).start()
+
+    def stage(s):
+        @pl.loop(0, chunks)
+        def _(j):
+            for kind, b, go, edge, acc, got in (
+                (0, n - 1 - s, n - 1 - s > c, c == 0, send_right, recv_right),
+                (1, s, s < c, c == n - 1, send_left, recv_left),
+            ):
+                @pl.when(go)
+                def _():
+                    @pl.when(edge)
+                    def _():
+                        reduce(kind, b, j, part_ref).start()
+
+                    @pl.when(jnp.logical_not(edge))
+                    def _():
+                        rows = span(b * own + j * m, m)
+                        reduce(kind, b, j, acc).wait_recv()
+                        acc[rows, :] = (part_ref[rows, :].astype(wide) + got[rows, :].astype(wide)).astype(low)
+                        reduce(kind, b, j, acc).start()
+
+    stage(0)
+    for d in range(1, nr):
+        full_piece(d).wait_recv()
+        col_piece(d).wait_recv()
+    total = full_ref[:, span(r * width, width)].astype(wide)
+    col_total = col_ref[span(r * col_rows, col_rows), :].astype(wide)
+    for d in range(1, nr):
+        peer = lax.rem(r + d, nr)
+        total = total + full_recv[peer].astype(wide)
+        col_total = col_total + col_recv[peer].astype(wide)
+    full_sum[...] = total.astype(low)
+    owned[g, full_rows:, :] = col_total.astype(low)
+    for d in range(1, n):
+        last_piece(d).start()
+    stage(1)
+    for d in range(1, n):
+        last_piece(d).wait_recv()
+    last = full_sum[span(c * full_rows, full_rows), :].astype(wide)
+    for d in range(1, n):
+        last = last + full_last[lax.rem(c + d, n)].astype(wide)
+    owned[g, :full_rows, :] = last.astype(low)
+    for d in range(1, ndp):
+        tree_piece(d).start()
+        hot_piece(d).start()
+    for s in range(2, n - 1):
+        stage(s)
+
+    rows_own = c * own
+
+    @pl.loop(0, chunks)
+    def _(j):
+        rows = span(rows_own + j * m, m)
+        at = span(j * m, m)
+
+        @pl.when(c == 0)
+        def _():
+            reduce(1, c, j, send_left).wait_recv()
+            own_buf[at, :] = (part_ref[rows, :].astype(wide) + recv_left[rows, :].astype(wide)).astype(low)
+
+        @pl.when(c == n - 1)
+        def _():
+            reduce(0, c, j, send_right).wait_recv()
+            own_buf[at, :] = (part_ref[rows, :].astype(wide) + recv_right[rows, :].astype(wide)).astype(low)
+
+        @pl.when(jnp.logical_and(c > 0, c < n - 1))
+        def _():
+            reduce(0, c, j, send_right).wait_recv()
+            reduce(1, c, j, send_left).wait_recv()
+            own_buf[at, :] = (
+                part_ref[rows, :].astype(wide) + recv_right[rows, :].astype(wide) + recv_left[rows, :].astype(wide)
+            ).astype(low)
+
+        for d in range(1, nr):
+            width_piece(d, j).start()
+        width_local(j).start()
+
+    for d in range(1, ndp):
+        tree_piece(d).wait_recv()
+        hot_piece(d).wait_recv()
+    sets_own = sets_ref.shape[0]
+    for s in range(sets_own):
+        total = owned[0].astype(wide) * hot_all[0, pl.ds(g * sets_own + s, 1), :]
+        for t in range(1, ndp):
+            total = total + owned[t].astype(wide) * hot_all[t, pl.ds(g * sets_own + s, 1), :]
+        sets_ref[s] = total
+
+    @pl.loop(0, chunks)
+    def _(j):
+        for d in range(1, nr):
+            width_piece(d, j).wait()
+        width_local(j).wait()
+
+    grad_ref[...] = in_buf[...].astype(wide)
+    for d in range(1, nr):
+        full_piece(d).wait_send()
+        col_piece(d).wait_send()
+    for d in range(1, n):
+        last_piece(d).wait_send()
+    for d in range(1, ndp):
+        tree_piece(d).wait_send()
+        hot_piece(d).wait_send()
+    for s in range(n - 1):
+        @pl.loop(0, chunks)
+        def _(j):
+            @pl.when(n - 1 - s > c)
+            def _():
+                reduce(0, n - 1 - s, j, send_right).wait_send()
+
+            @pl.when(s < c)
+            def _():
+                reduce(1, s, j, send_left).wait_send()
+
+
+def finish(part, full, cols, hot, sets_own, n, nr, ndp, m=32):
+    rows_all, width_all = part.shape
+    own = rows_all // n
+    width = width_all // nr
+    chunks = own // m
+    full_rows = full.shape[0] // n
+    col_rows = cols.shape[0] // nr
+    dma = pltpu.SemaphoreType.DMA
+    big = pltpu.VMEM((rows_all, width_all), low)
+    return pl.pallas_call(
+        functools.partial(finish_kernel, n, nr, ndp, m),
+        out_shape=[
+            jax.ShapeDtypeStruct((own * nr, width), wide),
+            jax.ShapeDtypeStruct((sets_own, full_rows + col_rows, width), wide),
+        ],
+        in_specs=[VM] * 4,
+        out_specs=[VM] * 2,
+        scratch_shapes=[
+            big, big, big, big,
+            pltpu.VMEM((own, width_all), low),
+            pltpu.VMEM((own * nr, width), low),
+            pltpu.VMEM((nr, full.shape[0], width), low),
+            pltpu.VMEM((full.shape[0], width), low),
+            pltpu.VMEM((n, full_rows, width), low),
+            pltpu.VMEM((nr, col_rows, width), low),
+            pltpu.VMEM((ndp, full_rows + col_rows, width), low),
+            pltpu.VMEM((ndp,) + hot.shape, wide),
+            dma((2, n, chunks)), dma((2, n, chunks)), dma((nr - 1, chunks)), dma((nr - 1, chunks)), dma((chunks,)),
+            dma((nr - 1,)), dma((nr - 1,)), dma((nr - 1,)), dma((nr - 1,)), dma((n - 1,)), dma((n - 1,)),
+            dma((ndp - 1,)), dma((ndp - 1,)), dma((ndp - 1,)), dma((ndp - 1,)),
+        ],
+        compiler_params=params(6),
+        name="finish",
+    )(part, full, cols, hot)
+
+
 def per_device(
     tokens,
     cotangent,
@@ -418,18 +1082,6 @@
     w_gu = lax.all_gather(gate_up_weight, "row", axis=0, tiled=True).reshape(D, 2 * hidden_col)
     w_down = lax.all_gather(down_weight, "row", axis=1, tiled=True)
 
-    def to_tokens(values):
-        return lax.all_to_all(values, "row", split_axis=0, concat_axis=1, tiled=True)
-
-    def to_width(values):
-        return lax.all_to_all(values, "row", split_axis=1, concat_axis=0, tiled=True)
-
-    def gather_col(values):
-        return lax.all_gather(values, "col", axis=0, tiled=True)
-
-    def scatter_col(values):
-        return lax.psum_scatter(values.astype(low), "col", scatter_dimension=0, tiled=True).astype(wide)
-
     def to_heads(values, parts):
         by_head = values.reshape(group, parts, heads_col, HEAD).transpose(2, 0, 1, 3).reshape(heads_col, group, parts * HEAD)
         moved = lax.all_to_all(by_head, "row", split_axis=0, concat_axis=0, tiled=True)
@@ -450,34 +1102,19 @@
 
     first = lax.axis_index("col") == 0
     final = lax.axis_index("col") == col_count - 1
-    x_own = to_tokens(tokens)
-    g_own = to_tokens(cotangent)
-    g_moved = lax.ppermute(g_own, "col", [(1, 0), (col_count - 2, col_count - 1)])
-    g_half = jnp.concatenate([jnp.where(first, g_own, g_moved), jnp.where(first, g_moved, g_own)], axis=0)
-    x = gather_col(x_own)
+    x = enter(tokens, col_count, row_count)
     red_qkv = dot_t(x, a_qkv).astype(low)
     raw = dot(x, w_qkv)
     extra = jnp.concatenate([dot(red_qkv[:, RANK * j : RANK * (j + 1)], b_qkv[j]) for j in range(3)], axis=1)
     raw = raw + extra
-    q_raw = raw[:, :width_col]
-    k_raw = raw[:, width_col : 2 * width_col]
-    v_raw = raw[:, 2 * width_col :]
-    square_qk = lax.psum(jnp.stack([jnp.sum(q_raw * q_raw, axis=1), jnp.sum(k_raw * k_raw, axis=1)]), "col")
-    q_factor = norm_factor(square_qk[0])
-    k_factor = norm_factor(square_qk[1])
-    q_flat = q_raw * q_factor[:, None]
-    k_flat = k_raw * k_factor[:, None]
     pos_own = lax.dynamic_index_in_dim(
         positions.reshape(col_count, row_count, own), row_at, 1, keepdims=False
     ).reshape(group)
-    cos_own, sin_own = angles(pos_own)
-
-    def turn(values, sine):
-        return rotate(values.reshape(group, heads_col, HEAD), cos_own, sine).reshape(group, width_col)
-
-    q_low = turn(q_flat * gain_q, sin_own).astype(low)
-    k_low = turn(k_flat * gain_k, sin_own).astype(low)
-    qkv_head = to_heads(jnp.concatenate([q_low, k_low, v_raw.astype(low)], axis=1), 3)
+    cosine, sine = angles(pos_own)
+    cos2 = jnp.concatenate([cosine, cosine], axis=1)
+    sin2 = jnp.concatenate([-sine, sine], axis=1)
+    gq, gk = gain_q[None, :], gain_k[None, :]
+    qkv_head, factors, g_half = to_heads_call(raw, gq, gk, cos2, sin2, cotangent, col_count, row_count)
     parent_at, branch_flag = tree_tables(seg_ids, parents)
     pos_down, pos_across = positions[:, None], positions[None, :]
     attn_head, lse = attend(qkv_head, parent_at, branch_flag, pos_down, pos_across)
@@ -495,12 +1132,6 @@
     red_down = dot_t(hidden, a_down).astype(low)
     part_f = (dot(hidden, w_down) + dot(red_down, b_down)).astype(low)
     d_f, out_half = relay("ffn", part_f, (x, gains, a_raw, g_half), col_count)
-    out_moved = lax.ppermute(
-        jnp.where(first, out_half[own:], out_half[:own]), "col", [(0, 1), (col_count - 1, col_count - 2)]
-    )
-    out_own = jnp.where(first, out_half[:own], jnp.where(final, out_half[own:], out_moved))
-    layer_out = to_width(out_own)
-
     back_down = dot_t(d_f, b_down).astype(low)
     d_hidden = dot_t(d_f, w_down) + dot(back_down, a_down)
     d_gate = (d_hidden * up * sigma * (1.0 + gate * (1.0 - sigma))).astype(low)
@@ -519,43 +1150,33 @@
     d_qkv_head = attend_back(
         qkv_head, d_attn_head, parent_at, branch_flag, pos_down, pos_across, lse
     )
-    d_qkv = from_heads(d_qkv_head, 3)
-    dq_n = turn(d_qkv[:, :width_col].astype(wide), -sin_own) * gain_q
-    dk_n = turn(d_qkv[:, width_col : 2 * width_col].astype(wide), -sin_own) * gain_k
-    cross_qk = lax.psum(jnp.stack([jnp.sum(dq_n * q_flat, axis=1), jnp.sum(dk_n * k_flat, axis=1)]), "col")
-    d_q = norm_back(dq_n, q_flat, q_factor, cross_qk[0]).astype(low)
-    d_k = norm_back(dk_n, k_flat, k_factor, cross_qk[1]).astype(low)
-    d_v = d_qkv[:, 2 * width_col :]
-    d_raw = jnp.concatenate([d_q, d_k, d_v], axis=1)
+    d_raw, layer_out = from_heads_call(
+        d_qkv_head, raw, factors, gq, gk, cos2, sin2, out_half, col_count, row_count
+    )
+    d_q, d_k, d_v = (d_raw[:, width_col * j : width_col * (j + 1)] for j in range(3))
     back_qkv = jnp.concatenate(
         [dot_t(d, b) for d, b in zip((d_q, d_k, d_v), (b_qkv[0], b_qkv[1], b_qkv[2]))], axis=1
     ).astype(low)
     d_h_all = jnp.concatenate([jnp.where(first, d_h_half, 0.0), jnp.where(final, d_h_half, 0.0)], axis=0)
-    in_own = scatter_col(dot_t(d_raw, w_qkv) + dot(back_qkv, a_qkv) + d_h_all)
-    input_grad = to_width(in_own.astype(low)).astype(wide)
-
-    full_width = jnp.concatenate(
+    part_in = (dot_t(d_raw, w_qkv) + dot(back_qkv, a_qkv) + d_h_all).astype(low)
+
+    rank_own = RANK // col_count
+    full = jnp.concatenate(
         [t_dot(back_qkv, x), t_dot(back_gu, h), t_dot(red_out, d_a), t_dot(red_down, d_f)], axis=0
     ).astype(low)
-    full_width = lax.psum_scatter(full_width, "row", scatter_dimension=1, tiled=True)
-    full_width = full_width.reshape(7, col_count, RANK // col_count, width_row).transpose(1, 0, 2, 3)
-    full_width = lax.psum_scatter(full_width, "col", scatter_dimension=0, tiled=False)
-    col_width = jnp.concatenate(
+    full = full.reshape(7, col_count, rank_own, D).transpose(1, 0, 2, 3).reshape(col_count, 7 * rank_own, D)
+    full = jnp.pad(full, ((0, 0), (0, rank_own), (0, 0))).reshape(col_count * 8 * rank_own, D)
+    cols = jnp.concatenate(
         [t_dot(red_qkv[:, RANK * j : RANK * (j + 1)], d) for j, d in enumerate((d_q, d_k, d_v))]
         + [t_dot(back_out, attn), t_dot(red_gu[:, :RANK], d_gate), t_dot(red_gu[:, RANK:], d_up), t_dot(back_down, hidden)],
         axis=1,
     ).astype(low)
-    col_width = lax.psum_scatter(col_width, "row", scatter_dimension=0, tiled=True)
-    onehot = (tree_set == jnp.arange(set_count, dtype=jnp.int32)).astype(wide)
-    owner = jnp.concatenate([full_width.reshape(-1), col_width.reshape(-1)])
-    owner_all = lax.all_gather(owner, "dp", axis=0, tiled=False).astype(wide)
-    onehot_all = lax.all_gather(onehot, "dp", axis=0, tiled=False)
+    cols = cols.reshape(RANK * 16, width_row)
+    hot = (tree_set == lax.broadcasted_iota(jnp.int32, (set_count, width_row), 0)).astype(wide)
     sets_own = set_count // dp_count
-    onehot_own = lax.dynamic_slice_in_dim(onehot_all, lax.axis_index("dp") * sets_own, sets_own, 1)
-    per_set = jnp.sum(onehot_own[:, :, None] * owner_all[:, None, :], axis=0)
-    split_at = full_width.size
-    full_sets = per_set[:, :split_at].reshape(sets_own, 7, RANK // col_count, width_row)
-    col_sets = per_set[:, split_at:].reshape(sets_own, RANK // row_count, -1)
+    input_grad, sets = finish(part_in, full, cols, hot, sets_own, col_count, row_count, dp_count)
+    full_sets = sets[:, : 7 * rank_own].reshape(sets_own, 7, rank_own, width_row)
+    col_sets = sets[:, 8 * rank_own :].reshape(sets_own, RANK // row_count, 16 * width_row)
     grad_a_qkv = full_sets[:, :3].transpose(1, 0, 2, 3)
     grad_a_gu = full_sets[:, 3:5].transpose(1, 0, 2, 3)
     grad_b_out = full_sets[:, 5]

time: 886 us -> 768 us (0.87)
  Pallas kernels: 260 us -> 509 us
  waiting for transfers between devices: 211 us -> 7.23 us
  blocking collectives: 99.5 us -> 29.9 us
  local copies, waits for them, and re-layouts: 89.1 us -> 45 us
  starting transfers between devices: 31.7 us -> 7.27 us
  other arithmetic: 32.3 us -> 10.7 us
    pallas_call x0 -> x4, Pallas kernels: none -> 244 us  [the longest x1 77.5 us: to_heads_call(): pl.pallas_call(functools.partial(heads_kernel, n, nr, m), out_shape=[jax....]
    reduce_scatter x2 -> x0, waiting for transfers between devices: 47.2 us -> none  [the longest x1 43.6 us: scatter_col(): lax.psum_scatter(values.astype(low), 'col', scatter_dimension=0, tiled=True)]
    all_gather x1, waiting for transfers between devices: 40.9 us -> 0.01 us  [per_device(): lax.all_gather(query_key_value_weight, 'row', axis=0, tiled=True)]
    all_to_all x2 -> x1, waiting for transfers between devices: 30.7 us -> 0.01 us  [from_heads(): lax.all_to_all(by_row, 'row', split_axis=0, concat_axis=0, tiled=True)]
    all_gather x1 -> x0, waiting for transfers between devices: 30.1 us -> none  [gather_col(): return lax.all_gather(values, 'col', axis=0, tiled=True)]
    unnamed x11 -> x4, waiting for transfers between devices: 31.4 us -> 1.92 us
    all_gather x1, blocking collectives: 42.8 us -> 19.2 us  [per_device(): lax.all_gather(jnp.stack([gain_attn, gain_ffn]), 'row', axis=1, tiled=True)]
    psum x2 -> x0, blocking collectives: 22.9 us -> none  [the longest x1 12.1 us: per_device(): lax.psum(jnp.stack([jnp.sum(q_raw * q_raw, axis=1), jnp.sum(k_raw * k_raw...]
  transfers between devices with their start and end apart: 18 -> 6, of which waited for: 11 -> 1; matrix products, arithmetic and copies ran while one was open for 17% -> 10% of each run, Pallas kernels for 11% -> 30%
where the time goes in v3:
time: 768 us; the launch traced here: 756 us
  Pallas kernels  509 us (66%)
  matrix products  131 us (17%)
  local copies, waits for them, and re-layouts  45 us (6%)
  blocking collectives  29.9 us (4%)
  between operations  15.6 us (2%)
  other arithmetic  10.7 us (1%)
    pallas_call x3, Pallas kernels, relay(): pl.pallas_call(functools.partial(relay_kernel, mode, n, m, hop, len(ins))...  230 us
    pallas_call x1, Pallas kernels, to_heads_call(): pl.pallas_call(functools.partial(heads_kernel, n, nr, m), out_shape=[jax....  77.5 us
    dot_general x16, matrix products, dot(): return jnp.dot(left, right, preferred_element_type=wide)  72.2 us
    pallas_call x1, Pallas kernels, finish(): pl.pallas_call(functools.partial(finish_kernel, n, nr, ndp, m), out_shape...  69.2 us
    pallas_call x1, Pallas kernels, enter(): pl.pallas_call(functools.partial(enter_kernel, n, nr, m), out_shape=jax.S...  54.5 us
    dot_general x16, matrix products, dot_t(): return lax.dot_general(left, right, last_last, preferred_element_type=wide)  52.3 us
    pallas_call x1, Pallas kernels, from_heads_call(): pl.pallas_call(functools.partial(unheads_kernel, n, nr), out_shape=[jax.S...  42.8 us
    unnamed x95, local copies, waits for them, and re-layouts  26.1 us
  transfers between devices with their start and end apart: 6, of which 1 were waited for; matrix products, arithmetic and copies ran while one was open for 10% of the time, Pallas kernels for 30%

profile of v3, /device:TPU:0, one launch (start us, length us, event | category | flops | bytes accessed | tf_op | source)
XLA Modules:
  0.0 756.4 jit_solution(11574823285525597061)
XLA Ops:
  18.8 10.8 %all_gather.19 = bf16[7,16,2048]{2,1,0:T(8,128)(2,1)S(1)} all-gather(bf16[7,16,512]{2,1,0:T(8,128)(2,1)S(1)} %pad_maximum_fusion.4), channel_id=1, replica_groups=mesh['dp'=2,'row'=4,'col'=4] {'row'}, dimensions={2}, use_global_device_ids=true | all-gather | bytes 573440 | tf_op jit(solution)/shard_map/all_gather | solution.py:1069
  29.6 54.5 %enter.1.refs_0_ = bf16[640,2048]{1,0:T(8,128)(2,1)} custom-call(bf16[640,512]{1,0:T(8,128)(2,1)} %tok_ref.1), custom_call_target="tpu_custom_call" | custom-call | tf_op jit(solution)/shard_map/enter/pallas_call | solution.py:464
  94.2 11.1 %maximum_add_fusion.1.raw_ref = f32[640,1536]{1,0:T(8,128)} fusion(f32[640,512]{1,0:T(8,128)} %fusion.36, f32[640,512]{1,0:T(8,128)} %fusion.39, f32[640,512]{1,0:T(8,128)} %fusion.42, bf16[640,2048]{1,0:T(8,128)(2,1)} %enter.1.refs_0_, bf16[2048,1536]{0,1:T(8,128)(2,1)} %bitcast.174), kind=kOutput, calls=%fused_computation.18 | convolution fusion | flops 4029480960 | bytes 16777216 | tf_op jit(solution)/shard_map/dot_general | solution.py:30
  105.3 77.5 %to_heads.1 = (bf16[2560,384]{1,0:T(8,128)(2,1)}, f32[8,640]{1,0:T(8,128)}, bf16[320,2048]{1,0:T(8,128)(2,1)}) custom-call(f32[640,1536]{1,0:T(8,128)} %maximum_add_fusion.1.raw_ref, f32[1,512]{1,0:T(1,128)} %bitcast.168, f32[1,512]{1,0:T(1,128)} %bitcast.170, f32[640,128]{1,0:T(8,128)} %get-tuple-element.90.cos_ref, f32[640,128]{1,0:T(8,128)} %get-tuple-element.91.sin_ref, ...), custom_call_target="tpu_custom_call" | custom-call | tf_op jit(solution)/shard_map/to_heads/pallas_call | solution.py:625
  182.8 15.4 %attend.1 = (bf16[2560,128]{1,0:T(8,128)(2,1)}, f32[2560,1]{1,0:T(8,128)}) custom-call(s32[12]{0:T(128)} %select_reduce_fusion.parent_ref, s32[12]{0:T(128)} %compare_convert_fusion.1.flag_ref, bf16[2560,384]{1,0:T(8,128)(2,1)} %get-tuple-element.25.q_ref.k_ref.v_ref, bf16[2560,384]{1,0:T(8,128)(2,1)} %get-tuple-element.25.q_ref.k_ref.v_ref, ...), custom_call_target="tpu_custom_call" | custom-call | tf_op jit(solution)/shard_map/attend/pallas_call | solution.py:145
  203.8 19.2 %all_gather.21.refs_1_.refs_0_ = f32[2,2048]{1,0:T(2,128)} all-gather(f32[2,512]{1,0:T(2,128)S(1)} %pad_maximum_fusion.12), channel_id=1, replica_groups=mesh['dp'=2,'row'=4,'col'=4] {'row'}, dimensions={1}, use_global_device_ids=true | all-gather | bytes 20480 | tf_op jit(solution)/shard_map/all_gather | solution.py:1078
  231.0 76.3 %relay_attn.1 = (bf16[640,2048]{1,0:T(8,128)(2,1)}, f32[320,2048]{1,0:T(8,128)}) custom-call(bf16[640,2048]{1,0:T(8,128)(2,1)} %add_convert_fusion.2.part_ref, bf16[640,2048]{1,0:T(8,128)(2,1)} %enter.1.refs_0_, f32[2,2048]{1,0:T(2,128)} %all_gather.21.refs_1_.refs_0_), custom_call_target="tpu_custom_call" | custom-call | tf_op jit(solution)/shard_map/relay_attn/pallas_call | solution.py:329
  310.0 12.4 %copy.95 = bf16[256,8,2,2048]{3,1,2,0:T(8,128)(2,1)S(1)} copy(bf16[256,8,2,2048]{3,2,1,0:T(2,128)(2,1)} %bitcast.144) | data formatting | bytes 33554432
  322.4 5.6 fusion.6
  328.9 5.6 fusion.2
  341.1 8.8 %fusion.58 = f32[640,2048]{1,0:T(8,128)S(1)} fusion(bf16[640,2048]{1,0:T(8,128)(2,1)} %copy-done.7, bf16[2048,2048]{1,0:T(8,128)(2,1)} %all-gather.11.cloned.1.call-done), kind=kOutput, calls=%fused_computation.134 | convolution fusion | flops 5368709120 | bytes 16252928 | tf_op jit(solution)/shard_map/dot_general | solution.py:30
  353.0 83.9 %relay_ffn.1 = (bf16[640,2048]{1,0:T(8,128)(2,1)}, bf16[320,2048]{1,0:T(8,128)(2,1)}) custom-call(bf16[640,2048]{1,0:T(8,128)(2,1)} %add_convert_fusion.1.part_ref, bf16[640,2048]{1,0:T(8,128)(2,1)} %enter.1.refs_0_, f32[2,2048]{1,0:T(2,128)} %all_gather.21.refs_1_.refs_0_, f32[320,2048]{1,0:T(8,128)} %get-tuple-element.28.refs_2_.refs_1_, ...), custom_call_target="tpu_custom_call" | custom-call | tf_op jit(solution)/shard_map/relay_ffn/pallas_call | solution.py:329
  439.6 9.7 %fusion.59 = f32[640,2048]{1,0:T(8,128)} fusion(bf16[640,2048]{1,0:T(8,128)(2,1)S(1)} %copy-done.15, bf16[2048,2048]{1,0:T(8,128)(2,1)} %all-gather.11.cloned.1.call-done), kind=kOutput, calls=%fused_computation.135 | convolution fusion | flops 5368709120 | bytes 16252928 | tf_op jit(solution)/shard_map/dot_general | solution.py:34
  449.4 9.8 %multiply_convert_fusion = (bf16[640,2048]{1,0:T(8,128)(2,1)S(1)}, bf16[640,2048]{1,0:T(8,128)(2,1)}) fusion(f32[640,2048]{1,0:T(8,128)} %copy-done.18, f32[640,2048]{1,0:T(8,128)} %get-tuple-element.87, f32[640,2048]{1,0:T(8,128)} %fusion.59, bf16[640,16]{0,1:T(8,128)(2,1)S(1)} %convolution_convert_fusion.16, f32[8,16,2048]{2,1,0:T(8,128)} %param.42, ...), kind=kOutput, calls=%fused_computation.11 | convolution fusion | flops 60293120 | bytes 21057540 | tf_op jit(solution)/shard_map/dot_general | solution.py:30
  459.2 7.5 fusion
  467.5 9.2 %fusion.4 = f32[640,2048]{1,0:T(8,128)} fusion(bf16[640,2048]{1,0:T(8,128)(2,1)} %get-tuple-element.71, bf16[2048,4096]{1,0:T(8,128)(2,1)S(1)} %bitcast.150), kind=kOutput, calls=%fused_computation.4 | convolution fusion | flops 5368709120 | bytes 16252928 | tf_op jit(solution)/shard_map/dot_general | solution.py:34
  478.9 6.5 add_convert_fusion.part_ref
  485.4 70.2 %relay_back.1 = (bf16[640,2048]{1,0:T(8,128)(2,1)}, f32[320,2048]{1,0:T(8,128)}) custom-call(bf16[640,2048]{1,0:T(8,128)(2,1)} %add_convert_fusion.part_ref, f32[2,2048]{1,0:T(2,128)} %all_gather.21.refs_1_.refs_0_, f32[320,2048]{1,0:T(8,128)} %get-tuple-element.28.refs_2_.refs_1_, bf16[320,2048]{1,0:T(8,128)(2,1)} %get-tuple-element.29.refs_3_.refs_2_), custom_call_target="tpu_custom_call" | custom-call | tf_op jit(solution)/shard_map/relay_back/pallas_call | solution.py:329
  572.6 5.3 all-to-all-done.1
  578.7 19.9 %attend_back.1.d_ref = bf16[2560,384]{1,0:T(8,128)(2,1)} custom-call(s32[12]{0:T(128)} %select_reduce_fusion.parent_ref, s32[12]{0:T(128)} %compare_convert_fusion.1.flag_ref, bf16[2560,384]{1,0:T(8,128)(2,1)} %get-tuple-element.25.q_ref.k_ref.v_ref, bf16[2560,384]{1,0:T(8,128)(2,1)} %get-tuple-element.25.q_ref.k_ref.v_ref, ...), custom_call_target="tpu_custom_call" | custom-call | tf_op jit(solution)/shard_map/attend_back/pallas_call | solution.py:157
  598.7 42.8 %from_heads.1 = (bf16[640,1536]{1,0:T(8,128)(2,1)}, bf16[640,512]{1,0:T(8,128)(2,1)}) custom-call(bf16[2560,384]{1,0:T(8,128)(2,1)} %attend_back.1.d_ref, f32[640,1536]{1,0:T(8,128)} %maximum_add_fusion.1.raw_ref, f32[8,640]{1,0:T(8,128)} %get-tuple-element.33.factor_ref, f32[1,512]{1,0:T(1,128)} %bitcast.169, f32[1,512]{1,0:T(1,128)} %bitcast.171, ...), custom_call_target="tpu_custom_call" | custom-call | tf_op jit(solution)/shard_map/from_heads/pallas_call | solution.py:780
  641.5 10.1 %fusion.61 = f32[640,2048]{1,0:T(8,128)} fusion(bf16[640,1536]{1,0:T(8,128)(2,1)} %get-tuple-element.36, bf16[2048,1536]{0,1:T(8,128)(2,1)} %bitcast.175), kind=kOutput, calls=%fused_computation.137 | convolution fusion | flops 4026531840 | bytes 13500416 | tf_op jit(solution)/shard_map/dot_general | solution.py:34
  661.7 6.5 fusion.8.part_ref
  668.8 69.2 %finish.1 = (f32[640,512]{1,0:T(8,128)}, f32[4,96,512]{2,1,0:T(8,128)}) custom-call(bf16[640,2048]{1,0:T(8,128)(2,1)} %fusion.8.part_ref, bf16[128,2048]{1,0:T(8,128)(2,1)} %bitcast.158, bf16[256,512]{1,0:T(8,128)(2,1)} %convert_element_type.129.col_ref, f32[8,512]{1,0:T(8,128)} %iota.23.hot_ref), custom_call_target="tpu_custom_call" | custom-call | tf_op jit(solution)/shard_map/finish/pallas_call | solution.py:991
  (187 shorter events, 93.4 us)
Async XLA Ops:
  7.2 216.3 %copy-start = (f32[2,8,16,2048]{3,2,1,0:T(8,128)S(1)}, f32[2,8,16,2048]{3,2,1,0:T(8,128)}, u32[]{:S(2)}) copy-start(f32[2,8,16,2048]{3,2,1,0:T(8,128)} %param.41) | copy-start | bytes 6291460
  7.2 87.0 %all-gather.5.cloned.1.call-start = ((), (), s32[]{:S(2)}) async-start(), calls=%async_computation.2 | async-start | bytes 7864320 | tf_op jit(solution)/shard_map/all_gather | solution.py:1080
  10.0 215.5 %all-gather.7.cloned.1.call-start = ((), (), s32[]{:S(2)}) async-start(), calls=%async_computation.3 | async-start | bytes 2621440 | tf_op jit(solution)/shard_map/all_gather | solution.py:1081
  10.8 299.2 %all-gather.9.cloned.1.call-start = ((), (), s32[]{:S(2)}) async-start(), calls=%async_computation.4 | async-start | bytes 20971520 | tf_op jit(solution)/shard_map/all_gather | solution.py:1082
  11.5 329.6 %all-gather.11.cloned.1.call-start = ((), (), s32[]{:S(2)}) async-start(), calls=%async_computation.5 | async-start | bytes 10485760 | tf_op jit(solution)/shard_map/all_gather | solution.py:1083
  14.1 71.1 %copy-start.38 = (s32[1,13]{1,0:T(1,128)S(1)}, s32[1,13]{1,0:T(1,128)}, u32[]{:S(2)}) copy-start(s32[1,13]{1,0:T(1,128)} %param.26) | copy-start | bytes 160
  29.5 199.1 %copy-start.19 = (bf16[7,16,2048]{2,1,0:T(8,128)(2,1)}, bf16[7,16,2048]{2,1,0:T(8,128)(2,1)S(1)}, u32[]{:S(2)}) copy-start(bf16[7,16,2048]{2,1,0:T(8,128)(2,1)S(1)} %all_gather.19) | copy-start | bytes 1376260
  29.6 59.4 %copy-start.21 = (bf16[3,16,2048]{2,1,0:T(8,128)(2,1)}, bf16[3,16,2048]{2,1,0:T(8,128)(2,1)S(1)}, u32[]{:S(2)}) copy-start(bf16[3,16,2048]{2,1,0:T(8,128)(2,1)S(1)} %slice.149) | copy-start | bytes 589828
  85.3 7.5 copy-start.30
  89.9 15.4 %copy-start.26 = (bf16[640,48]{0,1:T(8,128)(2,1)}, bf16[640,48]{0,1:T(8,128)(2,1)S(1)}, u32[]{:S(2)}) copy-start(bf16[640,48]{0,1:T(8,128)(2,1)S(1)} %fusion.14) | copy-start | bytes 184324
  200.1 24.1 %all-to-all-start = ((bf16[4,640,128]{2,1,0:T(8,128)(2,1)}), bf16[4,640,128]{2,1,0:T(8,128)(2,1)S(1)}, u32[]{:S(2)}, u32[]{:S(2)}) async-start(bf16[4,640,128]{2,1,0:T(8,128)(2,1)} %bitcast.14), calls=%async_computation | async-start | bytes 1310720 | tf_op jit(solution)/shard_map/all_to_all | solution.py:1100
  309.9 24.6 %copy-start.28 = (bf16[640,32]{0,1:T(8,128)(2,1)}, bf16[640,32]{0,1:T(8,128)(2,1)S(1)}, u32[]{:S(2)}) copy-start(bf16[640,32]{0,1:T(8,128)(2,1)S(1)} %convolution_convert_fusion.8) | copy-start | bytes 122884
  310.0 12.4 %copy-start.13 = (bf16[640,2048]{1,0:T(8,128)(2,1)S(1)}, bf16[640,2048]{1,0:T(8,128)(2,1)}, u32[]{:S(2)}) copy-start(bf16[640,2048]{1,0:T(8,128)(2,1)} %get-tuple-element.27) | copy-start | bytes 7864324
  439.6 19.6 %slice-start = ((s8[16777216]{0:T(1024)(128)(4,1)}), s8[4194304]{0:T(1024)(128)(4,1)S(1)}, s32[]{:S(2)}) async-start(s8[16777216]{0:T(1024)(128)(4,1)} %bitcast.147), calls=%async_computation.6 | async-start | bytes 8388608
  439.6 19.6 %slice-start.1 = ((s8[16777216]{0:T(1024)(128)(4,1)}), s8[4194304]{0:T(1024)(128)(4,1)S(1)}, s32[]{:S(2)}) async-start(s8[16777216]{0:T(1024)(128)(4,1)} %bitcast.147), calls=%async_computation.7 | async-start | bytes 8388608
  439.6 19.6 %slice-start.2 = ((s8[16777216]{0:T(1024)(128)(4,1)}), s8[4194304]{0:T(1024)(128)(4,1)S(1)}, s32[]{:S(2)}) async-start(s8[16777216]{0:T(1024)(128)(4,1)} %bitcast.147), calls=%async_computation.8 | async-start | bytes 8388608
  449.4 9.8 %slice-start.3 = ((s8[16777216]{0:T(1024)(128)(4,1)}), s8[4194304]{0:T(1024)(128)(4,1)S(1)}, s32[]{:S(2)}) async-start(s8[16777216]{0:T(1024)(128)(4,1)} %bitcast.147), calls=%async_computation.9 | async-start | bytes 8388608
  459.2 7.5 copy-start.9
  467.5 9.3 %copy-start.11 = (bf16[640,2048]{1,0:T(8,128)(2,1)S(1)}, bf16[640,2048]{1,0:T(8,128)(2,1)}, u32[]{:S(2)}) copy-start(bf16[640,2048]{1,0:T(8,128)(2,1)} %get-tuple-element.71) | copy-start | bytes 7864324
  564.2 13.7 %all-to-all-start.1 = ((bf16[4,640,128]{2,1,0:T(8,128)(2,1)}), bf16[4,640,128]{2,1,0:T(8,128)(2,1)S(1)}, u32[]{:S(2)}, u32[]{:S(2)}) async-start(bf16[4,640,128]{2,1,0:T(8,128)(2,1)} %bitcast.29), calls=%async_computation.1 | async-start | bytes 1310720 | tf_op jit(solution)/shard_map/all_to_all | solution.py:1087
  641.4 10.1 %copy-start.23 = (bf16[640,1536]{1,0:T(8,128)(2,1)S(1)}, bf16[640,1536]{1,0:T(8,128)(2,1)}, u32[]{:S(2)}) copy-start(bf16[640,1536]{1,0:T(8,128)(2,1)} %get-tuple-element.36) | copy-start | bytes 5898244
  641.4 10.1 %copy-start.31 = (bf16[3,1,16,512]{3,2,1,0:T(8,128)(2,1)S(1)}, bf16[3,1,16,512]{3,2,1,0:T(8,128)(2,1)}, u32[]{:S(2)}) copy-start(bf16[3,1,16,512]{3,2,1,0:T(8,128)(2,1)} %copy-done.30) | copy-start | bytes 147460
  641.4 10.9 %copy-start.27 = (bf16[640,48]{0,1:T(8,128)(2,1)S(1)}, bf16[640,48]{0,1:T(8,128)(2,1)}, u32[]{:S(2)}) copy-start(bf16[640,48]{0,1:T(8,128)(2,1)} %copy-done.26) | copy-start | bytes 184324
  741.4 8.0 %copy-start.1 = (f32[2,8,16,2048]{3,2,1,0:T(8,128)S(1)}, f32[2,8,16,2048]{3,2,1,0:T(8,128)}, u32[]{:S(2)}) copy-start(f32[2,8,16,2048]{3,2,1,0:T(8,128)} %param.41) | copy-start | bytes 6291460
  (25 other events, 92.9 us)
Sparse Core Ops, SparseCore 0:
  10.1 58.4 all-gather.4
  70.2 22.6 all-gather.6
  94.5 148.1 all-gather.8
  244.1 58.2 all-gather.10

commit v4 on v3

--- a/solution.py
+++ b/solution.py
@@ -178,166 +178,6 @@
 
 def row_sum(v): return jnp.sum(v, axis=1, keepdims=True)
 
-def owner_step(mode, total, rows_all, rows_own, ins, outs):
-    if mode == "attn":
-        x_ref, gain_ref = ins
-        (raw_ref,) = outs
-        raw_ref[rows_own, :] = total
-        flat = total * norm_factor(row_sum(total * total))
-        return (x_ref[rows_all, :].astype(wide) + flat * gain_ref[0:1, :]).astype(low)
-    if mode == "ffn":
-        x_ref, gain_ref, raw_ref, cot_ref = ins
-        (out_ref,) = outs
-        raw = raw_ref[rows_own, :]
-        h = x_ref[rows_all, :].astype(wide) + raw * norm_factor(row_sum(raw * raw)) * gain_ref[0:1, :]
-        factor = norm_factor(row_sum(total * total))
-        flat = total * factor
-        gain = gain_ref[1:2, :]
-        out_ref[rows_own, :] = (h + flat * gain).astype(low)
-        scaled = cot_ref[rows_own, :].astype(wide) * gain
-        return (factor * (scaled - flat * (row_sum(scaled * flat) * (1.0 / D)))).astype(low)
-    gain_ref, raw_ref, cot_ref = ins
-    (grad_ref,) = outs
-    grad = cot_ref[rows_own, :].astype(wide) + total
-    grad_ref[rows_own, :] = grad
-    raw = raw_ref[rows_own, :]
-    factor = norm_factor(row_sum(raw * raw))
-    flat = raw * factor
-    scaled = grad * gain_ref[0:1, :]
-    return (factor * (scaled - flat * (row_sum(scaled * flat) * (1.0 / D)))).astype(low)
-
-def relay_kernel(mode, n, m, hop, n_in, part_ref, *refs):
-    ins = refs[:n_in]
-    all_ref = refs[n_in]
-    outs = refs[n_in + 1:n_in + 2]
-    recv_right, recv_left, send_right, send_left, sems_send, sems_recv = refs[n_in + 2:]
-    c = lax.axis_index("col")
-    half = part_ref.shape[0] // 2
-    chunks = half // m
-    left = {"col": jnp.maximum(c - 1, 0)}
-    right = {"col": jnp.minimum(c + 1, n - 1)}
-    first = c == 0
-    last = c == n - 1
-    inner = jnp.logical_and(c > 0, c < n - 1)
-
-    def rows(j, base=0):
-        return pl.ds(pl.multiple_of(base + j * m, m), m)
-
-    def send(kind, j, src, dst, to):
-        return pltpu.make_async_remote_copy(src_ref=src, dst_ref=dst, send_sem=sems_send.at[kind, j],
-                                            recv_sem=sems_recv.at[kind, j], device_id=to, device_id_type=MESH)
-
-    def reduce_right(j):
-        return send(0, j, part_ref.at[rows(j, half)], recv_right.at[rows(j)], right)
-    def reduce_right_mid(j):
-        return send(0, j, send_right.at[rows(j)], recv_right.at[rows(j)], right)
-    def reduce_left(j):
-        return send(1, j, part_ref.at[rows(j)], recv_left.at[rows(j)], left)
-    def reduce_left_mid(j):
-        return send(1, j, send_left.at[rows(j)], recv_left.at[rows(j)], left)
-    def spread_left(j):
-        return send(2, j, all_ref.at[rows(j, half)], all_ref.at[rows(j, half)], left)
-    def spread_right(j):
-        return send(3, j, all_ref.at[rows(j)], all_ref.at[rows(j)], right)
-
-    barrier = pltpu.get_barrier_semaphore()
-    @pl.when(c > 0)
-    def _():
-        pl.semaphore_signal(barrier, inc=1, device_id=left, device_id_type=MESH)
-    @pl.when(c < n - 1)
-    def _():
-        pl.semaphore_signal(barrier, inc=1, device_id=right, device_id_type=MESH)
-    @pl.when(inner)
-    def _():
-        pl.semaphore_wait(barrier, 2)
-    @pl.when(jnp.logical_not(inner))
-    def _():
-        pl.semaphore_wait(barrier, 1)
-
-    @pl.loop(0, chunks + hop * 2 * (n - 1))
-    def _(i):
-        def on(offset, who, run):
-            j = i - offset
-            @pl.when(jnp.logical_and(who, jnp.logical_and(j >= 0, j < chunks)))
-            def _():
-                run(j)
-
-        def first_right(j):
-            reduce_right(j).start()
-        def mid_right(j):
-            reduce_right_mid(j).wait_recv()
-            send_right[rows(j), :] = (part_ref[rows(j, half), :].astype(wide) + recv_right[rows(j), :].astype(wide)).astype(low)
-            reduce_right_mid(j).start()
-        def end_right(j):
-            reduce_right_mid(j).wait_recv()
-            total = part_ref[rows(j, half), :].astype(wide) + recv_right[rows(j), :].astype(wide)
-            all_ref[rows(j, half), :] = owner_step(mode, total, rows(j, half), rows(j), ins, outs)
-            spread_left(j).start()
-        def first_left(j):
-            reduce_left(j).start()
-        def mid_left(j):
-            reduce_left_mid(j).wait_recv()
-            send_left[rows(j), :] = (part_ref[rows(j), :].astype(wide) + recv_left[rows(j), :].astype(wide)).astype(low)
-            reduce_left_mid(j).start()
-        def end_left(j):
-            reduce_left_mid(j).wait_recv()
-            total = part_ref[rows(j), :].astype(wide) + recv_left[rows(j), :].astype(wide)
-            all_ref[rows(j), :] = owner_step(mode, total, rows(j), rows(j), ins, outs)
-            spread_right(j).start()
-        def pass_left(j):
-            spread_left(j).wait_recv()
-            spread_left(j).start()
-        def pass_right(j):
-            spread_right(j).wait_recv()
-            spread_right(j).start()
-
-        on(0, first, first_right)
-        on(0, last, first_left)
-        on(hop * c, inner, mid_right)
-        on(hop * (n - 1 - c), inner, mid_left)
-        on(hop * (n - 1), last, end_right)
-        on(hop * (n - 1), first, end_left)
-        on(hop * (2 * (n - 1) - c), inner, pass_left)
-        on(hop * (n - 1 + c), inner, pass_right)
-
-    @pl.loop(0, chunks)
-    def _(j):
-        @pl.when(first)
-        def _():
-            reduce_right(j).wait_send()
-            spread_right(j).wait_send()
-            spread_left(j).wait_recv()
-        @pl.when(last)
-        def _():
-            reduce_left(j).wait_send()
-            spread_left(j).wait_send()
-            spread_right(j).wait_recv()
-        @pl.when(inner)
-        def _():
-            reduce_right_mid(j).wait_send()
-            reduce_left_mid(j).wait_send()
-            spread_left(j).wait_send()
-            spread_right(j).wait_send()
-
-kinds = {"attn": 0, "ffn": 1, "back": 2}
-
-def relay(mode, part, ins, n, m=16, hop=2):
-    group, width = part.shape
-    half = group // 2
-    chunks = half // m
-    saved = jax.ShapeDtypeStruct((half, width), low if mode == "ffn" else wide)
-    return pl.pallas_call(
-        functools.partial(relay_kernel, mode, n, m, hop, len(ins)),
-        out_shape=[jax.ShapeDtypeStruct((group, width), low), saved],
-        in_specs=[VM] * (1 + len(ins)),
-        out_specs=[VM] * 2,
-        scratch_shapes=[pltpu.VMEM((half, width), low)] * 4
-        + [pltpu.SemaphoreType.DMA((4, chunks))] * 2,
-        compiler_params=pltpu.CompilerParams(collective_id=kinds[mode], has_side_effects=True, vmem_limit_bytes=60 << 20),
-        name="relay_" + mode,
-    )(part, *ins)
-
-
 def params(collective):
     return pltpu.CompilerParams(collective_id=collective, has_side_effects=True, vmem_limit_bytes=60 << 20)
 
@@ -365,7 +205,8 @@
     pl.semaphore_wait(barrier, n * nr - 1)
 
 
-def enter_kernel(n, nr, m, tok_ref, x_ref, send_a, recv_a, send_z, recv_z, local_sem):
+def enter_kernel(n, nr, m, tok_ref, table_ref, gain_ref, x_ref, table_all, gain_all,
+                 send_a, recv_a, send_z, recv_z, send_t, recv_t, local_sem):
     r, c = lax.axis_index("row"), lax.axis_index("col")
     own = tok_ref.shape[0] // nr
     width = tok_ref.shape[1]
@@ -385,10 +226,19 @@
         rows = span(at * own + j * m, m)
         return remote(x_ref.at[rows], x_ref.at[rows], send_z.at[kind, s, j], recv_z.at[kind, s, j], to)
 
+    def table_piece(d, kind):
+        src, dst = ((table_ref, table_all), (gain_ref, gain_all))[kind]
+        to = {"row": lax.rem(r + d, nr)}
+        return remote(src, dst.at[:, span(r * width, width)], send_t.at[kind, d - 1], recv_t.at[kind, d - 1], to)
+
     keep = pltpu.make_async_copy(
-        tok_ref.at[span(r * own, own)], x_ref.at[span(c * own, own), span(r * width, width)], local_sem
+        tok_ref.at[span(r * own, own)], x_ref.at[span(c * own, own), span(r * width, width)], local_sem.at[0]
     )
+    keep_table = pltpu.make_async_copy(table_ref, table_all.at[:, span(r * width, width)], local_sem.at[1])
+    keep_gain = pltpu.make_async_copy(gain_ref, gain_all.at[:, span(r * width, width)], local_sem.at[2])
     keep.start()
+    keep_table.start()
+    keep_gain.start()
     barrier = pltpu.get_barrier_semaphore()
     for d in range(1, nr):
         pl.semaphore_signal(barrier, inc=1, device_id={"row": lax.rem(r + d, nr)}, device_id_type=MESH)
@@ -416,7 +266,12 @@
         for d in range(1, nr):
             piece(d, j).start()
 
+    for d in range(1, nr):
+        table_piece(d, 0).start()
+        table_piece(d, 1).start()
     keep.wait()
+    keep_table.wait()
+    keep_gain.wait()
 
     for s in range(n):
         @pl.loop(0, chunks)
@@ -443,6 +298,10 @@
                     def _():
                         block(1, s, jnp.minimum(c + s, n - 1), j, left).start()
 
+    for d in range(1, nr):
+        table_piece(d, 0).wait()
+        table_piece(d, 1).wait()
+
     @pl.loop(0, chunks)
     def _(j):
         for d in range(1, nr):
@@ -457,19 +316,26 @@
                 block(1, s, jnp.minimum(c + s, n - 1), j, left).wait_send()
 
 
-def enter(tokens, n, nr, m=32):
+def enter(tokens, table, gain, n, nr, m=32):
     own = tokens.shape[0] // nr
     chunks = own // m
     dma = pltpu.SemaphoreType.DMA
     return pl.pallas_call(
         functools.partial(enter_kernel, n, nr, m),
-        out_shape=jax.ShapeDtypeStruct((own * n, tokens.shape[1] * nr), tokens.dtype),
-        in_specs=[VM],
-        out_specs=VM,
-        scratch_shapes=[dma((nr - 1, chunks)), dma((nr - 1, chunks)), dma((2, n - 1, chunks)), dma((2, n - 1, chunks)), dma],
+        out_shape=[
+            jax.ShapeDtypeStruct((own * n, tokens.shape[1] * nr), tokens.dtype),
+            jax.ShapeDtypeStruct((table.shape[0], table.shape[1] * nr), table.dtype),
+            jax.ShapeDtypeStruct((gain.shape[0], gain.shape[1] * nr), gain.dtype),
+        ],
+        in_specs=[VM] * 3,
+        out_specs=[VM] * 3,
+        scratch_shapes=[
+            dma((nr - 1, chunks)), dma((nr - 1, chunks)), dma((2, n - 1, chunks)), dma((2, n - 1, chunks)),
+            dma((2, nr - 1)), dma((2, nr - 1)), dma((3,)),
+        ],
         compiler_params=params(3),
         name="enter",
-    )(tokens)
+    )(tokens, table, gain)
 
 
 def row_sums(first, second):
@@ -1015,6 +881,458 @@
     )(part, full, cols, hot)
 
 
+def middle_kernel(n, nr, m, hop, head_ref, x_hbm, cot_hbm, gain_ref, wo_hbm, wg_hbm, wd_hbm,
+                  ao_ref, bo_ref, ag_ref, bg_ref, ad_ref, bd_ref,
+                  dhead_ref, out_half, grad_half, full_ref, co_ref, cg_ref, cd_ref,
+                  wo, wg, wd, x_half, cot_half, raw, attn, d_attn, h_all, df_all, da_all, gu, part,
+                  recv_right, recv_left, hid, red_gu, red_down, back_gu, back_down,
+                  sems_send, sems_recv, send_in, recv_in, send_out, recv_out, local_in, local_out, load, load_w):
+    r, c = lax.axis_index("row"), lax.axis_index("col")
+    rows_all, width_all = part.shape
+    half = rows_all // 2
+    own = rows_all // n
+    tree_part = own * nr
+    chunks = half // m
+    blocks = 4
+    band = half // blocks
+    hidden = ad_ref.shape[1]
+    width = width_all // nr
+    left = {"col": jnp.maximum(c - 1, 0)}
+    right = {"col": jnp.minimum(c + 1, n - 1)}
+    first = c == 0
+    last = c == n - 1
+    inner = jnp.logical_and(c > 0, c < n - 1)
+
+    base = jnp.where(last, half, 0)
+    a_cut = hidden // 4
+    loads = [pltpu.make_async_copy(wo_hbm, wo, load.at[0])]
+    loads_a = []
+    for k in range(4):
+        lanes = slice(k * a_cut, (k + 1) * a_cut)
+        up_lanes = slice(hidden + k * a_cut, hidden + (k + 1) * a_cut)
+        loads_a.append(pltpu.make_async_copy(wg_hbm.at[:, lanes], wg.at[:, lanes], load_w.at[2 * k]))
+        loads_a.append(pltpu.make_async_copy(wg_hbm.at[:, up_lanes], wg.at[:, up_lanes], load_w.at[2 * k + 1]))
+    load_x = pltpu.make_async_copy(x_hbm.at[span(base, half)], x_half, load.at[1])
+    load_cot = pltpu.make_async_copy(cot_hbm, cot_half, load.at[2])
+    load_d = pltpu.make_async_copy(wd_hbm, wd, load.at[3])
+    loads[0].start()
+
+    def piece_in(d, b):
+        peer = lax.rem(r + d, nr)
+        return remote(
+            head_ref.at[span(b * tree_part + peer * own, own)],
+            attn.at[span(b * own, own), span(r * HEAD, HEAD)],
+            send_in.at[d - 1, b], recv_in.at[d - 1, b], {"row": peer},
+        )
+
+    def local_piece_in(b):
+        return pltpu.make_async_copy(
+            head_ref.at[span(b * tree_part + r * own, own)],
+            attn.at[span(b * own, own), span(r * HEAD, HEAD)], local_in.at[b]
+        )
+
+    def piece_out(d, b):
+        peer = lax.rem(r + d, nr)
+        return remote(
+            d_attn.at[span(b * own, own), span(peer * HEAD, HEAD)],
+            dhead_ref.at[span(b * tree_part + r * own, own)],
+            send_out.at[d - 1, b], recv_out.at[d - 1, b], {"row": peer},
+        )
+
+    def local_piece_out(b):
+        return pltpu.make_async_copy(
+            d_attn.at[span(b * own, own), span(r * HEAD, HEAD)],
+            dhead_ref.at[span(b * tree_part + r * own, own)], local_out.at[b]
+        )
+
+    for b in range(n):
+        local_piece_in(b).start()
+    barrier = pltpu.get_barrier_semaphore()
+    for d in range(1, nr):
+        pl.semaphore_signal(barrier, inc=1, device_id={"row": lax.rem(r + d, nr)}, device_id_type=MESH)
+
+    @pl.when(c > 0)
+    def _():
+        pl.semaphore_signal(barrier, inc=1, device_id=left, device_id_type=MESH)
+
+    @pl.when(c < n - 1)
+    def _():
+        pl.semaphore_signal(barrier, inc=1, device_id=right, device_id_type=MESH)
+
+    full_ref[...] = jnp.zeros_like(full_ref)
+    co_ref[...] = jnp.zeros_like(co_ref)
+    cg_ref[...] = jnp.zeros_like(cg_ref)
+    cd_ref[...] = jnp.zeros_like(cd_ref)
+
+    @pl.when(inner)
+    def _():
+        pl.semaphore_wait(barrier, nr + 1)
+
+    @pl.when(jnp.logical_not(inner))
+    def _():
+        pl.semaphore_wait(barrier, nr)
+
+    middle = n // 2
+    for b in range(middle):
+        for block in (b, middle + b):
+            for d in range(1, nr):
+                piece_in(d, block).start()
+    for copy in loads_a:
+        copy.start()
+    load_x.start()
+    load_d.start()
+    load_cot.start()
+
+    def rows(j, start=0):
+        return span(start + j * m, m)
+
+    def band_rows(b):
+        return span(b * band, band), span(half + b * band, band)
+
+    def take(ref, b):
+        low_rows, high_rows = band_rows(b)
+        return jnp.concatenate([ref[low_rows, :], ref[high_rows, :]], axis=0)
+
+    def put(b, lanes, value):
+        low_rows, high_rows = band_rows(b)
+        part[low_rows, lanes] = value[:band].astype(low)
+        part[high_rows, lanes] = value[band:].astype(low)
+
+    def relay_stage(stage, per, work, owner_step, all_ref):
+        def send(kind, j, src, dst, to):
+            return remote(src, dst, sems_send.at[stage, kind, j], sems_recv.at[stage, kind, j], to)
+
+        def reduce_right(j):
+            return send(0, j, part.at[rows(j, half)], recv_right.at[rows(j)], right)
+
+        def reduce_left(j):
+            return send(1, j, part.at[rows(j)], recv_left.at[rows(j)], left)
+
+        def spread_left(j):
+            return send(2, j, all_ref.at[rows(j, half)], all_ref.at[rows(j, half)], left)
+
+        def spread_right(j):
+            return send(3, j, all_ref.at[rows(j)], all_ref.at[rows(j)], right)
+
+        total_slices = per * blocks
+        each = chunks // blocks
+
+        def slices_before(i):
+            late = per + (jnp.maximum(i - per, 0) * per) // each
+            return jnp.minimum(jnp.where(i < per, i, late), total_slices)
+
+        @pl.loop(0, per + chunks + hop * 2 * (n - 1))
+        def _(ii):
+            i = ii - per
+
+            def on(offset, who, run):
+                j = i - offset
+
+                @pl.when(jnp.logical_and(who, jnp.logical_and(j >= 0, j < chunks)))
+                def _():
+                    run(j)
+
+            def mid_right(j):
+                reduce_right(j).wait_recv()
+                at = rows(j, half)
+                part[at, :] = (part[at, :].astype(wide) + recv_right[rows(j), :].astype(wide)).astype(low)
+                reduce_right(j).start()
+
+            def mid_left(j):
+                reduce_left(j).wait_recv()
+                at = rows(j)
+                part[at, :] = (part[at, :].astype(wide) + recv_left[at, :].astype(wide)).astype(low)
+                reduce_left(j).start()
+
+            def end_right(j):
+                reduce_right(j).wait_recv()
+                total = part[rows(j, half), :].astype(wide) + recv_right[rows(j), :].astype(wide)
+                all_ref[rows(j, half), :] = owner_step(total, rows(j))
+                spread_left(j).start()
+
+            def end_left(j):
+                reduce_left(j).wait_recv()
+                total = part[rows(j), :].astype(wide) + recv_left[rows(j), :].astype(wide)
+                all_ref[rows(j), :] = owner_step(total, rows(j))
+                spread_right(j).start()
+
+            def pass_left(j):
+                spread_left(j).wait_recv()
+                spread_left(j).start()
+
+            def pass_right(j):
+                spread_right(j).wait_recv()
+                spread_right(j).start()
+
+            on(0, first, lambda j: reduce_right(j).start())
+            on(0, last, lambda j: reduce_left(j).start())
+            on(hop * c, inner, mid_right)
+            on(hop * (n - 1 - c), inner, mid_left)
+            on(hop * (n - 1), last, end_right)
+            on(hop * (n - 1), first, end_left)
+            on(hop * (2 * (n - 1) - c), inner, pass_left)
+            on(hop * (n - 1 + c), inner, pass_right)
+
+            @pl.loop(slices_before(ii), slices_before(ii + 1))
+            def _(t):
+                work(t // per, lax.rem(t, per))
+
+        @pl.loop(0, chunks)
+        def _(j):
+            @pl.when(first)
+            def _():
+                reduce_right(j).wait_send()
+                spread_right(j).wait_send()
+                spread_left(j).wait_recv()
+
+            @pl.when(last)
+            def _():
+                reduce_left(j).wait_send()
+                spread_left(j).wait_send()
+                spread_right(j).wait_recv()
+
+            @pl.when(inner)
+            def _():
+                reduce_right(j).wait_send()
+                reduce_left(j).wait_send()
+                spread_left(j).wait_send()
+                spread_right(j).wait_send()
+
+    def out_work(b, k):
+        @pl.when(b == 0)
+        def _():
+            loads[0].wait()
+
+        @pl.when(lax.rem(b, blocks // middle) == 0)
+        def _():
+            at = b // (blocks // middle)
+            for block in (at, middle + at):
+                for d in range(1, nr):
+                    piece_in(d, block).wait_recv()
+                local_piece_in(block).wait()
+
+        rows_in = take(attn, b)
+        red = dot_t(rows_in, ao_ref[...]).astype(low)
+        for j in range(nr):
+            lanes = slice(j * width, (j + 1) * width)
+            put(b, lanes, dot(rows_in, wo[j]) + dot(red, bo_ref[:, lanes]))
+
+    gain_a = gain_ref[0:1, :]
+    gain_f = gain_ref[1:2, :]
+
+    def attn_owner(total, at):
+        raw[at, :] = total
+        flat = total * norm_factor(row_sum(total * total))
+        return (x_half[at, :].astype(wide) + flat * gain_a).astype(low)
+
+    load_x.wait()
+    relay_stage(0, 1, out_work, attn_owner, h_all)
+
+    def gate_slice(b, k):
+        @pl.when(b == 0)
+        def _():
+            for s in range(4):
+                @pl.when(k == s)
+                def _():
+                    loads_a[2 * s].wait()
+                    loads_a[2 * s + 1].wait()
+
+        rows_in = take(h_all, b)
+
+        @pl.when(k == 0)
+        def _():
+            red_gu[b] = dot_t(rows_in, ag_ref[...]).astype(low)
+
+        at = pl.multiple_of(k * a_cut, a_cut)
+        lanes = pl.ds(at, a_cut)
+        up_lanes = pl.ds(pl.multiple_of(hidden + at, a_cut), a_cut)
+        red = red_gu[b]
+        gate = dot(rows_in, wg[:, lanes]) + dot(red[:, :RANK], bg_ref[0, :, lanes])
+        up = dot(rows_in, wg[:, up_lanes]) + dot(red[:, RANK:], bg_ref[1, :, lanes])
+        gu[b, :, lanes] = gate.astype(low)
+        gu[b, :, up_lanes] = up.astype(low)
+        hid[:, lanes] = (gate * jax.nn.sigmoid(gate) * up).astype(low)
+
+    def down_slice(b, k):
+        @pl.when(jnp.logical_and(b == 0, k == 0))
+        def _():
+            load_d.wait()
+
+        rows_in = hid[:, :hidden]
+
+        @pl.when(k == 0)
+        def _():
+            red_down[b] = dot_t(rows_in, ad_ref[...]).astype(low)
+
+        for s in range(nr // 2):
+            j = k * (nr // 2) + s
+            lanes = span(j * width, width)
+            put(b, lanes, dot(rows_in, wd[j]) + dot(red_down[b], bd_ref[:, lanes]))
+
+    def ffn_work(b, k):
+        @pl.when(k < 4)
+        def _():
+            gate_slice(b, k)
+
+        @pl.when(k >= 4)
+        def _():
+            down_slice(b, k - 4)
+
+    def ffn_owner(total, at):
+        a_raw = raw[at, :]
+        h = x_half[at, :].astype(wide) + a_raw * norm_factor(row_sum(a_raw * a_raw)) * gain_a
+        factor = norm_factor(row_sum(total * total))
+        flat = total * factor
+        out_half[at, :] = (h + flat * gain_f).astype(low)
+        scaled = cot_half[at, :].astype(wide) * gain_f
+        return (factor * (scaled - flat * (row_sum(scaled * flat) * (1.0 / D)))).astype(low)
+
+    load_cot.wait()
+    relay_stage(1, 6, ffn_work, ffn_owner, df_all)
+
+    b_cut = hidden // 2
+
+    def hidden_back(b, k):
+        rows_in = take(df_all, b)
+
+        @pl.when(k == 0)
+        def _():
+            back_down[...] = dot_t(rows_in, bd_ref[...]).astype(low)
+
+        at = pl.multiple_of(k * b_cut, b_cut)
+        lanes = pl.ds(at, b_cut)
+        up_lanes = pl.ds(pl.multiple_of(hidden + at, b_cut), b_cut)
+        back = back_down[...]
+        grad = dot(back, ad_ref[:, lanes])
+        for j in range(nr):
+            grad = grad + dot_t(rows_in[:, j * width:(j + 1) * width], wd[j, lanes, :])
+        gate = gu[b, :, lanes].astype(wide)
+        up = gu[b, :, up_lanes].astype(wide)
+        sigma = jax.nn.sigmoid(gate)
+        silu = gate * sigma
+        d_gate = (grad * up * sigma * (1.0 + gate * (1.0 - sigma))).astype(low)
+        d_up = (grad * silu).astype(low)
+        hid[:, lanes] = d_gate
+        hid[:, up_lanes] = d_up
+        cd_ref[:, lanes] += t_dot(back, (silu * up).astype(low))
+        red = red_gu[b]
+        cg_ref[0, :, lanes] += t_dot(red[:, :RANK], d_gate)
+        cg_ref[1, :, lanes] += t_dot(red[:, RANK:], d_up)
+
+    o_cut = width_all // 4
+
+    def gate_back(b, k):
+        @pl.when(k == 0)
+        def _():
+            back_gu[:, :RANK] = dot_t(hid[:, :hidden], bg_ref[0]).astype(low)
+            back_gu[:, RANK:] = dot_t(hid[:, hidden:], bg_ref[1]).astype(low)
+
+        lanes = span(k * o_cut, o_cut)
+        put(b, lanes, dot_t(hid[...], wg[lanes, :]) + dot(back_gu[...], ag_ref[:, lanes]))
+
+        @pl.when(k == 3)
+        def _():
+            full_ref[:2 * RANK, :] += t_dot(back_gu[...], take(h_all, b))
+            full_ref[3 * RANK:, :] += t_dot(red_down[b], take(df_all, b))
+
+    def back_work(b, k):
+        @pl.when(k < 2)
+        def _():
+            hidden_back(b, k)
+
+        @pl.when(k >= 2)
+        def _():
+            gate_back(b, k - 2)
+
+    def back_owner(total, at):
+        grad = cot_half[at, :].astype(wide) + total
+        grad_half[at, :] = grad
+        a_raw = raw[at, :]
+        factor = norm_factor(row_sum(a_raw * a_raw))
+        flat = a_raw * factor
+        scaled = grad * gain_a
+        return (factor * (scaled - flat * (row_sum(scaled * flat) * (1.0 / D)))).astype(low)
+
+    relay_stage(2, 6, back_work, back_owner, da_all)
+
+    @pl.loop(0, n)
+    def _(b):
+        at = span(b * own, own)
+        rows_in = da_all[at, :]
+        back = dot_t(rows_in, bo_ref[...]).astype(low)
+        grad = dot(back, ao_ref[...])
+        for j in range(nr):
+            grad = grad + dot_t(rows_in[:, j * width:(j + 1) * width], wo[j])
+        d_attn[at, :] = grad.astype(low)
+        for d in range(1, nr):
+            piece_out(d, b).start()
+        local_piece_out(b).start()
+        attn_rows = attn[at, :]
+        co_ref[...] += t_dot(back, attn_rows)
+        red = dot_t(attn_rows, ao_ref[...]).astype(low)
+        full_ref[2 * RANK:3 * RANK, :] += t_dot(red, rows_in)
+
+    @pl.loop(0, n)
+    def _(b):
+        for d in range(1, nr):
+            piece_in(d, b).wait_send()
+            piece_out(d, b).wait()
+        local_piece_out(b).wait()
+
+
+def middle(attn_head, x, cot_half, gains, w_out, w_gu, w_down, a_out, b_out, a_gu, b_gu, a_down, b_down, n, nr, m=16, hop=2):
+    group, width_all = x.shape
+    half = group // 2
+    width = width_all // nr
+    hidden = a_down.shape[1]
+    chunks = half // m
+    band = group // 4
+    dma = pltpu.SemaphoreType.DMA
+    any_space = pl.BlockSpec(memory_space=pl.ANY)
+    shape = jax.ShapeDtypeStruct
+    return pl.pallas_call(
+        functools.partial(middle_kernel, n, nr, m, hop),
+        out_shape=[
+            shape(attn_head.shape, low),
+            shape((half, width_all), low),
+            shape((half, width_all), wide),
+            shape((4 * RANK, width_all), wide),
+            shape((RANK, a_out.shape[1]), wide),
+            shape((2, RANK, hidden), wide),
+            shape((RANK, hidden), wide),
+        ],
+        in_specs=[VM, any_space, any_space, VM, any_space, any_space, any_space] + [VM] * 6,
+        out_specs=[VM] * 7,
+        scratch_shapes=[
+            pltpu.VMEM(w_out.shape, low),
+            pltpu.VMEM(w_gu.shape, low),
+            pltpu.VMEM(w_down.shape, low),
+            pltpu.VMEM((half, width_all), low),
+            pltpu.VMEM((half, width_all), low),
+            pltpu.VMEM((half, width_all), wide),
+            pltpu.VMEM((group, a_out.shape[1]), low),
+            pltpu.VMEM((group, a_out.shape[1]), low),
+            pltpu.VMEM((group, width_all), low),
+            pltpu.VMEM((group, width_all), low),
+            pltpu.VMEM((group, width_all), low),
+            pltpu.VMEM((4, band, 2 * hidden), low),
+            pltpu.VMEM((group, width_all), low),
+            pltpu.VMEM((half, width_all), low),
+            pltpu.VMEM((half, width_all), low),
+            pltpu.VMEM((band, 2 * hidden), low),
+            pltpu.VMEM((4, band, 2 * RANK), low),
+            pltpu.VMEM((4, band, RANK), low),
+            pltpu.VMEM((band, 2 * RANK), low),
+            pltpu.VMEM((band, RANK), low),
+            dma((3, 4, chunks)), dma((3, 4, chunks)),
+            dma((nr - 1, n)), dma((nr - 1, n)), dma((nr - 1, n)), dma((nr - 1, n)), dma((n,)), dma((n,)),
+            dma((4,)), dma((8,)),
+        ],
+        compiler_params=pltpu.CompilerParams(collective_id=0, has_side_effects=True, vmem_limit_bytes=67043328),
+        name="middle",
+    )(attn_head, x, cot_half, gains, w_out, w_gu, w_down, a_out, b_out, a_gu, b_gu, a_down, b_down)
+
+
 def per_device(
     tokens,
     cotangent,
@@ -1066,43 +1384,29 @@
         ],
         axis=0,
     ).astype(low)
-    narrow_all = lax.all_gather(narrow, "row", axis=2, tiled=True)
-    a_qkv = narrow_all[:3].reshape(3 * RANK, D)
-    a_gu = narrow_all[3:5].reshape(2 * RANK, D)
-    b_out = narrow_all[5]
-    b_down = narrow_all[6]
+    gain_pair = jnp.pad(jnp.stack([gain_attn, gain_ffn]), ((0, 6), (0, 0)))
+    x, table, gains = enter(tokens, narrow.reshape(7 * RANK, width_row), gain_pair, col_count, row_count)
+    a_qkv = table[: 3 * RANK]
+    a_gu = table[3 * RANK : 5 * RANK]
+    b_out = table[5 * RANK : 6 * RANK]
+    b_down = table[6 * RANK :]
     b_qkv = pick(query_key_value_adapter_second, 1).astype(low)
     b_gu = pick(gate_up_adapter_second, 1).astype(low)
     a_out = pick(output_adapter_first, 0).astype(low)
     a_down = pick(down_adapter_first, 0).astype(low)
-    gains = lax.all_gather(jnp.stack([gain_attn, gain_ffn]), "row", axis=1, tiled=True)
-
-    w_qkv = lax.all_gather(query_key_value_weight, "row", axis=0, tiled=True).reshape(D, 3 * width_col)
-    w_out = lax.all_gather(output_weight, "row", axis=1, tiled=True)
-    w_gu = lax.all_gather(gate_up_weight, "row", axis=0, tiled=True).reshape(D, 2 * hidden_col)
-    w_down = lax.all_gather(down_weight, "row", axis=1, tiled=True)
-
-    def to_heads(values, parts):
-        by_head = values.reshape(group, parts, heads_col, HEAD).transpose(2, 0, 1, 3).reshape(heads_col, group, parts * HEAD)
-        moved = lax.all_to_all(by_head, "row", split_axis=0, concat_axis=0, tiled=True)
-        return (
-            moved.reshape(row_count, col_count, own, parts * HEAD)
-            .transpose(1, 0, 2, 3)
-            .reshape(tree_tokens, parts * HEAD)
-        )
-
-    def from_heads(values, parts):
-        by_row = (
-            values.reshape(col_count, row_count, own, parts * HEAD)
-            .transpose(1, 0, 2, 3)
-            .reshape(row_count, group, parts * HEAD)
-        )
-        moved = lax.all_to_all(by_row, "row", split_axis=0, concat_axis=0, tiled=True)
-        return moved.reshape(heads_col, group, parts, HEAD).transpose(1, 2, 0, 3).reshape(group, parts * width_col)
+
+    def gather_rows(weight, stacked):
+        share = weight.shape[0] // dp_count
+        mine = lax.dynamic_slice_in_dim(weight, lax.axis_index("dp") * share, share, 0)
+        return lax.all_gather(mine, ("row", "dp"), axis=0, tiled=not stacked)
+
+    w_qkv = gather_rows(query_key_value_weight.reshape(width_row, 3 * width_col), False)
+    w_gu = gather_rows(gate_up_weight.reshape(width_row, 2 * hidden_col), False)
+    w_down = gather_rows(down_weight, True).reshape(row_count, hidden_col, width_row)
+    w_out = gather_rows(output_weight, True).reshape(row_count, width_col, width_row)
 
     first = lax.axis_index("col") == 0
     final = lax.axis_index("col") == col_count - 1
-    x = enter(tokens, col_count, row_count)
     red_qkv = dot_t(x, a_qkv).astype(low)
     raw = dot(x, w_qkv)
     extra = jnp.concatenate([dot(red_qkv[:, RANK * j : RANK * (j + 1)], b_qkv[j]) for j in range(3)], axis=1)
@@ -1118,35 +1422,9 @@
     parent_at, branch_flag = tree_tables(seg_ids, parents)
     pos_down, pos_across = positions[:, None], positions[None, :]
     attn_head, lse = attend(qkv_head, parent_at, branch_flag, pos_down, pos_across)
-    attn = from_heads(attn_head, 1)
-
-    red_out = dot_t(attn, a_out).astype(low)
-    part_a = (dot(attn, w_out) + dot(red_out, b_out)).astype(low)
-    h, a_raw = relay("attn", part_a, (x, gains), col_count)
-
-    red_gu = dot_t(h, a_gu).astype(low)
-    gate = dot(h, w_gu[:, :hidden_col]) + dot(red_gu[:, :RANK], b_gu[0])
-    up = dot(h, w_gu[:, hidden_col:]) + dot(red_gu[:, RANK:], b_gu[1])
-    sigma = jax.nn.sigmoid(gate)
-    hidden = (gate * sigma * up).astype(low)
-    red_down = dot_t(hidden, a_down).astype(low)
-    part_f = (dot(hidden, w_down) + dot(red_down, b_down)).astype(low)
-    d_f, out_half = relay("ffn", part_f, (x, gains, a_raw, g_half), col_count)
-    back_down = dot_t(d_f, b_down).astype(low)
-    d_hidden = dot_t(d_f, w_down) + dot(back_down, a_down)
-    d_gate = (d_hidden * up * sigma * (1.0 + gate * (1.0 - sigma))).astype(low)
-    d_up = (d_hidden * (gate * sigma)).astype(low)
-    back_gate = dot_t(d_gate, b_gu[0]).astype(low)
-    back_up = dot_t(d_up, b_gu[1]).astype(low)
-    back_gu = jnp.concatenate([back_gate, back_up], axis=1)
-    part_h = (
-        dot_t(d_gate, w_gu[:, :hidden_col]) + dot_t(d_up, w_gu[:, hidden_col:]) + dot(back_gu, a_gu)
-    ).astype(low)
-    d_a, d_h_half = relay("back", part_h, (gains, a_raw, g_half), col_count)
-    back_out = dot_t(d_a, b_out).astype(low)
-    d_attn = (dot_t(d_a, w_out) + dot(back_out, a_out)).astype(low)
-
-    d_attn_head = to_heads(d_attn, 1)
+    d_attn_head, out_half, d_h_half, full_mid, part_ao, part_bgu, part_ad = middle(
+        attn_head, x, g_half, gains, w_out, w_gu, w_down, a_out, b_out, a_gu, b_gu, a_down, b_down, col_count, row_count
+    )
     d_qkv_head = attend_back(
         qkv_head, d_attn_head, parent_at, branch_flag, pos_down, pos_across, lse
     )
@@ -1162,13 +1440,13 @@
 
     rank_own = RANK // col_count
     full = jnp.concatenate(
-        [t_dot(back_qkv, x), t_dot(back_gu, h), t_dot(red_out, d_a), t_dot(red_down, d_f)], axis=0
+        [t_dot(back_qkv, x), full_mid], axis=0
     ).astype(low)
     full = full.reshape(7, col_count, rank_own, D).transpose(1, 0, 2, 3).reshape(col_count, 7 * rank_own, D)
     full = jnp.pad(full, ((0, 0), (0, rank_own), (0, 0))).reshape(col_count * 8 * rank_own, D)
     cols = jnp.concatenate(
         [t_dot(red_qkv[:, RANK * j : RANK * (j + 1)], d) for j, d in enumerate((d_q, d_k, d_v))]
-        + [t_dot(back_out, attn), t_dot(red_gu[:, :RANK], d_gate), t_dot(red_gu[:, RANK:], d_up), t_dot(back_down, hidden)],
+        + [part_ao, part_bgu[0], part_bgu[1], part_ad],
         axis=1,
     ).astype(low)
     cols = cols.reshape(RANK * 16, width_row)

time: 768 us -> 707 us (0.921)
  matrix products: 131 us -> 30.8 us
  waiting for transfers between devices: 7.23 us -> 75.3 us
  blocking collectives: 29.9 us -> 0 us
  Pallas kernels: 509 us -> 536 us
    all_gather x4, waiting for transfers between devices: 0.06 us -> 75.2 us  [gather_rows(): return lax.all_gather(mine, ('row', 'dp'), axis=0, tiled=not stacked)]
    dot_general x16 -> x5, matrix products: 72.2 us -> 16.7 us  [dot(): return jnp.dot(left, right, preferred_element_type=wide)]
    dot_general x16 -> x5, matrix products: 52.3 us -> 11.6 us  [dot_t(): return lax.dot_general(left, right, last_last, preferred_element_type=wide)]
    pallas_call x4 -> x2, Pallas kernels: 285 us -> 318 us  [the longest x1 262 us: middle(): pl.pallas_call(functools.partial(middle_kernel, n, nr, m, hop), out_shape...]
    all_gather x2 -> x0, blocking collectives: 29.9 us -> none  [the longest x1 19.2 us: per_device(): lax.all_gather(jnp.stack([gain_attn, gain_ffn]), 'row', axis=1, tiled=True)]
    unnamed x95 -> x67, local copies, waits for them, and re-layouts: 26.1 us -> 12.2 us
  transfers between devices with their start and end apart: 6 -> 4, of which waited for: 1 -> 1; matrix products, arithmetic and copies ran while one was open for 10% -> 6% of each run, Pallas kernels for 30% -> 20%
where the time goes in v4:
time: 707 us; the launch traced here: 703 us
  Pallas kernels  536 us (76%)
  waiting for transfers between devices  75.3 us (11%)
  local copies, waits for them, and re-layouts  38.2 us (5%)
  matrix products  30.8 us (4%)
  between operations  14.9 us (2%)
  other arithmetic  7.75 us (1%)
    pallas_call x1, Pallas kernels, middle(): pl.pallas_call(functools.partial(middle_kernel, n, nr, m, hop), out_shape...  262 us
    all_gather x4, waiting for transfers between devices, gather_rows(): return lax.all_gather(mine, ('row', 'dp'), axis=0, tiled=not stacked)  75.2 us
    pallas_call x1, Pallas kernels, to_heads_call(): pl.pallas_call(functools.partial(heads_kernel, n, nr, m), out_shape=[jax....  71.3 us
    pallas_call x1, Pallas kernels, finish(): pl.pallas_call(functools.partial(finish_kernel, n, nr, ndp, m), out_shape...  69 us
    pallas_call x1, Pallas kernels, enter(): pl.pallas_call(functools.partial(enter_kernel, n, nr, m), out_shape=[jax....  55.9 us
    pallas_call x1, Pallas kernels, from_heads_call(): pl.pallas_call(functools.partial(unheads_kernel, n, nr), out_shape=[jax.S...  42.6 us
    pallas_call x1, Pallas kernels, attend_back(): pl.pallas_call(bwd_kernel, grid_spec=pltpu.PrefetchScalarGridSpec(num_sca...  19.9 us
    dot_general x5, matrix products, dot(): return jnp.dot(left, right, preferred_element_type=wide)  16.7 us
  transfers between devices with their start and end apart: 4, of which 1 were waited for; matrix products, arithmetic and copies ran while one was open for 6% of the time, Pallas kernels for 20%

profile of v4, /device:TPU:0, one launch (start us, length us, event | category | flops | bytes accessed | tf_op | source)
XLA Modules:
  0.0 702.9 jit_solution(3149993753620073474)
XLA Ops:
  7.2 1.8 copy.55
  10.9 2.3 constant_dynamic-slice_fusion
  13.2 4.6 copy.74
  17.8 1.5 constant_dynamic-slice_fusion.1
  19.4 2.0 broadcast_in_dim.62.posq_ref
  27.4 55.9 %enter.1 = (bf16[640,2048]{1,0:T(8,128)(2,1)}, bf16[112,2048]{1,0:T(8,128)(2,1)}, f32[8,2048]{1,0:T(8,128)}) custom-call(bf16[640,512]{1,0:T(8,128)(2,1)} %tok_ref.1, bf16[112,512]{1,0:T(8,128)(2,1)} %bitcast.89, f32[8,512]{1,0:T(8,128)} %select_maximum_fusion.gain_ref), custom_call_target="tpu_custom_call" | custom-call | tf_op jit(solution)/shard_map/enter/pallas_call | solution.py:323
  83.4 1.7 slice.107.ag_ref
  91.7 1.5 fusion.14.ad_ref
  93.2 1.6 fusion.12.bg_ref
  95.7 1.4 fusion.23
  97.2 1.4 fusion.26
  100.7 9.1 %maximum_add_fusion.1.raw_ref = f32[640,1536]{1,0:T(8,128)} fusion(f32[640,512]{1,0:T(8,128)} %fusion.20, f32[640,512]{1,0:T(8,128)} %fusion.23, f32[640,512]{1,0:T(8,128)} %fusion.26, bf16[640,2048]{1,0:T(8,128)(2,1)S(1)} %copy-done, bf16[2048,1536]{0,1:T(8,128)(2,1)} %all-gather.7.cloned.1.call-done), kind=kOutput, calls=%fused_computation.2 | convolution fusion | flops 4029480960 | bytes 16777216 | tf_op jit(solution)/shard_map/dot_general | solution.py:30
  109.8 71.3 %to_heads.1 = (bf16[2560,384]{1,0:T(8,128)(2,1)}, f32[8,640]{1,0:T(8,128)}, bf16[320,2048]{1,0:T(8,128)(2,1)}) custom-call(f32[640,1536]{1,0:T(8,128)} %maximum_add_fusion.1.raw_ref, f32[1,512]{1,0:T(1,128)} %bitcast.90, f32[1,512]{1,0:T(1,128)} %bitcast.92, f32[640,128]{1,0:T(8,128)} %get-tuple-element.86.cos_ref, f32[640,128]{1,0:T(8,128)} %get-tuple-element.87.sin_ref, ...), custom_call_target="tpu_custom_call" | custom-call | tf_op jit(solution)/shard_map/to_heads/pallas_call | solution.py:491
  181.1 15.4 %attend.1 = (bf16[2560,128]{1,0:T(8,128)(2,1)}, f32[2560,1]{1,0:T(8,128)}) custom-call(s32[12]{0:T(128)} %select_reduce_fusion.parent_ref, s32[12]{0:T(128)} %compare_convert_fusion.1.flag_ref, bf16[2560,384]{1,0:T(8,128)(2,1)} %get-tuple-element.31.q_ref.k_ref.v_ref, bf16[2560,384]{1,0:T(8,128)(2,1)} %get-tuple-element.31.q_ref.k_ref.v_ref, ...), custom_call_target="tpu_custom_call" | custom-call | tf_op jit(solution)/shard_map/attend/pallas_call | solution.py:145
  196.5 75.2 %all-gather.9.cloned.1.call-done.wg_hbm = bf16[2048,4096]{1,0:T(8,128)(2,1)} async-done(((bf16[256,4096]{1,0:T(8,128)(2,1)}), bf16[2048,4096]{1,0:T(8,128)(2,1)}) %all-gather.9.cloned.1.call-update) | async-done | bytes 16777232 | tf_op jit(solution)/shard_map/all_gather | solution.py:1401
  271.6 261.8 %middle.1 = (bf16[2560,128]{1,0:T(8,128)(2,1)}, bf16[320,2048]{1,0:T(8,128)(2,1)}, f32[320,2048]{1,0:T(8,128)}, f32[64,2048]{1,0:T(8,128)}, f32[16,512]{1,0:T(8,...) custom-call(bf16[2560,128]{1,0:T(8,128)(2,1)} %get-tuple-element.32.head_ref, ...), custom_call_target="tpu_custom_call" | custom-call | tf_op jit(solution)/shard_map/middle/pallas_call | solution.py:1293
  533.5 19.9 %attend_back.1.d_ref = bf16[2560,384]{1,0:T(8,128)(2,1)} custom-call(s32[12]{0:T(128)} %select_reduce_fusion.parent_ref, s32[12]{0:T(128)} %compare_convert_fusion.1.flag_ref, bf16[2560,384]{1,0:T(8,128)(2,1)} %get-tuple-element.31.q_ref.k_ref.v_ref, bf16[2560,384]{1,0:T(8,128)(2,1)} %get-tuple-element.31.q_ref.k_ref.v_ref, ...), custom_call_target="tpu_custom_call" | custom-call | tf_op jit(solution)/shard_map/attend_back/pallas_call | solution.py:157
  553.4 42.6 %from_heads.1 = (bf16[640,1536]{1,0:T(8,128)(2,1)}, bf16[640,512]{1,0:T(8,128)(2,1)}) custom-call(bf16[2560,384]{1,0:T(8,128)(2,1)} %attend_back.1.d_ref, f32[640,1536]{1,0:T(8,128)} %maximum_add_fusion.1.raw_ref, f32[8,640]{1,0:T(8,128)} %get-tuple-element.37.factor_ref, f32[1,512]{1,0:T(1,128)} %bitcast.91, f32[1,512]{1,0:T(1,128)} %bitcast.93, ...), custom_call_target="tpu_custom_call" | custom-call | tf_op jit(solution)/shard_map/from_heads/pallas_call | solution.py:646
  596.0 1.4 fusion.3
  597.4 1.4 convolution_convert_fusion.2
  598.8 1.5 convolution_convert_fusion.3
  607.1 6.5 fusion.34
  613.6 3.3 fusion.part_ref
  617.5 69.0 %finish.1 = (f32[640,512]{1,0:T(8,128)}, f32[4,96,512]{2,1,0:T(8,128)}) custom-call(bf16[640,2048]{1,0:T(8,128)(2,1)} %fusion.part_ref, bf16[128,2048]{1,0:T(8,128)(2,1)} %bitcast.84, bf16[256,512]{1,0:T(8,128)(2,1)} %convert_element_type.75.col_ref, f32[8,512]{1,0:T(8,128)} %iota.23.hot_ref), custom_call_target="tpu_custom_call" | custom-call | tf_op jit(solution)/shard_map/finish/pallas_call | solution.py:857
  (127 shorter events, 33.9 us)
Async XLA Ops:
  7.2 93.5 %all-gather.7.cloned.1.call-start = ((), (), s32[]{:S(2)}) async-start(), calls=%async_computation | async-start | bytes 7077888 | tf_op jit(solution)/shard_map/all_gather | solution.py:1401
  10.0 186.5 %all-gather.11.cloned.1.call-start = ((), (), s32[]{:S(2)}) async-start(), calls=%async_computation.2 | async-start | bytes 2359296 | tf_op jit(solution)/shard_map/all_gather | solution.py:1401
  10.8 185.7 %all-gather.13.cloned.1.call-start = ((), (), s32[]{:S(2)}) async-start(), calls=%async_computation.3 | async-start | bytes 9437184 | tf_op jit(solution)/shard_map/all_gather | solution.py:1401
  13.2 258.5 %all-gather.9.cloned.1.call-start = ((), (), s32[]{:S(2)}) async-start(), calls=%async_computation.1 | async-start | bytes 18874368 | tf_op jit(solution)/shard_map/all_gather | solution.py:1401
  19.3 4.3 copy-start.24
  19.3 4.3 copy-start.25
  19.3 68.6 %copy-start.27 = (s32[1,13]{1,0:T(1,128)S(1)}, s32[1,13]{1,0:T(1,128)}, u32[]{:S(2)}) copy-start(s32[1,13]{1,0:T(1,128)} %param.26) | copy-start | bytes 160
  83.4 11.5 %copy-start = (bf16[640,2048]{1,0:T(8,128)(2,1)S(1)}, bf16[640,2048]{1,0:T(8,128)(2,1)}, u32[]{:S(2)}) copy-start(bf16[640,2048]{1,0:T(8,128)(2,1)} %get-tuple-element.29.x_hbm) | copy-start | bytes 7864324
  83.4 11.5 %copy-start.4 = (bf16[112,2048]{1,0:T(8,128)(2,1)S(1)}, bf16[112,2048]{1,0:T(8,128)(2,1)}, u32[]{:S(2)}) copy-start(bf16[112,2048]{1,0:T(8,128)(2,1)} %get-tuple-element.30) | copy-start | bytes 1376260
  87.9 10.7 %copy-start.12 = (bf16[3,1,16,512]{3,2,1,0:T(8,128)(2,1)}, bf16[3,1,16,512]{3,2,1,0:T(8,128)(2,1)S(1)}, u32[]{:S(2)}) copy-start(bf16[3,1,16,512]{3,2,1,0:T(8,128)(2,1)S(1)} %dynamic-slice_convert_fusion.1) | copy-start | bytes 147460
  553.4 42.6 %copy-start.8 = (bf16[640,48]{0,1:T(8,128)(2,1)S(1)}, bf16[640,48]{0,1:T(8,128)(2,1)}, u32[]{:S(2)}) copy-start(bf16[640,48]{0,1:T(8,128)(2,1)} %copy-done.7) | copy-start | bytes 184324
  553.4 44.1 %copy-start.13 = (bf16[3,1,16,512]{3,2,1,0:T(8,128)(2,1)S(1)}, bf16[3,1,16,512]{3,2,1,0:T(8,128)(2,1)}, u32[]{:S(2)}) copy-start(bf16[3,1,16,512]{3,2,1,0:T(8,128)(2,1)} %copy-done.12) | copy-start | bytes 147460
  595.9 5.8 copy-start.5
  595.9 6.2 copy-start.11
  595.9 6.3 copy-start.23
  596.0 6.3 copy-start.15
  597.4 5.7 copy-start.10
  598.8 4.3 copy-start.17
  598.8 4.3 copy-start.1
  607.1 6.5 copy-start.18
  607.1 6.5 copy-start.20
  607.1 6.5 copy-start.22
  687.6 6.9 copy-start.9
  688.0 7.4 %copy-start.3 = (f32[640,512]{1,0:T(8,128)S(1)}, f32[640,512]{1,0:T(8,128)}, u32[]{:S(2)}) copy-start(f32[640,512]{1,0:T(8,128)} %get-tuple-element.99) | copy-start | bytes 3932164
  (8 other events, 19.2 us)
Sparse Core Ops, SparseCore 0:
  10.1 56.0 all-gather.6
  68.7 28.6 all-gather.10
  99.2 81.1 all-gather.12
  182.2 89.4 all-gather.8

commit v5 on v4

--- a/solution.py
+++ b/solution.py
@@ -49,122 +49,6 @@
     return lax.rsqrt(square_sum * (1.0 / D) + epsilon)
 
 
-def tail_scores(q, k_ref, own_at, parent_at, has_parent, pos_q, pos_k):
-    scale = HEAD ** -0.5
-    s_trunk = dot_t(q, k_ref[:TRUNK, :]) * scale
-    s_par = dot_t(q, k_ref[pl.ds(parent_at, SEG), :]) * scale
-    s_par = jnp.where(has_parent > 0, s_par, masked_out)
-    s_own = dot_t(q, k_ref[pl.ds(own_at, SEG), :]) * scale
-    s_own = jnp.where(pos_k <= pos_q, s_own, masked_out)
-    return s_trunk, s_par, s_own
-
-def trunk_scores(q, k_ref, pos_q, pos_k):
-    s = dot_t(q, k_ref[:TRUNK, :]) * HEAD ** -0.5
-    return jnp.where(pos_k <= pos_q, s, masked_out)
-
-def fwd_kernel(parent_ref, flag_ref, q_ref, k_ref, v_ref, posq_ref, posk_ref, o_ref, lse_ref):
-    tails = (q_ref.shape[0] - TRUNK) // SEG
-    @pl.loop(0, TRUNK // QT)
-    def _(i):
-        at = pl.multiple_of(i * QT, QT)
-        s = trunk_scores(q_ref[pl.ds(at, QT), :], k_ref, posq_ref[pl.ds(at, QT), :], posk_ref[:, :TRUNK])
-        top = jnp.max(s, axis=1, keepdims=True)
-        e = jnp.exp(s - top)
-        total = jnp.sum(e, axis=1, keepdims=True)
-        p = (e * (1.0 / total)).astype(low)
-        o_ref[pl.ds(at, QT), :] = dot(p, v_ref[:TRUNK, :]).astype(low)
-        lse_ref[pl.ds(at, QT), :] = top + jnp.log(total)
-    @pl.loop(0, tails)
-    def _(j):
-        at = pl.multiple_of(TRUNK + j * SEG, SEG)
-        par = pl.multiple_of(parent_ref[j] * SEG, SEG)
-        s1, s2, s3 = tail_scores(q_ref[pl.ds(at, SEG), :], k_ref, at, par, flag_ref[j],
-                                 posq_ref[pl.ds(at, SEG), :], posk_ref[:, pl.ds(at, SEG)])
-        top = jnp.maximum(jnp.maximum(jnp.max(s1, axis=1, keepdims=True), jnp.max(s2, axis=1, keepdims=True)),
-                          jnp.max(s3, axis=1, keepdims=True))
-        e1 = jnp.exp(s1 - top); e2 = jnp.exp(s2 - top); e3 = jnp.exp(s3 - top)
-        total = jnp.sum(e1, axis=1, keepdims=True) + jnp.sum(e2, axis=1, keepdims=True) + jnp.sum(e3, axis=1, keepdims=True)
-        inv = 1.0 / total
-        o = dot((e1 * inv).astype(low), v_ref[:TRUNK, :])
-        o += dot((e2 * inv).astype(low), v_ref[pl.ds(par, SEG), :])
-        o += dot((e3 * inv).astype(low), v_ref[pl.ds(at, SEG), :])
-        o_ref[pl.ds(at, SEG), :] = o.astype(low)
-        lse_ref[pl.ds(at, SEG), :] = top + jnp.log(total)
-
-def bwd_kernel(parent_ref, flag_ref, q_ref, k_ref, v_ref, do_ref, posq_ref, posk_ref, lse_ref, d_ref, dk_acc, dv_acc):
-    scale = HEAD ** -0.5
-    tails = (q_ref.shape[0] - TRUNK) // SEG
-    dk_acc[...] = jnp.zeros_like(dk_acc)
-    dv_acc[...] = jnp.zeros_like(dv_acc)
-    @pl.loop(0, TRUNK // QT)
-    def _(i):
-        at = pl.multiple_of(i * QT, QT)
-        q = q_ref[pl.ds(at, QT), :]
-        do = do_ref[pl.ds(at, QT), :]
-        s = trunk_scores(q, k_ref, posq_ref[pl.ds(at, QT), :], posk_ref[:, :TRUNK])
-        p = jnp.exp(s - lse_ref[pl.ds(at, QT), :])
-        dp = dot_t(do, v_ref[:TRUNK, :])
-        inner = jnp.sum(p * dp, axis=1, keepdims=True)
-        ds = (p * (dp - inner)).astype(low)
-        d_ref[pl.ds(at, QT), :HEAD] = (dot(ds, k_ref[:TRUNK, :]) * scale).astype(low)
-        dk_acc[:TRUNK, :] += t_dot(ds, q)
-        dv_acc[:TRUNK, :] += t_dot(p.astype(low), do)
-    @pl.loop(0, tails)
-    def _(j):
-        at = pl.multiple_of(TRUNK + j * SEG, SEG)
-        par = pl.multiple_of(parent_ref[j] * SEG, SEG)
-        q = q_ref[pl.ds(at, SEG), :]
-        do = do_ref[pl.ds(at, SEG), :]
-        lse = lse_ref[pl.ds(at, SEG), :]
-        s1, s2, s3 = tail_scores(q, k_ref, at, par, flag_ref[j],
-                                 posq_ref[pl.ds(at, SEG), :], posk_ref[:, pl.ds(at, SEG)])
-        p1 = jnp.exp(s1 - lse); p2 = jnp.exp(s2 - lse); p3 = jnp.exp(s3 - lse)
-        d1 = dot_t(do, v_ref[:TRUNK, :])
-        d2 = dot_t(do, v_ref[pl.ds(par, SEG), :])
-        d3 = dot_t(do, v_ref[pl.ds(at, SEG), :])
-        inner = jnp.sum(p1 * d1, axis=1, keepdims=True) + jnp.sum(p2 * d2, axis=1, keepdims=True) + jnp.sum(p3 * d3, axis=1, keepdims=True)
-        g1 = (p1 * (d1 - inner)).astype(low)
-        g2 = (p2 * (d2 - inner)).astype(low)
-        g3 = (p3 * (d3 - inner)).astype(low)
-        dq = dot(g1, k_ref[:TRUNK, :]) + dot(g2, k_ref[pl.ds(par, SEG), :]) + dot(g3, k_ref[pl.ds(at, SEG), :])
-        d_ref[pl.ds(at, SEG), :HEAD] = (dq * scale).astype(low)
-        dk_acc[:TRUNK, :] += t_dot(g1, q)
-        dv_acc[:TRUNK, :] += t_dot(p1.astype(low), do)
-        dk_acc[pl.ds(par, SEG), :] += t_dot(g2, q)
-        dv_acc[pl.ds(par, SEG), :] += t_dot(p2.astype(low), do)
-        dk_acc[pl.ds(at, SEG), :] += t_dot(g3, q)
-        dv_acc[pl.ds(at, SEG), :] += t_dot(p3.astype(low), do)
-    d_ref[:, HEAD:2 * HEAD] = (dk_acc[...] * scale).astype(low)
-    d_ref[:, 2 * HEAD:] = dv_acc[...].astype(low)
-
-def whole(shape, at=0):
-    return pl.BlockSpec(shape, lambda i, *_: (0, at))
-
-def attend(qkv, parent_at, flag, posq, posk):
-    n = qkv.shape[0]
-    return pl.pallas_call(
-        fwd_kernel,
-        grid_spec=pltpu.PrefetchScalarGridSpec(
-            num_scalar_prefetch=2, grid=(1,),
-            in_specs=[whole((n, HEAD), 0), whole((n, HEAD), 1), whole((n, HEAD), 2), whole((n, 1)), whole((1, n))],
-            out_specs=[whole((n, HEAD)), whole((n, 1))]),
-        out_shape=[jax.ShapeDtypeStruct((n, HEAD), low), jax.ShapeDtypeStruct((n, 1), wide)],
-        name="attend",
-    )(parent_at, flag, qkv, qkv, qkv, posq, posk)
-
-def attend_back(qkv, d_o, parent_at, flag, posq, posk, lse):
-    n = qkv.shape[0]
-    return pl.pallas_call(
-        bwd_kernel,
-        grid_spec=pltpu.PrefetchScalarGridSpec(
-            num_scalar_prefetch=2, grid=(1,),
-            in_specs=[whole((n, HEAD), 0), whole((n, HEAD), 1), whole((n, HEAD), 2), whole((n, HEAD)), whole((n, 1)), whole((1, n)), whole((n, 1))],
-            out_specs=whole((n, 3 * HEAD)),
-            scratch_shapes=[pltpu.VMEM((n, HEAD), wide), pltpu.VMEM((n, HEAD), wide)]),
-        out_shape=jax.ShapeDtypeStruct((n, 3 * HEAD), low),
-        name="attend_back",
-    )(parent_at, flag, qkv, qkv, qkv, d_o, posq, posk, lse)
-
 def tree_tables(seg_ids, parents):
     tail_seg = seg_ids[TRUNK::SEG]
     labels = jnp.arange(parents.shape[1], dtype=jnp.int32)
@@ -172,8 +56,8 @@
     hit = (tail_seg[None, :] == tail_parent[:, None])
     at = jnp.arange(tail_seg.shape[0], dtype=jnp.int32) + TRUNK // SEG
     parent_at = jnp.sum(jnp.where(hit, at[None, :], 0), axis=1)
-    flag = (tail_parent > 0).astype(jnp.int32)
-    return parent_at, flag
+    bias = jnp.where(tail_parent > 0, 0.0, masked_out).astype(wide)
+    return parent_at, jnp.broadcast_to(bias[:, None], (tail_seg.shape[0], SEG))
 
 
 def row_sum(v): return jnp.sum(v, axis=1, keepdims=True)
@@ -192,7 +76,7 @@
     )
 
 
-def greet(n, nr):
+def greet(n, nr, extra=0):
     r, c = lax.axis_index("row"), lax.axis_index("col")
     me = r * n + c
     barrier = pltpu.get_barrier_semaphore()
@@ -202,140 +86,7 @@
         peer = lax.rem(me + d, n * nr)
         pl.semaphore_signal(barrier, inc=1, device_id={"row": peer // n, "col": lax.rem(peer, n)}, device_id_type=MESH)
 
-    pl.semaphore_wait(barrier, n * nr - 1)
-
-
-def enter_kernel(n, nr, m, tok_ref, table_ref, gain_ref, x_ref, table_all, gain_all,
-                 send_a, recv_a, send_z, recv_z, send_t, recv_t, local_sem):
-    r, c = lax.axis_index("row"), lax.axis_index("col")
-    own = tok_ref.shape[0] // nr
-    width = tok_ref.shape[1]
-    chunks = own // m
-    left = {"col": jnp.maximum(c - 1, 0)}
-    right = {"col": jnp.minimum(c + 1, n - 1)}
-
-    def piece(d, j):
-        peer = lax.rem(r + d, nr)
-        return remote(
-            tok_ref.at[span(peer * own + j * m, m)],
-            x_ref.at[span(c * own + j * m, m), span(r * width, width)],
-            send_a.at[d - 1, j], recv_a.at[d - 1, j], {"row": peer},
-        )
-
-    def block(kind, s, at, j, to):
-        rows = span(at * own + j * m, m)
-        return remote(x_ref.at[rows], x_ref.at[rows], send_z.at[kind, s, j], recv_z.at[kind, s, j], to)
-
-    def table_piece(d, kind):
-        src, dst = ((table_ref, table_all), (gain_ref, gain_all))[kind]
-        to = {"row": lax.rem(r + d, nr)}
-        return remote(src, dst.at[:, span(r * width, width)], send_t.at[kind, d - 1], recv_t.at[kind, d - 1], to)
-
-    keep = pltpu.make_async_copy(
-        tok_ref.at[span(r * own, own)], x_ref.at[span(c * own, own), span(r * width, width)], local_sem.at[0]
-    )
-    keep_table = pltpu.make_async_copy(table_ref, table_all.at[:, span(r * width, width)], local_sem.at[1])
-    keep_gain = pltpu.make_async_copy(gain_ref, gain_all.at[:, span(r * width, width)], local_sem.at[2])
-    keep.start()
-    keep_table.start()
-    keep_gain.start()
-    barrier = pltpu.get_barrier_semaphore()
-    for d in range(1, nr):
-        pl.semaphore_signal(barrier, inc=1, device_id={"row": lax.rem(r + d, nr)}, device_id_type=MESH)
-
-    @pl.when(c > 0)
-    def _():
-        pl.semaphore_signal(barrier, inc=1, device_id=left, device_id_type=MESH)
-
-    @pl.when(c < n - 1)
-    def _():
-        pl.semaphore_signal(barrier, inc=1, device_id=right, device_id_type=MESH)
-
-    inner = jnp.logical_and(c > 0, c < n - 1)
-
-    @pl.when(inner)
-    def _():
-        pl.semaphore_wait(barrier, nr + 1)
-
-    @pl.when(jnp.logical_not(inner))
-    def _():
-        pl.semaphore_wait(barrier, nr)
-
-    @pl.loop(0, chunks)
-    def _(j):
-        for d in range(1, nr):
-            piece(d, j).start()
-
-    for d in range(1, nr):
-        table_piece(d, 0).start()
-        table_piece(d, 1).start()
-    keep.wait()
-    keep_table.wait()
-    keep_gain.wait()
-
-    for s in range(n):
-        @pl.loop(0, chunks)
-        def _(j):
-            if s == 0:
-                for d in range(1, nr):
-                    piece(d, j).wait_recv()
-
-            @pl.when(c - s >= 0)
-            def _():
-                if s > 0:
-                    block(0, s - 1, jnp.maximum(c - s, 0), j, right).wait_recv()
-                if s < n - 1:
-                    @pl.when(c < n - 1)
-                    def _():
-                        block(0, s, jnp.maximum(c - s, 0), j, right).start()
-
-            @pl.when(c + s <= n - 1)
-            def _():
-                if s > 0:
-                    block(1, s - 1, jnp.minimum(c + s, n - 1), j, left).wait_recv()
-                if s < n - 1:
-                    @pl.when(c > 0)
-                    def _():
-                        block(1, s, jnp.minimum(c + s, n - 1), j, left).start()
-
-    for d in range(1, nr):
-        table_piece(d, 0).wait()
-        table_piece(d, 1).wait()
-
-    @pl.loop(0, chunks)
-    def _(j):
-        for d in range(1, nr):
-            piece(d, j).wait_send()
-        for s in range(n - 1):
-            @pl.when(jnp.logical_and(c - s >= 0, c < n - 1))
-            def _():
-                block(0, s, jnp.maximum(c - s, 0), j, right).wait_send()
-
-            @pl.when(jnp.logical_and(c + s <= n - 1, c > 0))
-            def _():
-                block(1, s, jnp.minimum(c + s, n - 1), j, left).wait_send()
-
-
-def enter(tokens, table, gain, n, nr, m=32):
-    own = tokens.shape[0] // nr
-    chunks = own // m
-    dma = pltpu.SemaphoreType.DMA
-    return pl.pallas_call(
-        functools.partial(enter_kernel, n, nr, m),
-        out_shape=[
-            jax.ShapeDtypeStruct((own * n, tokens.shape[1] * nr), tokens.dtype),
-            jax.ShapeDtypeStruct((table.shape[0], table.shape[1] * nr), table.dtype),
-            jax.ShapeDtypeStruct((gain.shape[0], gain.shape[1] * nr), gain.dtype),
-        ],
-        in_specs=[VM] * 3,
-        out_specs=[VM] * 3,
-        scratch_shapes=[
-            dma((nr - 1, chunks)), dma((nr - 1, chunks)), dma((2, n - 1, chunks)), dma((2, n - 1, chunks)),
-            dma((2, nr - 1)), dma((2, nr - 1)), dma((3,)),
-        ],
-        compiler_params=params(3),
-        name="enter",
-    )(tokens, table, gain)
+    pl.semaphore_wait(barrier, n * nr - 1 + extra)
 
 
 def row_sums(first, second):
@@ -362,152 +113,6 @@
         copy(d).start()
     for d in range(1, n):
         copy(d).wait()
-
-
-def heads_kernel(n, nr, m, raw_ref, gq_ref, gk_ref, cos_ref, sin_ref, cot_ref, out_ref, factor_ref, half_ref,
-                 stats, buf, fq, fk, send_s, recv_s, send_h, recv_h, send_g, recv_g, local_sem, local_g):
-    r, c = lax.axis_index("row"), lax.axis_index("col")
-    rows_all = raw_ref.shape[0]
-    own = rows_all // n
-    width = gq_ref.shape[1]
-    heads = width // HEAD
-    tree_part = own * nr
-    q_all = raw_ref[:, :width]
-    k_all = raw_ref[:, width:2 * width]
-    stats[c] = row_sums(q_all * q_all, k_all * k_all)
-    greet(n, nr)
-    middle = n // 2
-    owner = jnp.where(c < middle, 0, n - 1)
-    at_owner = jnp.where(c < middle, c, c - middle)
-    cot_width = cot_ref.shape[1]
-
-    def cot_piece(d):
-        peer = lax.rem(r + d, nr)
-        return remote(
-            cot_ref.at[span(peer * own, own)],
-            half_ref.at[span(at_owner * own, own), span(r * cot_width, cot_width)],
-            send_g.at[d], recv_g.at[at_owner, d], {"row": peer, "col": owner},
-        )
-
-    def cot_local():
-        return pltpu.make_async_copy(
-            cot_ref.at[span(r * own, own)],
-            half_ref.at[span(at_owner * own, own), span(r * cot_width, cot_width)], local_g
-        )
-
-    swap_stats(stats, n, send_s, recv_s)
-    for d in range(1, nr):
-        cot_piece(d).start()
-
-    @pl.when(owner == c)
-    def _():
-        cot_local().start()
-
-    @pl.when(owner != c)
-    def _():
-        cot_piece(0).start()
-
-    total = stats[0]
-    for s in range(1, n):
-        total = total + stats[s]
-    factor = lax.rsqrt(total * (1.0 / D) + epsilon)
-    factor_ref[...] = factor
-    fq[...] = down_columns(factor, 0)
-    fk[...] = down_columns(factor, 4)
-
-    def piece(d, i, at):
-        peer = lax.rem(r + d, nr)
-        block = i // (own // m)
-        inside = lax.rem(i, own // m)
-        return remote(
-            buf.at[peer, span(i * m, m)],
-            out_ref.at[span(block * tree_part + r * own + inside * m, m)],
-            send_h.at[d - 1, i], recv_h.at[d - 1, i], {"row": peer},
-        )
-
-    def local(i):
-        block = i // (own // m)
-        inside = lax.rem(i, own // m)
-        return pltpu.make_async_copy(
-            buf.at[r, span(i * m, m)], out_ref.at[span(block * tree_part + r * own + inside * m, m)], local_sem.at[i]
-        )
-
-    steps = rows_all // m
-
-    @pl.loop(0, steps)
-    def _(i):
-        rows = span(i * m, m)
-        cosine = cos_ref[rows, :]
-        sine = sin_ref[rows, :]
-        for h in range(heads):
-            lanes = slice(h * HEAD, (h + 1) * HEAD)
-            u = raw_ref[rows, lanes] * fq[rows, :] * gq_ref[:, lanes]
-            buf[h, rows, :HEAD] = (u * cosine + pltpu.roll(u, HEAD // 2, 1) * sine).astype(low)
-            k_lanes = slice(width + h * HEAD, width + (h + 1) * HEAD)
-            u = raw_ref[rows, k_lanes] * fk[rows, :] * gk_ref[:, lanes]
-            buf[h, rows, HEAD:2 * HEAD] = (u * cosine + pltpu.roll(u, HEAD // 2, 1) * sine).astype(low)
-            v_lanes = slice(2 * width + h * HEAD, 2 * width + (h + 1) * HEAD)
-            buf[h, rows, 2 * HEAD:] = raw_ref[rows, v_lanes].astype(low)
-        for d in range(1, nr):
-            piece(d, i, 0).start()
-        local(i).start()
-
-    @pl.loop(0, steps)
-    def _(i):
-        for d in range(1, nr):
-            piece(d, i, 0).wait()
-        local(i).wait()
-
-    for d in range(1, nr):
-        cot_piece(d).wait_send()
-
-    @pl.when(owner != c)
-    def _():
-        cot_piece(0).wait_send()
-
-    @pl.when(owner == c)
-    def _():
-        cot_local().wait()
-        for b in range(middle):
-            for d in range(nr):
-                def take():
-                    remote(
-                        cot_ref.at[span(r * own, own)],
-                        half_ref.at[span(b * own, own), span(0, cot_width)],
-                        send_g.at[d], recv_g.at[b, d], {"row": r, "col": c},
-                    ).wait_recv()
-                if d == 0:
-                    pl.when(b != at_owner)(take)
-                else:
-                    take()
-
-
-def to_heads_call(raw, gain_q, gain_k, cos2, sin2, cot, n, nr, m=80):
-    rows_all, wide3 = raw.shape
-    width = wide3 // 3
-    own = rows_all // n
-    dma = pltpu.SemaphoreType.DMA
-    steps = rows_all // m
-    return pl.pallas_call(
-        functools.partial(heads_kernel, n, nr, m),
-        out_shape=[
-            jax.ShapeDtypeStruct((own * n * nr, 3 * HEAD), low),
-            jax.ShapeDtypeStruct((8, rows_all), wide),
-            jax.ShapeDtypeStruct((own * n // 2, cot.shape[1] * nr), low),
-        ],
-        in_specs=[VM] * 6,
-        out_specs=[VM] * 3,
-        scratch_shapes=[
-            pltpu.VMEM((n, 8, rows_all), wide),
-            pltpu.VMEM((width // HEAD, rows_all, 3 * HEAD), low),
-            pltpu.VMEM((rows_all, HEAD), wide),
-            pltpu.VMEM((rows_all, HEAD), wide),
-            dma((n - 1,)), dma((n - 1,)), dma((nr - 1, steps)), dma((nr - 1, steps)),
-            dma((nr,)), dma((n // 2, nr)), dma((steps,)), dma,
-        ],
-        compiler_params=params(4),
-        name="to_heads",
-    )(raw, gain_q, gain_k, cos2, sin2, cot)
 
 
 def unheads_kernel(n, nr, d_ref, raw_ref, factor_ref, gq_ref, gk_ref, cos_ref, sin_ref, res_ref, out_ref, res_out,
@@ -881,13 +486,557 @@
     )(part, full, cols, hot)
 
 
-def middle_kernel(n, nr, m, hop, head_ref, x_hbm, cot_hbm, gain_ref, wo_hbm, wg_hbm, wd_hbm,
-                  ao_ref, bo_ref, ag_ref, bg_ref, ad_ref, bd_ref,
+def flip(v):
+    return v + 1 - 2 * lax.rem(v, 2)
+
+
+class Share:
+    def __init__(self, src, dst, cuts, sems):
+        self.send, self.recv, self.local = sems
+        self.src, self.cuts = src, cuts
+        g, r = lax.axis_index("dp"), lax.axis_index("row")
+        size = src.shape[0]
+        half = size // 2
+        step = half // cuts
+        far = lax.rem(r + 2, 4)
+        mine = lax.rem(g, 2)
+        near_to, far_to, twin_to = {"row": flip(r)}, {"row": far}, {"dp": flip(g)}
+
+        def rows(shard, part, i):
+            return pl.ds(pl.multiple_of(shard * size + part * half + i * step, step), step)
+
+        def copy(kind, i, src, dst, to):
+            return remote(src, dst, self.send.at[kind, i], self.recv.at[kind, i], to)
+
+        def hand(kind, part, to):
+            return lambda i: copy(kind, i, dst.at[rows(far, part, i)], dst.at[rows(far, part, i)], to)
+
+        whole = span(r * size, size)
+        self.own = pltpu.make_async_copy(src, dst.at[whole], self.local)
+        self.near = copy(0, 0, src, dst.at[whole], near_to)
+        self.far = lambda i: copy(
+            1, i, src.at[pl.ds(pl.multiple_of(mine * half + i * step, step), step)], dst.at[rows(r, mine, i)], far_to
+        )
+        self.far_near = hand(2, mine, near_to)
+        self.far_twin = hand(3, mine, twin_to)
+        self.twin_near = hand(4, 1 - mine, near_to)
+
+    def start_far(self):
+        for i in range(self.cuts):
+            self.far(i).start()
+
+    def start_near(self):
+        self.own.start()
+        self.near.start()
+
+    def pass_far(self, i):
+        self.far(i).wait_recv()
+        self.far_twin(i).start()
+        self.far_near(i).start()
+
+    def pass_twin(self, i):
+        self.far_twin(i).wait_recv()
+        self.twin_near(i).start()
+
+    def wait_all(self):
+        self.own.wait()
+        self.near.wait_recv()
+        for i in range(self.cuts):
+            self.far_near(i).wait_recv()
+            self.twin_near(i).wait_recv()
+
+    def drain(self):
+        self.near.wait_send()
+        for i in range(self.cuts):
+            self.far(i).wait_send()
+            self.far_near(i).wait_send()
+            self.far_twin(i).wait_send()
+            self.twin_near(i).wait_send()
+
+
+def share_sems(cuts):
+    dma = pltpu.SemaphoreType.DMA
+    return [dma((5, cuts)), dma((5, cuts)), dma]
+
+
+def prep_kernel(set_ref, fq_ref, sq_ref, fo_ref, so_ref, fg_ref, sg_ref, fd_ref, sd_ref,
+                narrow_ref, bq_ref, ao_ref, bg_ref, ad_ref):
+    for j in range(3):
+        narrow_ref[j * RANK:(j + 1) * RANK, :] = fq_ref[j, 0].astype(low)
+        bq_ref[j * RANK:(j + 1) * RANK, :] = sq_ref[j, 0].astype(low)
+    for j in range(2):
+        narrow_ref[(3 + j) * RANK:(4 + j) * RANK, :] = fg_ref[j, 0].astype(low)
+        bg_ref[j] = sg_ref[j, 0].astype(low)
+    narrow_ref[5 * RANK:6 * RANK, :] = so_ref[0].astype(low)
+    narrow_ref[6 * RANK:, :] = sd_ref[0].astype(low)
+    ao_ref[...] = fo_ref[0].astype(low)
+    ad_ref[...] = fd_ref[0].astype(low)
+
+
+def prep(tree_sets, tables):
+    fq, sq, fo, so, fg, sg, fd, sd = tables
+
+    def pick(table):
+        if table.ndim == 4:
+            return pl.BlockSpec((table.shape[0], 1) + table.shape[2:], lambda i, s: (0, s[0], 0, 0))
+        return pl.BlockSpec((1,) + table.shape[1:], lambda i, s: (s[0], 0, 0))
+
+    def out(*shape):
+        return pl.BlockSpec(shape, lambda i, s: (0,) * len(shape)), jax.ShapeDtypeStruct(shape, low)
+
+    outs = [
+        out(7 * RANK, fq.shape[-1]), out(3 * RANK, sq.shape[-1]), out(RANK, fo.shape[-1]),
+        out(2, RANK, sg.shape[-1]), out(RANK, fd.shape[-1]),
+    ]
+    return pl.pallas_call(
+        prep_kernel,
+        grid_spec=pltpu.PrefetchScalarGridSpec(
+            num_scalar_prefetch=1, grid=(1,), in_specs=[pick(t) for t in tables], out_specs=[o[0] for o in outs]
+        ),
+        out_shape=[o[1] for o in outs],
+        name="prep",
+    )(tree_sets, *tables)
+
+
+def lower_mask(size):
+    return lax.broadcasted_iota(jnp.int32, (size, size), 1) <= lax.broadcasted_iota(jnp.int32, (size, size), 0)
+
+
+def softmax_parts(parts):
+    top = jnp.max(parts[0], axis=1, keepdims=True)
+    for s in parts[1:]:
+        top = jnp.maximum(top, jnp.max(s, axis=1, keepdims=True))
+    raised = [jnp.exp(s - top) for s in parts]
+    total = jnp.sum(raised[0], axis=1, keepdims=True)
+    for e in raised[1:]:
+        total = total + jnp.sum(e, axis=1, keepdims=True)
+    inverse = 1.0 / total
+    return [e * inverse for e in raised], top + jnp.log(total)
+
+
+def tail_parts(q, qkv, at, parent, flag):
+    scale = HEAD ** -0.5
+    k_lanes = slice(HEAD, 2 * HEAD)
+    trunk = dot_t(q, qkv[:TRUNK, k_lanes]) * scale
+    branch = dot_t(q, qkv[pl.ds(parent, SEG), k_lanes]) * scale + flag
+    own = jnp.where(lower_mask(SEG), dot_t(q, qkv[pl.ds(at, SEG), k_lanes]) * scale, masked_out)
+    return [trunk, branch, own]
+
+
+def trunk_parts(q, qkv, i):
+    scale = HEAD ** -0.5
+    k_lanes = slice(HEAD, 2 * HEAD)
+    own = dot_t(q, qkv[i * QT:(i + 1) * QT, k_lanes]) * scale
+    parts = [jnp.where(lower_mask(QT), own, masked_out)]
+    if i:
+        parts.append(dot_t(q, qkv[:i * QT, k_lanes]) * scale)
+    return parts
+
+
+def attend_body(parent_ref, flag_ref, qkv, o_ref, lse_ref):
+    v_lanes = slice(2 * HEAD, 3 * HEAD)
+    for i in range(TRUNK // QT):
+        at = slice(i * QT, (i + 1) * QT)
+        p, lse = softmax_parts(trunk_parts(qkv[at, :HEAD], qkv, i))
+        o = dot(p[0].astype(low), qkv[at, v_lanes])
+        if i:
+            o = o + dot(p[1].astype(low), qkv[:i * QT, v_lanes])
+        o_ref[at, :] = o.astype(low)
+        lse_ref[at, :] = lse
+
+    @pl.loop(0, (qkv.shape[0] - TRUNK) // SEG)
+    def _(j):
+        at = pl.multiple_of(TRUNK + j * SEG, SEG)
+        parent = pl.multiple_of(parent_ref[j] * SEG, SEG)
+        rows = pl.ds(at, SEG)
+        p, lse = softmax_parts(tail_parts(qkv[rows, :HEAD], qkv, at, parent, flag_ref[pl.ds(j, 1), :]))
+        o = dot(p[0].astype(low), qkv[:TRUNK, v_lanes])
+        o = o + dot(p[1].astype(low), qkv[pl.ds(parent, SEG), v_lanes])
+        o = o + dot(p[2].astype(low), qkv[rows, v_lanes])
+        o_ref[rows, :] = o.astype(low)
+        lse_ref[rows, :] = lse
+
+
+def back_parts(scores, lse, d_out, keys, values):
+    probs = [jnp.exp(s - lse) for s in scores]
+    grads = [dot_t(d_out, v) for v in values]
+    inner = sum(jnp.sum(p * g, axis=1, keepdims=True) for p, g in zip(probs, grads))
+    d_scores = [(p * (g - inner)).astype(low) for p, g in zip(probs, grads)]
+    dq = sum(dot(d, k) for d, k in zip(d_scores, keys))
+    return d_scores, [p.astype(low) for p in probs], dq
+
+
+def attend_back_kernel(parent_ref, flag_ref, qkv, do_ref, lse_ref, d_ref, dk_acc, dv_acc):
+    scale = HEAD ** -0.5
+    k_lanes = slice(HEAD, 2 * HEAD)
+    v_lanes = slice(2 * HEAD, 3 * HEAD)
+    dk_acc[...] = jnp.zeros_like(dk_acc)
+    dv_acc[...] = jnp.zeros_like(dv_acc)
+    for i in range(TRUNK // QT):
+        at = slice(i * QT, (i + 1) * QT)
+        spans = [at] + ([slice(0, i * QT)] if i else [])
+        q, d_out = qkv[at, :HEAD], do_ref[at, :]
+        d_scores, probs, dq = back_parts(
+            trunk_parts(q, qkv, i), lse_ref[at, :], d_out, [qkv[s, k_lanes] for s in spans], [qkv[s, v_lanes] for s in spans]
+        )
+        d_ref[at, :HEAD] = (dq * scale).astype(low)
+        for s, d, p in zip(spans, d_scores, probs):
+            dk_acc[s, :] += t_dot(d, q)
+            dv_acc[s, :] += t_dot(p, d_out)
+
+    @pl.loop(0, (qkv.shape[0] - TRUNK) // SEG)
+    def _(j):
+        at = pl.multiple_of(TRUNK + j * SEG, SEG)
+        parent = pl.multiple_of(parent_ref[j] * SEG, SEG)
+        rows = pl.ds(at, SEG)
+        spans = [slice(0, TRUNK), pl.ds(parent, SEG), rows]
+        q, d_out = qkv[rows, :HEAD], do_ref[rows, :]
+        d_scores, probs, dq = back_parts(
+            tail_parts(q, qkv, at, parent, flag_ref[pl.ds(j, 1), :]), lse_ref[rows, :], d_out,
+            [qkv[s, k_lanes] for s in spans], [qkv[s, v_lanes] for s in spans],
+        )
+        d_ref[rows, :HEAD] = (dq * scale).astype(low)
+        for s, d, p in zip(spans, d_scores, probs):
+            dk_acc[s, :] += t_dot(d, q)
+            dv_acc[s, :] += t_dot(p, d_out)
+
+    d_ref[:, k_lanes] = (dk_acc[...] * scale).astype(low)
+    d_ref[:, v_lanes] = dv_acc[...].astype(low)
+
+
+def attend(qkv, parent_at, flag):
+    n = qkv.shape[0]
+
+    def whole(*shape):
+        return pl.BlockSpec(shape, lambda i, *_: (0, 0))
+
+    return pl.pallas_call(
+        attend_body,
+        grid_spec=pltpu.PrefetchScalarGridSpec(
+            num_scalar_prefetch=1,
+            grid=(1,),
+            in_specs=[whole(*flag.shape), whole(n, 3 * HEAD)],
+            out_specs=[whole(n, HEAD), whole(n, 1)],
+        ),
+        out_shape=[jax.ShapeDtypeStruct((n, HEAD), low), jax.ShapeDtypeStruct((n, 1), wide)],
+        name="attend",
+    )(parent_at, flag, qkv)
+
+
+def attend_back(qkv, d_o, parent_at, flag, lse):
+    n = qkv.shape[0]
+
+    def whole(*shape):
+        return pl.BlockSpec(shape, lambda i, *_: (0, 0))
+
+    return pl.pallas_call(
+        attend_back_kernel,
+        grid_spec=pltpu.PrefetchScalarGridSpec(
+            num_scalar_prefetch=1,
+            grid=(1,),
+            in_specs=[whole(*flag.shape), whole(n, 3 * HEAD), whole(n, HEAD), whole(n, 1)],
+            out_specs=whole(n, 3 * HEAD),
+            scratch_shapes=[pltpu.VMEM((n, HEAD), wide), pltpu.VMEM((n, HEAD), wide)],
+        ),
+        out_shape=jax.ShapeDtypeStruct((n, 3 * HEAD), low),
+        name="attend_back",
+    )(parent_at, flag, qkv, d_o, lse)
+
+
+def front_kernel(n, nr, m, mh, tok_ref, table_ref, gain_ref, cot_ref, wq_hbm, wo_hbm, bq_ref, gq_ref, gk_ref,
+                 cos_ref, sin_ref,
+                 x_ref, table_all, gain_all, half_ref, raw_ref, factor_ref, qkv_ref, wq_out, wo_out,
+                 wq, wo, stats, buf, fq, fk,
+                 send_a, recv_a, send_z, recv_z, send_t, recv_t, local_sem,
+                 send_s, recv_s, send_h, recv_h, send_g, recv_g, local_h, local_g,
+                 send_q, recv_q, local_q, send_o, recv_o, local_o, out_sems):
+    g, r, c = lax.axis_index("dp"), lax.axis_index("row"), lax.axis_index("col")
+    own = tok_ref.shape[0] // nr
+    width = tok_ref.shape[1]
+    rows_all = own * n
+    heads = width // HEAD
+    tree_part = own * nr
+    chunks = own // m
+    left = {"col": jnp.maximum(c - 1, 0)}
+    right = {"col": jnp.minimum(c + 1, n - 1)}
+    share_q = Share(wq_hbm, wq, 2, (send_q, recv_q, local_q))
+    share_o = Share(wo_hbm, wo, 2, (send_o, recv_o, local_o))
+
+    def piece(d, j):
+        peer = lax.rem(r + d, nr)
+        return remote(
+            tok_ref.at[span(peer * own + j * m, m)],
+            x_ref.at[span(c * own + j * m, m), span(r * width, width)],
+            send_a.at[d - 1, j], recv_a.at[d - 1, j], {"row": peer},
+        )
+
+    def block(kind, s, at, j, to):
+        rows = span(at * own + j * m, m)
+        return remote(x_ref.at[rows], x_ref.at[rows], send_z.at[kind, s, j], recv_z.at[kind, s, j], to)
+
+    def table_piece(d, kind):
+        src, dst = ((table_ref, table_all), (gain_ref, gain_all))[kind]
+        to = {"row": lax.rem(r + d, nr)}
+        return remote(src, dst.at[:, span(r * width, width)], send_t.at[kind, d - 1], recv_t.at[kind, d - 1], to)
+
+    keep = pltpu.make_async_copy(
+        tok_ref.at[span(r * own, own)], x_ref.at[span(c * own, own), span(r * width, width)], local_sem.at[0]
+    )
+    keep_table = pltpu.make_async_copy(table_ref, table_all.at[:, span(r * width, width)], local_sem.at[1])
+    keep_gain = pltpu.make_async_copy(gain_ref, gain_all.at[:, span(r * width, width)], local_sem.at[2])
+    keep.start()
+    keep_table.start()
+    keep_gain.start()
+    barrier = pltpu.get_barrier_semaphore()
+    pl.semaphore_signal(barrier, inc=1, device_id={"dp": flip(g)}, device_id_type=MESH)
+    greet(n, nr, 1)
+
+    @pl.loop(0, chunks)
+    def _(j):
+        for d in range(1, nr):
+            piece(d, j).start()
+
+    share_q.start_far()
+    share_q.start_near()
+    for d in range(1, nr):
+        table_piece(d, 0).start()
+        table_piece(d, 1).start()
+    share_o.start_far()
+    share_o.start_near()
+    keep.wait()
+
+    for s in range(n):
+        @pl.loop(0, chunks)
+        def _(j):
+            if s == 0:
+                for d in range(1, nr):
+                    piece(d, j).wait_recv()
+
+            @pl.when(c - s >= 0)
+            def _():
+                if s > 0:
+                    block(0, s - 1, jnp.maximum(c - s, 0), j, right).wait_recv()
+                if s < n - 1:
+                    @pl.when(c < n - 1)
+                    def _():
+                        block(0, s, jnp.maximum(c - s, 0), j, right).start()
+
+            @pl.when(c + s <= n - 1)
+            def _():
+                if s > 0:
+                    block(1, s - 1, jnp.minimum(c + s, n - 1), j, left).wait_recv()
+                if s < n - 1:
+                    @pl.when(c > 0)
+                    def _():
+                        block(1, s, jnp.minimum(c + s, n - 1), j, left).start()
+
+        if s == 1:
+            for i in range(2):
+                share_q.pass_far(i)
+        if s == 2:
+            for i in range(2):
+                share_o.pass_far(i)
+                share_q.pass_twin(i)
+    for i in range(2):
+        share_o.pass_twin(i)
+
+    for d in range(1, nr):
+        table_piece(d, 0).wait_recv()
+        table_piece(d, 1).wait_recv()
+    keep_table.wait()
+    keep_gain.wait()
+    share_q.wait_all()
+    copy_wq = pltpu.make_async_copy(wq, wq_out, out_sems.at[0])
+    copy_wq.start()
+
+    red = dot_t(x_ref[...], table_all[:3 * RANK, :]).astype(low)
+    for j in range(3):
+        lanes = slice(j * width, (j + 1) * width)
+        raw_ref[:, lanes] = dot(x_ref[...], wq[:, lanes]) + dot(
+            red[:, j * RANK:(j + 1) * RANK], bq_ref[j * RANK:(j + 1) * RANK, :]
+        )
+    q_all = raw_ref[:, :width]
+    k_all = raw_ref[:, width:2 * width]
+    stats[c] = row_sums(q_all * q_all, k_all * k_all)
+
+    middle_at = n // 2
+    owner = jnp.where(c < middle_at, 0, n - 1)
+    at_owner = jnp.where(c < middle_at, c, c - middle_at)
+
+    def cot_piece(d):
+        peer = lax.rem(r + d, nr)
+        return remote(
+            cot_ref.at[span(peer * own, own)],
+            half_ref.at[span(at_owner * own, own), span(r * width, width)],
+            send_g.at[d], recv_g.at[at_owner, d], {"row": peer, "col": owner},
+        )
+
+    def cot_local():
+        return pltpu.make_async_copy(
+            cot_ref.at[span(r * own, own)], half_ref.at[span(at_owner * own, own), span(r * width, width)], local_g
+        )
+
+    swap_stats(stats, n, send_s, recv_s)
+    total = stats[0]
+    for s in range(1, n):
+        total = total + stats[s]
+    factor = lax.rsqrt(total * (1.0 / D) + epsilon)
+    factor_ref[...] = factor
+    fq[...] = down_columns(factor, 0)
+    fk[...] = down_columns(factor, 4)
+
+    def head_rows(i):
+        block_at = i // (own // mh)
+        inside = lax.rem(i, own // mh)
+        return span(block_at * tree_part + r * own + inside * mh, mh)
+
+    def head_piece(d, i):
+        peer = lax.rem(r + d, nr)
+        return remote(
+            buf.at[peer, span(i * mh, mh)], qkv_ref.at[head_rows(i)], send_h.at[d - 1, i], recv_h.at[d - 1, i], {"row": peer}
+        )
+
+    def head_local(i):
+        return pltpu.make_async_copy(buf.at[r, span(i * mh, mh)], qkv_ref.at[head_rows(i)], local_h.at[i])
+
+    steps = rows_all // mh
+
+    @pl.loop(0, steps)
+    def _(i):
+        rows = span(i * mh, mh)
+        cosine = cos_ref[rows, :]
+        sine = sin_ref[rows, :]
+        for h in range(heads):
+            lanes = slice(h * HEAD, (h + 1) * HEAD)
+            u = raw_ref[rows, lanes] * fq[rows, :] * gq_ref[:, lanes]
+            buf[h, rows, :HEAD] = (u * cosine + pltpu.roll(u, HEAD // 2, 1) * sine).astype(low)
+            k_lanes = slice(width + h * HEAD, width + (h + 1) * HEAD)
+            u = raw_ref[rows, k_lanes] * fk[rows, :] * gk_ref[:, lanes]
+            buf[h, rows, HEAD:2 * HEAD] = (u * cosine + pltpu.roll(u, HEAD // 2, 1) * sine).astype(low)
+            v_lanes = slice(2 * width + h * HEAD, 2 * width + (h + 1) * HEAD)
+            buf[h, rows, 2 * HEAD:] = raw_ref[rows, v_lanes].astype(low)
+        for d in range(1, nr):
+            head_piece(d, i).start()
+        head_local(i).start()
+
+    for d in range(1, nr):
+        cot_piece(d).start()
+
+    @pl.when(owner == c)
+    def _():
+        cot_local().start()
+
+    @pl.when(owner != c)
+    def _():
+        cot_piece(0).start()
+
+    share_o.wait_all()
+    copy_wo = pltpu.make_async_copy(wo, wo_out, out_sems.at[1])
+    copy_wo.start()
+
+    @pl.loop(0, steps)
+    def _(i):
+        for d in range(1, nr):
+            head_piece(d, i).wait()
+        head_local(i).wait()
+
+    for d in range(1, nr):
+        cot_piece(d).wait_send()
+
+    @pl.when(owner != c)
+    def _():
+        cot_piece(0).wait_send()
+
+    @pl.when(owner == c)
+    def _():
+        cot_local().wait()
+        for b in range(middle_at):
+            for d in range(nr):
+                def take():
+                    remote(
+                        cot_ref.at[span(0, own)], half_ref.at[span(b * own, own), span(0, width)],
+                        send_g.at[d], recv_g.at[b, d], {"row": flip(r)},
+                    ).wait_recv()
+                if d == 0:
+                    pl.when(b != at_owner)(take)
+                else:
+                    take()
+
+    @pl.loop(0, chunks)
+    def _(j):
+        for d in range(1, nr):
+            piece(d, j).wait_send()
+        for s in range(n - 1):
+            @pl.when(jnp.logical_and(c - s >= 0, c < n - 1))
+            def _():
+                block(0, s, jnp.maximum(c - s, 0), j, right).wait_send()
+
+            @pl.when(jnp.logical_and(c + s <= n - 1, c > 0))
+            def _():
+                block(1, s, jnp.minimum(c + s, n - 1), j, left).wait_send()
+
+    for d in range(1, nr):
+        table_piece(d, 0).wait_send()
+        table_piece(d, 1).wait_send()
+    share_q.drain()
+    share_o.drain()
+    copy_wq.wait()
+    copy_wo.wait()
+
+
+def front(tokens, table, gain, cot, w_qkv, w_out, b_qkv, gain_q, gain_k, cos2, sin2, n, nr, m=32, mh=80):
+    own = tokens.shape[0] // nr
+    width = tokens.shape[1]
+    rows_all = own * n
+    tree = own * n * nr
+    chunks = own // m
+    steps = rows_all // mh
+    dma = pltpu.SemaphoreType.DMA
+    shape = jax.ShapeDtypeStruct
+    any_space = pl.BlockSpec(memory_space=pl.ANY)
+    return pl.pallas_call(
+        functools.partial(front_kernel, n, nr, m, mh),
+        out_shape=[
+            shape((rows_all, width * nr), low),
+            shape((table.shape[0], width * nr), low),
+            shape((gain.shape[0], width * nr), wide),
+            shape((rows_all // 2, width * nr), low),
+            shape((rows_all, 3 * width), wide),
+            shape((8, rows_all), wide),
+            shape((tree, 3 * HEAD), low),
+            shape((w_qkv.shape[0] * nr, w_qkv.shape[1]), low),
+            shape((w_out.shape[0] * nr, w_out.shape[1]), low),
+        ],
+        in_specs=[VM, VM, VM, VM, any_space, any_space] + [VM] * 5,
+        out_specs=[VM] * 7 + [any_space, any_space],
+        scratch_shapes=[
+            pltpu.VMEM((w_qkv.shape[0] * nr, w_qkv.shape[1]), low),
+            pltpu.VMEM((w_out.shape[0] * nr, w_out.shape[1]), low),
+            pltpu.VMEM((n, 8, rows_all), wide),
+            pltpu.VMEM((width // HEAD, rows_all, 3 * HEAD), low),
+            pltpu.VMEM((rows_all, HEAD), wide),
+            pltpu.VMEM((rows_all, HEAD), wide),
+            dma((nr - 1, chunks)), dma((nr - 1, chunks)), dma((2, n - 1, chunks)), dma((2, n - 1, chunks)),
+            dma((2, nr - 1)), dma((2, nr - 1)), dma((3,)),
+            dma((n - 1,)), dma((n - 1,)), dma((nr - 1, steps)), dma((nr - 1, steps)),
+            dma((nr,)), dma((n // 2, nr)), dma((steps,)), dma,
+        ] + share_sems(2) + share_sems(2) + [dma((2,))],
+        compiler_params=params(3),
+        name="front",
+    )(tokens, table, gain, cot, w_qkv, w_out, b_qkv, gain_q, gain_k, cos2, sin2)
+
+
+def middle_kernel(n, nr, m, hop, cuts, head_ref, x_hbm, cot_hbm, gain_ref, wo_hbm, wg_hbm, wd_hbm,
+                  table_ref, ao_ref, bg_ref, ad_ref,
                   dhead_ref, out_half, grad_half, full_ref, co_ref, cg_ref, cd_ref,
                   wo, wg, wd, x_half, cot_half, raw, attn, d_attn, h_all, df_all, da_all, gu, part,
                   recv_right, recv_left, hid, red_gu, red_down, back_gu, back_down,
-                  sems_send, sems_recv, send_in, recv_in, send_out, recv_out, local_in, local_out, load, load_w):
-    r, c = lax.axis_index("row"), lax.axis_index("col")
+                  sems_send, sems_recv, send_in, recv_in, send_out, recv_out, local_in, local_out, load,
+                  send_g, recv_g, local_g, send_d, recv_d, local_d):
+    g, r, c = lax.axis_index("dp"), lax.axis_index("row"), lax.axis_index("col")
+    ag_ref = table_ref.at[3 * RANK:5 * RANK]
+    bo_ref = table_ref.at[5 * RANK:6 * RANK]
+    bd_ref = table_ref.at[6 * RANK:]
     rows_all, width_all = part.shape
     half = rows_all // 2
     own = rows_all // n
@@ -905,16 +1054,11 @@
 
     base = jnp.where(last, half, 0)
     a_cut = hidden // 4
+    share_g = Share(wg_hbm, wg, cuts, (send_g, recv_g, local_g))
+    share_d = Share(wd_hbm, wd, cuts // 2, (send_d, recv_d, local_d))
     loads = [pltpu.make_async_copy(wo_hbm, wo, load.at[0])]
-    loads_a = []
-    for k in range(4):
-        lanes = slice(k * a_cut, (k + 1) * a_cut)
-        up_lanes = slice(hidden + k * a_cut, hidden + (k + 1) * a_cut)
-        loads_a.append(pltpu.make_async_copy(wg_hbm.at[:, lanes], wg.at[:, lanes], load_w.at[2 * k]))
-        loads_a.append(pltpu.make_async_copy(wg_hbm.at[:, up_lanes], wg.at[:, up_lanes], load_w.at[2 * k + 1]))
     load_x = pltpu.make_async_copy(x_hbm.at[span(base, half)], x_half, load.at[1])
     load_cot = pltpu.make_async_copy(cot_hbm, cot_half, load.at[2])
-    load_d = pltpu.make_async_copy(wd_hbm, wd, load.at[3])
     loads[0].start()
 
     def piece_in(d, b):
@@ -959,6 +1103,7 @@
     def _():
         pl.semaphore_signal(barrier, inc=1, device_id=right, device_id_type=MESH)
 
+    pl.semaphore_signal(barrier, inc=1, device_id={"dp": flip(g)}, device_id_type=MESH)
     full_ref[...] = jnp.zeros_like(full_ref)
     co_ref[...] = jnp.zeros_like(co_ref)
     cg_ref[...] = jnp.zeros_like(cg_ref)
@@ -966,22 +1111,23 @@
 
     @pl.when(inner)
     def _():
-        pl.semaphore_wait(barrier, nr + 1)
+        pl.semaphore_wait(barrier, nr + 2)
 
     @pl.when(jnp.logical_not(inner))
     def _():
-        pl.semaphore_wait(barrier, nr)
+        pl.semaphore_wait(barrier, nr + 1)
 
     middle = n // 2
     for b in range(middle):
         for block in (b, middle + b):
             for d in range(1, nr):
                 piece_in(d, block).start()
-    for copy in loads_a:
-        copy.start()
     load_x.start()
-    load_d.start()
     load_cot.start()
+    share_g.start_far()
+    share_d.start_far()
+    share_g.start_near()
+    share_d.start_near()
 
     def rows(j, start=0):
         return span(start + j * m, m)
@@ -998,7 +1144,7 @@
         part[low_rows, lanes] = value[:band].astype(low)
         part[high_rows, lanes] = value[band:].astype(low)
 
-    def relay_stage(stage, per, work, owner_step, all_ref):
+    def relay_stage(stage, per, work, owner_step, all_ref, pump=None):
         def send(kind, j, src, dst, to):
             return remote(src, dst, sems_send.at[stage, kind, j], sems_recv.at[stage, kind, j], to)
 
@@ -1077,6 +1223,9 @@
             def _(t):
                 work(t // per, lax.rem(t, per))
 
+            if pump is not None:
+                pump(ii)
+
         @pl.loop(0, chunks)
         def _(j):
             @pl.when(first)
@@ -1098,6 +1247,9 @@
                 spread_left(j).wait_send()
                 spread_right(j).wait_send()
 
+    def shard(j, ref):
+        return slice(j * (ref.shape[0] // nr), (j + 1) * (ref.shape[0] // nr))
+
     def out_work(b, k):
         @pl.when(b == 0)
         def _():
@@ -1115,7 +1267,7 @@
         red = dot_t(rows_in, ao_ref[...]).astype(low)
         for j in range(nr):
             lanes = slice(j * width, (j + 1) * width)
-            put(b, lanes, dot(rows_in, wo[j]) + dot(red, bo_ref[:, lanes]))
+            put(b, lanes, dot(rows_in, wo[shard(j, wo), :]) + dot(red, bo_ref[:, lanes]))
 
     gain_a = gain_ref[0:1, :]
     gain_f = gain_ref[1:2, :]
@@ -1125,18 +1277,47 @@
         flat = total * norm_factor(row_sum(total * total))
         return (x_half[at, :].astype(wide) + flat * gain_a).astype(low)
 
+    first_pass = 5
+    apart = 3
+    late = 2
+    passes = cuts + cuts // 2
+
+    def pump(ii):
+        at = ii - first_pass
+
+        @pl.when(jnp.logical_and(at >= 0, lax.rem(at, apart) == 0))
+        def _():
+            t = at // apart
+
+            @pl.when(t < cuts)
+            def _():
+                share_g.pass_far(t)
+
+            @pl.when(jnp.logical_and(t >= cuts, t < passes))
+            def _():
+                share_d.pass_far(t - cuts)
+
+            t = t - late
+
+            @pl.when(jnp.logical_and(t >= 0, t < cuts))
+            def _():
+                share_g.pass_twin(t)
+
+            @pl.when(jnp.logical_and(t >= cuts, t < passes))
+            def _():
+                share_d.pass_twin(t - cuts)
+
     load_x.wait()
-    relay_stage(0, 1, out_work, attn_owner, h_all)
+    relay_stage(0, 1, out_work, attn_owner, h_all, pump)
+    in_loop = 1 + chunks + hop * 2 * (n - 1)
+
+    @pl.loop(in_loop, jnp.maximum(in_loop, first_pass + apart * (passes + late)))
+    def _(ii):
+        pump(ii)
+
+    share_g.wait_all()
 
     def gate_slice(b, k):
-        @pl.when(b == 0)
-        def _():
-            for s in range(4):
-                @pl.when(k == s)
-                def _():
-                    loads_a[2 * s].wait()
-                    loads_a[2 * s + 1].wait()
-
         rows_in = take(h_all, b)
 
         @pl.when(k == 0)
@@ -1156,7 +1337,7 @@
     def down_slice(b, k):
         @pl.when(jnp.logical_and(b == 0, k == 0))
         def _():
-            load_d.wait()
+            share_d.wait_all()
 
         rows_in = hid[:, :hidden]
 
@@ -1167,7 +1348,8 @@
         for s in range(nr // 2):
             j = k * (nr // 2) + s
             lanes = span(j * width, width)
-            put(b, lanes, dot(rows_in, wd[j]) + dot(red_down[b], bd_ref[:, lanes]))
+            down_rows = pl.ds(pl.multiple_of(j * hidden, hidden), hidden)
+            put(b, lanes, dot(rows_in, wd[down_rows, :]) + dot(red_down[b], bd_ref[:, lanes]))
 
     def ffn_work(b, k):
         @pl.when(k < 4)
@@ -1205,7 +1387,8 @@
         back = back_down[...]
         grad = dot(back, ad_ref[:, lanes])
         for j in range(nr):
-            grad = grad + dot_t(rows_in[:, j * width:(j + 1) * width], wd[j, lanes, :])
+            down_rows = pl.ds(pl.multiple_of(j * hidden + at, b_cut), b_cut)
+            grad = grad + dot_t(rows_in[:, j * width:(j + 1) * width], wd[down_rows, :])
         gate = gu[b, :, lanes].astype(wide)
         up = gu[b, :, up_lanes].astype(wide)
         sigma = jax.nn.sigmoid(gate)
@@ -1262,7 +1445,7 @@
         back = dot_t(rows_in, bo_ref[...]).astype(low)
         grad = dot(back, ao_ref[...])
         for j in range(nr):
-            grad = grad + dot_t(rows_in[:, j * width:(j + 1) * width], wo[j])
+            grad = grad + dot_t(rows_in[:, j * width:(j + 1) * width], wo[shard(j, wo), :])
         d_attn[at, :] = grad.astype(low)
         for d in range(1, nr):
             piece_out(d, b).start()
@@ -1279,8 +1462,11 @@
             piece_out(d, b).wait()
         local_piece_out(b).wait()
 
-
-def middle(attn_head, x, cot_half, gains, w_out, w_gu, w_down, a_out, b_out, a_gu, b_gu, a_down, b_down, n, nr, m=16, hop=2):
+    share_g.drain()
+    share_d.drain()
+
+
+def middle(attn_head, x, cot_half, gains, w_out, w_gu, w_down, table, a_out, b_gu, a_down, n, nr, m=16, hop=2, cuts=8):
     group, width_all = x.shape
     half = group // 2
     width = width_all // nr
@@ -1291,7 +1477,7 @@
     any_space = pl.BlockSpec(memory_space=pl.ANY)
     shape = jax.ShapeDtypeStruct
     return pl.pallas_call(
-        functools.partial(middle_kernel, n, nr, m, hop),
+        functools.partial(middle_kernel, n, nr, m, hop, cuts),
         out_shape=[
             shape(attn_head.shape, low),
             shape((half, width_all), low),
@@ -1301,12 +1487,12 @@
             shape((2, RANK, hidden), wide),
             shape((RANK, hidden), wide),
         ],
-        in_specs=[VM, any_space, any_space, VM, any_space, any_space, any_space] + [VM] * 6,
+        in_specs=[VM, any_space, any_space, VM, any_space, any_space, any_space] + [VM] * 4,
         out_specs=[VM] * 7,
         scratch_shapes=[
             pltpu.VMEM(w_out.shape, low),
-            pltpu.VMEM(w_gu.shape, low),
-            pltpu.VMEM(w_down.shape, low),
+            pltpu.VMEM((w_gu.shape[0] * nr, w_gu.shape[1]), low),
+            pltpu.VMEM((w_down.shape[0] * nr, w_down.shape[1]), low),
             pltpu.VMEM((half, width_all), low),
             pltpu.VMEM((half, width_all), low),
             pltpu.VMEM((half, width_all), wide),
@@ -1326,11 +1512,11 @@
             pltpu.VMEM((band, RANK), low),
             dma((3, 4, chunks)), dma((3, 4, chunks)),
             dma((nr - 1, n)), dma((nr - 1, n)), dma((nr - 1, n)), dma((nr - 1, n)), dma((n,)), dma((n,)),
-            dma((4,)), dma((8,)),
-        ],
+            dma((3,)),
+        ] + share_sems(cuts) + share_sems(cuts // 2),
         compiler_params=pltpu.CompilerParams(collective_id=0, has_side_effects=True, vmem_limit_bytes=67043328),
         name="middle",
-    )(attn_head, x, cot_half, gains, w_out, w_gu, w_down, a_out, b_out, a_gu, b_gu, a_down, b_down)
+    )(attn_head, x, cot_half, gains, w_out, w_gu, w_down, table, a_out, b_gu, a_down)
 
 
 def per_device(
@@ -1372,45 +1558,18 @@
     heads_col = width_col // HEAD
     tree_set = tree_sets[0]
 
-    def pick(table, axis):
-        return lax.dynamic_index_in_dim(table, tree_set, axis, keepdims=False)
-
-    narrow = jnp.concatenate(
-        [
-            pick(query_key_value_adapter_first, 1),
-            pick(gate_up_adapter_first, 1),
-            pick(output_adapter_second, 0)[None],
-            pick(down_adapter_second, 0)[None],
-        ],
-        axis=0,
-    ).astype(low)
+    tables = (
+        query_key_value_adapter_first,
+        query_key_value_adapter_second,
+        output_adapter_first,
+        output_adapter_second,
+        gate_up_adapter_first,
+        gate_up_adapter_second,
+        down_adapter_first,
+        down_adapter_second,
+    )
+    narrow, b_qkv, a_out, b_gu, a_down = prep(tree_sets, tables)
     gain_pair = jnp.pad(jnp.stack([gain_attn, gain_ffn]), ((0, 6), (0, 0)))
-    x, table, gains = enter(tokens, narrow.reshape(7 * RANK, width_row), gain_pair, col_count, row_count)
-    a_qkv = table[: 3 * RANK]
-    a_gu = table[3 * RANK : 5 * RANK]
-    b_out = table[5 * RANK : 6 * RANK]
-    b_down = table[6 * RANK :]
-    b_qkv = pick(query_key_value_adapter_second, 1).astype(low)
-    b_gu = pick(gate_up_adapter_second, 1).astype(low)
-    a_out = pick(output_adapter_first, 0).astype(low)
-    a_down = pick(down_adapter_first, 0).astype(low)
-
-    def gather_rows(weight, stacked):
-        share = weight.shape[0] // dp_count
-        mine = lax.dynamic_slice_in_dim(weight, lax.axis_index("dp") * share, share, 0)
-        return lax.all_gather(mine, ("row", "dp"), axis=0, tiled=not stacked)
-
-    w_qkv = gather_rows(query_key_value_weight.reshape(width_row, 3 * width_col), False)
-    w_gu = gather_rows(gate_up_weight.reshape(width_row, 2 * hidden_col), False)
-    w_down = gather_rows(down_weight, True).reshape(row_count, hidden_col, width_row)
-    w_out = gather_rows(output_weight, True).reshape(row_count, width_col, width_row)
-
-    first = lax.axis_index("col") == 0
-    final = lax.axis_index("col") == col_count - 1
-    red_qkv = dot_t(x, a_qkv).astype(low)
-    raw = dot(x, w_qkv)
-    extra = jnp.concatenate([dot(red_qkv[:, RANK * j : RANK * (j + 1)], b_qkv[j]) for j in range(3)], axis=1)
-    raw = raw + extra
     pos_own = lax.dynamic_index_in_dim(
         positions.reshape(col_count, row_count, own), row_at, 1, keepdims=False
     ).reshape(group)
@@ -1418,23 +1577,49 @@
     cos2 = jnp.concatenate([cosine, cosine], axis=1)
     sin2 = jnp.concatenate([-sine, sine], axis=1)
     gq, gk = gain_q[None, :], gain_k[None, :]
-    qkv_head, factors, g_half = to_heads_call(raw, gq, gk, cos2, sin2, cotangent, col_count, row_count)
     parent_at, branch_flag = tree_tables(seg_ids, parents)
-    pos_down, pos_across = positions[:, None], positions[None, :]
-    attn_head, lse = attend(qkv_head, parent_at, branch_flag, pos_down, pos_across)
+    first = lax.axis_index("col") == 0
+    final = lax.axis_index("col") == col_count - 1
+    x, table, gains, g_half, raw, factors, qkv_head, w_qkv, w_out = front(
+        tokens,
+        narrow,
+        gain_pair,
+        cotangent,
+        query_key_value_weight.reshape(width_row, 3 * width_col),
+        output_weight,
+        b_qkv,
+        gq,
+        gk,
+        cos2,
+        sin2,
+        col_count,
+        row_count,
+    )
+    attn_head, lse = attend(qkv_head, parent_at, branch_flag)
+    a_qkv = table[: 3 * RANK]
     d_attn_head, out_half, d_h_half, full_mid, part_ao, part_bgu, part_ad = middle(
-        attn_head, x, g_half, gains, w_out, w_gu, w_down, a_out, b_out, a_gu, b_gu, a_down, b_down, col_count, row_count
+        attn_head,
+        x,
+        g_half,
+        gains,
+        w_out,
+        gate_up_weight.reshape(width_row, 2 * hidden_col),
+        down_weight,
+        table,
+        a_out,
+        b_gu,
+        a_down,
+        col_count,
+        row_count,
     )
-    d_qkv_head = attend_back(
-        qkv_head, d_attn_head, parent_at, branch_flag, pos_down, pos_across, lse
-    )
+    d_qkv_head = attend_back(qkv_head, d_attn_head, parent_at, branch_flag, lse)
     d_raw, layer_out = from_heads_call(
         d_qkv_head, raw, factors, gq, gk, cos2, sin2, out_half, col_count, row_count
     )
     d_q, d_k, d_v = (d_raw[:, width_col * j : width_col * (j + 1)] for j in range(3))
-    back_qkv = jnp.concatenate(
-        [dot_t(d, b) for d, b in zip((d_q, d_k, d_v), (b_qkv[0], b_qkv[1], b_qkv[2]))], axis=1
-    ).astype(low)
+    b_qkv = b_qkv.reshape(3, RANK, width_col)
+    back_qkv = jnp.concatenate([dot_t(d, b) for d, b in zip((d_q, d_k, d_v), b_qkv)], axis=1).astype(low)
+    red_qkv = dot_t(x, a_qkv).astype(low)
     d_h_all = jnp.concatenate([jnp.where(first, d_h_half, 0.0), jnp.where(final, d_h_half, 0.0)], axis=0)
     part_in = (dot_t(d_raw, w_qkv) + dot(back_qkv, a_qkv) + d_h_all).astype(low)
 

time: 707 us -> 598 us (0.85)
  waiting for transfers between devices: 75.3 us -> 0 us
  matrix products: 30.8 us -> 13.7 us
  local copies, waits for them, and re-layouts: 38.2 us -> 23.2 us
  between operations: 14.9 us -> 1.8 us
  Pallas kernels: 536 us -> 546 us
    all_gather x4 -> x0, waiting for transfers between devices: 75.2 us -> none  [gather_rows(): return lax.all_gather(mine, ('row', 'dp'), axis=0, tiled=not stacked)]
    dot_general x5 -> x1, matrix products: 16.7 us -> 3.48 us  [dot(): return jnp.dot(left, right, preferred_element_type=wide)]
    pallas_call x1, Pallas kernels: 42.6 us -> 51 us  [from_heads_call(): pl.pallas_call(functools.partial(unheads_kernel, n, nr), out_shape=[jax.S...]
  transfers between devices with their start and end apart: 4 -> 0, of which waited for: 1 -> 0; matrix products, arithmetic and copies ran while one was open for 6% -> 0% of each run, Pallas kernels for 20% -> 0%
where the time goes in v5:
time: 598 us; the launch traced here: 591 us
  Pallas kernels  546 us (91%)
  local copies, waits for them, and re-layouts  23.2 us (4%)
  matrix products  13.7 us (2%)
  other arithmetic  6.65 us (1%)
    pallas_call x1, Pallas kernels, middle(): pl.pallas_call(functools.partial(middle_kernel, n, nr, m, hop, cuts), out...  282 us
    pallas_call x1, Pallas kernels, front(): pl.pallas_call(functools.partial(front_kernel, n, nr, m, mh), out_shape=[...  109 us
    pallas_call x1, Pallas kernels, finish(): pl.pallas_call(functools.partial(finish_kernel, n, nr, ndp, m), out_shape...  71 us
    pallas_call x1, Pallas kernels, from_heads_call(): pl.pallas_call(functools.partial(unheads_kernel, n, nr), out_shape=[jax.S...  51 us
    pallas_call x1, Pallas kernels, attend_back(): pl.pallas_call(attend_back_kernel, grid_spec=pltpu.PrefetchScalarGridSpec...  17.6 us
    pallas_call x1, Pallas kernels, attend(): pl.pallas_call(attend_body, grid_spec=pltpu.PrefetchScalarGridSpec(num_sc...  14.1 us
    unnamed x41, local copies, waits for them, and re-layouts  13.1 us

profile of v5, /device:TPU:0, one launch (start us, length us, event | category | flops | bytes accessed | tf_op | source)
XLA Modules:
  0.0 591.5 jit_solution(938936513734447769)
XLA Ops:
  0.7 0.8 slice.74
  1.4 0.8 select_reduce_fusion.1
  4.3 2.0 prep.1
  7.7 1.6 copy.48.wq_hbm
  9.5 1.2 fusion.12
  10.8 1.1 pad_maximum_fusion.1
  11.8 108.6 %front.1 = (bf16[640,2048]{1,0:T(8,128)(2,1)}, bf16[112,2048]{1,0:T(8,128)(2,1)}, f32[8,2048]{1,0:T(8,128)}, bf16[320,2048]{1,0:T(8,128)(2,1)}, f32[640,1536]{1,...) custom-call(bf16[640,512]{1,0:T(8,128)(2,1)} %tok_ref.1, ...), custom_call_target="tpu_custom_call" | custom-call | tf_op jit(solution)/shard_map/front/pallas_call | solution.py:997
  120.4 14.1 %attend.1 = (bf16[2560,128]{1,0:T(8,128)(2,1)}, f32[2560,1]{1,0:T(8,128)}) custom-call(s32[12]{0:T(128)} %select_reduce_fusion.parent_ref, f32[12,128]{1,0:T(8,128)} %broadcast_in_dim.65.flag_ref, bf16[2560,384]{1,0:T(8,128)(2,1)} %get-tuple-element.39.qkv), custom_call_target="tpu_custom_call" | custom-call | tf_op jit(solution)/shard_map/attend/pallas_call | solution.py:713
  134.5 6.6 %copy.57 = bf16[64,8,2,2048]{3,1,2,0:T(8,128)(2,1)} copy(bf16[64,8,2,2048]{3,2,1,0:T(2,128)(2,1)} %bitcast.47) | data formatting | bytes 8388608
  141.1 281.8 %middle.1 = (bf16[2560,128]{1,0:T(8,128)(2,1)}, bf16[320,2048]{1,0:T(8,128)(2,1)}, f32[320,2048]{1,0:T(8,128)}, f32[64,2048]{1,0:T(8,128)}, f32[16,512]{1,0:T(8,...) custom-call(bf16[2560,128]{1,0:T(8,128)(2,1)} %get-tuple-element.40.head_ref, ...), custom_call_target="tpu_custom_call" | custom-call | tf_op jit(solution)/shard_map/middle/pallas_call | solution.py:1479
  422.9 17.6 %attend_back.1.d_ref = bf16[2560,384]{1,0:T(8,128)(2,1)} custom-call(s32[12]{0:T(128)} %select_reduce_fusion.parent_ref, f32[12,128]{1,0:T(8,128)} %broadcast_in_dim.65.flag_ref, bf16[2560,384]{1,0:T(8,128)(2,1)} %get-tuple-element.39.qkv, bf16[2560,128]{1,0:T(8,128)(2,1)} %get-tuple-element.49.do_ref, f32[2560,1]{1,0:T(8,128)} %get-tuple-element.50.lse_ref), custom_call_target="tpu_custom_call" | custom-call | tf_op jit(solution)/shard_map/attend_back/pallas_call | solution.py:732
  440.5 51.0 %from_heads.1 = (bf16[640,1536]{1,0:T(8,128)(2,1)}, bf16[640,512]{1,0:T(8,128)(2,1)}) custom-call(bf16[2560,384]{1,0:T(8,128)(2,1)} %attend_back.1.d_ref, f32[640,1536]{1,0:T(8,128)} %get-tuple-element.51.raw_ref, f32[8,640]{1,0:T(8,128)} %get-tuple-element.52.factor_ref, f32[1,512]{1,0:T(1,128)} %bitcast.54, f32[1,512]{1,0:T(1,128)} %bitcast.56, ...), custom_call_target="tpu_custom_call" | custom-call | tf_op jit(solution)/shard_map/from_heads/pallas_call | solution.py:251
  492.2 0.9 copy-done.4
  493.1 6.4 %fusion.25 = f32[640,2048]{1,0:T(8,128)S(1)} fusion(bf16[640,1536]{1,0:T(8,128)(2,1)S(1)} %copy-done.4, bf16[2048,1536]{1,0:T(8,128)(2,1)} %get-tuple-element.56), kind=kOutput, calls=%fused_computation.67 | convolution fusion | flops 4026531840 | bytes 13500416 | tf_op jit(solution)/shard_map/dot_general | solution.py:34
  500.4 3.5 fusion.part_ref
  505.4 0.9 pad.9.clone
  506.2 1.9 convolution_convert_fusion.1
  508.8 0.8 convert_element_type.39.col_ref
  510.3 71.0 %finish.1 = (f32[640,512]{1,0:T(8,128)}, f32[4,96,512]{2,1,0:T(8,128)}) custom-call(bf16[640,2048]{1,0:T(8,128)(2,1)} %fusion.part_ref, bf16[128,2048]{1,0:T(8,128)(2,1)} %bitcast.48, bf16[256,512]{1,0:T(8,128)(2,1)} %convert_element_type.39.col_ref, f32[8,512]{1,0:T(8,128)} %iota.23.hot_ref), custom_call_target="tpu_custom_call" | custom-call | tf_op jit(solution)/shard_map/finish/pallas_call | solution.py:462
  581.3 1.0 slice.84
  583.2 1.2 slice.86
  588.0 0.8 pad_maximum_fusion.3
  589.4 0.8 copy.67
  590.2 1.1 copy.68
  (71 shorter events, 12.3 us)
Async XLA Ops:
  4.3 2.1 copy-start.13
  4.3 2.0 copy-start.14
  4.3 2.6 copy-start.2
  7.0 2.3 copy-start.12
  440.5 51.1 %copy-start.1 = (f32[320,2048]{1,0:T(8,128)S(1)}, f32[320,2048]{1,0:T(8,128)}, u32[]{:S(2)}) copy-start(f32[320,2048]{1,0:T(8,128)} %get-tuple-element.57) | copy-start | bytes 7864324
  491.6 1.5 copy-start.4
  493.1 6.4 %copy-start.10 = (bf16[48,512]{1,0:T(8,128)(2,1)S(1)}, bf16[48,512]{1,0:T(8,128)(2,1)}, u32[]{:S(2)}) copy-start(bf16[48,512]{1,0:T(8,128)(2,1)} %get-tuple-element.38.bq_ref) | copy-start | bytes 147460
  500.4 3.5 copy-start.7
  500.4 3.5 copy-start
  505.4 2.7 copy-start.5
  506.2 2.5 copy-start.11
  506.2 2.5 copy-start.8
  506.2 2.6 copy-start.9
  582.3 7.1 %copy-start.6 = (bf16[640,512]{1,0:T(8,128)(2,1)S(1)}, bf16[640,512]{1,0:T(8,128)(2,1)}, u32[]{:S(2)}) copy-start(bf16[640,512]{1,0:T(8,128)(2,1)} %get-tuple-element.110) | copy-start | bytes 1966084
  583.2 7.0 %copy-start.3 = (f32[640,512]{1,0:T(8,128)S(1)}, f32[640,512]{1,0:T(8,128)}, u32[]{:S(2)}) copy-start(f32[640,512]{1,0:T(8,128)} %get-tuple-element.111) | copy-start | bytes 3932164

commit v6 on v5

--- a/solution.py
+++ b/solution.py
@@ -100,390 +100,6 @@
 def down_columns(values, at):
     pick = (lax.broadcasted_iota(jnp.int32, (8, HEAD), 0) == at).astype(wide)
     return lax.dot_general(values, pick, first_first, preferred_element_type=wide, precision=precise)
-
-
-def swap_stats(stats, n, send_sem, recv_sem):
-    c = lax.axis_index("col")
-
-    def copy(d):
-        peer = lax.rem(c + d, n)
-        return remote(stats.at[c], stats.at[c], send_sem.at[d - 1], recv_sem.at[d - 1], {"col": peer})
-
-    for d in range(1, n):
-        copy(d).start()
-    for d in range(1, n):
-        copy(d).wait()
-
-
-def unheads_kernel(n, nr, d_ref, raw_ref, factor_ref, gq_ref, gk_ref, cos_ref, sin_ref, res_ref, out_ref, res_out,
-                   stats, buf, nq, nk, pq, pk, fq, fk, send_s, recv_s, send_h, recv_h, send_o, recv_o, local_sem, local_o):
-    r, c = lax.axis_index("row"), lax.axis_index("col")
-    rows_all = raw_ref.shape[0]
-    own = rows_all // n
-    width = gq_ref.shape[1]
-    heads = width // HEAD
-    tree_part = own * nr
-    middle = n // 2
-    out_width = res_out.shape[1]
-
-    def piece(d, b):
-        peer = lax.rem(r + d, nr)
-        return remote(
-            d_ref.at[span(b * tree_part + peer * own, own)],
-            buf.at[r, span(b * own, own)],
-            send_h.at[d - 1, b], recv_h.at[d - 1, b], {"row": peer},
-        )
-
-    def local(b):
-        return pltpu.make_async_copy(
-            d_ref.at[span(b * tree_part + r * own, own)], buf.at[r, span(b * own, own)], local_sem.at[b]
-        )
-
-    is_owner = jnp.logical_or(c == 0, c == n - 1)
-    base = jnp.where(c == 0, 0, middle)
-
-    def result_piece(b, d):
-        peer = lax.rem(r + d, nr)
-        return remote(
-            res_ref.at[span(b * own, own), span(peer * out_width, out_width)],
-            res_out.at[span(r * own, own)],
-            send_o.at[b, d], recv_o.at[d], {"row": peer, "col": base + b},
-        )
-
-    def result_local(b):
-        return pltpu.make_async_copy(
-            res_ref.at[span(b * own, own), span(r * out_width, out_width)], res_out.at[span(r * own, own)], local_o
-        )
-
-    for b in range(n):
-        local(b).start()
-    greet(n, nr)
-    for b in range(n):
-        for d in range(1, nr):
-            piece(d, b).start()
-
-    @pl.when(is_owner)
-    def _():
-        for b in range(middle):
-            for d in range(nr):
-                if d == 0:
-                    @pl.when(base + b == c)
-                    def _():
-                        result_local(b).start()
-
-                    @pl.when(base + b != c)
-                    def _():
-                        result_piece(b, d).start()
-                else:
-                    result_piece(b, d).start()
-
-    fq[...] = down_columns(factor_ref[...], 0)
-    fk[...] = down_columns(factor_ref[...], 4)
-    for b in range(n):
-        for d in range(1, nr):
-            piece(d, b).wait_recv()
-        local(b).wait()
-        rows = slice(b * own, (b + 1) * own)
-        cosine = cos_ref[rows, :]
-        sine = sin_ref[rows, :]
-        for h in range(heads):
-            lanes = slice(h * HEAD, (h + 1) * HEAD)
-            u = buf[h, rows, :HEAD].astype(wide)
-            u = (u * cosine - pltpu.roll(u, HEAD // 2, 1) * sine) * gq_ref[:, lanes]
-            nq[rows, lanes] = u
-            pq[rows, lanes] = u * raw_ref[rows, lanes] * fq[rows, :]
-            u = buf[h, rows, HEAD:2 * HEAD].astype(wide)
-            u = (u * cosine - pltpu.roll(u, HEAD // 2, 1) * sine) * gk_ref[:, lanes]
-            nk[rows, lanes] = u
-            pk[rows, lanes] = u * raw_ref[rows, slice(width + h * HEAD, width + (h + 1) * HEAD)] * fk[rows, :]
-            out_ref[rows, slice(2 * width + h * HEAD, 2 * width + (h + 1) * HEAD)] = buf[h, rows, 2 * HEAD:]
-    stats[c] = row_sums(pq[...], pk[...])
-    swap_stats(stats, n, send_s, recv_s)
-    total = stats[0]
-    for s in range(1, n):
-        total = total + stats[s]
-    mean = total * (1.0 / D) * factor_ref[...]
-    pq[:, :HEAD] = down_columns(mean, 0)
-    pk[:, :HEAD] = down_columns(mean, 4)
-    for b in range(n):
-        rows = slice(b * own, (b + 1) * own)
-        for h in range(heads):
-            lanes = slice(h * HEAD, (h + 1) * HEAD)
-            k_lanes = slice(width + h * HEAD, width + (h + 1) * HEAD)
-            out_ref[rows, lanes] = (fq[rows, :] * (nq[rows, lanes] - raw_ref[rows, lanes] * pq[rows, :HEAD])).astype(low)
-            out_ref[rows, k_lanes] = (fk[rows, :] * (nk[rows, lanes] - raw_ref[rows, k_lanes] * pk[rows, :HEAD])).astype(low)
-    for b in range(n):
-        for d in range(1, nr):
-            piece(d, b).wait_send()
-
-    @pl.when(is_owner)
-    def _():
-        for b in range(middle):
-            for d in range(nr):
-                if d == 0:
-                    @pl.when(base + b == c)
-                    def _():
-                        result_local(b).wait()
-
-                    @pl.when(base + b != c)
-                    def _():
-                        result_piece(b, d).wait_send()
-                else:
-                    result_piece(b, d).wait_send()
-
-    for d in range(nr):
-        def take():
-            remote(
-                res_ref.at[span(0, own), span(0, out_width)], res_out.at[span(r * own, own)],
-                send_o.at[0, d], recv_o.at[d], {"row": r, "col": c},
-            ).wait_recv()
-        if d == 0:
-            pl.when(jnp.logical_not(is_owner))(take)
-        else:
-            take()
-
-
-def from_heads_call(d_head, raw, factor, gain_q, gain_k, cos2, sin2, result, n, nr):
-    rows_all, wide3 = raw.shape
-    width = wide3 // 3
-    dma = pltpu.SemaphoreType.DMA
-    square = pltpu.VMEM((rows_all, width), wide)
-    return pl.pallas_call(
-        functools.partial(unheads_kernel, n, nr),
-        out_shape=[
-            jax.ShapeDtypeStruct((rows_all, wide3), low),
-            jax.ShapeDtypeStruct((rows_all // n * nr, result.shape[1] // nr), low),
-        ],
-        in_specs=[VM] * 8,
-        out_specs=[VM] * 2,
-        scratch_shapes=[
-            pltpu.VMEM((n, 8, rows_all), wide),
-            pltpu.VMEM((nr, rows_all, 3 * HEAD), low),
-            square, square, square, square,
-            pltpu.VMEM((rows_all, HEAD), wide),
-            pltpu.VMEM((rows_all, HEAD), wide),
-            dma((n - 1,)), dma((n - 1,)), dma((nr - 1, n)), dma((nr - 1, n)),
-            dma((n // 2, nr)), dma((nr,)), dma((n,)), dma,
-        ],
-        compiler_params=params(5),
-        name="from_heads",
-    )(d_head, raw, factor, gain_q, gain_k, cos2, sin2, result)
-
-
-def finish_kernel(n, nr, ndp, m, part_ref, full_ref, col_ref, hot_ref, grad_ref, sets_ref,
-                  recv_right, recv_left, send_right, send_left, own_buf, in_buf, full_recv, full_sum, full_last,
-                  col_recv, owned, hot_all,
-                  send_z, recv_z, send_w, recv_w, local_w, send_f, recv_f, send_c, recv_c, send_l, recv_l,
-                  send_d, recv_d, send_k, recv_k):
-    g, r, c = lax.axis_index("dp"), lax.axis_index("row"), lax.axis_index("col")
-    own = part_ref.shape[0] // n
-    width = in_buf.shape[1]
-    chunks = own // m
-    left = {"col": jnp.maximum(c - 1, 0)}
-    right = {"col": jnp.minimum(c + 1, n - 1)}
-    full_rows = full_last.shape[1]
-    col_rows = col_recv.shape[1]
-
-    def full_piece(d):
-        peer = lax.rem(r + d, nr)
-        return remote(full_ref.at[:, span(peer * width, width)], full_recv.at[r], send_f.at[d - 1], recv_f.at[d - 1], {"row": peer})
-
-    def col_piece(d):
-        peer = lax.rem(r + d, nr)
-        return remote(col_ref.at[span(peer * col_rows, col_rows)], col_recv.at[r], send_c.at[d - 1], recv_c.at[d - 1], {"row": peer})
-
-    def last_piece(d):
-        peer = lax.rem(c + d, n)
-        return remote(full_sum.at[span(peer * full_rows, full_rows)], full_last.at[c], send_l.at[d - 1], recv_l.at[d - 1], {"col": peer})
-
-    def tree_piece(d):
-        peer = lax.rem(g + d, ndp)
-        return remote(owned.at[g], owned.at[g], send_d.at[d - 1], recv_d.at[d - 1], {"dp": peer})
-
-    def hot_piece(d):
-        peer = lax.rem(g + d, ndp)
-        return remote(hot_all.at[g], hot_all.at[g], send_k.at[d - 1], recv_k.at[d - 1], {"dp": peer})
-
-    def reduce(kind, b, j, src):
-        rows = span(b * own + j * m, m)
-        dst, to = ((recv_right, right), (recv_left, left))[kind]
-        return remote(src.at[rows], dst.at[rows], send_z.at[kind, b, j], recv_z.at[kind, b, j], to)
-
-    def width_piece(d, j):
-        peer = lax.rem(r + d, nr)
-        return remote(
-            own_buf.at[span(j * m, m), span(peer * width, width)], in_buf.at[span(r * own + j * m, m)],
-            send_w.at[d - 1, j], recv_w.at[d - 1, j], {"row": peer},
-        )
-
-    def width_local(j):
-        return pltpu.make_async_copy(
-            own_buf.at[span(j * m, m), span(r * width, width)], in_buf.at[span(r * own + j * m, m)], local_w.at[j]
-        )
-
-    me = r * n + c
-    barrier = pltpu.get_barrier_semaphore()
-    for d in range(1, ndp):
-        pl.semaphore_signal(barrier, inc=1, device_id={"dp": lax.rem(g + d, ndp)}, device_id_type=MESH)
-
-    @pl.loop(1, n * nr)
-    def _(d):
-        peer = lax.rem(me + d, n * nr)
-        pl.semaphore_signal(barrier, inc=1, device_id={"row": peer // n, "col": lax.rem(peer, n)}, device_id_type=MESH)
-
-    pl.semaphore_wait(barrier, n * nr - 1 + ndp - 1)
-    hot_all[g] = hot_ref[...]
-    for d in range(1, nr):
-        full_piece(d).start()
-        col_piece(d).start()
-
-    def stage(s):
-        @pl.loop(0, chunks)
-        def _(j):
-            for kind, b, go, edge, acc, got in (
-                (0, n - 1 - s, n - 1 - s > c, c == 0, send_right, recv_right),
-                (1, s, s < c, c == n - 1, send_left, recv_left),
-            ):
-                @pl.when(go)
-                def _():
-                    @pl.when(edge)
-                    def _():
-                        reduce(kind, b, j, part_ref).start()
-
-                    @pl.when(jnp.logical_not(edge))
-                    def _():
-                        rows = span(b * own + j * m, m)
-                        reduce(kind, b, j, acc).wait_recv()
-                        acc[rows, :] = (part_ref[rows, :].astype(wide) + got[rows, :].astype(wide)).astype(low)
-                        reduce(kind, b, j, acc).start()
-
-    stage(0)
-    for d in range(1, nr):
-        full_piece(d).wait_recv()
-        col_piece(d).wait_recv()
-    total = full_ref[:, span(r * width, width)].astype(wide)
-    col_total = col_ref[span(r * col_rows, col_rows), :].astype(wide)
-    for d in range(1, nr):
-        peer = lax.rem(r + d, nr)
-        total = total + full_recv[peer].astype(wide)
-        col_total = col_total + col_recv[peer].astype(wide)
-    full_sum[...] = total.astype(low)
-    owned[g, full_rows:, :] = col_total.astype(low)
-    for d in range(1, n):
-        last_piece(d).start()
-    stage(1)
-    for d in range(1, n):
-        last_piece(d).wait_recv()
-    last = full_sum[span(c * full_rows, full_rows), :].astype(wide)
-    for d in range(1, n):
-        last = last + full_last[lax.rem(c + d, n)].astype(wide)
-    owned[g, :full_rows, :] = last.astype(low)
-    for d in range(1, ndp):
-        tree_piece(d).start()
-        hot_piece(d).start()
-    for s in range(2, n - 1):
-        stage(s)
-
-    rows_own = c * own
-
-    @pl.loop(0, chunks)
-    def _(j):
-        rows = span(rows_own + j * m, m)
-        at = span(j * m, m)
-
-        @pl.when(c == 0)
-        def _():
-            reduce(1, c, j, send_left).wait_recv()
-            own_buf[at, :] = (part_ref[rows, :].astype(wide) + recv_left[rows, :].astype(wide)).astype(low)
-
-        @pl.when(c == n - 1)
-        def _():
-            reduce(0, c, j, send_right).wait_recv()
-            own_buf[at, :] = (part_ref[rows, :].astype(wide) + recv_right[rows, :].astype(wide)).astype(low)
-
-        @pl.when(jnp.logical_and(c > 0, c < n - 1))
-        def _():
-            reduce(0, c, j, send_right).wait_recv()
-            reduce(1, c, j, send_left).wait_recv()
-            own_buf[at, :] = (
-                part_ref[rows, :].astype(wide) + recv_right[rows, :].astype(wide) + recv_left[rows, :].astype(wide)
-            ).astype(low)
-
-        for d in range(1, nr):
-            width_piece(d, j).start()
-        width_local(j).start()
-
-    for d in range(1, ndp):
-        tree_piece(d).wait_recv()
-        hot_piece(d).wait_recv()
-    sets_own = sets_ref.shape[0]
-    for s in range(sets_own):
-        total = owned[0].astype(wide) * hot_all[0, pl.ds(g * sets_own + s, 1), :]
-        for t in range(1, ndp):
-            total = total + owned[t].astype(wide) * hot_all[t, pl.ds(g * sets_own + s, 1), :]
-        sets_ref[s] = total
-
-    @pl.loop(0, chunks)
-    def _(j):
-        for d in range(1, nr):
-            width_piece(d, j).wait()
-        width_local(j).wait()
-
-    grad_ref[...] = in_buf[...].astype(wide)
-    for d in range(1, nr):
-        full_piece(d).wait_send()
-        col_piece(d).wait_send()
-    for d in range(1, n):
-        last_piece(d).wait_send()
-    for d in range(1, ndp):
-        tree_piece(d).wait_send()
-        hot_piece(d).wait_send()
-    for s in range(n - 1):
-        @pl.loop(0, chunks)
-        def _(j):
-            @pl.when(n - 1 - s > c)
-            def _():
-                reduce(0, n - 1 - s, j, send_right).wait_send()
-
-            @pl.when(s < c)
-            def _():
-                reduce(1, s, j, send_left).wait_send()
-
-
-def finish(part, full, cols, hot, sets_own, n, nr, ndp, m=32):
-    rows_all, width_all = part.shape
-    own = rows_all // n
-    width = width_all // nr
-    chunks = own // m
-    full_rows = full.shape[0] // n
-    col_rows = cols.shape[0] // nr
-    dma = pltpu.SemaphoreType.DMA
-    big = pltpu.VMEM((rows_all, width_all), low)
-    return pl.pallas_call(
-        functools.partial(finish_kernel, n, nr, ndp, m),
-        out_shape=[
-            jax.ShapeDtypeStruct((own * nr, width), wide),
-            jax.ShapeDtypeStruct((sets_own, full_rows + col_rows, width), wide),
-        ],
-        in_specs=[VM] * 4,
-        out_specs=[VM] * 2,
-        scratch_shapes=[
-            big, big, big, big,
-            pltpu.VMEM((own, width_all), low),
-            pltpu.VMEM((own * nr, width), low),
-            pltpu.VMEM((nr, full.shape[0], width), low),
-            pltpu.VMEM((full.shape[0], width), low),
-            pltpu.VMEM((n, full_rows, width), low),
-            pltpu.VMEM((nr, col_rows, width), low),
-            pltpu.VMEM((ndp, full_rows + col_rows, width), low),
-            pltpu.VMEM((ndp,) + hot.shape, wide),
-            dma((2, n, chunks)), dma((2, n, chunks)), dma((nr - 1, chunks)), dma((nr - 1, chunks)), dma((chunks,)),
-            dma((nr - 1,)), dma((nr - 1,)), dma((nr - 1,)), dma((nr - 1,)), dma((n - 1,)), dma((n - 1,)),
-            dma((ndp - 1,)), dma((ndp - 1,)), dma((ndp - 1,)), dma((ndp - 1,)),
-        ],
-        compiler_params=params(6),
-        name="finish",
-    )(part, full, cols, hot)
 
 
 def flip(v):
@@ -746,9 +362,9 @@
 def front_kernel(n, nr, m, mh, tok_ref, table_ref, gain_ref, cot_ref, wq_hbm, wo_hbm, bq_ref, gq_ref, gk_ref,
                  cos_ref, sin_ref,
                  x_ref, table_all, gain_all, half_ref, raw_ref, factor_ref, qkv_ref, wq_out, wo_out,
-                 wq, wo, stats, buf, fq, fk,
+                 wq, wo, stats, buf, fq, fk, red, cot_own,
                  send_a, recv_a, send_z, recv_z, send_t, recv_t, local_sem,
-                 send_s, recv_s, send_h, recv_h, send_g, recv_g, local_h, local_g,
+                 send_s, recv_s, send_h, recv_h, send_g, recv_g, local_h, local_g, send_e, recv_e,
                  send_q, recv_q, local_q, send_o, recv_o, local_o, out_sems):
     g, r, c = lax.axis_index("dp"), lax.axis_index("row"), lax.axis_index("col")
     own = tok_ref.shape[0] // nr
@@ -796,6 +412,23 @@
         for d in range(1, nr):
             piece(d, j).start()
 
+    middle_at = n // 2
+    owner = jnp.where(c < middle_at, 0, n - 1)
+    at_owner = jnp.where(c < middle_at, c, c - middle_at)
+    is_owner = owner == c
+
+    def cot_piece(d):
+        peer = lax.rem(r + d, nr)
+        return remote(
+            cot_ref.at[span(peer * own, own)], cot_own.at[:, span(r * width, width)], send_g.at[d - 1], recv_g.at[d - 1], {"row": peer}
+        )
+
+    cot_local = pltpu.make_async_copy(cot_ref.at[span(r * own, own)], cot_own.at[:, span(r * width, width)], local_g.at[0])
+    cot_keep = pltpu.make_async_copy(cot_own, half_ref.at[span(at_owner * own, own)], local_g.at[1])
+
+    def cot_move(b):
+        return remote(cot_own, half_ref.at[span(b * own, own)], send_e, recv_e.at[b], {"col": owner})
+
     share_q.start_far()
     share_q.start_near()
     for d in range(1, nr):
@@ -803,7 +436,114 @@
         table_piece(d, 1).start()
     share_o.start_far()
     share_o.start_near()
+    cot_local.start()
+    for d in range(1, nr):
+        cot_piece(d).start()
     keep.wait()
+
+    def head_rows(i):
+        block_at = i // (own // mh)
+        inside = lax.rem(i, own // mh)
+        return span(block_at * tree_part + r * own + inside * mh, mh)
+
+    def head_piece(d, i):
+        peer = lax.rem(r + d, nr)
+        return remote(
+            buf.at[peer, span(i * mh, mh)], qkv_ref.at[head_rows(i)], send_h.at[d - 1, i], recv_h.at[d - 1, i], {"row": peer}
+        )
+
+    def head_local(i):
+        return pltpu.make_async_copy(buf.at[r, span(i * mh, mh)], qkv_ref.at[head_rows(i)], local_h.at[i])
+
+    def stat_copy(b, d):
+        peer = lax.rem(c + d, n)
+        return remote(stats.at[c, b], stats.at[c, b], send_s.at[b, d - 1], recv_s.at[b, d - 1], {"col": peer})
+
+    def product_block(b):
+        rows = span(b * own, own)
+        x_rows = x_ref[rows, :]
+        red[...] = dot_t(x_rows, table_all[:3 * RANK, :]).astype(low)
+        for j in range(3):
+            lanes = slice(j * width, (j + 1) * width)
+            raw_ref[rows, lanes] = dot(x_rows, wq[:, lanes]) + dot(
+                red[:, j * RANK:(j + 1) * RANK], bq_ref[j * RANK:(j + 1) * RANK, :]
+            )
+        q_rows = raw_ref[rows, :width]
+        k_rows = raw_ref[rows, width:2 * width]
+        stats[c, b] = row_sums(q_rows * q_rows, k_rows * k_rows)
+        for d in range(1, n):
+            stat_copy(b, d).start()
+
+    per = own // mh
+
+    def head_block(b):
+        for d in range(1, n):
+            stat_copy(b, d).wait()
+        total = stats[0, b]
+        for s in range(1, n):
+            total = total + stats[s, b]
+        factor = lax.rsqrt(total * (1.0 / D) + epsilon)
+        factor_ref[b] = factor
+        fq[...] = down_columns(factor, 0)
+        fk[...] = down_columns(factor, 4)
+
+        @pl.loop(0, per)
+        def _(i):
+            rows = span(b * own + i * mh, mh)
+            inside = span(i * mh, mh)
+            cosine = cos_ref[rows, :]
+            sine = sin_ref[rows, :]
+            for h in range(heads):
+                lanes = slice(h * HEAD, (h + 1) * HEAD)
+                u = raw_ref[rows, lanes] * fq[inside, :] * gq_ref[:, lanes]
+                buf[h, rows, :HEAD] = (u * cosine + pltpu.roll(u, HEAD // 2, 1) * sine).astype(low)
+                k_lanes = slice(width + h * HEAD, width + (h + 1) * HEAD)
+                u = raw_ref[rows, k_lanes] * fk[inside, :] * gk_ref[:, lanes]
+                buf[h, rows, HEAD:2 * HEAD] = (u * cosine + pltpu.roll(u, HEAD // 2, 1) * sine).astype(low)
+                v_lanes = slice(2 * width + h * HEAD, 2 * width + (h + 1) * HEAD)
+                buf[h, rows, 2 * HEAD:] = raw_ref[rows, v_lanes].astype(low)
+            for d in range(1, nr):
+                head_piece(d, b * per + i).start()
+            head_local(b * per + i).start()
+
+    def early():
+        for d in range(1, nr):
+            table_piece(d, 0).wait_recv()
+            table_piece(d, 1).wait_recv()
+        keep_table.wait()
+        keep_gain.wait()
+        share_q.wait_all()
+        copy_wq.start()
+
+        @pl.loop(1, n - 1)
+        def _(b):
+            product_block(b)
+
+        @pl.when(jnp.logical_not(is_owner))
+        def _():
+            cot_move(at_owner).start()
+
+        @pl.when(is_owner)
+        def _():
+            cot_keep.start()
+
+        @pl.loop(1, n - 1)
+        def _(b):
+            head_block(b)
+
+    def late():
+        @pl.loop(0, 2)
+        def _(i):
+            product_block(i * (n - 1))
+
+        for i in range(2):
+            share_o.pass_twin(i)
+
+        @pl.loop(0, 2)
+        def _(i):
+            head_block(i * (n - 1))
+
+    copy_wq = pltpu.make_async_copy(wq, wq_out, out_sems.at[0])
 
     for s in range(n):
         @pl.loop(0, chunks)
@@ -833,102 +573,17 @@
         if s == 1:
             for i in range(2):
                 share_q.pass_far(i)
-        if s == 2:
+        if s == n - 2:
             for i in range(2):
                 share_o.pass_far(i)
                 share_q.pass_twin(i)
-    for i in range(2):
-        share_o.pass_twin(i)
-
-    for d in range(1, nr):
-        table_piece(d, 0).wait_recv()
-        table_piece(d, 1).wait_recv()
-    keep_table.wait()
-    keep_gain.wait()
-    share_q.wait_all()
-    copy_wq = pltpu.make_async_copy(wq, wq_out, out_sems.at[0])
-    copy_wq.start()
-
-    red = dot_t(x_ref[...], table_all[:3 * RANK, :]).astype(low)
-    for j in range(3):
-        lanes = slice(j * width, (j + 1) * width)
-        raw_ref[:, lanes] = dot(x_ref[...], wq[:, lanes]) + dot(
-            red[:, j * RANK:(j + 1) * RANK], bq_ref[j * RANK:(j + 1) * RANK, :]
-        )
-    q_all = raw_ref[:, :width]
-    k_all = raw_ref[:, width:2 * width]
-    stats[c] = row_sums(q_all * q_all, k_all * k_all)
-
-    middle_at = n // 2
-    owner = jnp.where(c < middle_at, 0, n - 1)
-    at_owner = jnp.where(c < middle_at, c, c - middle_at)
-
-    def cot_piece(d):
-        peer = lax.rem(r + d, nr)
-        return remote(
-            cot_ref.at[span(peer * own, own)],
-            half_ref.at[span(at_owner * own, own), span(r * width, width)],
-            send_g.at[d], recv_g.at[at_owner, d], {"row": peer, "col": owner},
-        )
-
-    def cot_local():
-        return pltpu.make_async_copy(
-            cot_ref.at[span(r * own, own)], half_ref.at[span(at_owner * own, own), span(r * width, width)], local_g
-        )
-
-    swap_stats(stats, n, send_s, recv_s)
-    total = stats[0]
-    for s in range(1, n):
-        total = total + stats[s]
-    factor = lax.rsqrt(total * (1.0 / D) + epsilon)
-    factor_ref[...] = factor
-    fq[...] = down_columns(factor, 0)
-    fk[...] = down_columns(factor, 4)
-
-    def head_rows(i):
-        block_at = i // (own // mh)
-        inside = lax.rem(i, own // mh)
-        return span(block_at * tree_part + r * own + inside * mh, mh)
-
-    def head_piece(d, i):
-        peer = lax.rem(r + d, nr)
-        return remote(
-            buf.at[peer, span(i * mh, mh)], qkv_ref.at[head_rows(i)], send_h.at[d - 1, i], recv_h.at[d - 1, i], {"row": peer}
-        )
-
-    def head_local(i):
-        return pltpu.make_async_copy(buf.at[r, span(i * mh, mh)], qkv_ref.at[head_rows(i)], local_h.at[i])
-
+            cot_local.wait()
+            for d in range(1, nr):
+                cot_piece(d).wait_recv()
+            early()
+        if s == n - 1:
+            late()
     steps = rows_all // mh
-
-    @pl.loop(0, steps)
-    def _(i):
-        rows = span(i * mh, mh)
-        cosine = cos_ref[rows, :]
-        sine = sin_ref[rows, :]
-        for h in range(heads):
-            lanes = slice(h * HEAD, (h + 1) * HEAD)
-            u = raw_ref[rows, lanes] * fq[rows, :] * gq_ref[:, lanes]
-            buf[h, rows, :HEAD] = (u * cosine + pltpu.roll(u, HEAD // 2, 1) * sine).astype(low)
-            k_lanes = slice(width + h * HEAD, width + (h + 1) * HEAD)
-            u = raw_ref[rows, k_lanes] * fk[rows, :] * gk_ref[:, lanes]
-            buf[h, rows, HEAD:2 * HEAD] = (u * cosine + pltpu.roll(u, HEAD // 2, 1) * sine).astype(low)
-            v_lanes = slice(2 * width + h * HEAD, 2 * width + (h + 1) * HEAD)
-            buf[h, rows, 2 * HEAD:] = raw_ref[rows, v_lanes].astype(low)
-        for d in range(1, nr):
-            head_piece(d, i).start()
-        head_local(i).start()
-
-    for d in range(1, nr):
-        cot_piece(d).start()
-
-    @pl.when(owner == c)
-    def _():
-        cot_local().start()
-
-    @pl.when(owner != c)
-    def _():
-        cot_piece(0).start()
 
     share_o.wait_all()
     copy_wo = pltpu.make_async_copy(wo, wo_out, out_sems.at[1])
@@ -943,24 +598,17 @@
     for d in range(1, nr):
         cot_piece(d).wait_send()
 
-    @pl.when(owner != c)
+    @pl.when(jnp.logical_not(is_owner))
     def _():
-        cot_piece(0).wait_send()
-
-    @pl.when(owner == c)
+        cot_move(at_owner).wait_send()
+
+    @pl.when(is_owner)
     def _():
-        cot_local().wait()
+        cot_keep.wait()
         for b in range(middle_at):
-            for d in range(nr):
-                def take():
-                    remote(
-                        cot_ref.at[span(0, own)], half_ref.at[span(b * own, own), span(0, width)],
-                        send_g.at[d], recv_g.at[b, d], {"row": flip(r)},
-                    ).wait_recv()
-                if d == 0:
-                    pl.when(b != at_owner)(take)
-                else:
-                    take()
+            @pl.when(b != at_owner)
+            def _():
+                remote(cot_own, half_ref.at[span(b * own, own)], send_e, recv_e.at[b], {"row": flip(r)}).wait_recv()
 
     @pl.loop(0, chunks)
     def _(j):
@@ -1002,7 +650,7 @@
             shape((gain.shape[0], width * nr), wide),
             shape((rows_all // 2, width * nr), low),
             shape((rows_all, 3 * width), wide),
-            shape((8, rows_all), wide),
+            shape((n, 8, own), wide),
             shape((tree, 3 * HEAD), low),
             shape((w_qkv.shape[0] * nr, w_qkv.shape[1]), low),
             shape((w_out.shape[0] * nr, w_out.shape[1]), low),
@@ -1012,18 +660,470 @@
         scratch_shapes=[
             pltpu.VMEM((w_qkv.shape[0] * nr, w_qkv.shape[1]), low),
             pltpu.VMEM((w_out.shape[0] * nr, w_out.shape[1]), low),
-            pltpu.VMEM((n, 8, rows_all), wide),
+            pltpu.VMEM((n, n, 8, own), wide),
             pltpu.VMEM((width // HEAD, rows_all, 3 * HEAD), low),
-            pltpu.VMEM((rows_all, HEAD), wide),
-            pltpu.VMEM((rows_all, HEAD), wide),
+            pltpu.VMEM((own, HEAD), wide),
+            pltpu.VMEM((own, HEAD), wide),
+            pltpu.VMEM((own, 3 * RANK), low),
+            pltpu.VMEM((own, width * nr), low),
             dma((nr - 1, chunks)), dma((nr - 1, chunks)), dma((2, n - 1, chunks)), dma((2, n - 1, chunks)),
             dma((2, nr - 1)), dma((2, nr - 1)), dma((3,)),
-            dma((n - 1,)), dma((n - 1,)), dma((nr - 1, steps)), dma((nr - 1, steps)),
-            dma((nr,)), dma((n // 2, nr)), dma((steps,)), dma,
+            dma((n, n - 1)), dma((n, n - 1)), dma((nr - 1, steps)), dma((nr - 1, steps)),
+            dma((nr - 1,)), dma((nr - 1,)), dma((steps,)), dma((2,)), dma, dma((n // 2,)),
         ] + share_sems(2) + share_sems(2) + [dma((2,))],
         compiler_params=params(3),
         name="front",
     )(tokens, table, gain, cot, w_qkv, w_out, b_qkv, gain_q, gain_k, cos2, sin2)
+
+
+def one_hot_rows(out_rows, in_rows, source):
+    at = lax.broadcasted_iota(jnp.int32, (out_rows, in_rows), 0)
+    return (lax.broadcasted_iota(jnp.int32, (out_rows, in_rows), 1) == source(at)).astype(low)
+
+
+def rear_kernel(n, nr, ndp, m, d_ref, raw_ref, factor_ref, gq_ref, gk_ref, cos_ref, sin_ref, res_ref, x_ref, wq_hbm,
+                table_ref, bq_ref, dh_ref, full_ref, co_ref, cg_ref, cd_ref, hot_ref,
+                grad_ref, layer_ref, sets_ref,
+                wq, stats, buf, nq, nk, pq, pk, fq, fk, d_raw, part, recv_right, recv_left, own_buf, layer_own,
+                back, red, full, cols, full_recv, full_sum, full_last, col_recv, owned, hot_all,
+                send_s, recv_s, send_h, recv_h, local_h, send_o, recv_o, local_o, load,
+                send_z, recv_z, send_w, recv_w, local_w, send_v, recv_v, local_v,
+                send_f, recv_f, send_c, recv_c, send_l, recv_l, send_d, recv_d, send_k, recv_k):
+    g, r, c = lax.axis_index("dp"), lax.axis_index("row"), lax.axis_index("col")
+    rows_all, width_all = part.shape
+    own = rows_all // n
+    width = gq_ref.shape[1]
+    heads = width // HEAD
+    tree_part = own * nr
+    middle_at = n // 2
+    chunks = own // m
+    left = {"col": jnp.maximum(c - 1, 0)}
+    right = {"col": jnp.minimum(c + 1, n - 1)}
+    load_w = pltpu.make_async_copy(wq_hbm, wq, load)
+    load_w.start()
+
+    def piece(d, b):
+        peer = lax.rem(r + d, nr)
+        return remote(
+            d_ref.at[span(b * tree_part + peer * own, own)], buf.at[r, span(b * own, own)],
+            send_h.at[d - 1, b], recv_h.at[d - 1, b], {"row": peer},
+        )
+
+    def local(b):
+        return pltpu.make_async_copy(
+            d_ref.at[span(b * tree_part + r * own, own)], buf.at[r, span(b * own, own)], local_h.at[b]
+        )
+
+    is_owner = jnp.logical_or(c == 0, c == n - 1)
+    base = jnp.where(c == 0, 0, middle_at)
+
+    def result_piece(b):
+        return remote(res_ref.at[span(b * own, own)], layer_own, send_o.at[b], recv_o, {"col": base + b})
+
+    def result_local(b):
+        return pltpu.make_async_copy(res_ref.at[span(b * own, own)], layer_own, local_o)
+
+    def width_piece(src, dst, send_sem, recv_sem, d, j, size):
+        peer = lax.rem(r + d, nr)
+        return remote(
+            src.at[span(j * size, size), span(peer * width, width)], dst.at[span(r * own + j * size, size)],
+            send_sem.at[d - 1, j], recv_sem.at[d - 1, j], {"row": peer},
+        )
+
+    def width_local(src, dst, sem, j, size):
+        return pltpu.make_async_copy(
+            src.at[span(j * size, size), span(r * width, width)], dst.at[span(r * own + j * size, size)], sem.at[j]
+        )
+
+    for b in range(n):
+        local(b).start()
+    me = r * n + c
+    barrier = pltpu.get_barrier_semaphore()
+    for d in range(1, ndp):
+        pl.semaphore_signal(barrier, inc=1, device_id={"dp": lax.rem(g + d, ndp)}, device_id_type=MESH)
+    greet(n, nr, ndp - 1)
+    for b in (0, n - 1) + tuple(range(1, n - 1)):
+        for d in range(1, nr):
+            piece(d, b).start()
+
+    @pl.when(is_owner)
+    def _():
+        for b in range(middle_at):
+            @pl.when(base + b == c)
+            def _():
+                result_local(b).start()
+
+            @pl.when(base + b != c)
+            def _():
+                result_piece(b).start()
+
+    hot_all[g] = hot_ref[...]
+    red[...] = dot_t(x_ref[...], table_ref[:3 * RANK, :]).astype(low)
+
+    def stat_copy(b, d):
+        peer = lax.rem(c + d, n)
+        return remote(stats.at[c, b], stats.at[c, b], send_s.at[b, d - 1], recv_s.at[b, d - 1], {"col": peer})
+
+    def norm_block(b):
+        for d in range(1, nr):
+            piece(d, b).wait_recv()
+        local(b).wait()
+        rows = span(b * own, own)
+        fq[rows, :] = down_columns(factor_ref[b], 0)
+        fk[rows, :] = down_columns(factor_ref[b], 4)
+        cosine = cos_ref[rows, :]
+        sine = sin_ref[rows, :]
+        for h in range(heads):
+            lanes = slice(h * HEAD, (h + 1) * HEAD)
+            k_lanes = slice(width + h * HEAD, width + (h + 1) * HEAD)
+            v_lanes = slice(2 * width + h * HEAD, 2 * width + (h + 1) * HEAD)
+            u = buf[h, rows, :HEAD].astype(wide)
+            u = (u * cosine - pltpu.roll(u, HEAD // 2, 1) * sine) * gq_ref[:, lanes]
+            nq[rows, lanes] = u
+            pq[rows, lanes] = u * raw_ref[rows, lanes] * fq[rows, :]
+            u = buf[h, rows, HEAD:2 * HEAD].astype(wide)
+            u = (u * cosine - pltpu.roll(u, HEAD // 2, 1) * sine) * gk_ref[:, lanes]
+            nk[rows, lanes] = u
+            pk[rows, lanes] = u * raw_ref[rows, k_lanes] * fk[rows, :]
+            d_raw[rows, v_lanes] = buf[h, rows, 2 * HEAD:]
+        stats[c, b] = row_sums(pq[rows, :], pk[rows, :])
+        for d in range(1, n):
+            stat_copy(b, d).start()
+
+    def mean_block(b):
+        for d in range(1, n):
+            stat_copy(b, d).wait()
+        total = stats[0, b]
+        for s in range(1, n):
+            total = total + stats[s, b]
+        mean = total * (1.0 / D) * factor_ref[b]
+        rows = span(b * own, own)
+        pq[rows, :HEAD] = down_columns(mean, 0)
+        pk[rows, :HEAD] = down_columns(mean, 4)
+
+    def back_block(b):
+        rows = span(b * own, own)
+        for h in range(heads):
+            lanes = slice(h * HEAD, (h + 1) * HEAD)
+            k_lanes = slice(width + h * HEAD, width + (h + 1) * HEAD)
+            d_raw[rows, lanes] = (fq[rows, :] * (nq[rows, lanes] - raw_ref[rows, lanes] * pq[rows, :HEAD])).astype(low)
+            d_raw[rows, k_lanes] = (fk[rows, :] * (nk[rows, lanes] - raw_ref[rows, k_lanes] * pk[rows, :HEAD])).astype(low)
+        for j in range(3):
+            back[rows, j * RANK:(j + 1) * RANK] = dot_t(
+                d_raw[rows, j * width:(j + 1) * width], bq_ref[j * RANK:(j + 1) * RANK, :]
+            ).astype(low)
+        mine = jnp.where(b < middle_at, c == 0, c == n - 1)
+        held = span(lax.rem(b, middle_at) * own, own)
+        for k in range(width_all // width):
+            lanes = slice(k * width, (k + 1) * width)
+            value = dot_t(d_raw[rows, :], wq[lanes, :]) + dot(back[rows, :], table_ref[:3 * RANK, lanes])
+            part[rows, lanes] = (value + jnp.where(mine, dh_ref[held, lanes], 0.0)).astype(low)
+
+    def reduce(kind, b, j):
+        rows = span(b * own + j * m, m)
+        dst, to = ((recv_right, right), (recv_left, left))[kind]
+        return remote(part.at[rows], dst.at[rows], send_z.at[kind, b, j], recv_z.at[kind, b, j], to)
+
+    def stage(s, at_edge=True, inside=True):
+        @pl.loop(0, chunks)
+        def _(j):
+            for kind, b, go, edge, got in (
+                (0, n - 1 - s, n - 1 - s > c, c == 0, recv_right),
+                (1, s, s < c, c == n - 1, recv_left),
+            ):
+                if at_edge:
+                    @pl.when(jnp.logical_and(go, edge))
+                    def _():
+                        reduce(kind, b, j).start()
+
+                if inside:
+                    @pl.when(jnp.logical_and(go, jnp.logical_not(edge)))
+                    def _():
+                        rows = span(b * own + j * m, m)
+                        reduce(kind, b, j).wait_recv()
+                        part[rows, :] = (part[rows, :].astype(wide) + got[rows, :].astype(wide)).astype(low)
+                        reduce(kind, b, j).start()
+
+    def full_piece(d):
+        peer = lax.rem(r + d, nr)
+        return remote(full.at[:, span(peer * width, width)], full_recv.at[r], send_f.at[d - 1], recv_f.at[d - 1], {"row": peer})
+
+    col_rows = col_recv.shape[1]
+    full_rows = full_last.shape[1]
+
+    def col_piece(d):
+        peer = lax.rem(r + d, nr)
+        return remote(cols.at[span(peer * col_rows, col_rows)], col_recv.at[r], send_c.at[d - 1], recv_c.at[d - 1], {"row": peer})
+
+    def last_piece(d):
+        peer = lax.rem(c + d, n)
+        return remote(full_sum.at[span(peer * full_rows, full_rows)], full_last.at[c], send_l.at[d - 1], recv_l.at[d - 1], {"col": peer})
+
+    def tree_piece(d):
+        return remote(owned.at[g], owned.at[g], send_d.at[d - 1], recv_d.at[d - 1], {"dp": lax.rem(g + d, ndp)})
+
+    def hot_piece(d):
+        return remote(hot_all.at[g], hot_all.at[g], send_k.at[d - 1], recv_k.at[d - 1], {"dp": lax.rem(g + d, ndp)})
+
+    @pl.loop(0, 2)
+    def _(i):
+        norm_block(i * (n - 1))
+
+    load_w.wait()
+
+    @pl.loop(0, 2)
+    def _(i):
+        mean_block(i * (n - 1))
+        back_block(i * (n - 1))
+
+    stage(0, inside=False)
+
+    @pl.loop(1, n - 1)
+    def _(b):
+        norm_block(b)
+
+    stage(0, at_edge=False)
+
+    @pl.loop(1, n - 1)
+    def _(b):
+        mean_block(b)
+        back_block(b)
+
+    rank_own = RANK // n
+    groups = full.shape[0] // (n * rank_own) - 1
+    stacked = jnp.concatenate([t_dot(back[...], x_ref[...]), full_ref[...]], axis=0).astype(low)
+    order = one_hot_rows(
+        full.shape[0], stacked.shape[0],
+        lambda o: jnp.where(
+            lax.rem(o, full_rows) < groups * rank_own,
+            lax.rem(o, full_rows) // rank_own * RANK + o // full_rows * rank_own + lax.rem(o, rank_own), -1
+        ),
+    )
+    full[...] = dot(order, stacked).astype(low)
+    pieces = [t_dot(red[:, j * RANK:(j + 1) * RANK], d_raw[:, j * width:(j + 1) * width]) for j in range(3)]
+    pieces.append(co_ref[...])
+    for j in range(2):
+        pieces += [cg_ref[j, :, k * width:(k + 1) * width] for k in range(cg_ref.shape[2] // width)]
+    pieces += [cd_ref[:, k * width:(k + 1) * width] for k in range(cd_ref.shape[1] // width)]
+    stacked = jnp.concatenate(pieces, axis=0).astype(low)
+    rank_row = RANK // nr
+    order = one_hot_rows(
+        cols.shape[0], stacked.shape[0],
+        lambda o: lax.rem(o, col_rows) // rank_row * RANK + o // col_rows * rank_row + lax.rem(o, rank_row),
+    )
+    cols[...] = dot(order, stacked).astype(low)
+    for d in range(1, nr):
+        full_piece(d).start()
+        col_piece(d).start()
+    stage(1)
+
+    @pl.when(is_owner)
+    def _():
+        for b in range(middle_at):
+            @pl.when(base + b == c)
+            def _():
+                result_local(b).wait()
+
+            @pl.when(base + b != c)
+            def _():
+                result_piece(b).wait_send()
+
+    @pl.when(jnp.logical_not(is_owner))
+    def _():
+        remote(res_ref.at[span(0, own)], layer_own, send_o.at[0], recv_o, right).wait_recv()
+
+    for d in range(1, nr):
+        width_piece(layer_own, layer_ref, send_v, recv_v, d, 0, own).start()
+    width_local(layer_own, layer_ref, local_v, 0, own).start()
+    for d in range(1, nr):
+        full_piece(d).wait_recv()
+        col_piece(d).wait_recv()
+    total = full[:, span(r * width, width)].astype(wide)
+    col_total = cols[span(r * col_rows, col_rows), :].astype(wide)
+    for d in range(1, nr):
+        peer = lax.rem(r + d, nr)
+        total = total + full_recv[peer].astype(wide)
+        col_total = col_total + col_recv[peer].astype(wide)
+    full_sum[...] = total.astype(low)
+    owned[g, full_rows:, :] = col_total.astype(low)
+    for d in range(1, n):
+        last_piece(d).start()
+    for s in range(2, n - 1):
+        stage(s)
+    for d in range(1, n):
+        last_piece(d).wait_recv()
+    last = full_sum[span(c * full_rows, full_rows), :].astype(wide)
+    for d in range(1, n):
+        last = last + full_last[lax.rem(c + d, n)].astype(wide)
+    owned[g, :full_rows, :] = last.astype(low)
+    for d in range(1, ndp):
+        tree_piece(d).start()
+        hot_piece(d).start()
+
+    @pl.loop(0, chunks)
+    def _(j):
+        rows = span(c * own + j * m, m)
+        at = span(j * m, m)
+        own_buf[at, :] = part[rows, :]
+
+        @pl.when(c > 0)
+        def _():
+            reduce(0, c, j).wait_recv()
+            own_buf[at, :] = (own_buf[at, :].astype(wide) + recv_right[rows, :].astype(wide)).astype(low)
+
+        @pl.when(c < n - 1)
+        def _():
+            reduce(1, c, j).wait_recv()
+            own_buf[at, :] = (own_buf[at, :].astype(wide) + recv_left[rows, :].astype(wide)).astype(low)
+
+        for d in range(1, nr):
+            width_piece(own_buf, grad_ref, send_w, recv_w, d, j, m).start()
+        width_local(own_buf, grad_ref, local_w, j, m).start()
+
+    for d in range(1, ndp):
+        tree_piece(d).wait_recv()
+        hot_piece(d).wait_recv()
+    sets_own = sets_ref.shape[0]
+    for s in range(sets_own):
+        total = owned[0].astype(wide) * hot_all[0, pl.ds(g * sets_own + s, 1), :]
+        for t in range(1, ndp):
+            total = total + owned[t].astype(wide) * hot_all[t, pl.ds(g * sets_own + s, 1), :]
+        sets_ref[s] = total
+
+    @pl.loop(0, chunks)
+    def _(j):
+        for d in range(1, nr):
+            width_piece(own_buf, grad_ref, send_w, recv_w, d, j, m).wait()
+        width_local(own_buf, grad_ref, local_w, j, m).wait()
+
+    for d in range(1, nr):
+        width_piece(layer_own, layer_ref, send_v, recv_v, d, 0, own).wait()
+        full_piece(d).wait_send()
+        col_piece(d).wait_send()
+        for b in range(n):
+            piece(d, b).wait_send()
+    width_local(layer_own, layer_ref, local_v, 0, own).wait()
+    for d in range(1, n):
+        last_piece(d).wait_send()
+    for d in range(1, ndp):
+        tree_piece(d).wait_send()
+        hot_piece(d).wait_send()
+    for s in range(n - 1):
+        @pl.loop(0, chunks)
+        def _(j):
+            @pl.when(n - 1 - s > c)
+            def _():
+                reduce(0, n - 1 - s, j).wait_send()
+
+            @pl.when(s < c)
+            def _():
+                reduce(1, s, j).wait_send()
+
+
+def rear(d_head, raw, factor, gain_q, gain_k, cos2, sin2, result, x, w_qkv, table, b_qkv, d_h, full_mid, part_ao,
+         part_bgu, part_ad, hot, sets_own, n, nr, ndp, m=32):
+    rows_all, wide3 = raw.shape
+    width = wide3 // 3
+    width_all = x.shape[1]
+    own = rows_all // n
+    chunks = own // m
+    full_rows = 8 * RANK // n
+    col_blocks = 4 + 3 * part_ad.shape[1] // width
+    col_rows = col_blocks * RANK // nr
+    dma = pltpu.SemaphoreType.DMA
+    shape = jax.ShapeDtypeStruct
+    any_space = pl.BlockSpec(memory_space=pl.ANY)
+    square = pltpu.VMEM((rows_all, width), wide)
+    lane = pltpu.VMEM((rows_all, HEAD), wide)
+    big = pltpu.VMEM((rows_all, width_all), low)
+    return pl.pallas_call(
+        functools.partial(rear_kernel, n, nr, ndp, m),
+        out_shape=[
+            shape((own * nr, width), low),
+            shape((own * nr, width), low),
+            shape((sets_own, full_rows + col_rows, width), wide),
+        ],
+        in_specs=[VM] * 9 + [any_space] + [VM] * 8,
+        out_specs=[VM] * 3,
+        scratch_shapes=[
+            pltpu.VMEM(w_qkv.shape, low),
+            pltpu.VMEM((n, n, 8, own), wide),
+            pltpu.VMEM((nr, rows_all, 3 * HEAD), low),
+            square, square, square, square, lane, lane,
+            pltpu.VMEM((rows_all, wide3), low),
+            big, big, big,
+            pltpu.VMEM((own, width_all), low),
+            pltpu.VMEM((own, width_all), low),
+            pltpu.VMEM((rows_all, 3 * RANK), low),
+            pltpu.VMEM((rows_all, 3 * RANK), low),
+            pltpu.VMEM((n * full_rows, width_all), low),
+            pltpu.VMEM((nr * col_rows, width), low),
+            pltpu.VMEM((nr, n * full_rows, width), low),
+            pltpu.VMEM((n * full_rows, width), low),
+            pltpu.VMEM((n, full_rows, width), low),
+            pltpu.VMEM((nr, col_rows, width), low),
+            pltpu.VMEM((ndp, full_rows + col_rows, width), low),
+            pltpu.VMEM((ndp,) + hot.shape, wide),
+            dma((n, n - 1)), dma((n, n - 1)), dma((nr - 1, n)), dma((nr - 1, n)), dma((n,)),
+            dma((n // 2,)), dma, dma, dma,
+            dma((2, n, chunks)), dma((2, n, chunks)), dma((nr - 1, chunks)), dma((nr - 1, chunks)), dma((chunks,)),
+            dma((nr - 1, 1)), dma((nr - 1, 1)), dma((1,)),
+            dma((nr - 1,)), dma((nr - 1,)), dma((nr - 1,)), dma((nr - 1,)), dma((n - 1,)), dma((n - 1,)),
+            dma((ndp - 1,)), dma((ndp - 1,)), dma((ndp - 1,)), dma((ndp - 1,)),
+        ],
+        compiler_params=params(5),
+        name="rear",
+    )(d_head, raw, factor, gain_q, gain_k, cos2, sin2, result, x, w_qkv, table, b_qkv, d_h, full_mid, part_ao, part_bgu, part_ad, hot)
+
+
+def unpack_kernel(rank_own, rank_row, grad_ref, layer_ref, sets_ref, layer_out, input_grad, a_qkv, b_qkv, a_out, b_out, a_gu, b_gu, a_down, b_down):
+    layer_out[...] = layer_ref[...]
+    input_grad[...] = grad_ref[...].astype(wide)
+    width = grad_ref.shape[1]
+    first = 8 * rank_own
+
+    def column(s, at):
+        return sets_ref[s, first + at * rank_row:first + (at + 1) * rank_row, :]
+
+    for s in range(sets_ref.shape[0]):
+        for j in range(3):
+            a_qkv[j, s] = sets_ref[s, j * rank_own:(j + 1) * rank_own, :]
+            b_qkv[j, s] = column(s, j)
+        for j in range(2):
+            a_gu[j, s] = sets_ref[s, (3 + j) * rank_own:(4 + j) * rank_own, :]
+        b_out[s] = sets_ref[s, 5 * rank_own:6 * rank_own, :]
+        b_down[s] = sets_ref[s, 6 * rank_own:7 * rank_own, :]
+        a_out[s] = column(s, 3)
+        per = a_down.shape[2] // width
+        for k in range(per):
+            lanes = slice(k * width, (k + 1) * width)
+            b_gu[0, s, :, lanes] = column(s, 4 + k)
+            b_gu[1, s, :, lanes] = column(s, 4 + per + k)
+            a_down[s, :, lanes] = column(s, 4 + 2 * per + k)
+
+
+def unpack(grad, layer, sets, rank_own, rank_row, hidden):
+    sets_own = sets.shape[0]
+    width = grad.shape[1]
+    shape = jax.ShapeDtypeStruct
+    return pl.pallas_call(
+        functools.partial(unpack_kernel, rank_own, rank_row),
+        out_shape=[
+            shape(layer.shape, low),
+            shape(grad.shape, wide),
+            shape((3, sets_own, rank_own, width), wide),
+            shape((3, sets_own, rank_row, width), wide),
+            shape((sets_own, rank_row, width), wide),
+            shape((sets_own, rank_own, width), wide),
+            shape((2, sets_own, rank_own, width), wide),
+            shape((2, sets_own, rank_row, hidden), wide),
+            shape((sets_own, rank_row, hidden), wide),
+            shape((sets_own, rank_own, width), wide),
+        ],
+        in_specs=[VM] * 3,
+        out_specs=[VM] * 10,
+        name="unpack",
+    )(grad, layer, sets)
 
 
 def middle_kernel(n, nr, m, hop, cuts, head_ref, x_hbm, cot_hbm, gain_ref, wo_hbm, wg_hbm, wd_hbm,
@@ -1555,7 +1655,6 @@
     width_row = tokens.shape[1]
     width_col = gain_q.shape[0]
     hidden_col = down_weight.shape[0]
-    heads_col = width_col // HEAD
     tree_set = tree_sets[0]
 
     tables = (
@@ -1578,8 +1677,6 @@
     sin2 = jnp.concatenate([-sine, sine], axis=1)
     gq, gk = gain_q[None, :], gain_k[None, :]
     parent_at, branch_flag = tree_tables(seg_ids, parents)
-    first = lax.axis_index("col") == 0
-    final = lax.axis_index("col") == col_count - 1
     x, table, gains, g_half, raw, factors, qkv_head, w_qkv, w_out = front(
         tokens,
         narrow,
@@ -1596,7 +1693,6 @@
         row_count,
     )
     attn_head, lse = attend(qkv_head, parent_at, branch_flag)
-    a_qkv = table[: 3 * RANK]
     d_attn_head, out_half, d_h_half, full_mid, part_ao, part_bgu, part_ad = middle(
         attn_head,
         x,
@@ -1613,54 +1709,32 @@
         row_count,
     )
     d_qkv_head = attend_back(qkv_head, d_attn_head, parent_at, branch_flag, lse)
-    d_raw, layer_out = from_heads_call(
-        d_qkv_head, raw, factors, gq, gk, cos2, sin2, out_half, col_count, row_count
+    hot = (tree_set == lax.broadcasted_iota(jnp.int32, (set_count, width_row), 0)).astype(wide)
+    in_grad, layer, sets = rear(
+        d_qkv_head,
+        raw,
+        factors,
+        gq,
+        gk,
+        cos2,
+        sin2,
+        out_half,
+        x,
+        w_qkv,
+        table,
+        b_qkv,
+        d_h_half,
+        full_mid,
+        part_ao,
+        part_bgu,
+        part_ad,
+        hot,
+        set_count // dp_count,
+        col_count,
+        row_count,
+        dp_count,
     )
-    d_q, d_k, d_v = (d_raw[:, width_col * j : width_col * (j + 1)] for j in range(3))
-    b_qkv = b_qkv.reshape(3, RANK, width_col)
-    back_qkv = jnp.concatenate([dot_t(d, b) for d, b in zip((d_q, d_k, d_v), b_qkv)], axis=1).astype(low)
-    red_qkv = dot_t(x, a_qkv).astype(low)
-    d_h_all = jnp.concatenate([jnp.where(first, d_h_half, 0.0), jnp.where(final, d_h_half, 0.0)], axis=0)
-    part_in = (dot_t(d_raw, w_qkv) + dot(back_qkv, a_qkv) + d_h_all).astype(low)
-
-    rank_own = RANK // col_count
-    full = jnp.concatenate(
-        [t_dot(back_qkv, x), full_mid], axis=0
-    ).astype(low)
-    full = full.reshape(7, col_count, rank_own, D).transpose(1, 0, 2, 3).reshape(col_count, 7 * rank_own, D)
-    full = jnp.pad(full, ((0, 0), (0, rank_own), (0, 0))).reshape(col_count * 8 * rank_own, D)
-    cols = jnp.concatenate(
-        [t_dot(red_qkv[:, RANK * j : RANK * (j + 1)], d) for j, d in enumerate((d_q, d_k, d_v))]
-        + [part_ao, part_bgu[0], part_bgu[1], part_ad],
-        axis=1,
-    ).astype(low)
-    cols = cols.reshape(RANK * 16, width_row)
-    hot = (tree_set == lax.broadcasted_iota(jnp.int32, (set_count, width_row), 0)).astype(wide)
-    sets_own = set_count // dp_count
-    input_grad, sets = finish(part_in, full, cols, hot, sets_own, col_count, row_count, dp_count)
-    full_sets = sets[:, : 7 * rank_own].reshape(sets_own, 7, rank_own, width_row)
-    col_sets = sets[:, 8 * rank_own :].reshape(sets_own, RANK // row_count, 16 * width_row)
-    grad_a_qkv = full_sets[:, :3].transpose(1, 0, 2, 3)
-    grad_a_gu = full_sets[:, 3:5].transpose(1, 0, 2, 3)
-    grad_b_out = full_sets[:, 5]
-    grad_b_down = full_sets[:, 6]
-    grad_b_qkv = jnp.stack([col_sets[..., width_col * j : width_col * (j + 1)] for j in range(3)])
-    grad_a_out = col_sets[..., 3 * width_col : 4 * width_col]
-    gu_at = 4 * width_col
-    grad_b_gu = jnp.stack([col_sets[..., gu_at + hidden_col * j : gu_at + hidden_col * (j + 1)] for j in range(2)])
-    grad_a_down = col_sets[..., gu_at + 2 * hidden_col :]
-    return (
-        layer_out,
-        input_grad,
-        grad_a_qkv,
-        grad_b_qkv,
-        grad_a_out,
-        grad_b_out,
-        grad_a_gu,
-        grad_b_gu,
-        grad_a_down,
-        grad_b_down,
-    )
+    return tuple(unpack(in_grad, layer, sets, RANK // col_count, RANK // row_count, hidden_col))
 
 
 def solution(mesh):

time: 598 us -> 534 us (0.89); the launches traced: 591 us -> 534 us
  Pallas kernels: 546 us -> 517 us
  matrix products: 13.7 us -> 0 us
  local copies, waits for them, and re-layouts: 23.2 us -> 11.9 us
    pallas_call x1, Pallas kernels: 109 us -> 88.6 us  [front(): pl.pallas_call(functools.partial(front_kernel, n, nr, m, mh), out_shape=[...]
    dot_general x10 -> x0, matrix products: 13.7 us -> none  [the longest x5 9.08 us: dot_t(): return lax.dot_general(left, right, last_last, preferred_element_type=wide)]
    pallas_call x2, Pallas kernels: 122 us -> 114 us  [the longest x1 111 us: rear(): pl.pallas_call(functools.partial(rear_kernel, n, nr, ndp, m), out_shape=[...]
    unnamed x41 -> x10, local copies, waits for them, and re-layouts: 13.1 us -> 7.33 us
where the time goes in v6:
time: 534 us
  Pallas kernels  517 us (97%)
  local copies, waits for them, and re-layouts  11.9 us (2%)
    pallas_call x1, Pallas kernels, middle(): pl.pallas_call(functools.partial(middle_kernel, n, nr, m, hop, cuts), out...  280 us
    pallas_call x1, Pallas kernels, rear(): pl.pallas_call(functools.partial(rear_kernel, n, nr, ndp, m), out_shape=[...  111 us
    pallas_call x1, Pallas kernels, front(): pl.pallas_call(functools.partial(front_kernel, n, nr, m, mh), out_shape=[...  88.6 us
    pallas_call x1, Pallas kernels, attend_back(): pl.pallas_call(attend_back_kernel, grid_spec=pltpu.PrefetchScalarGridSpec...  17.9 us
    pallas_call x1, Pallas kernels, attend(): pl.pallas_call(attend_body, grid_spec=pltpu.PrefetchScalarGridSpec(num_sc...  14.1 us

profile of v6, /device:TPU:0, one launch (start us, length us, event | category | flops | bytes accessed | tf_op | source)
XLA Modules:
  0.0 534.0 jit_solution(14696933677501215154)
XLA Ops:
  0.6 0.8 reshape.56
  1.5 0.1 convert_element_type.16
  1.6 1.2 fusion
  2.8 1.1 pad_maximum_fusion
  4.5 0.0 copy-start
  4.5 2.0 prep.1
  6.5 0.0 copy-done
  6.5 0.7 copy.35
  7.3 0.0 copy-start.1
  7.3 0.0 copy-start.2
  7.3 1.6 copy.36.wq_hbm
  8.9 0.6 select_maximum_fusion.gain_ref
  9.5 88.6 %front.1 = (bf16[640,2048]{1,0:T(8,128)(2,1)}, bf16[112,2048]{1,0:T(8,128)(2,1)}, f32[8,2048]{1,0:T(8,128)}, bf16[320,2048]{1,0:T(8,128)(2,1)}, f32[640,1536]{1,...) custom-call(bf16[640,512]{1,0:T(8,128)(2,1)} %tok_ref.1, ...), custom_call_target="tpu_custom_call" | custom-call | tf_op jit(solution)/shard_map/front/pallas_call | solution.py:645
  98.1 0.8 slice.3
  98.9 0.2 select_reduce_fusion.1
  99.1 0.7 select_reduce_fusion.parent_ref
  99.8 0.7 broadcast_in_dim.60.flag_ref
  100.4 14.1 %attend.1 = (bf16[2560,128]{1,0:T(8,128)(2,1)}, f32[2560,1]{1,0:T(8,128)}) custom-call(s32[12]{0:T(128)} %select_reduce_fusion.parent_ref, f32[12,128]{1,0:T(8,128)} %broadcast_in_dim.60.flag_ref, bf16[2560,384]{1,0:T(8,128)(2,1)} %get-tuple-element.38.qkv), custom_call_target="tpu_custom_call" | custom-call | tf_op jit(solution)/shard_map/attend/pallas_call | solution.py:329
  114.5 6.6 %copy.37 = bf16[64,8,2,2048]{3,1,2,0:T(8,128)(2,1)} copy(bf16[64,8,2,2048]{3,2,1,0:T(2,128)(2,1)} %bitcast.12) | data formatting | bytes 8388608
  121.1 279.9 %middle.1 = (bf16[2560,128]{1,0:T(8,128)(2,1)}, bf16[320,2048]{1,0:T(8,128)(2,1)}, f32[320,2048]{1,0:T(8,128)}, f32[64,2048]{1,0:T(8,128)}, f32[16,512]{1,0:T(8,...) custom-call(bf16[2560,128]{1,0:T(8,128)(2,1)} %get-tuple-element.39.head_ref, ...), custom_call_target="tpu_custom_call" | custom-call | tf_op jit(solution)/shard_map/middle/pallas_call | solution.py:1579
  401.1 17.9 %attend_back.1.d_ref = bf16[2560,384]{1,0:T(8,128)(2,1)} custom-call(s32[12]{0:T(128)} %select_reduce_fusion.parent_ref, f32[12,128]{1,0:T(8,128)} %broadcast_in_dim.60.flag_ref, bf16[2560,384]{1,0:T(8,128)(2,1)} %get-tuple-element.38.qkv, bf16[2560,128]{1,0:T(8,128)(2,1)} %get-tuple-element.48.do_ref, f32[2560,1]{1,0:T(8,128)} %get-tuple-element.49.lse_ref), custom_call_target="tpu_custom_call" | custom-call | tf_op jit(solution)/shard_map/attend_back/pallas_call | solution.py:348
  419.0 0.7 iota.23.hot_ref
  419.6 111.1 %rear.1 = (bf16[640,512]{1,0:T(8,128)(2,1)}, bf16[640,512]{1,0:T(8,128)(2,1)}, f32[4,96,512]{2,1,0:T(8,128)}) custom-call(bf16[2560,384]{1,0:T(8,128)(2,1)} %attend_back.1.d_ref, f32[640,1536]{1,0:T(8,128)} %get-tuple-element.50.raw_ref, f32[4,8,160]{2,1,0:T(8,128)} %get-tuple-element.51.factor_ref, f32[1,512]{1,0:T(1,128)} %bitcast.14, f32[1,512]{1,0:T(1,128)} %bitcast.16, ...), custom_call_target="tpu_custom_call" | custom-call | tf_op jit(solution)/shard_map/rear/pallas_call | solution.py:1039
  530.7 3.1 unpack.1
  (9 shorter events, 0.1 us)
Async XLA Ops:
  4.5 2.0 copy-start
  7.3 1.6 copy-start.1
  7.3 1.6 copy-start.2
  9.5 89.4 %copy-start.3 = (s32[1,13]{1,0:T(1,128)S(1)}, s32[1,13]{1,0:T(1,128)}, u32[]{:S(2)}) copy-start(s32[1,13]{1,0:T(1,128)} %param.26) | copy-start | bytes 160

commit v7 on v6

--- a/solution.py
+++ b/solution.py
@@ -681,11 +681,11 @@
     return (lax.broadcasted_iota(jnp.int32, (out_rows, in_rows), 1) == source(at)).astype(low)
 
 
-def rear_kernel(n, nr, ndp, m, d_ref, raw_ref, factor_ref, gq_ref, gk_ref, cos_ref, sin_ref, res_ref, x_ref, wq_hbm,
-                table_ref, bq_ref, dh_ref, full_ref, co_ref, cg_ref, cd_ref, hot_ref,
+def rear_kernel(n, nr, ndp, m, d_ref, raw_hbm, factor_ref, gq_ref, gk_ref, cos_ref, sin_ref, res_ref, x_hbm, wq_hbm,
+                table_ref, bq_ref, dh_hbm, full_hbm, co_hbm, cg_hbm, cd_hbm, hot_ref,
                 grad_ref, layer_ref, sets_ref,
-                wq, stats, buf, nq, nk, pq, pk, fq, fk, d_raw, part, recv_right, recv_left, own_buf, layer_own,
-                back, red, full, cols, full_recv, full_sum, full_last, col_recv, owned, hot_all,
+                raw_ref, x_ref, dh_ref, full_ref, co_ref, cg_ref, cd_ref, wq, stats, buf, nq, nk, pq, pk, fq, fk, d_raw, part, recv_right, recv_left, own_buf, layer_own,
+                back, red, full, cols, col_stack, full_recv, full_sum, full_last, col_recv, owned, hot_all,
                 send_s, recv_s, send_h, recv_h, local_h, send_o, recv_o, local_o, load,
                 send_z, recv_z, send_w, recv_w, local_w, send_v, recv_v, local_v,
                 send_f, recv_f, send_c, recv_c, send_l, recv_l, send_d, recv_d, send_k, recv_k):
@@ -697,10 +697,19 @@
     tree_part = own * nr
     middle_at = n // 2
     chunks = own // m
+    hop = 2
+    ahead = 2
     left = {"col": jnp.maximum(c - 1, 0)}
     right = {"col": jnp.minimum(c + 1, n - 1)}
-    load_w = pltpu.make_async_copy(wq_hbm, wq, load)
-    load_w.start()
+    load_raw = pltpu.make_async_copy(raw_hbm, raw_ref, load.at[0])
+    load_x = pltpu.make_async_copy(x_hbm, x_ref, load.at[1])
+    load_w = pltpu.make_async_copy(wq_hbm, wq, load.at[2])
+    loads = [
+        pltpu.make_async_copy(src, dst, load.at[3 + i])
+        for i, (src, dst) in enumerate(
+            ((dh_hbm, dh_ref), (full_hbm, full_ref), (co_hbm, co_ref), (cg_hbm, cg_ref), (cd_hbm, cd_ref))
+        )
+    ]
 
     def piece(d, b):
         peer = lax.rem(r + d, nr)
@@ -737,6 +746,11 @@
 
     for b in range(n):
         local(b).start()
+    load_raw.start()
+    load_x.start()
+    load_w.start()
+    for copy in loads:
+        copy.start()
     me = r * n + c
     barrier = pltpu.get_barrier_semaphore()
     for d in range(1, ndp):
@@ -758,7 +772,9 @@
                 result_piece(b).start()
 
     hot_all[g] = hot_ref[...]
+    load_x.wait()
     red[...] = dot_t(x_ref[...], table_ref[:3 * RANK, :]).astype(low)
+    load_raw.wait()
 
     def stat_copy(b, d):
         peer = lax.rem(c + d, n)
@@ -824,16 +840,24 @@
         dst, to = ((recv_right, right), (recv_left, left))[kind]
         return remote(part.at[rows], dst.at[rows], send_z.at[kind, b, j], recv_z.at[kind, b, j], to)
 
-    def stage(s, at_edge=True, inside=True):
-        @pl.loop(0, chunks)
-        def _(j):
-            for kind, b, go, edge, got in (
-                (0, n - 1 - s, n - 1 - s > c, c == 0, recv_right),
-                (1, s, s < c, c == n - 1, recv_left),
+    def stage(s, at_edge=True, inside=True, jobs=()):
+        @pl.loop(0, chunks + hop * (n - 2))
+        def _(i):
+            for at, job in enumerate(jobs):
+                pl.when(i == at)(job)
+
+            for kind, b, go, edge, got, j in (
+                (0, n - 1 - s, n - 1 - s > c, c == 0, recv_right, i - hop * c),
+                (1, s, s < c, c == n - 1, recv_left, i - hop * (n - 1 - c)),
             ):
+                go = jnp.logical_and(go, jnp.logical_and(j >= 0, j < chunks))
                 if at_edge:
                     @pl.when(jnp.logical_and(go, edge))
                     def _():
+                        @pl.when(j >= ahead)
+                        def _():
+                            reduce(kind, b, j - ahead).wait_send()
+
                         reduce(kind, b, j).start()
 
                 if inside:
@@ -870,52 +894,68 @@
         norm_block(i * (n - 1))
 
     load_w.wait()
+    loads[0].wait()
 
     @pl.loop(0, 2)
     def _(i):
         mean_block(i * (n - 1))
         back_block(i * (n - 1))
 
-    stage(0, inside=False)
-
     @pl.loop(1, n - 1)
     def _(b):
         norm_block(b)
 
-    stage(0, at_edge=False)
+    stage(0)
 
     @pl.loop(1, n - 1)
     def _(b):
         mean_block(b)
         back_block(b)
 
+    for copy in loads[1:]:
+        copy.wait()
+
     rank_own = RANK // n
     groups = full.shape[0] // (n * rank_own) - 1
-    stacked = jnp.concatenate([t_dot(back[...], x_ref[...]), full_ref[...]], axis=0).astype(low)
-    order = one_hot_rows(
-        full.shape[0], stacked.shape[0],
-        lambda o: jnp.where(
-            lax.rem(o, full_rows) < groups * rank_own,
-            lax.rem(o, full_rows) // rank_own * RANK + o // full_rows * rank_own + lax.rem(o, rank_own), -1
-        ),
-    )
-    full[...] = dot(order, stacked).astype(low)
-    pieces = [t_dot(red[:, j * RANK:(j + 1) * RANK], d_raw[:, j * width:(j + 1) * width]) for j in range(3)]
-    pieces.append(co_ref[...])
-    for j in range(2):
-        pieces += [cg_ref[j, :, k * width:(k + 1) * width] for k in range(cg_ref.shape[2] // width)]
-    pieces += [cd_ref[:, k * width:(k + 1) * width] for k in range(cd_ref.shape[1] // width)]
-    stacked = jnp.concatenate(pieces, axis=0).astype(low)
     rank_row = RANK // nr
-    order = one_hot_rows(
-        cols.shape[0], stacked.shape[0],
-        lambda o: lax.rem(o, col_rows) // rank_row * RANK + o // col_rows * rank_row + lax.rem(o, rank_row),
-    )
-    cols[...] = dot(order, stacked).astype(low)
+    per_wide = cd_ref.shape[1] // width
+
+    def full_job():
+        stacked = jnp.concatenate([t_dot(back[...], x_ref[...]), full_ref[...]], axis=0).astype(low)
+        order = one_hot_rows(
+            full.shape[0], stacked.shape[0],
+            lambda o: jnp.where(
+                lax.rem(o, full_rows) < groups * rank_own,
+                lax.rem(o, full_rows) // rank_own * RANK + o // full_rows * rank_own + lax.rem(o, rank_own), -1
+            ),
+        )
+        full[...] = dot(order, stacked).astype(low)
+
+    def raw_job():
+        for j in range(3):
+            col_stack[j * RANK:(j + 1) * RANK, :] = t_dot(
+                red[:, j * RANK:(j + 1) * RANK], d_raw[:, j * width:(j + 1) * width]
+            ).astype(low)
+        col_stack[3 * RANK:4 * RANK, :] = co_ref[...].astype(low)
+
+    def wide_job():
+        for k in range(per_wide):
+            lanes = slice(k * width, (k + 1) * width)
+            for j, value in enumerate((cg_ref[0, :, lanes], cg_ref[1, :, lanes], cd_ref[:, lanes])):
+                at = (4 + j * per_wide + k) * RANK
+                col_stack[at:at + RANK, :] = value.astype(low)
+
+    def col_job():
+        order = one_hot_rows(
+            cols.shape[0], cols.shape[0],
+            lambda o: lax.rem(o, col_rows) // rank_row * RANK + o // col_rows * rank_row + lax.rem(o, rank_row),
+        )
+        cols[...] = dot(order, col_stack[...]).astype(low)
+
+    stage(1, jobs=(wide_job, raw_job, col_job, full_job))
     for d in range(1, nr):
         full_piece(d).start()
         col_piece(d).start()
-    stage(1)
 
     @pl.when(is_owner)
     def _():
@@ -935,21 +975,22 @@
     for d in range(1, nr):
         width_piece(layer_own, layer_ref, send_v, recv_v, d, 0, own).start()
     width_local(layer_own, layer_ref, local_v, 0, own).start()
-    for d in range(1, nr):
-        full_piece(d).wait_recv()
-        col_piece(d).wait_recv()
-    total = full[:, span(r * width, width)].astype(wide)
-    col_total = cols[span(r * col_rows, col_rows), :].astype(wide)
-    for d in range(1, nr):
-        peer = lax.rem(r + d, nr)
-        total = total + full_recv[peer].astype(wide)
-        col_total = col_total + col_recv[peer].astype(wide)
-    full_sum[...] = total.astype(low)
-    owned[g, full_rows:, :] = col_total.astype(low)
-    for d in range(1, n):
-        last_piece(d).start()
-    for s in range(2, n - 1):
-        stage(s)
+    def row_job():
+        for d in range(1, nr):
+            full_piece(d).wait_recv()
+            col_piece(d).wait_recv()
+        total = full[:, span(r * width, width)].astype(wide)
+        col_total = cols[span(r * col_rows, col_rows), :].astype(wide)
+        for d in range(1, nr):
+            peer = lax.rem(r + d, nr)
+            total = total + full_recv[peer].astype(wide)
+            col_total = col_total + col_recv[peer].astype(wide)
+        full_sum[...] = total.astype(low)
+        owned[g, full_rows:, :] = col_total.astype(low)
+        for d in range(1, n):
+            last_piece(d).start()
+
+    stage(2, jobs=(lambda: None, row_job))
     for d in range(1, n):
         last_piece(d).wait_recv()
     last = full_sum[span(c * full_rows, full_rows), :].astype(wide)
@@ -1011,11 +1052,13 @@
     for s in range(n - 1):
         @pl.loop(0, chunks)
         def _(j):
-            @pl.when(n - 1 - s > c)
+            late = j >= chunks - ahead
+
+            @pl.when(jnp.logical_and(n - 1 - s > c, jnp.logical_or(c > 0, late)))
             def _():
                 reduce(0, n - 1 - s, j).wait_send()
 
-            @pl.when(s < c)
+            @pl.when(jnp.logical_and(s < c, jnp.logical_or(c < n - 1, late)))
             def _():
                 reduce(1, s, j).wait_send()
 
@@ -1043,9 +1086,16 @@
             shape((own * nr, width), low),
             shape((sets_own, full_rows + col_rows, width), wide),
         ],
-        in_specs=[VM] * 9 + [any_space] + [VM] * 8,
+        in_specs=[any_space] * 2 + [VM] * 5 + [any_space] * 3 + [VM] * 2 + [any_space] * 5 + [VM],
         out_specs=[VM] * 3,
         scratch_shapes=[
+            pltpu.VMEM(raw.shape, wide),
+            pltpu.VMEM(x.shape, low),
+            pltpu.VMEM(d_h.shape, wide),
+            pltpu.VMEM(full_mid.shape, wide),
+            pltpu.VMEM(part_ao.shape, wide),
+            pltpu.VMEM(part_bgu.shape, wide),
+            pltpu.VMEM(part_ad.shape, wide),
             pltpu.VMEM(w_qkv.shape, low),
             pltpu.VMEM((n, n, 8, own), wide),
             pltpu.VMEM((nr, rows_all, 3 * HEAD), low),
@@ -1058,6 +1108,7 @@
             pltpu.VMEM((rows_all, 3 * RANK), low),
             pltpu.VMEM((n * full_rows, width_all), low),
             pltpu.VMEM((nr * col_rows, width), low),
+            pltpu.VMEM((nr * col_rows, width), low),
             pltpu.VMEM((nr, n * full_rows, width), low),
             pltpu.VMEM((n * full_rows, width), low),
             pltpu.VMEM((n, full_rows, width), low),
@@ -1065,7 +1116,7 @@
             pltpu.VMEM((ndp, full_rows + col_rows, width), low),
             pltpu.VMEM((ndp,) + hot.shape, wide),
             dma((n, n - 1)), dma((n, n - 1)), dma((nr - 1, n)), dma((nr - 1, n)), dma((n,)),
-            dma((n // 2,)), dma, dma, dma,
+            dma((n // 2,)), dma, dma, dma((8,)),
             dma((2, n, chunks)), dma((2, n, chunks)), dma((nr - 1, chunks)), dma((nr - 1, chunks)), dma((chunks,)),
             dma((nr - 1, 1)), dma((nr - 1, 1)), dma((1,)),
             dma((nr - 1,)), dma((nr - 1,)), dma((nr - 1,)), dma((nr - 1,)), dma((n - 1,)), dma((n - 1,)),
@@ -1175,19 +1226,24 @@
             attn.at[span(b * own, own), span(r * HEAD, HEAD)], local_in.at[b]
         )
 
-    def piece_out(d, b):
+    per_block = blocks // (n // 2)
+
+    def out_rows(b, side):
+        at = side * (n // 2) + b // per_block
+        inside = lax.rem(b, per_block) * band
+        return span(at * own + inside, band), span(at * tree_part + r * own + inside, band)
+
+    def piece_out(d, b, side):
         peer = lax.rem(r + d, nr)
+        here, there = out_rows(b, side)
         return remote(
-            d_attn.at[span(b * own, own), span(peer * HEAD, HEAD)],
-            dhead_ref.at[span(b * tree_part + r * own, own)],
-            send_out.at[d - 1, b], recv_out.at[d - 1, b], {"row": peer},
+            d_attn.at[here, span(peer * HEAD, HEAD)], dhead_ref.at[there],
+            send_out.at[side * (nr - 1) + d - 1, b], recv_out.at[side * (nr - 1) + d - 1, b], {"row": peer},
         )
 
-    def local_piece_out(b):
-        return pltpu.make_async_copy(
-            d_attn.at[span(b * own, own), span(r * HEAD, HEAD)],
-            dhead_ref.at[span(b * tree_part + r * own, own)], local_out.at[b]
-        )
+    def local_piece_out(b, side):
+        here, there = out_rows(b, side)
+        return pltpu.make_async_copy(d_attn.at[here, span(r * HEAD, HEAD)], dhead_ref.at[there], local_out.at[side, b])
 
     for b in range(n):
         local_piece_in(b).start()
@@ -1244,7 +1300,10 @@
         part[low_rows, lanes] = value[:band].astype(low)
         part[high_rows, lanes] = value[band:].astype(low)
 
-    def relay_stage(stage, per, work, owner_step, all_ref, pump=None):
+    around = hop * 2 * (n - 1)
+    each = chunks // blocks
+
+    def relay_stage(stage, per, done, work, owner_step, all_ref, pump=None, coming=None):
         def send(kind, j, src, dst, to):
             return remote(src, dst, sems_send.at[stage, kind, j], sems_recv.at[stage, kind, j], to)
 
@@ -1261,15 +1320,17 @@
             return send(3, j, all_ref.at[rows(j)], all_ref.at[rows(j)], right)
 
         total_slices = per * blocks
-        each = chunks // blocks
+        lead = 0 if done else per
 
         def slices_before(i):
+            if done:
+                return jnp.minimum(done + i, total_slices)
             late = per + (jnp.maximum(i - per, 0) * per) // each
             return jnp.minimum(jnp.where(i < per, i, late), total_slices)
 
-        @pl.loop(0, per + chunks + hop * 2 * (n - 1))
+        @pl.loop(0, lead + chunks + around)
         def _(ii):
-            i = ii - per
+            i = ii - lead
 
             def on(offset, who, run):
                 j = i - offset
@@ -1309,6 +1370,22 @@
             def pass_right(j):
                 spread_right(j).wait_recv()
                 spread_right(j).start()
+
+            def arrived(j):
+                @pl.when(first)
+                def _():
+                    reduce_right(j).wait_send()
+                    spread_left(j).wait_recv()
+
+                @pl.when(last)
+                def _():
+                    reduce_left(j).wait_send()
+                    spread_right(j).wait_recv()
+
+                @pl.when(inner)
+                def _():
+                    reduce_right(j).wait_send()
+                    reduce_left(j).wait_send()
 
             on(0, first, lambda j: reduce_right(j).start())
             on(0, last, lambda j: reduce_left(j).start())
@@ -1318,10 +1395,18 @@
             on(hop * (n - 1), first, end_left)
             on(hop * (2 * (n - 1) - c), inner, pass_left)
             on(hop * (n - 1 + c), inner, pass_right)
+            on(around, True, arrived)
 
             @pl.loop(slices_before(ii), slices_before(ii + 1))
             def _(t):
                 work(t // per, lax.rem(t, per))
+
+            if coming is not None:
+                next_work, next_per, next_before = coming
+
+                @pl.loop(next_before(i), next_before(i + 1))
+                def _(t):
+                    next_work(t // next_per, lax.rem(t, next_per))
 
             if pump is not None:
                 pump(ii)
@@ -1330,20 +1415,14 @@
         def _(j):
             @pl.when(first)
             def _():
-                reduce_right(j).wait_send()
                 spread_right(j).wait_send()
-                spread_left(j).wait_recv()
 
             @pl.when(last)
             def _():
-                reduce_left(j).wait_send()
                 spread_left(j).wait_send()
-                spread_right(j).wait_recv()
 
             @pl.when(inner)
             def _():
-                reduce_right(j).wait_send()
-                reduce_left(j).wait_send()
                 spread_left(j).wait_send()
                 spread_right(j).wait_send()
 
@@ -1408,7 +1487,7 @@
                 share_d.pass_twin(t - cuts)
 
     load_x.wait()
-    relay_stage(0, 1, out_work, attn_owner, h_all, pump)
+    relay_stage(0, 1, 0, out_work, attn_owner, h_all, pump)
     in_loop = 1 + chunks + hop * 2 * (n - 1)
 
     @pl.loop(in_loop, jnp.maximum(in_loop, first_pass + apart * (passes + late)))
@@ -1468,9 +1547,6 @@
         out_half[at, :] = (h + flat * gain_f).astype(low)
         scaled = cot_half[at, :].astype(wide) * gain_f
         return (factor * (scaled - flat * (row_sum(scaled * flat) * (1.0 / D)))).astype(low)
-
-    load_cot.wait()
-    relay_stage(1, 6, ffn_work, ffn_owner, df_all)
 
     b_cut = hidden // 2
 
@@ -1536,31 +1612,46 @@
         scaled = grad * gain_a
         return (factor * (scaled - flat * (row_sum(scaled * flat) * (1.0 / D)))).astype(low)
 
-    relay_stage(2, 6, back_work, back_owner, da_all)
-
-    @pl.loop(0, n)
-    def _(b):
-        at = span(b * own, own)
-        rows_in = da_all[at, :]
+    def out_back(b, k):
+        rows_in = take(da_all, b)
         back = dot_t(rows_in, bo_ref[...]).astype(low)
         grad = dot(back, ao_ref[...])
         for j in range(nr):
             grad = grad + dot_t(rows_in[:, j * width:(j + 1) * width], wo[shard(j, wo), :])
-        d_attn[at, :] = grad.astype(low)
-        for d in range(1, nr):
-            piece_out(d, b).start()
-        local_piece_out(b).start()
-        attn_rows = attn[at, :]
+        for side in range(2):
+            d_attn[out_rows(b, side)[0], :] = grad[side * band:(side + 1) * band].astype(low)
+            for d in range(1, nr):
+                piece_out(d, b, side).start()
+            local_piece_out(b, side).start()
+        attn_rows = take(attn, b)
         co_ref[...] += t_dot(back, attn_rows)
         red = dot_t(attn_rows, ao_ref[...]).astype(low)
         full_ref[2 * RANK:3 * RANK, :] += t_dot(red, rows_in)
+
+    begin = around + each
+
+    def back_before(i):
+        return jnp.clip(i - begin, 0, chunks - each)
+
+    def out_before(i):
+        return jnp.clip((i - around - 1) // each, 0, blocks - 1)
+
+    load_cot.wait()
+    relay_stage(1, 6, 0, ffn_work, ffn_owner, df_all, None, (back_work, 6, back_before))
+    relay_stage(2, 6, chunks - each, back_work, back_owner, da_all, None, (out_back, 1, out_before))
+    out_back(blocks - 1, 0)
 
     @pl.loop(0, n)
     def _(b):
         for d in range(1, nr):
             piece_in(d, b).wait_send()
-            piece_out(d, b).wait()
-        local_piece_out(b).wait()
+
+    @pl.loop(0, blocks)
+    def _(b):
+        for side in range(2):
+            for d in range(1, nr):
+                piece_out(d, b, side).wait()
+            local_piece_out(b, side).wait()
 
     share_g.drain()
     share_d.drain()
@@ -1611,7 +1702,7 @@
             pltpu.VMEM((band, 2 * RANK), low),
             pltpu.VMEM((band, RANK), low),
             dma((3, 4, chunks)), dma((3, 4, chunks)),
-            dma((nr - 1, n)), dma((nr - 1, n)), dma((nr - 1, n)), dma((nr - 1, n)), dma((n,)), dma((n,)),
+            dma((nr - 1, n)), dma((nr - 1, n)), dma((2 * (nr - 1), 4)), dma((2 * (nr - 1), 4)), dma((n,)), dma((2, 4)),
             dma((3,)),
         ] + share_sems(cuts) + share_sems(cuts // 2),
         compiler_params=pltpu.CompilerParams(collective_id=0, has_side_effects=True, vmem_limit_bytes=67043328),

time: 534 us -> 501 us (0.938)
  Pallas kernels: 517 us -> 479 us
    pallas_call x1, Pallas kernels: 111 us -> 86.9 us  [rear(): pl.pallas_call(functools.partial(rear_kernel, n, nr, ndp, m), out_shape=[...]
    pallas_call x1, Pallas kernels: 280 us -> 267 us  [middle(): pl.pallas_call(functools.partial(middle_kernel, n, nr, m, hop, cuts), out...]
where the time goes in v7:
time: 501 us; the launch traced here: 497 us
  Pallas kernels  479 us (96%)
  local copies, waits for them, and re-layouts  11.9 us (2%)
    pallas_call x1, Pallas kernels, middle(): pl.pallas_call(functools.partial(middle_kernel, n, nr, m, hop, cuts), out...  267 us
    pallas_call x1, Pallas kernels, front(): pl.pallas_call(functools.partial(front_kernel, n, nr, m, mh), out_shape=[...  88.6 us
    pallas_call x1, Pallas kernels, rear(): pl.pallas_call(functools.partial(rear_kernel, n, nr, ndp, m), out_shape=[...  86.9 us
    pallas_call x1, Pallas kernels, attend_back(): pl.pallas_call(attend_back_kernel, grid_spec=pltpu.PrefetchScalarGridSpec...  17.6 us
    pallas_call x1, Pallas kernels, attend(): pl.pallas_call(attend_body, grid_spec=pltpu.PrefetchScalarGridSpec(num_sc...  14.1 us

profile of v7, /device:TPU:0, one launch (start us, length us, event | category | flops | bytes accessed | tf_op | source)
XLA Modules:
  0.0 496.8 jit_solution(5910621726012846912)
XLA Ops:
  0.6 0.8 reshape.56
  1.5 0.1 convert_element_type.16
  1.6 1.2 fusion
  2.8 1.1 pad_maximum_fusion
  4.5 0.0 copy-start
  4.5 2.0 prep.1
  6.5 0.7 copy.35
  7.3 0.0 copy-start.1
  7.3 0.0 copy-start.2
  7.3 1.6 copy.36.wq_hbm
  8.9 0.0 copy-done.1
  8.9 0.6 select_maximum_fusion.gain_ref
  9.5 88.6 %front.1 = (bf16[640,2048]{1,0:T(8,128)(2,1)}, bf16[112,2048]{1,0:T(8,128)(2,1)}, f32[8,2048]{1,0:T(8,128)}, bf16[320,2048]{1,0:T(8,128)(2,1)}, f32[640,1536]{1,...) custom-call(bf16[640,512]{1,0:T(8,128)(2,1)} %tok_ref.1, ...), custom_call_target="tpu_custom_call" | custom-call | tf_op jit(solution)/shard_map/front/pallas_call | solution.py:645
  98.1 0.8 slice.3
  98.9 0.2 select_reduce_fusion.1
  99.1 0.7 select_reduce_fusion.parent_ref
  99.8 0.7 broadcast_in_dim.60.flag_ref
  100.4 14.1 %attend.1 = (bf16[2560,128]{1,0:T(8,128)(2,1)}, f32[2560,1]{1,0:T(8,128)}) custom-call(s32[12]{0:T(128)} %select_reduce_fusion.parent_ref, f32[12,128]{1,0:T(8,128)} %broadcast_in_dim.60.flag_ref, bf16[2560,384]{1,0:T(8,128)(2,1)} %get-tuple-element.38.qkv), custom_call_target="tpu_custom_call" | custom-call | tf_op jit(solution)/shard_map/attend/pallas_call | solution.py:329
  114.5 6.6 %copy.37 = bf16[64,8,2,2048]{3,1,2,0:T(8,128)(2,1)} copy(bf16[64,8,2,2048]{3,2,1,0:T(2,128)(2,1)} %bitcast.12) | data formatting | bytes 8388608
  121.1 266.9 %middle.1 = (bf16[2560,128]{1,0:T(8,128)(2,1)}, bf16[320,2048]{1,0:T(8,128)(2,1)}, f32[320,2048]{1,0:T(8,128)}, f32[64,2048]{1,0:T(8,128)}, f32[16,512]{1,0:T(8,...) custom-call(bf16[2560,128]{1,0:T(8,128)(2,1)} %get-tuple-element.39.head_ref, ...), custom_call_target="tpu_custom_call" | custom-call | tf_op jit(solution)/shard_map/middle/pallas_call | solution.py:1670
  388.0 17.6 %attend_back.1.d_ref = bf16[2560,384]{1,0:T(8,128)(2,1)} custom-call(s32[12]{0:T(128)} %select_reduce_fusion.parent_ref, f32[12,128]{1,0:T(8,128)} %broadcast_in_dim.60.flag_ref, bf16[2560,384]{1,0:T(8,128)(2,1)} %get-tuple-element.38.qkv, bf16[2560,128]{1,0:T(8,128)(2,1)} %get-tuple-element.48.do_ref, f32[2560,1]{1,0:T(8,128)} %get-tuple-element.49.lse_ref), custom_call_target="tpu_custom_call" | custom-call | tf_op jit(solution)/shard_map/attend_back/pallas_call | solution.py:348
  405.6 0.7 iota.23.hot_ref
  406.3 86.9 %rear.1 = (bf16[640,512]{1,0:T(8,128)(2,1)}, bf16[640,512]{1,0:T(8,128)(2,1)}, f32[4,96,512]{2,1,0:T(8,128)}) custom-call(bf16[2560,384]{1,0:T(8,128)(2,1)} %attend_back.1.d_ref, f32[640,1536]{1,0:T(8,128)} %get-tuple-element.50.raw_hbm, f32[4,8,160]{2,1,0:T(8,128)} %get-tuple-element.51.factor_ref, f32[1,512]{1,0:T(1,128)} %bitcast.14, f32[1,512]{1,0:T(1,128)} %bitcast.16, ...), custom_call_target="tpu_custom_call" | custom-call | tf_op jit(solution)/shard_map/rear/pallas_call | solution.py:1082
  493.2 3.1 unpack.1
  (9 shorter events, 0.1 us)
Async XLA Ops:
  4.5 2.0 copy-start
  7.3 1.6 copy-start.1
  7.3 1.6 copy-start.2
  9.5 89.4 %copy-start.3 = (s32[1,13]{1,0:T(1,128)S(1)}, s32[1,13]{1,0:T(1,128)}, u32[]{:S(2)}) copy-start(s32[1,13]{1,0:T(1,128)} %param.26) | copy-start | bytes 160

commit v8 on v7

--- a/solution.py
+++ b/solution.py
@@ -39,10 +39,10 @@
 
 
 def angles(positions):
-    half_width = HEAD // 2
-    frequency = rope_base ** (-(jnp.arange(half_width, dtype=wide) * 2.0) / HEAD)
+    lane = jnp.arange(HEAD, dtype=jnp.int32)
+    frequency = rope_base ** (-((lane % (HEAD // 2)).astype(wide) * 2.0) / HEAD)
     angle_table = positions.astype(wide)[:, None] * frequency[None, :]
-    return (jnp.cos(angle_table), jnp.sin(angle_table))
+    return (jnp.cos(angle_table), jnp.where(lane < HEAD // 2, -1.0, 1.0) * jnp.sin(angle_table))
 
 
 def norm_factor(square_sum):
@@ -227,7 +227,7 @@
     for e in raised[1:]:
         total = total + jnp.sum(e, axis=1, keepdims=True)
     inverse = 1.0 / total
-    return [e * inverse for e in raised], top + jnp.log(total)
+    return raised, inverse, top + jnp.log(total)
 
 
 def tail_parts(q, qkv, at, parent, flag):
@@ -253,23 +253,23 @@
     v_lanes = slice(2 * HEAD, 3 * HEAD)
     for i in range(TRUNK // QT):
         at = slice(i * QT, (i + 1) * QT)
-        p, lse = softmax_parts(trunk_parts(qkv[at, :HEAD], qkv, i))
+        p, inverse, lse = softmax_parts(trunk_parts(qkv[at, :HEAD], qkv, i))
         o = dot(p[0].astype(low), qkv[at, v_lanes])
         if i:
             o = o + dot(p[1].astype(low), qkv[:i * QT, v_lanes])
-        o_ref[at, :] = o.astype(low)
+        o_ref[at, :] = (o * inverse).astype(low)
         lse_ref[at, :] = lse
 
-    @pl.loop(0, (qkv.shape[0] - TRUNK) // SEG)
+    @pl.loop(0, (qkv.shape[0] - TRUNK) // SEG, unroll=2)
     def _(j):
         at = pl.multiple_of(TRUNK + j * SEG, SEG)
         parent = pl.multiple_of(parent_ref[j] * SEG, SEG)
         rows = pl.ds(at, SEG)
-        p, lse = softmax_parts(tail_parts(qkv[rows, :HEAD], qkv, at, parent, flag_ref[pl.ds(j, 1), :]))
+        p, inverse, lse = softmax_parts(tail_parts(qkv[rows, :HEAD], qkv, at, parent, flag_ref[pl.ds(j, 1), :]))
         o = dot(p[0].astype(low), qkv[:TRUNK, v_lanes])
         o = o + dot(p[1].astype(low), qkv[pl.ds(parent, SEG), v_lanes])
         o = o + dot(p[2].astype(low), qkv[rows, v_lanes])
-        o_ref[rows, :] = o.astype(low)
+        o_ref[rows, :] = (o * inverse).astype(low)
         lse_ref[rows, :] = lse
 
 
@@ -300,7 +300,7 @@
             dk_acc[s, :] += t_dot(d, q)
             dv_acc[s, :] += t_dot(p, d_out)
 
-    @pl.loop(0, (qkv.shape[0] - TRUNK) // SEG)
+    @pl.loop(0, (qkv.shape[0] - TRUNK) // SEG, unroll=2)
     def _(j):
         at = pl.multiple_of(TRUNK + j * SEG, SEG)
         parent = pl.multiple_of(parent_ref[j] * SEG, SEG)
@@ -359,10 +359,10 @@
     )(parent_at, flag, qkv, d_o, lse)
 
 
-def front_kernel(n, nr, m, mh, tok_ref, table_ref, gain_ref, cot_ref, wq_hbm, wo_hbm, bq_ref, gq_ref, gk_ref,
+def front_kernel(n, nr, m, mh, tok_ref, table_ref, gain_ref, cot_ref, wq_hbm, wo_hbm, gu_hbm, bq_ref, gq_ref, gk_ref,
                  cos_ref, sin_ref,
-                 x_ref, table_all, gain_all, half_ref, raw_ref, factor_ref, qkv_ref, wq_out, wo_out,
-                 wq, wo, stats, buf, fq, fk, red, cot_own,
+                 x_out, table_all, gain_all, half_ref, raw_out, factor_ref, qkv_ref, wq_out, wo_out, gu_out,
+                 x_ref, raw_ref, gu_pair, gu_flat, wq, wo, stats, buf, fq, fk, red, cot_own,
                  send_a, recv_a, send_z, recv_z, send_t, recv_t, local_sem,
                  send_s, recv_s, send_h, recv_h, send_g, recv_g, local_h, local_g, send_e, recv_e,
                  send_q, recv_q, local_q, send_o, recv_o, local_o, out_sems):
@@ -412,6 +412,19 @@
         for d in range(1, nr):
             piece(d, j).start()
 
+
+    load_gu = pltpu.make_async_copy(gu_hbm, gu_pair, out_sems.at[4])
+    copy_gu = pltpu.make_async_copy(gu_flat, gu_out, out_sems.at[5])
+    gu_step = gu_flat.shape[0] // 8
+
+    def flatten(i):
+        @pl.when(i == 0)
+        def _():
+            load_gu.wait()
+
+        rows = span(i * gu_step, gu_step)
+        gu_flat[rows, :] = gu_pair[rows].reshape(gu_step, gu_flat.shape[1])
+
     middle_at = n // 2
     owner = jnp.where(c < middle_at, 0, n - 1)
     at_owner = jnp.where(c < middle_at, c, c - middle_at)
@@ -439,6 +452,7 @@
     cot_local.start()
     for d in range(1, nr):
         cot_piece(d).start()
+    load_gu.start()
     keep.wait()
 
     def head_rows(i):
@@ -506,7 +520,7 @@
                 head_piece(d, b * per + i).start()
             head_local(b * per + i).start()
 
-    def early():
+    def both_phases(last_step):
         for d in range(1, nr):
             table_piece(d, 0).wait_recv()
             table_piece(d, 1).wait_recv()
@@ -515,37 +529,43 @@
         share_q.wait_all()
         copy_wq.start()
 
-        @pl.loop(1, n - 1)
-        def _(b):
-            product_block(b)
-
-        @pl.when(jnp.logical_not(is_owner))
-        def _():
-            cot_move(at_owner).start()
-
-        @pl.when(is_owner)
-        def _():
-            cot_keep.start()
-
-        @pl.loop(1, n - 1)
-        def _(b):
-            head_block(b)
-
-    def late():
         @pl.loop(0, 2)
-        def _(i):
-            product_block(i * (n - 1))
-
-        for i in range(2):
-            share_o.pass_twin(i)
-
-        @pl.loop(0, 2)
-        def _(i):
-            head_block(i * (n - 1))
+        def _(phase):
+            def at(i):
+                return jnp.where(phase == 0, 1 + i, i * (n - 1))
+
+            pl.when(phase == 1)(last_step)
+
+            @pl.loop(0, 2)
+            def _(i):
+                product_block(at(i))
+
+            @pl.when(phase == 0)
+            def _():
+                @pl.when(jnp.logical_not(is_owner))
+                def _():
+                    cot_move(at_owner).start()
+
+                @pl.when(is_owner)
+                def _():
+                    cot_keep.start()
+
+            @pl.when(phase == 1)
+            def _():
+                copy_x.start()
+                copy_raw.start()
+                for i in range(2):
+                    share_o.pass_twin(i)
+
+            @pl.loop(0, 2)
+            def _(i):
+                head_block(at(i))
 
     copy_wq = pltpu.make_async_copy(wq, wq_out, out_sems.at[0])
-
-    for s in range(n):
+    copy_x = pltpu.make_async_copy(x_ref, x_out, out_sems.at[2])
+    copy_raw = pltpu.make_async_copy(raw_ref, raw_out, out_sems.at[3])
+
+    def ring_step(s):
         @pl.loop(0, chunks)
         def _(j):
             if s == 0:
@@ -570,9 +590,16 @@
                     def _():
                         block(1, s, jnp.minimum(c + s, n - 1), j, left).start()
 
+            if 0 < s < n - 1:
+                @pl.when(j < 8 // (n - 2))
+                def _():
+                    flatten((s - 1) * (8 // (n - 2)) + j)
+
         if s == 1:
             for i in range(2):
                 share_q.pass_far(i)
+        if s == n - 2:
+            copy_gu.start()
         if s == n - 2:
             for i in range(2):
                 share_o.pass_far(i)
@@ -580,10 +607,11 @@
             cot_local.wait()
             for d in range(1, nr):
                 cot_piece(d).wait_recv()
-            early()
-        if s == n - 1:
-            late()
     steps = rows_all // mh
+
+    for s in range(n - 1):
+        ring_step(s)
+    both_phases(lambda: ring_step(n - 1))
 
     share_o.wait_all()
     copy_wo = pltpu.make_async_copy(wo, wo_out, out_sems.at[1])
@@ -630,9 +658,12 @@
     share_o.drain()
     copy_wq.wait()
     copy_wo.wait()
-
-
-def front(tokens, table, gain, cot, w_qkv, w_out, b_qkv, gain_q, gain_k, cos2, sin2, n, nr, m=32, mh=80):
+    copy_x.wait()
+    copy_raw.wait()
+    copy_gu.wait()
+
+
+def front(tokens, table, gain, cot, w_qkv, w_out, w_gu, b_qkv, gain_q, gain_k, cos2, sin2, n, nr, m=32, mh=80):
     own = tokens.shape[0] // nr
     width = tokens.shape[1]
     rows_all = own * n
@@ -654,10 +685,15 @@
             shape((tree, 3 * HEAD), low),
             shape((w_qkv.shape[0] * nr, w_qkv.shape[1]), low),
             shape((w_out.shape[0] * nr, w_out.shape[1]), low),
+            shape((w_gu.shape[0], 2 * w_gu.shape[2]), low),
         ],
-        in_specs=[VM, VM, VM, VM, any_space, any_space] + [VM] * 5,
-        out_specs=[VM] * 7 + [any_space, any_space],
+        in_specs=[any_space, VM, VM] + [any_space] * 4 + [VM] * 5,
+        out_specs=[any_space, VM, VM, any_space, any_space, VM, any_space, any_space, any_space, any_space],
         scratch_shapes=[
+            pltpu.VMEM((rows_all, width * nr), low),
+            pltpu.VMEM((rows_all, 3 * width), wide),
+            pltpu.VMEM(w_gu.shape, low),
+            pltpu.VMEM((w_gu.shape[0], 2 * w_gu.shape[2]), low),
             pltpu.VMEM((w_qkv.shape[0] * nr, w_qkv.shape[1]), low),
             pltpu.VMEM((w_out.shape[0] * nr, w_out.shape[1]), low),
             pltpu.VMEM((n, n, 8, own), wide),
@@ -670,10 +706,10 @@
             dma((2, nr - 1)), dma((2, nr - 1)), dma((3,)),
             dma((n, n - 1)), dma((n, n - 1)), dma((nr - 1, steps)), dma((nr - 1, steps)),
             dma((nr - 1,)), dma((nr - 1,)), dma((steps,)), dma((2,)), dma, dma((n // 2,)),
-        ] + share_sems(2) + share_sems(2) + [dma((2,))],
+        ] + share_sems(2) + share_sems(2) + [dma((6,))],
         compiler_params=params(3),
         name="front",
-    )(tokens, table, gain, cot, w_qkv, w_out, b_qkv, gain_q, gain_k, cos2, sin2)
+    )(tokens, table, gain, cot, w_qkv, w_out, w_gu, b_qkv, gain_q, gain_k, cos2, sin2)
 
 
 def one_hot_rows(out_rows, in_rows, source):
@@ -835,6 +871,27 @@
             value = dot_t(d_raw[rows, :], wq[lanes, :]) + dot(back[rows, :], table_ref[:3 * RANK, lanes])
             part[rows, lanes] = (value + jnp.where(mine, dh_ref[held, lanes], 0.0)).astype(low)
 
+    def full_piece(d):
+        peer = lax.rem(r + d, nr)
+        return remote(full.at[:, span(peer * width, width)], full_recv.at[r], send_f.at[d - 1], recv_f.at[d - 1], {"row": peer})
+
+    col_rows = col_recv.shape[1]
+    full_rows = full_last.shape[1]
+
+    def col_piece(d):
+        peer = lax.rem(r + d, nr)
+        return remote(cols.at[span(peer * col_rows, col_rows)], col_recv.at[r], send_c.at[d - 1], recv_c.at[d - 1], {"row": peer})
+
+    def last_piece(d):
+        peer = lax.rem(c + d, n)
+        return remote(full_sum.at[span(peer * full_rows, full_rows)], full_last.at[c], send_l.at[d - 1], recv_l.at[d - 1], {"col": peer})
+
+    def tree_piece(d):
+        return remote(owned.at[g], owned.at[g], send_d.at[d - 1], recv_d.at[d - 1], {"dp": lax.rem(g + d, ndp)})
+
+    def hot_piece(d):
+        return remote(hot_all.at[g], hot_all.at[g], send_k.at[d - 1], recv_k.at[d - 1], {"dp": lax.rem(g + d, ndp)})
+
     def reduce(kind, b, j):
         rows = span(b * own + j * m, m)
         dst, to = ((recv_right, right), (recv_left, left))[kind]
@@ -868,49 +925,28 @@
                         part[rows, :] = (part[rows, :].astype(wide) + got[rows, :].astype(wide)).astype(low)
                         reduce(kind, b, j).start()
 
-    def full_piece(d):
-        peer = lax.rem(r + d, nr)
-        return remote(full.at[:, span(peer * width, width)], full_recv.at[r], send_f.at[d - 1], recv_f.at[d - 1], {"row": peer})
-
-    col_rows = col_recv.shape[1]
-    full_rows = full_last.shape[1]
-
-    def col_piece(d):
-        peer = lax.rem(r + d, nr)
-        return remote(cols.at[span(peer * col_rows, col_rows)], col_recv.at[r], send_c.at[d - 1], recv_c.at[d - 1], {"row": peer})
-
-    def last_piece(d):
-        peer = lax.rem(c + d, n)
-        return remote(full_sum.at[span(peer * full_rows, full_rows)], full_last.at[c], send_l.at[d - 1], recv_l.at[d - 1], {"col": peer})
-
-    def tree_piece(d):
-        return remote(owned.at[g], owned.at[g], send_d.at[d - 1], recv_d.at[d - 1], {"dp": lax.rem(g + d, ndp)})
-
-    def hot_piece(d):
-        return remote(hot_all.at[g], hot_all.at[g], send_k.at[d - 1], recv_k.at[d - 1], {"dp": lax.rem(g + d, ndp)})
-
     @pl.loop(0, 2)
-    def _(i):
-        norm_block(i * (n - 1))
-
-    load_w.wait()
-    loads[0].wait()
-
-    @pl.loop(0, 2)
-    def _(i):
-        mean_block(i * (n - 1))
-        back_block(i * (n - 1))
-
-    @pl.loop(1, n - 1)
-    def _(b):
-        norm_block(b)
-
-    stage(0)
-
-    @pl.loop(1, n - 1)
-    def _(b):
-        mean_block(b)
-        back_block(b)
+    def _(phase):
+        def at(i):
+            return jnp.where(phase == 0, i * (n - 1), 1 + i)
+
+        @pl.loop(0, 2)
+        def _(i):
+            norm_block(at(i))
+
+        @pl.when(phase == 0)
+        def _():
+            load_w.wait()
+            loads[0].wait()
+
+        @pl.when(phase == 1)
+        def _():
+            stage(0)
+
+        @pl.loop(0, 2)
+        def _(i):
+            mean_block(at(i))
+            back_block(at(i))
 
     for copy in loads[1:]:
         copy.wait()
@@ -1179,8 +1215,8 @@
 
 def middle_kernel(n, nr, m, hop, cuts, head_ref, x_hbm, cot_hbm, gain_ref, wo_hbm, wg_hbm, wd_hbm,
                   table_ref, ao_ref, bg_ref, ad_ref,
-                  dhead_ref, out_half, grad_half, full_ref, co_ref, cg_ref, cd_ref,
-                  wo, wg, wd, x_half, cot_half, raw, attn, d_attn, h_all, df_all, da_all, gu, part,
+                  dhead_ref, out_hbm, grad_hbm, full_ref, co_ref, cg_ref, cd_ref,
+                  out_half, grad_half, wo, wg, wd, x_half, cot_half, raw, attn, d_attn, h_all, df_all, da_all, gu, part,
                   recv_right, recv_left, hid, red_gu, red_down, back_gu, back_down,
                   sems_send, sems_recv, send_in, recv_in, send_out, recv_out, local_in, local_out, load,
                   send_g, recv_g, local_g, send_d, recv_d, local_d):
@@ -1210,6 +1246,9 @@
     loads = [pltpu.make_async_copy(wo_hbm, wo, load.at[0])]
     load_x = pltpu.make_async_copy(x_hbm.at[span(base, half)], x_half, load.at[1])
     load_cot = pltpu.make_async_copy(cot_hbm, cot_half, load.at[2])
+    store_out = pltpu.make_async_copy(out_half, out_hbm, load.at[3])
+    store_grad = pltpu.make_async_copy(grad_half, grad_hbm, load.at[4])
+    is_owner = jnp.logical_or(first, last)
     loads[0].start()
 
     def piece_in(d, b):
@@ -1328,7 +1367,7 @@
             late = per + (jnp.maximum(i - per, 0) * per) // each
             return jnp.minimum(jnp.where(i < per, i, late), total_slices)
 
-        @pl.loop(0, lead + chunks + around)
+        @pl.loop(0, lead + chunks + around + (1 if coming is not None else 0))
         def _(ii):
             i = ii - lead
 
@@ -1488,11 +1527,7 @@
 
     load_x.wait()
     relay_stage(0, 1, 0, out_work, attn_owner, h_all, pump)
-    in_loop = 1 + chunks + hop * 2 * (n - 1)
-
-    @pl.loop(in_loop, jnp.maximum(in_loop, first_pass + apart * (passes + late)))
-    def _(ii):
-        pump(ii)
+    in_loop = 1 + chunks + around
 
     share_g.wait_all()
 
@@ -1516,6 +1551,10 @@
     def down_slice(b, k):
         @pl.when(jnp.logical_and(b == 0, k == 0))
         def _():
+            @pl.loop(in_loop, jnp.maximum(in_loop, first_pass + apart * (passes + late)))
+            def _(ii):
+                pump(ii)
+
             share_d.wait_all()
 
         rows_in = hid[:, :hidden]
@@ -1634,12 +1673,13 @@
         return jnp.clip(i - begin, 0, chunks - each)
 
     def out_before(i):
-        return jnp.clip((i - around - 1) // each, 0, blocks - 1)
+        return jnp.clip((i - around - 1) // each, 0, blocks)
 
     load_cot.wait()
     relay_stage(1, 6, 0, ffn_work, ffn_owner, df_all, None, (back_work, 6, back_before))
+    pl.when(is_owner)(store_out.start)
     relay_stage(2, 6, chunks - each, back_work, back_owner, da_all, None, (out_back, 1, out_before))
-    out_back(blocks - 1, 0)
+    pl.when(is_owner)(store_grad.start)
 
     @pl.loop(0, n)
     def _(b):
@@ -1655,6 +1695,11 @@
 
     share_g.drain()
     share_d.drain()
+
+    @pl.when(is_owner)
+    def _():
+        store_out.wait()
+        store_grad.wait()
 
 
 def middle(attn_head, x, cot_half, gains, w_out, w_gu, w_down, table, a_out, b_gu, a_down, n, nr, m=16, hop=2, cuts=8):
@@ -1678,9 +1723,11 @@
             shape((2, RANK, hidden), wide),
             shape((RANK, hidden), wide),
         ],
-        in_specs=[VM, any_space, any_space, VM, any_space, any_space, any_space] + [VM] * 4,
-        out_specs=[VM] * 7,
+        in_specs=[any_space, any_space, any_space, VM, any_space, any_space, any_space] + [VM] * 4,
+        out_specs=[any_space] * 3 + [VM] * 4,
         scratch_shapes=[
+            pltpu.VMEM((half, width_all), low),
+            pltpu.VMEM((half, width_all), wide),
             pltpu.VMEM(w_out.shape, low),
             pltpu.VMEM((w_gu.shape[0] * nr, w_gu.shape[1]), low),
             pltpu.VMEM((w_down.shape[0] * nr, w_down.shape[1]), low),
@@ -1703,7 +1750,7 @@
             pltpu.VMEM((band, RANK), low),
             dma((3, 4, chunks)), dma((3, 4, chunks)),
             dma((nr - 1, n)), dma((nr - 1, n)), dma((2 * (nr - 1), 4)), dma((2 * (nr - 1), 4)), dma((n,)), dma((2, 4)),
-            dma((3,)),
+            dma((5,)),
         ] + share_sems(cuts) + share_sems(cuts // 2),
         compiler_params=pltpu.CompilerParams(collective_id=0, has_side_effects=True, vmem_limit_bytes=67043328),
         name="middle",
@@ -1763,18 +1810,17 @@
     pos_own = lax.dynamic_index_in_dim(
         positions.reshape(col_count, row_count, own), row_at, 1, keepdims=False
     ).reshape(group)
-    cosine, sine = angles(pos_own)
-    cos2 = jnp.concatenate([cosine, cosine], axis=1)
-    sin2 = jnp.concatenate([-sine, sine], axis=1)
+    cos2, sin2 = angles(pos_own)
     gq, gk = gain_q[None, :], gain_k[None, :]
     parent_at, branch_flag = tree_tables(seg_ids, parents)
-    x, table, gains, g_half, raw, factors, qkv_head, w_qkv, w_out = front(
+    x, table, gains, g_half, raw, factors, qkv_head, w_qkv, w_out, w_gu = front(
         tokens,
         narrow,
         gain_pair,
         cotangent,
         query_key_value_weight.reshape(width_row, 3 * width_col),
         output_weight,
+        gate_up_weight,
         b_qkv,
         gq,
         gk,
@@ -1790,7 +1836,7 @@
         g_half,
         gains,
         w_out,
-        gate_up_weight.reshape(width_row, 2 * hidden_col),
+        w_gu,
         down_weight,
         table,
         a_out,

time: 501 us -> 478 us (0.954)
  Pallas kernels: 479 us -> 467 us
  local copies, waits for them, and re-layouts: 11.9 us -> 5.33 us
    unnamed x10 -> x9, local copies, waits for them, and re-layouts: 7.33 us -> 0.72 us
    pallas_call x1, Pallas kernels: 267 us -> 261 us  [middle(): pl.pallas_call(functools.partial(middle_kernel, n, nr, m, hop, cuts), out...]
where the time goes in v8:
time: 478 us; the launch traced here: 477 us
  Pallas kernels  467 us (98%)
  local copies, waits for them, and re-layouts  5.33 us (1%)
    pallas_call x1, Pallas kernels, middle(): pl.pallas_call(functools.partial(middle_kernel, n, nr, m, hop, cuts), out...  261 us
    pallas_call x1, Pallas kernels, rear(): pl.pallas_call(functools.partial(rear_kernel, n, nr, ndp, m), out_shape=[...  86.9 us
    pallas_call x1, Pallas kernels, front(): pl.pallas_call(functools.partial(front_kernel, n, nr, m, mh), out_shape=[...  85.5 us
    pallas_call x1, Pallas kernels, attend_back(): pl.pallas_call(attend_back_kernel, grid_spec=pltpu.PrefetchScalarGridSpec...  16.8 us
    pallas_call x1, Pallas kernels, attend(): pl.pallas_call(attend_body, grid_spec=pltpu.PrefetchScalarGridSpec(num_sc...  11.7 us

profile of v8, /device:TPU:0, one launch (start us, length us, event | category | flops | bytes accessed | tf_op | source)
XLA Modules:
  0.0 477.4 jit_solution(708243849449929646)
XLA Ops:
  0.6 0.8 reshape.65
  1.5 0.1 convert_element_type.23
  1.6 2.1 fusion
  4.3 0.0 copy-start
  4.3 2.0 prep.1
  6.3 0.0 copy-done
  6.3 0.7 copy.35
  7.0 0.0 copy-start.1
  7.0 0.0 copy-start.2
  7.1 1.6 copy.36.wq_hbm
  8.7 0.0 copy-done.1
  8.7 0.0 copy-done.2
  8.7 0.6 select_maximum_fusion.gain_ref
  9.3 85.5 %front.1 = (bf16[640,2048]{1,0:T(8,128)(2,1)}, bf16[112,2048]{1,0:T(8,128)(2,1)}, f32[8,2048]{1,0:T(8,128)}, bf16[320,2048]{1,0:T(8,128)(2,1)}, f32[640,1536]{1,...) custom-call(bf16[640,512]{1,0:T(8,128)(2,1)} %tok_ref.1, ...), custom_call_target="tpu_custom_call" | custom-call | tf_op jit(solution)/shard_map/front/pallas_call | solution.py:676
  94.8 0.8 slice.3
  95.6 0.2 select_reduce_fusion.1
  95.8 0.7 select_reduce_fusion.parent_ref
  96.5 0.7 broadcast_in_dim.69.flag_ref
  97.1 11.7 %attend.1 = (bf16[2560,128]{1,0:T(8,128)(2,1)}, f32[2560,1]{1,0:T(8,128)}) custom-call(s32[12]{0:T(128)} %select_reduce_fusion.parent_ref, f32[12,128]{1,0:T(8,128)} %broadcast_in_dim.69.flag_ref, bf16[2560,384]{1,0:T(8,128)(2,1)} %get-tuple-element.39.qkv), custom_call_target="tpu_custom_call" | custom-call | tf_op jit(solution)/shard_map/attend/pallas_call | solution.py:329
  108.8 261.0 %middle.1 = (bf16[2560,128]{1,0:T(8,128)(2,1)}, bf16[320,2048]{1,0:T(8,128)(2,1)}, f32[320,2048]{1,0:T(8,128)}, f32[64,2048]{1,0:T(8,128)}, f32[16,512]{1,0:T(8,...) custom-call(bf16[2560,128]{1,0:T(8,128)(2,1)} %get-tuple-element.40.head_ref, ...), custom_call_target="tpu_custom_call" | custom-call | tf_op jit(solution)/shard_map/middle/pallas_call | solution.py:1715
  369.8 16.8 %attend_back.1.d_ref = bf16[2560,384]{1,0:T(8,128)(2,1)} custom-call(s32[12]{0:T(128)} %select_reduce_fusion.parent_ref, f32[12,128]{1,0:T(8,128)} %broadcast_in_dim.69.flag_ref, bf16[2560,384]{1,0:T(8,128)(2,1)} %get-tuple-element.39.qkv, bf16[2560,128]{1,0:T(8,128)(2,1)} %get-tuple-element.50.do_ref, f32[2560,1]{1,0:T(8,128)} %get-tuple-element.51.lse_ref), custom_call_target="tpu_custom_call" | custom-call | tf_op jit(solution)/shard_map/attend_back/pallas_call | solution.py:348
  386.6 0.7 iota.28.hot_ref
  387.3 86.9 %rear.1 = (bf16[640,512]{1,0:T(8,128)(2,1)}, bf16[640,512]{1,0:T(8,128)(2,1)}, f32[4,96,512]{2,1,0:T(8,128)}) custom-call(bf16[2560,384]{1,0:T(8,128)(2,1)} %attend_back.1.d_ref, f32[640,1536]{1,0:T(8,128)} %get-tuple-element.52.raw_hbm, f32[4,8,160]{2,1,0:T(8,128)} %get-tuple-element.53.factor_ref, f32[1,512]{1,0:T(1,128)} %bitcast.10, f32[1,512]{1,0:T(1,128)} %bitcast.12, ...), custom_call_target="tpu_custom_call" | custom-call | tf_op jit(solution)/shard_map/rear/pallas_call | solution.py:1118
  474.2 3.1 unpack.1
  (7 shorter events, 0.1 us)
Async XLA Ops:
  4.3 2.0 copy-start
  7.0 1.6 copy-start.1
  7.0 1.6 copy-start.2
  9.3 86.3 %copy-start.3 = (s32[1,13]{1,0:T(1,128)S(1)}, s32[1,13]{1,0:T(1,128)}, u32[]{:S(2)}) copy-start(s32[1,13]{1,0:T(1,128)} %param.26) | copy-start | bytes 160

commit v9 on v8

--- a/solution.py
+++ b/solution.py
@@ -260,7 +260,7 @@
         o_ref[at, :] = (o * inverse).astype(low)
         lse_ref[at, :] = lse
 
-    @pl.loop(0, (qkv.shape[0] - TRUNK) // SEG, unroll=2)
+    @pl.loop(0, (qkv.shape[0] - TRUNK) // SEG, unroll=4)
     def _(j):
         at = pl.multiple_of(TRUNK + j * SEG, SEG)
         parent = pl.multiple_of(parent_ref[j] * SEG, SEG)
@@ -300,7 +300,7 @@
             dk_acc[s, :] += t_dot(d, q)
             dv_acc[s, :] += t_dot(p, d_out)
 
-    @pl.loop(0, (qkv.shape[0] - TRUNK) // SEG, unroll=2)
+    @pl.loop(0, (qkv.shape[0] - TRUNK) // SEG, unroll=3)
     def _(j):
         at = pl.multiple_of(TRUNK + j * SEG, SEG)
         parent = pl.multiple_of(parent_ref[j] * SEG, SEG)
@@ -1342,7 +1342,7 @@
     around = hop * 2 * (n - 1)
     each = chunks // blocks
 
-    def relay_stage(stage, per, done, work, owner_step, all_ref, pump=None, coming=None):
+    def relay_stage(stage, owner_step, all_ref):
         def send(kind, j, src, dst, to):
             return remote(src, dst, sems_send.at[stage, kind, j], sems_recv.at[stage, kind, j], to)
 
@@ -1358,19 +1358,7 @@
         def spread_right(j):
             return send(3, j, all_ref.at[rows(j)], all_ref.at[rows(j)], right)
 
-        total_slices = per * blocks
-        lead = 0 if done else per
-
-        def slices_before(i):
-            if done:
-                return jnp.minimum(done + i, total_slices)
-            late = per + (jnp.maximum(i - per, 0) * per) // each
-            return jnp.minimum(jnp.where(i < per, i, late), total_slices)
-
-        @pl.loop(0, lead + chunks + around + (1 if coming is not None else 0))
-        def _(ii):
-            i = ii - lead
-
+        def step(i):
             def on(offset, who, run):
                 j = i - offset
 
@@ -1436,34 +1424,35 @@
             on(hop * (n - 1 + c), inner, pass_right)
             on(around, True, arrived)
 
-            @pl.loop(slices_before(ii), slices_before(ii + 1))
-            def _(t):
-                work(t // per, lax.rem(t, per))
-
-            if coming is not None:
-                next_work, next_per, next_before = coming
-
-                @pl.loop(next_before(i), next_before(i + 1))
-                def _(t):
-                    next_work(t // next_per, lax.rem(t, next_per))
-
-            if pump is not None:
-                pump(ii)
-
-        @pl.loop(0, chunks)
-        def _(j):
-            @pl.when(first)
-            def _():
-                spread_right(j).wait_send()
-
-            @pl.when(last)
-            def _():
-                spread_left(j).wait_send()
-
-            @pl.when(inner)
-            def _():
-                spread_left(j).wait_send()
-                spread_right(j).wait_send()
+        def rest():
+            @pl.loop(0, chunks)
+            def _(j):
+                @pl.when(first)
+                def _():
+                    spread_right(j).wait_send()
+
+                @pl.when(last)
+                def _():
+                    spread_left(j).wait_send()
+
+                @pl.when(inner)
+                def _():
+                    spread_left(j).wait_send()
+                    spread_right(j).wait_send()
+
+        return step, rest
+
+    def slices(before, i, per, work):
+        @pl.loop(before(i), before(i + 1))
+        def _(t):
+            work(t // per, lax.rem(t, per))
+
+    def paced(per):
+        def before(i):
+            late = per + (jnp.maximum(i - per, 0) * per) // each
+            return jnp.minimum(jnp.where(i < per, i, late), per * blocks)
+
+        return before
 
     def shard(j, ref):
         return slice(j * (ref.shape[0] // nr), (j + 1) * (ref.shape[0] // nr))
@@ -1495,9 +1484,9 @@
         flat = total * norm_factor(row_sum(total * total))
         return (x_half[at, :].astype(wide) + flat * gain_a).astype(low)
 
-    first_pass = 5
-    apart = 3
-    late = 2
+    first_pass = 4
+    apart = 2
+    late = 3
     passes = cuts + cuts // 2
 
     def pump(ii):
@@ -1526,8 +1515,17 @@
                 share_d.pass_twin(t - cuts)
 
     load_x.wait()
-    relay_stage(0, 1, 0, out_work, attn_owner, h_all, pump)
     in_loop = 1 + chunks + around
+    step, rest = relay_stage(0, attn_owner, h_all)
+    out_pace = paced(1)
+
+    @pl.loop(0, in_loop)
+    def _(ii):
+        step(ii - 1)
+        slices(out_pace, ii, 1, out_work)
+        pump(ii)
+
+    rest()
 
     share_g.wait_all()
 
@@ -1670,15 +1668,29 @@
     begin = around + each
 
     def back_before(i):
-        return jnp.clip(i - begin, 0, chunks - each)
+        return jnp.clip(i - begin, 0, 6 * blocks)
 
     def out_before(i):
         return jnp.clip((i - around - 1) // each, 0, blocks)
 
     load_cot.wait()
-    relay_stage(1, 6, 0, ffn_work, ffn_owner, df_all, None, (back_work, 6, back_before))
+    step_f, rest_f = relay_stage(1, ffn_owner, df_all)
+    step_b, rest_b = relay_stage(2, back_owner, da_all)
+    ffn_pace = paced(6)
+    period = 26
+
+    @pl.loop(0, 6 + period + chunks + around + 1)
+    def _(ii):
+        i = ii - 6
+        step_f(i)
+        step_b(i - period)
+        slices(ffn_pace, ii, 6, ffn_work)
+        slices(back_before, i, 6, back_work)
+        slices(out_before, i - period, 1, out_back)
+
     pl.when(is_owner)(store_out.start)
-    relay_stage(2, 6, chunks - each, back_work, back_owner, da_all, None, (out_back, 1, out_before))
+    rest_f()
+    rest_b()
     pl.when(is_owner)(store_grad.start)
 
     @pl.loop(0, n)

time: 478 us -> 459 us (0.960)
  Pallas kernels: 467 us -> 448 us
    pallas_call x1, Pallas kernels: 261 us -> 243 us  [middle(): pl.pallas_call(functools.partial(middle_kernel, n, nr, m, hop, cuts), out...]
where the time goes in v9:
time: 459 us
  Pallas kernels  448 us (98%)
  local copies, waits for them, and re-layouts  5.33 us (1%)
    pallas_call x1, Pallas kernels, middle(): pl.pallas_call(functools.partial(middle_kernel, n, nr, m, hop, cuts), out...  243 us
    pallas_call x1, Pallas kernels, rear(): pl.pallas_call(functools.partial(rear_kernel, n, nr, ndp, m), out_shape=[...  86.9 us
    pallas_call x1, Pallas kernels, front(): pl.pallas_call(functools.partial(front_kernel, n, nr, m, mh), out_shape=[...  85.5 us
    pallas_call x1, Pallas kernels, attend_back(): pl.pallas_call(attend_back_kernel, grid_spec=pltpu.PrefetchScalarGridSpec...  16.7 us
    pallas_call x1, Pallas kernels, attend(): pl.pallas_call(attend_body, grid_spec=pltpu.PrefetchScalarGridSpec(num_sc...  11.1 us

profile of v9, /device:TPU:0, one launch (start us, length us, event | category | flops | bytes accessed | tf_op | source)
XLA Modules:
  0.0 458.8 jit_solution(5870079321397689618)
XLA Ops:
  0.6 0.8 reshape.65
  1.5 0.1 convert_element_type.23
  1.6 2.1 fusion
  4.3 0.0 copy-start
  4.3 2.0 prep.1
  6.3 0.0 copy-done
  6.3 0.7 copy.35
  7.0 0.0 copy-start.1
  7.0 0.0 copy-start.2
  7.1 1.6 copy.36.wq_hbm
  8.7 0.0 copy-done.1
  8.7 0.6 select_maximum_fusion.gain_ref
  9.3 85.5 %front.1 = (bf16[640,2048]{1,0:T(8,128)(2,1)}, bf16[112,2048]{1,0:T(8,128)(2,1)}, f32[8,2048]{1,0:T(8,128)}, bf16[320,2048]{1,0:T(8,128)(2,1)}, f32[640,1536]{1,...) custom-call(bf16[640,512]{1,0:T(8,128)(2,1)} %tok_ref.1, ...), custom_call_target="tpu_custom_call" | custom-call | tf_op jit(solution)/shard_map/front/pallas_call | solution.py:676
  94.8 0.8 slice.3
  95.6 0.0 copy-done.3
  95.6 0.2 select_reduce_fusion.1
  95.8 0.7 select_reduce_fusion.parent_ref
  96.5 0.7 broadcast_in_dim.69.flag_ref
  97.1 11.1 %attend.1 = (bf16[2560,128]{1,0:T(8,128)(2,1)}, f32[2560,1]{1,0:T(8,128)}) custom-call(s32[12]{0:T(128)} %select_reduce_fusion.parent_ref, f32[12,128]{1,0:T(8,128)} %broadcast_in_dim.69.flag_ref, bf16[2560,384]{1,0:T(8,128)(2,1)} %get-tuple-element.39.qkv), custom_call_target="tpu_custom_call" | custom-call | tf_op jit(solution)/shard_map/attend/pallas_call | solution.py:329
  108.2 243.1 %middle.1 = (bf16[2560,128]{1,0:T(8,128)(2,1)}, bf16[320,2048]{1,0:T(8,128)(2,1)}, f32[320,2048]{1,0:T(8,128)}, f32[64,2048]{1,0:T(8,128)}, f32[16,512]{1,0:T(8,...) custom-call(bf16[2560,128]{1,0:T(8,128)(2,1)} %get-tuple-element.40.head_ref, ...), custom_call_target="tpu_custom_call" | custom-call | tf_op jit(solution)/shard_map/middle/pallas_call | solution.py:1727
  351.3 16.7 %attend_back.1.d_ref = bf16[2560,384]{1,0:T(8,128)(2,1)} custom-call(s32[12]{0:T(128)} %select_reduce_fusion.parent_ref, f32[12,128]{1,0:T(8,128)} %broadcast_in_dim.69.flag_ref, bf16[2560,384]{1,0:T(8,128)(2,1)} %get-tuple-element.39.qkv, bf16[2560,128]{1,0:T(8,128)(2,1)} %get-tuple-element.50.do_ref, f32[2560,1]{1,0:T(8,128)} %get-tuple-element.51.lse_ref), custom_call_target="tpu_custom_call" | custom-call | tf_op jit(solution)/shard_map/attend_back/pallas_call | solution.py:348
  368.0 0.7 iota.28.hot_ref
  368.7 86.9 %rear.1 = (bf16[640,512]{1,0:T(8,128)(2,1)}, bf16[640,512]{1,0:T(8,128)(2,1)}, f32[4,96,512]{2,1,0:T(8,128)}) custom-call(bf16[2560,384]{1,0:T(8,128)(2,1)} %attend_back.1.d_ref, f32[640,1536]{1,0:T(8,128)} %get-tuple-element.52.raw_hbm, f32[4,8,160]{2,1,0:T(8,128)} %get-tuple-element.53.factor_ref, f32[1,512]{1,0:T(1,128)} %bitcast.10, f32[1,512]{1,0:T(1,128)} %bitcast.12, ...), custom_call_target="tpu_custom_call" | custom-call | tf_op jit(solution)/shard_map/rear/pallas_call | solution.py:1118
  455.6 3.1 unpack.1
  (7 shorter events, 0.1 us)
Async XLA Ops:
  4.3 2.0 copy-start
  7.0 1.6 copy-start.1
  7.0 1.6 copy-start.2
  9.3 86.3 %copy-start.3 = (s32[1,13]{1,0:T(1,128)S(1)}, s32[1,13]{1,0:T(1,128)}, u32[]{:S(2)}) copy-start(s32[1,13]{1,0:T(1,128)} %param.26) | copy-start | bytes 160

commit v10 on v9

--- a/solution.py
+++ b/solution.py
@@ -230,12 +230,24 @@
     return raised, inverse, top + jnp.log(total)
 
 
-def tail_parts(q, qkv, at, parent, flag):
+def tail_spans(parent_ref, pair):
+    at = [pl.multiple_of(TRUNK + (2 * pair + side) * SEG, SEG) for side in range(2)]
+    parent = [pl.multiple_of(parent_ref[2 * pair + side] * SEG, SEG) for side in range(2)]
+    return pl.ds(at[0], 2 * SEG), [pl.ds(v, SEG) for v in at], [pl.ds(v, SEG) for v in parent]
+
+
+def by_side(product, left, rights):
+    return jnp.concatenate([product(left[i * SEG:(i + 1) * SEG], right) for i, right in enumerate(rights)], axis=0)
+
+
+def tail_parts(q, qkv, own, parents, flags):
     scale = HEAD ** -0.5
     k_lanes = slice(HEAD, 2 * HEAD)
     trunk = dot_t(q, qkv[:TRUNK, k_lanes]) * scale
-    branch = dot_t(q, qkv[pl.ds(parent, SEG), k_lanes]) * scale + flag
-    own = jnp.where(lower_mask(SEG), dot_t(q, qkv[pl.ds(at, SEG), k_lanes]) * scale, masked_out)
+    branch = by_side(dot_t, q, [qkv[rows, k_lanes] for rows in parents]) * scale
+    branch = branch + jnp.concatenate([jnp.broadcast_to(flag, (SEG, SEG)) for flag in flags], axis=0)
+    mask = jnp.concatenate([lower_mask(SEG)] * 2, axis=0)
+    own = jnp.where(mask, by_side(dot_t, q, [qkv[rows, k_lanes] for rows in own]) * scale, masked_out)
     return [trunk, branch, own]
 
 
@@ -260,15 +272,14 @@
         o_ref[at, :] = (o * inverse).astype(low)
         lse_ref[at, :] = lse
 
-    @pl.loop(0, (qkv.shape[0] - TRUNK) // SEG, unroll=4)
+    @pl.loop(0, (qkv.shape[0] - TRUNK) // (2 * SEG), unroll=3)
     def _(j):
-        at = pl.multiple_of(TRUNK + j * SEG, SEG)
-        parent = pl.multiple_of(parent_ref[j] * SEG, SEG)
-        rows = pl.ds(at, SEG)
-        p, inverse, lse = softmax_parts(tail_parts(qkv[rows, :HEAD], qkv, at, parent, flag_ref[pl.ds(j, 1), :]))
+        rows, own, parents = tail_spans(parent_ref, j)
+        flags = [flag_ref[pl.ds(2 * j + side, 1), :] for side in range(2)]
+        p, inverse, lse = softmax_parts(tail_parts(qkv[rows, :HEAD], qkv, own, parents, flags))
         o = dot(p[0].astype(low), qkv[:TRUNK, v_lanes])
-        o = o + dot(p[1].astype(low), qkv[pl.ds(parent, SEG), v_lanes])
-        o = o + dot(p[2].astype(low), qkv[rows, v_lanes])
+        o = o + by_side(dot, p[1].astype(low), [qkv[at, v_lanes] for at in parents])
+        o = o + by_side(dot, p[2].astype(low), [qkv[at, v_lanes] for at in own])
         o_ref[rows, :] = (o * inverse).astype(low)
         lse_ref[rows, :] = lse
 
@@ -300,21 +311,31 @@
             dk_acc[s, :] += t_dot(d, q)
             dv_acc[s, :] += t_dot(p, d_out)
 
-    @pl.loop(0, (qkv.shape[0] - TRUNK) // SEG, unroll=3)
+    @pl.loop(0, (qkv.shape[0] - TRUNK) // (2 * SEG), unroll=2)
     def _(j):
-        at = pl.multiple_of(TRUNK + j * SEG, SEG)
-        parent = pl.multiple_of(parent_ref[j] * SEG, SEG)
-        rows = pl.ds(at, SEG)
-        spans = [slice(0, TRUNK), pl.ds(parent, SEG), rows]
-        q, d_out = qkv[rows, :HEAD], do_ref[rows, :]
-        d_scores, probs, dq = back_parts(
-            tail_parts(q, qkv, at, parent, flag_ref[pl.ds(j, 1), :]), lse_ref[rows, :], d_out,
-            [qkv[s, k_lanes] for s in spans], [qkv[s, v_lanes] for s in spans],
-        )
+        rows, own, parents = tail_spans(parent_ref, j)
+        flags = [flag_ref[pl.ds(2 * j + side, 1), :] for side in range(2)]
+        q, d_out, lse = qkv[rows, :HEAD], do_ref[rows, :], lse_ref[rows, :]
+        probs = [jnp.exp(s - lse) for s in tail_parts(q, qkv, own, parents, flags)]
+        grads = [
+            dot_t(d_out, qkv[:TRUNK, v_lanes]),
+            by_side(dot_t, d_out, [qkv[at, v_lanes] for at in parents]),
+            by_side(dot_t, d_out, [qkv[at, v_lanes] for at in own]),
+        ]
+        inner = sum(jnp.sum(p * g, axis=1, keepdims=True) for p, g in zip(probs, grads))
+        d_scores = [(p * (g - inner)).astype(low) for p, g in zip(probs, grads)]
+        probs = [p.astype(low) for p in probs]
+        dq = dot(d_scores[0], qkv[:TRUNK, k_lanes])
+        dq = dq + by_side(dot, d_scores[1], [qkv[at, k_lanes] for at in parents])
+        dq = dq + by_side(dot, d_scores[2], [qkv[at, k_lanes] for at in own])
         d_ref[rows, :HEAD] = (dq * scale).astype(low)
-        for s, d, p in zip(spans, d_scores, probs):
-            dk_acc[s, :] += t_dot(d, q)
-            dv_acc[s, :] += t_dot(p, d_out)
+        dk_acc[:TRUNK, :] += t_dot(d_scores[0], q)
+        dv_acc[:TRUNK, :] += t_dot(probs[0], d_out)
+        for part, spans in ((1, parents), (2, own)):
+            for side, at in enumerate(spans):
+                half = slice(side * SEG, (side + 1) * SEG)
+                dk_acc[at, :] += t_dot(d_scores[part][half], q[half])
+                dv_acc[at, :] += t_dot(probs[part][half], d_out[half])
 
     d_ref[:, k_lanes] = (dk_acc[...] * scale).astype(low)
     d_ref[:, v_lanes] = dv_acc[...].astype(low)
@@ -663,7 +684,7 @@
     copy_gu.wait()
 
 
-def front(tokens, table, gain, cot, w_qkv, w_out, w_gu, b_qkv, gain_q, gain_k, cos2, sin2, n, nr, m=32, mh=80):
+def front(tokens, table, gain, cot, w_qkv, w_out, w_gu, b_qkv, gain_q, gain_k, cos2, sin2, n, nr, m=32, mh=160):
     own = tokens.shape[0] // nr
     width = tokens.shape[1]
     rows_all = own * n
@@ -733,7 +754,7 @@
     tree_part = own * nr
     middle_at = n // 2
     chunks = own // m
-    hop = 2
+    hop = 1
     ahead = 2
     left = {"col": jnp.maximum(c - 1, 0)}
     right = {"col": jnp.minimum(c + 1, n - 1)}

time: 459 us -> 457 us (level)
  no operation moved by 1% of the time
where the time goes in v10:
time: 457 us
  Pallas kernels  446 us (98%)
  local copies, waits for them, and re-layouts  5.33 us (1%)
    pallas_call x1, Pallas kernels, middle(): pl.pallas_call(functools.partial(middle_kernel, n, nr, m, hop, cuts), out...  245 us
    pallas_call x1, Pallas kernels, rear(): pl.pallas_call(functools.partial(rear_kernel, n, nr, ndp, m), out_shape=[...  86 us
    pallas_call x1, Pallas kernels, front(): pl.pallas_call(functools.partial(front_kernel, n, nr, m, mh), out_shape=[...  84.7 us
    pallas_call x1, Pallas kernels, attend_back(): pl.pallas_call(attend_back_kernel, grid_spec=pltpu.PrefetchScalarGridSpec...  15.7 us
    pallas_call x1, Pallas kernels, attend(): pl.pallas_call(attend_body, grid_spec=pltpu.PrefetchScalarGridSpec(num_sc...  9.76 us

profile of v10, /device:TPU:0, one launch (start us, length us, event | category | flops | bytes accessed | tf_op | source)
XLA Modules:
  0.0 456.9 jit_solution(10231351876200551097)
XLA Ops:
  0.6 0.8 reshape.65
  1.5 0.1 convert_element_type.23
  1.6 2.1 fusion
  4.3 0.0 copy-start
  4.3 2.0 prep.1
  6.3 0.0 copy-done
  6.3 0.7 copy.35
  7.0 0.0 copy-start.1
  7.0 0.0 copy-start.2
  7.1 1.6 copy.36.wq_hbm
  8.7 0.0 copy-done.2
  8.7 0.6 select_maximum_fusion.gain_ref
  9.3 84.7 %front.1 = (bf16[640,2048]{1,0:T(8,128)(2,1)}, bf16[112,2048]{1,0:T(8,128)(2,1)}, f32[8,2048]{1,0:T(8,128)}, bf16[320,2048]{1,0:T(8,128)(2,1)}, f32[640,1536]{1,...) custom-call(bf16[640,512]{1,0:T(8,128)(2,1)} %tok_ref.1, ...), custom_call_target="tpu_custom_call" | custom-call | tf_op jit(solution)/shard_map/front/pallas_call | solution.py:697
  94.0 0.8 slice.3
  94.8 0.0 copy-done.3
  94.8 0.2 select_reduce_fusion.1
  95.0 0.7 select_reduce_fusion.parent_ref
  95.7 0.7 broadcast_in_dim.69.flag_ref
  96.3 9.8 %attend.1 = (bf16[2560,128]{1,0:T(8,128)(2,1)}, f32[2560,1]{1,0:T(8,128)}) custom-call(s32[12]{0:T(128)} %select_reduce_fusion.parent_ref, f32[12,128]{1,0:T(8,128)} %broadcast_in_dim.69.flag_ref, bf16[2560,384]{1,0:T(8,128)(2,1)} %get-tuple-element.39.qkv), custom_call_target="tpu_custom_call" | custom-call | tf_op jit(solution)/shard_map/attend/pallas_call | solution.py:350
  106.1 245.1 %middle.1 = (bf16[2560,128]{1,0:T(8,128)(2,1)}, bf16[320,2048]{1,0:T(8,128)(2,1)}, f32[320,2048]{1,0:T(8,128)}, f32[64,2048]{1,0:T(8,128)}, f32[16,512]{1,0:T(8,...) custom-call(bf16[2560,128]{1,0:T(8,128)(2,1)} %get-tuple-element.40.head_ref, ...), custom_call_target="tpu_custom_call" | custom-call | tf_op jit(solution)/shard_map/middle/pallas_call | solution.py:1748
  351.2 15.7 %attend_back.1.d_ref = bf16[2560,384]{1,0:T(8,128)(2,1)} custom-call(s32[12]{0:T(128)} %select_reduce_fusion.parent_ref, f32[12,128]{1,0:T(8,128)} %broadcast_in_dim.69.flag_ref, bf16[2560,384]{1,0:T(8,128)(2,1)} %get-tuple-element.39.qkv, bf16[2560,128]{1,0:T(8,128)(2,1)} %get-tuple-element.50.do_ref, f32[2560,1]{1,0:T(8,128)} %get-tuple-element.51.lse_ref), custom_call_target="tpu_custom_call" | custom-call | tf_op jit(solution)/shard_map/attend_back/pallas_call | solution.py:369
  366.9 0.7 iota.28.hot_ref
  367.6 86.0 %rear.1 = (bf16[640,512]{1,0:T(8,128)(2,1)}, bf16[640,512]{1,0:T(8,128)(2,1)}, f32[4,96,512]{2,1,0:T(8,128)}) custom-call(bf16[2560,384]{1,0:T(8,128)(2,1)} %attend_back.1.d_ref, f32[640,1536]{1,0:T(8,128)} %get-tuple-element.52.raw_hbm, f32[4,8,160]{2,1,0:T(8,128)} %get-tuple-element.53.factor_ref, f32[1,512]{1,0:T(1,128)} %bitcast.10, f32[1,512]{1,0:T(1,128)} %bitcast.12, ...), custom_call_target="tpu_custom_call" | custom-call | tf_op jit(solution)/shard_map/rear/pallas_call | solution.py:1139
  453.6 3.1 unpack.1
  (7 shorter events, 0.1 us)
Async XLA Ops:
  4.3 2.0 copy-start
  7.0 1.6 copy-start.1
  7.0 1.6 copy-start.2
  9.3 85.5 %copy-start.3 = (s32[1,13]{1,0:T(1,128)S(1)}, s32[1,13]{1,0:T(1,128)}, u32[]{:S(2)}) copy-start(s32[1,13]{1,0:T(1,128)} %param.26) | copy-start | bytes 160

commit v11 on v10

--- a/solution.py
+++ b/solution.py
@@ -47,17 +47,6 @@
 
 def norm_factor(square_sum):
     return lax.rsqrt(square_sum * (1.0 / D) + epsilon)
-
-
-def tree_tables(seg_ids, parents):
-    tail_seg = seg_ids[TRUNK::SEG]
-    labels = jnp.arange(parents.shape[1], dtype=jnp.int32)
-    tail_parent = jnp.sum(jnp.where(tail_seg[:, None] == labels[None, :], parents[0][None, :], 0), axis=1)
-    hit = (tail_seg[None, :] == tail_parent[:, None])
-    at = jnp.arange(tail_seg.shape[0], dtype=jnp.int32) + TRUNK // SEG
-    parent_at = jnp.sum(jnp.where(hit, at[None, :], 0), axis=1)
-    bias = jnp.where(tail_parent > 0, 0.0, masked_out).astype(wide)
-    return parent_at, jnp.broadcast_to(bias[:, None], (tail_seg.shape[0], SEG))
 
 
 def row_sum(v): return jnp.sum(v, axis=1, keepdims=True)
@@ -175,8 +164,8 @@
     return [dma((5, cuts)), dma((5, cuts)), dma]
 
 
-def prep_kernel(set_ref, fq_ref, sq_ref, fo_ref, so_ref, fg_ref, sg_ref, fd_ref, sd_ref,
-                narrow_ref, bq_ref, ao_ref, bg_ref, ad_ref):
+def prep_kernel(set_ref, seg_ref, parents_ref, ga_ref, gf_ref, fq_ref, sq_ref, fo_ref, so_ref, fg_ref, sg_ref, fd_ref, sd_ref,
+                narrow_ref, bq_ref, ao_ref, bg_ref, ad_ref, gain_ref, hot_ref, flag_ref, at_ref):
     for j in range(3):
         narrow_ref[j * RANK:(j + 1) * RANK, :] = fq_ref[j, 0].astype(low)
         bq_ref[j * RANK:(j + 1) * RANK, :] = sq_ref[j, 0].astype(low)
@@ -187,31 +176,53 @@
     narrow_ref[6 * RANK:, :] = sd_ref[0].astype(low)
     ao_ref[...] = fo_ref[0].astype(low)
     ad_ref[...] = fd_ref[0].astype(low)
-
-
-def prep(tree_sets, tables):
+    gain_ref[...] = jnp.zeros_like(gain_ref)
+    gain_ref[0:1, :] = ga_ref[...]
+    gain_ref[1:2, :] = gf_ref[...]
+    hot_ref[...] = (lax.broadcasted_iota(jnp.int32, hot_ref.shape, 0) == set_ref[0]).astype(wide)
+    tails = flag_ref.shape[0]
+    segments = [seg_ref[TRUNK + j * SEG] for j in range(tails)]
+    for j in range(tails):
+        parent = parents_ref[0, segments[j]]
+        at = jnp.int32(0)
+        for k in range(tails):
+            at = jnp.where(segments[k] == parent, k + TRUNK // SEG, at)
+        at_ref[j] = at
+        flag_ref[j:j + 1, :] = jnp.full((1, SEG), jnp.where(parent > 0, 0.0, masked_out), wide)
+
+
+def prep(tree_sets, seg_ids, parents, gain_a, gain_f, tables):
     fq, sq, fo, so, fg, sg, fd, sd = tables
 
     def pick(table):
         if table.ndim == 4:
-            return pl.BlockSpec((table.shape[0], 1) + table.shape[2:], lambda i, s: (0, s[0], 0, 0))
-        return pl.BlockSpec((1,) + table.shape[1:], lambda i, s: (s[0], 0, 0))
-
-    def out(*shape):
-        return pl.BlockSpec(shape, lambda i, s: (0,) * len(shape)), jax.ShapeDtypeStruct(shape, low)
+            return pl.BlockSpec((table.shape[0], 1) + table.shape[2:], lambda i, s, *_: (0, s[0], 0, 0))
+        return pl.BlockSpec((1,) + table.shape[1:], lambda i, s, *_: (s[0], 0, 0))
+
+    def out(*shape, kind=low):
+        return pl.BlockSpec(shape, lambda i, *_: (0,) * len(shape)), jax.ShapeDtypeStruct(shape, kind)
+
+    tails = (seg_ids.shape[0] - TRUNK) // SEG
+    width = gain_a.shape[1]
+    gain_spec = pl.BlockSpec((1, width), lambda i, *_: (0, 0))
 
     outs = [
         out(7 * RANK, fq.shape[-1]), out(3 * RANK, sq.shape[-1]), out(RANK, fo.shape[-1]),
         out(2, RANK, sg.shape[-1]), out(RANK, fd.shape[-1]),
+        out(8, width, kind=wide), out(fo.shape[0], width, kind=wide), out(tails, SEG, kind=wide),
+        (pl.BlockSpec(memory_space=pltpu.SMEM), jax.ShapeDtypeStruct((tails,), jnp.int32)),
     ]
     return pl.pallas_call(
         prep_kernel,
         grid_spec=pltpu.PrefetchScalarGridSpec(
-            num_scalar_prefetch=1, grid=(1,), in_specs=[pick(t) for t in tables], out_specs=[o[0] for o in outs]
+            num_scalar_prefetch=3,
+            grid=(1,),
+            in_specs=[gain_spec, gain_spec] + [pick(t) for t in tables],
+            out_specs=[o[0] for o in outs],
         ),
         out_shape=[o[1] for o in outs],
         name="prep",
-    )(tree_sets, *tables)
+    )(tree_sets, seg_ids, parents, gain_a, gain_f, *tables)
 
 
 def lower_mask(size):
@@ -1838,14 +1849,14 @@
         down_adapter_first,
         down_adapter_second,
     )
-    narrow, b_qkv, a_out, b_gu, a_down = prep(tree_sets, tables)
-    gain_pair = jnp.pad(jnp.stack([gain_attn, gain_ffn]), ((0, 6), (0, 0)))
+    narrow, b_qkv, a_out, b_gu, a_down, gain_pair, hot, branch_flag, parent_at = prep(
+        tree_sets, seg_ids, parents, gain_attn[None, :], gain_ffn[None, :], tables
+    )
     pos_own = lax.dynamic_index_in_dim(
         positions.reshape(col_count, row_count, own), row_at, 1, keepdims=False
     ).reshape(group)
     cos2, sin2 = angles(pos_own)
     gq, gk = gain_q[None, :], gain_k[None, :]
-    parent_at, branch_flag = tree_tables(seg_ids, parents)
     x, table, gains, g_half, raw, factors, qkv_head, w_qkv, w_out, w_gu = front(
         tokens,
         narrow,
@@ -1879,7 +1890,6 @@
         row_count,
     )
     d_qkv_head = attend_back(qkv_head, d_attn_head, parent_at, branch_flag, lse)
-    hot = (tree_set == lax.broadcasted_iota(jnp.int32, (set_count, width_row), 0)).astype(wide)
     in_grad, layer, sets = rear(
         d_qkv_head,
         raw,

time: 457 us -> 454 us (level)
  no operation moved by 1% of the time
where the time goes in v11:
time: 454 us; the launch traced here: 453 us
  Pallas kernels  447 us (98%)
    pallas_call x1, Pallas kernels, middle(): pl.pallas_call(functools.partial(middle_kernel, n, nr, m, hop, cuts), out...  245 us
    pallas_call x1, Pallas kernels, rear(): pl.pallas_call(functools.partial(rear_kernel, n, nr, ndp, m), out_shape=[...  85.7 us
    pallas_call x1, Pallas kernels, front(): pl.pallas_call(functools.partial(front_kernel, n, nr, m, mh), out_shape=[...  84.7 us
    pallas_call x1, Pallas kernels, attend_back(): pl.pallas_call(attend_back_kernel, grid_spec=pltpu.PrefetchScalarGridSpec...  15.7 us
    pallas_call x1, Pallas kernels, attend(): pl.pallas_call(attend_body, grid_spec=pltpu.PrefetchScalarGridSpec(num_sc...  9.76 us

profile of v11, /device:TPU:0, one launch (start us, length us, event | category | flops | bytes accessed | tf_op | source)
XLA Modules:
  0.0 453.5 jit_solution(12252203986868949764)
XLA Ops:
  1.3 0.8 reshape.54
  2.1 0.1 convert_element_type.18
  2.2 0.0 copy-start
  2.2 2.9 prep.1
  5.2 2.1 fusion
  7.3 0.0 copy-done
  7.3 0.7 copy.33
  8.0 1.6 copy.34.wq_hbm
  9.6 84.7 %front.1 = (bf16[640,2048]{1,0:T(8,128)(2,1)}, bf16[112,2048]{1,0:T(8,128)(2,1)}, f32[8,2048]{1,0:T(8,128)}, bf16[320,2048]{1,0:T(8,128)(2,1)}, f32[640,1536]{1,...) custom-call(bf16[640,512]{1,0:T(8,128)(2,1)} %tok_ref.1, ...), custom_call_target="tpu_custom_call" | custom-call | tf_op jit(solution)/shard_map/front/pallas_call | solution.py:708
  94.2 9.8 %attend.1 = (bf16[2560,128]{1,0:T(8,128)(2,1)}, f32[2560,1]{1,0:T(8,128)}) custom-call(s32[12]{0:T(128)} %get-tuple-element.41.parent_ref, f32[12,128]{1,0:T(8,128)} %get-tuple-element.42.flag_ref, bf16[2560,384]{1,0:T(8,128)(2,1)} %get-tuple-element.46.qkv), custom_call_target="tpu_custom_call" | custom-call | tf_op jit(solution)/shard_map/attend/pallas_call | solution.py:361
  104.0 244.9 %middle.1 = (bf16[2560,128]{1,0:T(8,128)(2,1)}, bf16[320,2048]{1,0:T(8,128)(2,1)}, f32[320,2048]{1,0:T(8,128)}, f32[64,2048]{1,0:T(8,128)}, f32[16,512]{1,0:T(8,...) custom-call(bf16[2560,128]{1,0:T(8,128)(2,1)} %get-tuple-element.47.head_ref, ...), custom_call_target="tpu_custom_call" | custom-call | tf_op jit(solution)/shard_map/middle/pallas_call | solution.py:1759
  348.9 15.7 %attend_back.1.d_ref = bf16[2560,384]{1,0:T(8,128)(2,1)} custom-call(s32[12]{0:T(128)} %get-tuple-element.41.parent_ref, f32[12,128]{1,0:T(8,128)} %get-tuple-element.42.flag_ref, bf16[2560,384]{1,0:T(8,128)(2,1)} %get-tuple-element.46.qkv, bf16[2560,128]{1,0:T(8,128)(2,1)} %get-tuple-element.57.do_ref, f32[2560,1]{1,0:T(8,128)} %get-tuple-element.58.lse_ref), custom_call_target="tpu_custom_call" | custom-call | tf_op jit(solution)/shard_map/attend_back/pallas_call | solution.py:380
  364.6 85.7 %rear.1 = (bf16[640,512]{1,0:T(8,128)(2,1)}, bf16[640,512]{1,0:T(8,128)(2,1)}, f32[4,96,512]{2,1,0:T(8,128)}) custom-call(bf16[2560,384]{1,0:T(8,128)(2,1)} %attend_back.1.d_ref, f32[640,1536]{1,0:T(8,128)} %get-tuple-element.59.raw_hbm, f32[4,8,160]{2,1,0:T(8,128)} %get-tuple-element.60.factor_ref, f32[1,512]{1,0:T(1,128)} %bitcast.7, f32[1,512]{1,0:T(1,128)} %bitcast.9, ...), custom_call_target="tpu_custom_call" | custom-call | tf_op jit(solution)/shard_map/rear/pallas_call | solution.py:1150
  450.2 3.1 unpack.1
  (2 shorter events, 0.0 us)
Async XLA Ops:
  2.2 5.0 %copy-start = (bf16[512,3,512]{2,0,1:T(8,128)(2,1)S(1)}, bf16[512,3,512]{2,0,1:T(8,128)(2,1)}, u32[]{:S(2)}) copy-start(bf16[512,3,512]{2,0,1:T(8,128)(2,1)} %param.32) | copy-start | bytes 4718596

commit v12 on v11

--- a/solution.py
+++ b/solution.py
@@ -322,7 +322,7 @@
             dk_acc[s, :] += t_dot(d, q)
             dv_acc[s, :] += t_dot(p, d_out)
 
-    @pl.loop(0, (qkv.shape[0] - TRUNK) // (2 * SEG), unroll=2)
+    @pl.loop(0, (qkv.shape[0] - TRUNK) // (2 * SEG), unroll=3)
     def _(j):
         rows, own, parents = tail_spans(parent_ref, j)
         flags = [flag_ref[pl.ds(2 * j + side, 1), :] for side in range(2)]
@@ -766,7 +766,7 @@
     middle_at = n // 2
     chunks = own // m
     hop = 1
-    ahead = 2
+    ahead = 3
     left = {"col": jnp.maximum(c - 1, 0)}
     right = {"col": jnp.minimum(c + 1, n - 1)}
     load_raw = pltpu.make_async_copy(raw_hbm, raw_ref, load.at[0])

time: 454 us -> 454 us (level)
  no operation moved by 1% of the time
where the time goes in v12:
time: 454 us; the launch traced here: 453 us
  Pallas kernels  447 us (98%)
    pallas_call x1, Pallas kernels, middle(): pl.pallas_call(functools.partial(middle_kernel, n, nr, m, hop, cuts), out...  245 us
    pallas_call x1, Pallas kernels, rear(): pl.pallas_call(functools.partial(rear_kernel, n, nr, ndp, m), out_shape=[...  85.7 us
    pallas_call x1, Pallas kernels, front(): pl.pallas_call(functools.partial(front_kernel, n, nr, m, mh), out_shape=[...  84.7 us
    pallas_call x1, Pallas kernels, attend_back(): pl.pallas_call(attend_back_kernel, grid_spec=pltpu.PrefetchScalarGridSpec...  15.6 us
    pallas_call x1, Pallas kernels, attend(): pl.pallas_call(attend_body, grid_spec=pltpu.PrefetchScalarGridSpec(num_sc...  9.76 us

profile of v12, /device:TPU:0, one launch (start us, length us, event | category | flops | bytes accessed | tf_op | source)
XLA Modules:
  0.0 453.4 jit_solution(5051983617949113270)
XLA Ops:
  1.3 0.8 reshape.54
  2.1 0.1 convert_element_type.18
  2.2 0.0 copy-start
  2.2 2.9 prep.1
  5.2 2.1 fusion
  7.3 0.0 copy-done
  7.3 0.7 copy.33
  8.0 1.6 copy.34.wq_hbm
  9.6 84.7 %front.1 = (bf16[640,2048]{1,0:T(8,128)(2,1)}, bf16[112,2048]{1,0:T(8,128)(2,1)}, f32[8,2048]{1,0:T(8,128)}, bf16[320,2048]{1,0:T(8,128)(2,1)}, f32[640,1536]{1,...) custom-call(bf16[640,512]{1,0:T(8,128)(2,1)} %tok_ref.1, ...), custom_call_target="tpu_custom_call" | custom-call | tf_op jit(solution)/shard_map/front/pallas_call | solution.py:708
  94.2 9.8 %attend.1 = (bf16[2560,128]{1,0:T(8,128)(2,1)}, f32[2560,1]{1,0:T(8,128)}) custom-call(s32[12]{0:T(128)} %get-tuple-element.41.parent_ref, f32[12,128]{1,0:T(8,128)} %get-tuple-element.42.flag_ref, bf16[2560,384]{1,0:T(8,128)(2,1)} %get-tuple-element.46.qkv), custom_call_target="tpu_custom_call" | custom-call | tf_op jit(solution)/shard_map/attend/pallas_call | solution.py:361
  104.0 244.9 %middle.1 = (bf16[2560,128]{1,0:T(8,128)(2,1)}, bf16[320,2048]{1,0:T(8,128)(2,1)}, f32[320,2048]{1,0:T(8,128)}, f32[64,2048]{1,0:T(8,128)}, f32[16,512]{1,0:T(8,...) custom-call(bf16[2560,128]{1,0:T(8,128)(2,1)} %get-tuple-element.47.head_ref, ...), custom_call_target="tpu_custom_call" | custom-call | tf_op jit(solution)/shard_map/middle/pallas_call | solution.py:1759
  348.9 15.6 %attend_back.1.d_ref = bf16[2560,384]{1,0:T(8,128)(2,1)} custom-call(s32[12]{0:T(128)} %get-tuple-element.41.parent_ref, f32[12,128]{1,0:T(8,128)} %get-tuple-element.42.flag_ref, bf16[2560,384]{1,0:T(8,128)(2,1)} %get-tuple-element.46.qkv, bf16[2560,128]{1,0:T(8,128)(2,1)} %get-tuple-element.57.do_ref, f32[2560,1]{1,0:T(8,128)} %get-tuple-element.58.lse_ref), custom_call_target="tpu_custom_call" | custom-call | tf_op jit(solution)/shard_map/attend_back/pallas_call | solution.py:380
  364.5 85.7 %rear.1 = (bf16[640,512]{1,0:T(8,128)(2,1)}, bf16[640,512]{1,0:T(8,128)(2,1)}, f32[4,96,512]{2,1,0:T(8,128)}) custom-call(bf16[2560,384]{1,0:T(8,128)(2,1)} %attend_back.1.d_ref, f32[640,1536]{1,0:T(8,128)} %get-tuple-element.59.raw_hbm, f32[4,8,160]{2,1,0:T(8,128)} %get-tuple-element.60.factor_ref, f32[1,512]{1,0:T(1,128)} %bitcast.7, f32[1,512]{1,0:T(1,128)} %bitcast.9, ...), custom_call_target="tpu_custom_call" | custom-call | tf_op jit(solution)/shard_map/rear/pallas_call | solution.py:1150
  450.2 3.1 unpack.1
  (2 shorter events, 0.0 us)
Async XLA Ops:
  2.2 5.0 %copy-start = (bf16[512,3,512]{2,0,1:T(8,128)(2,1)S(1)}, bf16[512,3,512]{2,0,1:T(8,128)(2,1)}, u32[]{:S(2)}) copy-start(bf16[512,3,512]{2,0,1:T(8,128)(2,1)} %param.32) | copy-start | bytes 4718596
